TPU v7x, 32 devices: a whole 2x2x4 slice. The times are simulated.
32 devices in a mesh: dp: 8 (over z, x), tensor: 4 (over y, core).
Axes of the slice: x: 2, y: 2, z: 4, core: 2. Of those that a mesh axis runs over, the one named last changes fastest.
Arguments:
- x_in: bfloat16 [4096, 1536], P('dp'), may hold values from -6 to 6
- lengths: int32 [8], P('dp'), may hold values from 256 to 512, as said below
- routes: int32 [4096, 6], P('dp'), may hold values from 0 to 63, all different within a row; in each aligned block of 512 rows (0 to 511, 512 to 1023, ...) at most 64 rows name the same one
- route_w: float32 [4096, 6], P('dp'), may hold values from 0.08 to 0.32
- ln1_gain: float32 [1536], replicated, may hold values from 0.5 to 1.5
- w_zx: float32 [1536, 2, 3072], P('dp', None, 'tensor'), may hold values from -0.15625 to 0.15625
- w_bc: float32 [1536, 256], P('dp'), may hold values from -0.15625 to 0.15625
- w_dt: float32 [1536, 48], P('dp', 'tensor'), may hold values from -0.15625 to 0.15625
- conv_x: float32 [4, 3072], P(None, 'tensor'), may hold values from -3 to 3
- conv_x_bias: float32 [3072], P('tensor'), may hold values from -2 to 2
- conv_bc: float32 [4, 256], replicated, may hold values from -3 to 3
- conv_bc_bias: float32 [256], replicated, may hold values from -2 to 2
- dt_bias: float32 [48], P('tensor'), may hold values from -6 to -2
- a_log: float32 [48], P('tensor'), may hold values from 0 to 2.8
- d_skip: float32 [48], P('tensor'), may hold values from 0.5 to 1.5
- gnorm_gain: float32 [3072], P('tensor'), may hold values from 0.5 to 1.5
- w_out: float32 [1536, 3072], P('dp', 'tensor'), may hold values from -0.109375 to 0.109375
- ln2_gain: float32 [1536], replicated, may hold values from 0.5 to 1.5
- w_shared_gu: float32 [1536, 2, 1024], P('dp', None, 'tensor'), may hold values from -0.15625 to 0.15625
- w_shared_down: float32 [1536, 1024], P('dp', 'tensor'), may hold values from -0.1875 to 0.1875
- w_exp_gu: float32 [64, 1536, 2, 512], P('dp', None, None, 'tensor'), may hold values from -0.15625 to 0.15625
- w_exp_down: float32 [64, 512, 1536], P('dp', 'tensor'), may hold values from -0.25 to 0.25
- cotangent: bfloat16 [4096, 1536], P('dp'), may hold values from -6 to 6
Outputs:
- out: bfloat16 [4096, 1536], P('dp')
- grad_x: float32 [4096, 1536], P('dp')
- grad_ln1: float32 [1536], replicated
- grad_w_zx: float32 [1536, 2, 3072], P('dp', None, 'tensor')
- grad_w_bc: float32 [1536, 256], P('dp')
- grad_w_dt: float32 [1536, 48], P('dp', 'tensor')
- grad_conv_x: float32 [4, 3072], P(None, 'tensor')
- grad_conv_x_bias: float32 [3072], P('tensor')
- grad_conv_bc: float32 [4, 256], replicated
- grad_conv_bc_bias: float32 [256], replicated
- grad_dt_bias: float32 [48], P('tensor')
- grad_a_log: float32 [48], P('tensor')
- grad_d_skip: float32 [48], P('tensor')
- grad_gnorm: float32 [3072], P('tensor')
- grad_w_out: float32 [1536, 3072], P('dp', 'tensor')
- grad_ln2: float32 [1536], replicated
- grad_w_shared_gu: float32 [1536, 2, 1024], P('dp', None, 'tensor')
- grad_w_shared_down: float32 [1536, 1024], P('dp', 'tensor')
- grad_w_exp_gu: float32 [64, 1536, 2, 512], P('dp', None, None, 'tensor')
- grad_w_exp_down: float32 [64, 512, 1536], P('dp', 'tensor')
Inputs may be any that keep to these rules, and one draw needn't show every extreme that they name: `routes`: in the 512 rows of one index of dp no expert is named by more than 64 rows; in some of these blocks an expert is named by exactly 64. `lengths`: the sequence of one index of dp fills all 512 slots.
All inputs are finite; a program needn't handle non-finite values.
Results may differ from a plain program's by a relative error of at most 0.025.
Values may be sent and summed in bfloat16 or wider, within the bound.
A program may use at most 320 MiB of HBM per device.

v0:
```python
import jax
import jax.numpy as jnp
from jax import lax
from jax.sharding import PartitionSpec as P

BLOCK = 256


EPSILON = 1e-05
HIGHEST = lax.Precision.HIGHEST


def rms_scale(values):
    return lax.rsqrt(jnp.mean(values * values, axis=-1, keepdims=True) + EPSILON)


def silu_parts(values):
    sigmoid_val = jax.nn.sigmoid(values)
    return (values * sigmoid_val, sigmoid_val * (1.0 + values * (1.0 - sigmoid_val)))


def round_keep(values):
    return lax.optimization_barrier(values.astype(jnp.bfloat16)).astype(jnp.float32)


def causal_conv(signal, kernel, offset):
    kernel_width = kernel.shape[0]
    seq_length = signal.shape[0]
    padded = jnp.concatenate(
        [jnp.zeros((kernel_width - 1, signal.shape[1]), signal.dtype), signal], axis=0
    )
    summed = offset[None, :] + kernel[0][None, :] * padded[0:seq_length]
    for tap_index in range(1, kernel_width):
        summed = summed + kernel[tap_index][None, :] * padded[tap_index : tap_index + seq_length]
    return summed


def ssd_scan(head_values, step_sizes, log_rates, b_rows, c_rows, skip_gain, block_rows):
    seq_length, n_heads, head_size = head_values.shape
    n_state = b_rows.shape[1]
    n_blocks = seq_length // block_rows
    decay_rates = -jnp.exp(log_rates)[None, :] * step_sizes
    scaled = (head_values * step_sizes[:, :, None]).reshape(
        n_blocks, block_rows, n_heads, head_size
    )
    cumulative = jnp.cumsum(decay_rates.reshape(n_blocks, block_rows, n_heads), axis=1)
    b_block = b_rows.reshape(n_blocks, block_rows, n_state)
    c_block = c_rows.reshape(n_blocks, block_rows, n_state)
    positions = jnp.arange(block_rows)
    causal = (positions[:, None] >= positions[None, :])[None, :, :, None]
    differences = cumulative[:, :, None, :] - cumulative[:, None, :, :]
    decay_mask = jnp.where(causal, jnp.exp(jnp.where(causal, differences, 0.0)), 0.0)
    intersection = jnp.einsum("kin,kjn->kij", c_block, b_block, precision=HIGHEST)
    within = jnp.einsum("kij,kijh,kjhp->kihp", intersection, decay_mask, scaled, precision=HIGHEST)
    block_end = cumulative[:, -1, :]
    to_end = jnp.exp(block_end[:, None, :] - cumulative)
    states = jnp.einsum("kjn,kjh,kjhp->khnp", b_block, to_end, scaled, precision=HIGHEST)

    def carry_state(previous, inputs):
        block_decay, block_state = inputs
        return (block_decay[:, None, None] * previous + block_state, previous)

    final_state, entering = lax.scan(
        carry_state,
        jnp.zeros((n_heads, n_state, head_size), head_values.dtype),
        (jnp.exp(block_end), states),
    )
    across = jnp.einsum(
        "kin,khnp,kih->kihp", c_block, entering, jnp.exp(cumulative), precision=HIGHEST
    )
    return (within + across).reshape(seq_length, n_heads, head_size) + skip_gain[
        None, :, None
    ] * head_values


def local(
    x_in,
    lengths,
    routes,
    route_w,
    ln1_gain,
    w_zx,
    w_bc,
    w_dt,
    conv_x,
    conv_x_bias,
    conv_bc,
    conv_bc_bias,
    dt_bias,
    a_log,
    d_skip,
    gnorm_gain,
    w_out,
    ln2_gain,
    w_shared_gu,
    w_shared_down,
    w_exp_gu,
    w_exp_down,
    cotangent,
):
    slot_count = x_in.shape[0]
    model_width = x_in.shape[1]
    route_count = routes.shape[1]
    data_devices = lax.axis_size("dp")
    tensor_devices = lax.axis_size("tensor")
    local_experts = w_exp_gu.shape[0]
    expert_count = data_devices * local_experts
    capacity = slot_count * route_count * 4 // (3 * expert_count)
    local_heads = dt_bias.shape[0]
    local_inner = conv_x.shape[1]
    head_size = local_inner // local_heads
    state_size = conv_bc.shape[1] // 2
    full_inner = local_inner * tensor_devices
    pair_count = slot_count * route_count
    proj_zx, proj_bc, proj_dt, proj_out, shared_gu, shared_down = (
        lax.all_gather(w_zx.astype(jnp.bfloat16), "dp", axis=0, tiled=True),
        lax.all_gather(w_bc.astype(jnp.bfloat16), "dp", axis=0, tiled=True),
        lax.all_gather(w_dt.astype(jnp.bfloat16), "dp", axis=0, tiled=True),
        lax.all_gather(w_out.astype(jnp.bfloat16), "dp", axis=0, tiled=True),
        lax.all_gather(w_shared_gu.astype(jnp.bfloat16), "dp", axis=0, tiled=True),
        lax.all_gather(w_shared_down.astype(jnp.bfloat16), "dp", axis=0, tiled=True),
    )
    x_float = x_in.astype(jnp.float32)
    scale_one = rms_scale(x_float)
    normed_one = (x_float * scale_one * ln1_gain).astype(jnp.bfloat16)
    zx_proj = jnp.einsum("td,dcf->tcf", normed_one, proj_zx, preferred_element_type=jnp.float32)
    bc_proj = jnp.dot(normed_one, proj_bc, preferred_element_type=jnp.float32)
    dt_proj = jnp.dot(normed_one, proj_dt, preferred_element_type=jnp.float32)

    def conv_block(x_part, bc_part, kernel_x, offset_x, kernel_bc, offset_bc):
        return (
            jax.nn.silu(causal_conv(x_part, kernel_x, offset_x)),
            jax.nn.silu(causal_conv(bc_part, kernel_bc, offset_bc)),
        )

    (conv_values, conv_bc_values), conv_back = jax.vjp(
        conv_block, zx_proj[:, 1], bc_proj, conv_x, conv_x_bias, conv_bc, conv_bc_bias
    )
    head_input = round_keep(conv_values)
    bc_input = round_keep(conv_bc_values)

    def scan_block(head_flat, b_rows, c_rows, dt_part, z_part, dt_offset, log_rates, skip_gain):
        step_sizes = jax.nn.softplus(dt_part + dt_offset[None, :])
        output = ssd_scan(
            head_flat.reshape(slot_count, local_heads, head_size),
            step_sizes,
            log_rates,
            b_rows,
            c_rows,
            skip_gain,
            BLOCK,
        )
        return output.reshape(slot_count, local_inner) * jax.nn.silu(z_part)

    gated_mix, scan_back = jax.vjp(
        scan_block,
        head_input,
        bc_input[:, :state_size],
        bc_input[:, state_size:],
        dt_proj,
        zx_proj[:, 0],
        dt_bias,
        a_log,
        d_skip,
    )
    squares = lax.psum(jnp.sum(gated_mix * gated_mix, axis=-1), "tensor")
    scale_mix = lax.rsqrt(squares / full_inner + EPSILON)[:, None]
    normed_mix = (gated_mix * scale_mix * gnorm_gain).astype(jnp.bfloat16)
    mixer_out = lax.psum(
        jnp.einsum("tc,dc->td", normed_mix, proj_out, preferred_element_type=jnp.float32).astype(
            jnp.bfloat16
        ),
        "tensor",
    ).astype(jnp.float32)
    hidden_one = x_float + mixer_out
    scale_two = rms_scale(hidden_one)
    normed_two = (hidden_one * scale_two * ln2_gain).astype(jnp.bfloat16)
    shared_pre = jnp.einsum(
        "td,dcf->tcf", normed_two, shared_gu, preferred_element_type=jnp.float32
    )
    shared_silu, shared_slope = silu_parts(shared_pre[:, 0])
    shared_act = (shared_silu * shared_pre[:, 1]).astype(jnp.bfloat16)
    shared_part = jnp.einsum(
        "tf,df->td", shared_act, shared_down, preferred_element_type=jnp.float32
    )
    expert_ids = routes.reshape(pair_count)
    one_hot = (expert_ids[:, None] == jnp.arange(expert_count, dtype=jnp.int32)[None, :]).astype(
        jnp.int32
    )
    position = jnp.sum(jnp.cumsum(one_hot, axis=0) * one_hot, axis=1) - 1
    slot_of_pair = expert_ids * capacity + position
    pair_of_slot = (
        jnp.zeros((expert_count * capacity,), jnp.int32)
        .at[slot_of_pair]
        .set(jnp.arange(pair_count, dtype=jnp.int32))
    )
    filled = jnp.zeros((expert_count * capacity,), jnp.bool_).at[slot_of_pair].set(True)
    send_rows = jnp.where(
        filled[:, None], normed_two[pair_of_slot // route_count], jnp.zeros((), jnp.bfloat16)
    ).reshape(data_devices, local_experts, capacity, model_width)
    gate_weights = w_exp_gu.astype(jnp.bfloat16)
    down_weights = w_exp_down.astype(jnp.bfloat16)
    gate_use, down_use = (gate_weights, down_weights)
    member = jnp.zeros((), jnp.int32)
    owner_match = position // capacity == member
    local_slot = expert_ids * capacity + position % capacity

    def expert_front(routed_rows):
        return jnp.einsum(
            "secd,edgf->secgf", routed_rows, gate_use, preferred_element_type=jnp.float32
        )

    pre_act = expert_front(lax.all_to_all(send_rows, "dp", split_axis=0, concat_axis=0, tiled=True))
    activated = (jax.nn.silu(pre_act[:, :, :, 0]) * pre_act[:, :, :, 1]).astype(jnp.bfloat16)
    piece = jnp.einsum("secf,efd->secd", activated, down_use, preferred_element_type=jnp.float32)
    piece = round_keep(piece)
    total = piece
    partial_out = total.astype(jnp.bfloat16)
    dispatched = partial_out
    partial_out = dispatched
    returned = lax.all_to_all(partial_out, "dp", split_axis=0, concat_axis=0, tiled=True).astype(
        jnp.float32
    )
    returned = returned.reshape(expert_count * capacity, model_width)
    weights_flat = route_w.reshape(pair_count) * owner_match.astype(jnp.float32)
    moe_part = jnp.sum(
        (returned[local_slot] * weights_flat[:, None]).reshape(
            slot_count, route_count, model_width
        ),
        axis=1,
    )
    ffn_out = lax.psum((shared_part + moe_part).astype(jnp.bfloat16), "tensor").astype(jnp.float32)
    hidden_two = hidden_one + ffn_out
    layer_out = hidden_two.astype(jnp.bfloat16)
    live_mask = (jnp.arange(slot_count, dtype=jnp.int32) < lengths[0]).astype(jnp.float32)
    grad_two = cotangent.astype(jnp.float32) * live_mask[:, None]
    grad_low = grad_two.astype(jnp.bfloat16)
    grad_shared_down = jnp.einsum(
        "td,tf->df", grad_low, shared_act, preferred_element_type=jnp.float32
    )
    grad_shared_act = jnp.einsum(
        "td,df->tf", grad_low, shared_down, preferred_element_type=jnp.float32
    )
    grad_shared_pre = jnp.stack(
        [grad_shared_act * shared_pre[:, 1] * shared_slope, grad_shared_act * shared_silu], axis=1
    ).astype(jnp.bfloat16)
    grad_shared_gu = jnp.einsum(
        "td,tcf->dcf", normed_two, grad_shared_pre, preferred_element_type=jnp.float32
    )
    grad_normed_shared = jnp.einsum(
        "tcf,dcf->td", grad_shared_pre, shared_gu, preferred_element_type=jnp.float32
    )
    grad_pairs = (
        (grad_two[:, None, :] * route_w[:, :, None])
        .reshape(pair_count, model_width)
        .astype(jnp.bfloat16)
    )
    send_grads = jnp.where(
        filled[:, None], grad_pairs[pair_of_slot], jnp.zeros((), jnp.bfloat16)
    ).reshape(data_devices, local_experts, capacity, model_width)
    recv_grads, routed_rows = (
        lax.all_to_all(send_grads, "dp", split_axis=0, concat_axis=0, tiled=True),
        lax.all_to_all(send_rows, "dp", split_axis=0, concat_axis=0, tiled=True),
    )
    pre_act = expert_front(routed_rows)
    act_silu, act_slope = silu_parts(pre_act[:, :, :, 0])
    activated = (act_silu * pre_act[:, :, :, 1]).astype(jnp.bfloat16)
    grad_act = jnp.einsum(
        "secd,efd->secf", recv_grads, down_use, preferred_element_type=jnp.float32
    )
    grad_down_all = jnp.einsum(
        "secf,secd->efd", activated, recv_grads, preferred_element_type=jnp.float32
    )
    grad_pre = jnp.stack(
        [grad_act * pre_act[:, :, :, 1] * act_slope, grad_act * act_silu], axis=3
    ).astype(jnp.bfloat16)
    grad_gu_all = jnp.einsum(
        "secd,secgf->edgf", routed_rows, grad_pre, preferred_element_type=jnp.float32
    )
    piece = jnp.einsum("secgf,edgf->secd", grad_pre, gate_use, preferred_element_type=jnp.float32)
    piece = round_keep(piece)
    grad_exp_gu, grad_exp_down = (grad_gu_all, grad_down_all)
    grad_back = lax.all_to_all(
        piece.astype(jnp.bfloat16), "dp", split_axis=0, concat_axis=0, tiled=True
    ).astype(jnp.float32)
    grad_back = grad_back.reshape(expert_count * capacity, model_width)
    grad_normed_moe = jnp.sum(
        (grad_back[local_slot] * owner_match.astype(jnp.float32)[:, None]).reshape(
            slot_count, route_count, model_width
        ),
        axis=1,
    )
    grad_normed_two = lax.psum(
        (grad_normed_shared + grad_normed_moe).astype(jnp.bfloat16), "tensor"
    ).astype(jnp.float32)
    weighted_two = ln2_gain * grad_normed_two
    grad_ln2 = jnp.sum(grad_normed_two * hidden_one * scale_two, axis=0)
    grad_one = (
        grad_two
        + scale_two * weighted_two
        - hidden_one * scale_two**3 * jnp.mean(weighted_two * hidden_one, axis=-1, keepdims=True)
    )
    grad_mix_low = grad_one.astype(jnp.bfloat16)
    grad_out_proj = jnp.einsum(
        "td,tc->dc", grad_mix_low, normed_mix, preferred_element_type=jnp.float32
    )
    grad_normed_mix = jnp.einsum(
        "td,dc->tc", grad_mix_low, proj_out, preferred_element_type=jnp.float32
    )
    weighted_mix = gnorm_gain * grad_normed_mix
    grad_gnorm = jnp.sum(grad_normed_mix * gated_mix * scale_mix, axis=0)
    product_sum = lax.psum(jnp.sum(weighted_mix * gated_mix, axis=-1), "tensor")[:, None]
    grad_gated = scale_mix * weighted_mix - gated_mix * scale_mix**3 * product_sum / full_inner
    grad_head, grad_b, grad_c, grad_dt_proj, grad_z, grad_dt_bias, grad_a_log, grad_d_skip = (
        scan_back(grad_gated)
    )
    (
        grad_xs,
        grad_bc_part,
        grad_conv_x,
        grad_conv_x_bias,
        grad_conv_bc_part,
        grad_conv_bc_bias_part,
    ) = conv_back((grad_head, jnp.concatenate([grad_b, grad_c], axis=1)))
    grad_zx_low = jnp.stack([grad_z, grad_xs], axis=1).astype(jnp.bfloat16)
    grad_dt_low = grad_dt_proj.astype(jnp.bfloat16)
    grad_proj_zx = jnp.einsum(
        "td,tcf->dcf", normed_one, grad_zx_low, preferred_element_type=jnp.float32
    )
    grad_proj_dt = jnp.einsum(
        "td,th->dh", normed_one, grad_dt_low, preferred_element_type=jnp.float32
    )
    grad_bc_weight_part = jnp.dot(normed_one.astype(jnp.float32).T, grad_bc_part, precision=HIGHEST)
    grad_input_part = (
        jnp.einsum("tcf,dcf->td", grad_zx_low, proj_zx, preferred_element_type=jnp.float32)
        + jnp.einsum("th,dh->td", grad_dt_low, proj_dt, preferred_element_type=jnp.float32)
        + jnp.dot(grad_bc_part, proj_bc.astype(jnp.float32).T, precision=HIGHEST)
    )
    grad_normed_one, grad_proj_bc, grad_conv_bc, grad_conv_bc_bias = (
        lax.psum(grad_input_part.astype(jnp.bfloat16), "tensor").astype(jnp.float32),
        lax.psum(grad_bc_weight_part.astype(jnp.bfloat16), "tensor").astype(jnp.float32),
        lax.psum(grad_conv_bc_part.astype(jnp.bfloat16), "tensor").astype(jnp.float32),
        lax.psum(grad_conv_bc_bias_part.astype(jnp.bfloat16), "tensor").astype(jnp.float32),
    )
    weighted_one = ln1_gain * grad_normed_one
    grad_ln1 = jnp.sum(grad_normed_one * x_float * scale_one, axis=0)
    grad_input = (
        grad_one
        + scale_one * weighted_one
        - x_float * scale_one**3 * jnp.mean(weighted_one * x_float, axis=-1, keepdims=True)
    )
    (
        grad_zx_shard,
        grad_bc_shard,
        grad_dt_shard,
        grad_out_shard,
        grad_sgu_shard,
        grad_sdown_shard,
    ) = (
        lax.psum_scatter(
            grad_proj_zx.astype(jnp.bfloat16), "dp", scatter_dimension=0, tiled=True
        ).astype(jnp.float32),
        lax.psum_scatter(
            grad_proj_bc.astype(jnp.bfloat16), "dp", scatter_dimension=0, tiled=True
        ).astype(jnp.float32),
        lax.psum_scatter(
            grad_proj_dt.astype(jnp.bfloat16), "dp", scatter_dimension=0, tiled=True
        ).astype(jnp.float32),
        lax.psum_scatter(
            grad_out_proj.astype(jnp.bfloat16), "dp", scatter_dimension=0, tiled=True
        ).astype(jnp.float32),
        lax.psum_scatter(
            grad_shared_gu.astype(jnp.bfloat16), "dp", scatter_dimension=0, tiled=True
        ).astype(jnp.float32),
        lax.psum_scatter(
            grad_shared_down.astype(jnp.bfloat16), "dp", scatter_dimension=0, tiled=True
        ).astype(jnp.float32),
    )
    small_sums = (
        lax.psum(grad_ln1.astype(jnp.bfloat16), "dp").astype(jnp.float32),
        lax.psum(grad_ln2.astype(jnp.bfloat16), "dp").astype(jnp.float32),
        lax.psum(grad_conv_x.astype(jnp.bfloat16), "dp").astype(jnp.float32),
        lax.psum(grad_conv_x_bias.astype(jnp.bfloat16), "dp").astype(jnp.float32),
        lax.psum(grad_conv_bc.astype(jnp.bfloat16), "dp").astype(jnp.float32),
        lax.psum(grad_conv_bc_bias.astype(jnp.bfloat16), "dp").astype(jnp.float32),
        lax.psum(grad_dt_bias.astype(jnp.bfloat16), "dp").astype(jnp.float32),
        lax.psum(grad_a_log.astype(jnp.bfloat16), "dp").astype(jnp.float32),
        lax.psum(grad_d_skip.astype(jnp.bfloat16), "dp").astype(jnp.float32),
        lax.psum(grad_gnorm.astype(jnp.bfloat16), "dp").astype(jnp.float32),
    )
    return (
        layer_out,
        grad_input,
        small_sums[0],
        grad_zx_shard,
        grad_bc_shard,
        grad_dt_shard,
        small_sums[2],
        small_sums[3],
        small_sums[4],
        small_sums[5],
        small_sums[6],
        small_sums[7],
        small_sums[8],
        small_sums[9],
        grad_out_shard,
        small_sums[1],
        grad_sgu_shard,
        grad_sdown_shard,
        grad_exp_gu,
        grad_exp_down,
    )


def solution(mesh):
    return jax.shard_map(
        local,
        mesh=mesh,
        in_specs=(
            P("dp", None),
            P("dp"),
            P("dp", None),
            P("dp", None),
            P(),
            P("dp", None, "tensor"),
            P("dp", None),
            P("dp", "tensor"),
            P(None, "tensor"),
            P("tensor"),
            P(),
            P(),
            P("tensor"),
            P("tensor"),
            P("tensor"),
            P("tensor"),
            P("dp", "tensor"),
            P(),
            P("dp", None, "tensor"),
            P("dp", "tensor"),
            P("dp", None, None, "tensor"),
            P("dp", "tensor", None),
            P("dp", None),
        ),
        out_specs=(
            P("dp", None),
            P("dp", None),
            P(),
            P("dp", None, "tensor"),
            P("dp", None),
            P("dp", "tensor"),
            P(None, "tensor"),
            P("tensor"),
            P(),
            P(),
            P("tensor"),
            P("tensor"),
            P("tensor"),
            P("tensor"),
            P("dp", "tensor"),
            P(),
            P("dp", None, "tensor"),
            P("dp", "tensor"),
            P("dp", None, None, "tensor"),
            P("dp", "tensor", None),
        ),
        check_vma=False,
    )
```

profile of v0, /device:TPU:9, one launch (start us, length us, event | category | flops | bytes accessed | tf_op | source)
XLA Modules:
  0.0 2243.1 jit_solution(15063568436089207688)
XLA Ops:
  11.5 22.5 %all-gather = bf16[8,192,12]{1,2,0:T(8,128)(2,1)S(1)} all-gather(bf16[1,192,12]{1,2,0:T(8,128)(2,1)S(1)} %convert_bitcast_fusion.1), channel_id=1, replica_groups=mesh['dp'=8,'tensor'=4] {'dp'}, dimensions={0}, use_global_device_ids=true | all-gather | bytes 41472 | tf_op jit(solution)/shard_map/all_gather | solution.py:118
  40.3 31.0 %all_gather.18 = bf16[1536,256]{1,0:T(8,128)(2,1)S(1)} all-gather(bf16[192,256]{1,0:T(8,128)(2,1)S(1)} %convert_element_type.242), channel_id=1, replica_groups=mesh['dp'=8,'tensor'=4] {'dp'}, dimensions={0}, use_global_device_ids=true | all-gather | bytes 884736 | tf_op jit(solution)/shard_map/all_gather | solution.py:117
  75.3 31.9 %reduce-window.24 = s32[64,24,128]{2,1,0:T(8,128)S(1)} reduce-window(s32[64,24,128]{2,1,0:T(8,128)} %fusion.148, s32[]{:T(128)} %constant.150.clone.1), window={size=1x1x128 pad=0_0x0_0x127_0}, to_apply=%region_9.10 | reduce-window | flops 24969216 | bytes 1572868 | tf_op jit(solution)/shard_map/reduce-window.2
  124.2 22.2 mul.708
  202.7 16.3 psum.133
  225.9 11.8 scatter_custom_fusion.1
  237.7 13.4 scatter_custom_fusion
  251.2 30.2 %gather_fusion.2 = bf16[4096,1536]{1,0:T(8,128)(2,1)} fusion(bf16[3072,1536]{1,0:T(8,128)(2,1)} %multiply_convert_fusion, s32[4096]{0:T(1024)S(1)} %get-tuple-element.515), kind=kCustom, calls=%fused_computation.2 | custom fusion | bytes 25182208 | tf_op jit(solution)/shard_map/gather | solution.py:259
  284.7 19.3 gather_fusion
  303.9 13.6 broadcast_select_fusion
  317.6 278.3 %all_to_all.21 = bf16[8,8,64,1536]{3,2,1,0:T(8,128)(2,1)} all-to-all(bf16[8,8,64,1536]{3,2,1,0:T(8,128)(2,1)S(1)} %get-tuple-element.518), channel_id=1, replica_groups=mesh['dp'=8,'tensor'=4] {'dp'}, dimensions={0} | all-to-all | bytes 25165824 | tf_op jit(solution)/shard_map/all_to_all | solution.py:213
  611.8 11.8 fusion.68
  623.6 250.0 %all-to-all-done.2 = bf16[8,8,64,1536]{3,2,1,0:T(8,128)(2,1)} async-done(((bf16[8,8,64,1536]{3,2,1,0:T(8,128)(2,1)}), bf16[8,8,64,1536]{3,2,1,0:T(8,128)(2,1)}, u32[]{:S(2)}, u32[]{:S(2)}) %all-to-all-start.2) | async-done | bytes 12582944 | tf_op jit(solution)/shard_map/all_to_all | solution.py:262
  873.6 12.6 fusion.128
  886.2 12.1 fusion.20
  934.9 251.6 %all-to-all-done.3 = bf16[8,8,64,1536]{3,2,1,0:T(8,128)(2,1)} async-done(((bf16[8,8,64,1536]{3,2,1,0:T(8,128)(2,1)}), bf16[8,8,64,1536]{3,2,1,0:T(8,128)(2,1)}, u32[]{:S(2)}, u32[]{:S(2)}) %all-to-all-start.3) | async-done | bytes 12582944 | tf_op jit(solution)/shard_map/all_to_all | solution.py:283
  1194.3 308.2 %all_gather.23 = bf16[1536,256]{1,0:T(8,128)(2,1)} all-gather(bf16[192,256]{1,0:T(8,128)(2,1)S(1)} %convert_element_type.255), channel_id=1, replica_groups=mesh['dp'=8,'tensor'=4] {'dp'}, dimensions={0}, use_global_device_ids=true | all-gather | bytes 884736 | tf_op jit(solution)/shard_map/all_gather | solution.py:121
  1506.7 14.8 bitcast_convert_fusion.1
  1521.5 28.8 %gather_fusion.3 = f32[3072,1536]{1,0:T(8,128)} fusion(f32[4096,1536]{1,0:T(8,128)} %bitcast_convert_fusion.1, s32[3072]{0:T(1024)S(1)} %broadcast_clamp_fusion), kind=kCustom, calls=%fused_computation.3 | custom fusion | bytes 37761024 | tf_op jit(solution)/shard_map/gather | solution.py:288
  1550.2 21.3 gather.27
  1571.5 33.0 %multiply_reduce_fusion = f32[512,1536]{1,0:T(8,128)S(1)} fusion(f32[512,6,1536]{2,1,0:T(8,128)} %gather.27, f32[512,6]{1,0:T(8,128)S(1)} %get-tuple-element.479), kind=kLoop, calls=%fused_computation.20 | loop fusion | flops 8650752 | bytes 22032384 | tf_op jit(solution)/shard_map/reduce_sum | solution.py:287
  1606.8 47.9 %all-reduce.28.cloned.1.call-done = bf16[512,1536]{1,0:T(8,128)(2,1)} async-done(((bf16[512,1536]{1,0:T(8,128)(2,1)}), bf16[512,1536]{1,0:T(8,128)(2,1)}) %all-reduce.28.cloned.1.call-update) | async-done | bytes 1572880 | tf_op jit(solution)/shard_map/psum | solution.py:293
  1742.8 14.9 bitcast_convert_fusion.2
  1757.7 28.9 %gather_fusion.1 = f32[3072,1536]{1,0:T(8,128)} fusion(f32[4096,1536]{1,0:T(8,128)} %bitcast_convert_fusion.2, s32[3072]{0:T(1024)S(1)} %broadcast_clamp_fusion), kind=kCustom, calls=%fused_computation.1 | custom fusion | bytes 37761024 | tf_op jit(solution)/shard_map/gather | solution.py:227
  1786.5 21.3 gather.23
  1807.9 33.1 %multiply_reduce_fusion.1 = f32[512,1536]{1,0:T(8,128)S(1)} fusion(f32[512,6,1536]{2,1,0:T(8,128)} %gather.23, f32[512,6]{1,0:T(8,128)S(1)} %copy-done.47), kind=kLoop, calls=%fused_computation.21 | loop fusion | flops 8650752 | bytes 22032384 | tf_op jit(solution)/shard_map/reduce_sum | solution.py:226
  1902.3 20.7 reduce-scatter.13.cloned.1.call-done
  1932.3 35.2 %copy.300 = f32[8,1536,2,128]{3,2,1,0:T(2,128)} copy(f32[8,1536,2,128]{3,1,2,0:T(8,128)S(1)} %fusion.13) | data formatting | bytes 25165824
  1988.2 73.1 %all-reduce.30.cloned.1.call-done = (bf16[512,1536]{1,0:T(8,128)(2,1)}, bf16[512,1536]{1,0:T(8,128)(2,1)}, bf16[192,256]{1,0:T(8,128)(2,1)}) async-done(((bf16[512,1536]{1,0:T(8,128)(2,1)}, bf16[512,1536]{1,0:T(8,128)(2,1)}, bf16[192,256]{1,0:T(8,128)(2,1)}), (bf16[512,1536]{1,0:T(8,128)(2,1)}, bf16[512,1536]{1,0:T(8,128)(2,1)}, bf16[192,256]{1,0:T(8,128)(2,1)})) %all-reduce.30.cloned.1.call-update) | async-done | bytes 3244048 | tf_op jit(solution)/shard_map/psum | solution.py:232
  2064.1 28.3 %all-reduce.19 = (bf16[1536]{0:T(1024)(128)(2,1)S(1)}, bf16[4,768]{1,0:T(4,128)(2,1)S(1)}, bf16[768]{0:T(1024)(128)(2,1)S(1)}, bf16[4,256]{1,0:T(4,128)(2,1)S(1)...) all-reduce(bf16[1536]{0:T(1024)(128)(2,1)S(1)} %get-tuple-element.4, ...), channel_id=1, replica_groups=mesh['dp'=8,'tensor'=4] {'dp'}, use_global_device_ids=true, to_apply=%region_33.34 | all-reduce | flops 8996 | bytes 35984 | tf_op jit(solution)/shard_map/psum | solution.py:380
  2103.8 29.2 %reduce-scatter.11.cloned.1.call-done = bf16[192,768]{1,0:T(8,128)(2,1)} async-done(((bf16[1536,768]{1,0:T(8,128)(2,1)}), bf16[192,768]{1,0:T(8,128)(2,1)}) %reduce-scatter.11.cloned.1.call-update) | async-done | bytes 294928 | tf_op jit(solution)/shard_map/reduce_scatter | solution.py:369
  2134.8 98.5 %reduce-scatter.9.cloned.1.call-done = bf16[192,2,768]{2,0,1:T(8,128)(2,1)} async-done(((bf16[1536,2,768]{2,0,1:T(8,128)(2,1)}), bf16[192,2,768]{2,0,1:T(8,128)(2,1)}) %reduce-scatter.9.cloned.1.call-update) | async-done | bytes 589840 | tf_op jit(solution)/shard_map/reduce_scatter | solution.py:360
  (580 shorter events, 378.5 us)
Async XLA Ops:
  7.2 152.3 %all-gather.5.cloned.1.call-start = ((), (), s32[]{:S(2)}) async-start(), calls=%async_computation.10 | async-start | bytes 5308416 | tf_op jit(solution)/shard_map/all_gather | solution.py:116
  9.6 210.0 %all-gather.7.cloned.1.call-start = ((), (), s32[]{:S(2)}) async-start(), calls=%async_computation.11 | async-start | bytes 2654208 | tf_op jit(solution)/shard_map/all_gather | solution.py:119
  10.4 270.9 %all-reduce.26.cloned.1.call-start = ((), (), s32[]{:S(2)}) async-start(), calls=%async_computation.12 | async-start | bytes 3145728 | tf_op jit(solution)/shard_map/psum | solution.py:169
  11.5 59.9 %copy-start.115 = (f32[512]{0:T(512)}, f32[512]{0:T(512)S(1)}, u32[]{:S(2)}) copy-start(f32[512]{0:T(512)S(1)} %get-tuple-element.524) | copy-start | bytes 6148
  35.5 38.1 %copy-start.77 = (f32[512,12]{0,1:T(8,128)}, f32[512,12]{0,1:T(8,128)S(1)}, u32[]{:S(2)}) copy-start(f32[512,12]{0,1:T(8,128)S(1)} %get-tuple-element.511) | copy-start | bytes 73732
  37.8 134.9 %copy-start.49 = (f32[2,256,12]{1,2,0:T(8,128)}, f32[2,256,12]{1,2,0:T(8,128)S(1)}, u32[]{:S(2)}) copy-start(f32[2,256,12]{1,2,0:T(8,128)S(1)} %get-tuple-element.510) | copy-start | bytes 73732
  73.5 73.1 %copy-start.34 = (bf16[512,128]{1,0:T(8,128)(2,1)}, bf16[512,128]{1,0:T(8,128)(2,1)S(1)}, u32[]{:S(2)}) copy-start(bf16[512,128]{1,0:T(8,128)(2,1)S(1)} %get-tuple-element.506) | copy-start | bytes 393220
  73.5 99.2 %copy-start.32 = (bf16[512,128]{1,0:T(8,128)(2,1)}, bf16[512,128]{1,0:T(8,128)(2,1)S(1)}, u32[]{:S(2)}) copy-start(bf16[512,128]{1,0:T(8,128)(2,1)S(1)} %get-tuple-element.507) | copy-start | bytes 393220
  73.6 99.1 %copy-start.56 = (f32[2,256,12]{1,2,0:T(8,128)}, f32[2,256,12]{1,2,0:T(8,128)S(1)}, u32[]{:S(2)}) copy-start(f32[2,256,12]{1,2,0:T(8,128)S(1)} %copy.250) | copy-start | bytes 73732
  74.4 125.6 %copy-start.89 = (f32[768]{0:T(1024)}, f32[768]{0:T(1024)S(1)}, u32[]{:S(2)}) copy-start(f32[768]{0:T(1024)S(1)} %mul.675) | copy-start | bytes 9220
  110.6 113.9 %copy-start.78 = (s32[3072]{0:T(1024)}, s32[3072]{0:T(1024)S(1)}, u32[]{:S(2)}) copy-start(s32[3072]{0:T(1024)S(1)} %broadcast_add_fusion.3) | copy-start | bytes 36868
  595.9 277.7 %all-to-all-start.2 = ((bf16[8,8,64,1536]{3,2,1,0:T(8,128)(2,1)}), bf16[8,8,64,1536]{3,2,1,0:T(8,128)(2,1)}, u32[]{:S(2)}, u32[]{:S(2)}) async-start(bf16[8,8,64,1536]{3,2,1,0:T(8,128)(2,1)} %get-tuple-element.517), calls=%async_computation.2 | async-start | bytes 25165824 | tf_op jit(solution)/shard_map/all_to_all | solution.py:262
  909.1 277.5 %all-to-all-start.3 = ((bf16[8,8,64,1536]{3,2,1,0:T(8,128)(2,1)}), bf16[8,8,64,1536]{3,2,1,0:T(8,128)(2,1)}, u32[]{:S(2)}, u32[]{:S(2)}) async-start(bf16[8,8,64,1536]{3,2,1,0:T(8,128)(2,1)} %bitcast.361), calls=%async_computation.3 | async-start | bytes 25165824 | tf_op jit(solution)/shard_map/all_to_all | solution.py:283
  934.8 257.6 %copy-start.66 = (f32[192,2,256]{2,1,0:T(2,128)S(1)}, f32[192,2,256]{2,1,0:T(2,128)}, u32[]{:S(2)}) copy-start(f32[192,2,256]{2,1,0:T(2,128)} %param.45) | copy-start | bytes 1179652
  934.9 258.4 %copy-start.79 = (s32[3072]{0:T(1024)S(1)}, s32[3072]{0:T(1024)}, u32[]{:S(2)}) copy-start(s32[3072]{0:T(1024)} %copy-done.78) | copy-start | bytes 36868
  934.9 258.6 %copy-start.76 = (f32[192,256]{1,0:T(8,128)S(1)}, f32[192,256]{1,0:T(8,128)}, u32[]{:S(2)}) copy-start(f32[192,256]{1,0:T(8,128)} %param.46) | copy-start | bytes 589828
  934.9 258.7 %copy-start.92 = (s32[3072,1]{0,1:T(1,128)S(1)}, s32[3072,1]{0,1:T(1,128)}, u32[]{:S(2)}) copy-start(s32[3072,1]{0,1:T(1,128)} %get-tuple-element.513) | copy-start | bytes 36868
  1186.5 556.2 %all-to-all-start.1 = ((bf16[8,8,64,1536]{3,2,1,0:T(8,128)(2,1)}), bf16[8,8,64,1536]{3,2,1,0:T(8,128)(2,1)}, u32[]{:S(2)}, u32[]{:S(2)}) async-start(bf16[8,8,64,1536]{3,2,1,0:T(8,128)(2,1)} %copy.267), calls=%async_computation.1 | async-start | bytes 25165824 | tf_op jit(solution)/shard_map/all_to_all | solution.py:221
  1192.1 310.4 %all-gather.9.cloned.1.call-start = ((), (), s32[]{:S(2)}) async-start(), calls=%async_computation.13 | async-start | bytes 1769472 | tf_op jit(solution)/shard_map/all_gather | solution.py:120
  1193.2 461.4 %all-reduce.28.cloned.1.call-start = ((), (), s32[]{:S(2)}) async-start(), calls=%async_computation.14 | async-start | bytes 3145728 | tf_op jit(solution)/shard_map/psum | solution.py:293
  1606.7 48.0 %copy-start.82 = (f32[1536]{0:T(1024)S(1)}, f32[1536]{0:T(1024)}, u32[]{:S(2)}) copy-start(f32[1536]{0:T(1024)} %param.44) | copy-start | bytes 18436
  1606.7 48.0 %copy-start.106 = (f32[512]{0:T(512)S(1)}, f32[512]{0:T(512)}, u32[]{:S(2)}) copy-start(f32[512]{0:T(512)} %copy-done.105) | copy-start | bytes 6148
  1606.7 281.4 %reduce-scatter.17.cloned.1.call-start = ((), (), s32[]{:S(2)}) async-start(), calls=%async_computation.19 | async-start | bytes 884736 | tf_op jit(solution)/shard_map/reduce_scatter | solution.py:363
  1606.8 52.2 %copy-start.135 = (f32[512]{0:T(512)S(1)}, f32[512]{0:T(512)}, u32[]{:S(2)}) copy-start(f32[512]{0:T(512)} %get-tuple-element.527) | copy-start | bytes 6148
  1729.0 171.7 %reduce-scatter.15.cloned.1.call-start = ((), (), s32[]{:S(2)}) async-start(), calls=%async_computation.18 | async-start | bytes 884736 | tf_op jit(solution)/shard_map/reduce_scatter | solution.py:375
  1732.2 190.8 %reduce-scatter.13.cloned.1.call-start = ((), (), s32[]{:S(2)}) async-start(), calls=%async_computation.17 | async-start | bytes 1769472 | tf_op jit(solution)/shard_map/reduce_scatter | solution.py:372
  1742.7 244.0 %reduce-scatter.19.cloned.1.call-start = ((), (), s32[]{:S(2)}) async-start(), calls=%async_computation.20 | async-start | bytes 442368
  1878.4 182.9 %all-reduce.30.cloned.1.call-start = ((), (), s32[]{:S(2)}) async-start(), calls=%async_computation.21 | async-start | bytes 6488064 | tf_op jit(solution)/shard_map/psum | solution.py:232
  1888.2 244.8 %reduce-scatter.11.cloned.1.call-start = ((), (), s32[]{:S(2)}) async-start(), calls=%async_computation.16 | async-start | bytes 2654208 | tf_op jit(solution)/shard_map/reduce_scatter | solution.py:369
  1894.5 338.8 %reduce-scatter.9.cloned.1.call-start = ((), (), s32[]{:S(2)}) async-start(), calls=%async_computation.15 | async-start | bytes 5308416 | tf_op jit(solution)/shard_map/reduce_scatter | solution.py:360
  2061.4 37.5 %copy-start.5 = (bf16[512,1536]{1,0:T(8,128)(2,1)S(1)}, bf16[512,1536]{1,0:T(8,128)(2,1)}, u32[]{:S(2)}) copy-start(bf16[512,1536]{1,0:T(8,128)(2,1)} %all-reduce.26.cloned.1.call-done) | copy-start | bytes 4718596
  2061.4 37.5 %copy-start.137 = (f32[512]{0:T(512)S(1)}, f32[512]{0:T(512)}, u32[]{:S(2)}) copy-start(f32[512]{0:T(512)} %get-tuple-element.523) | copy-start | bytes 6148
  (149 other events, 968.2 us)
Sparse Core Ops, SparseCore 0:
  10.8 92.9 all-gather.4
  106.5 51.0 all-gather.6
  224.6 45.0 all-reduce.25
  1195.3 228.5 all-gather.8
  1606.8 47.7 all-reduce.27
  1729.2 61.1 reduce-scatter.16
  1794.1 61.4 reduce-scatter.14
  1859.0 63.9 reduce-scatter.12
  1926.6 60.1 reduce-scatter.18
  1989.8 71.4 all-reduce.29
  2065.2 67.6 reduce-scatter.10
  2136.9 96.3 reduce-scatter.8
where the time goes:
time: 2250 us; the launch traced here: 2240 us
  waiting for transfers between devices  773 us (34%)
  blocking collectives  698 us (31%)
  local copies, waits for them, and re-layouts  329 us (15%)
  other arithmetic  240 us (11%)
  matrix products  166 us (7%)
    all_gather x1, blocking collectives, local(): lax.all_gather(w_shared_down.astype(jnp.bfloat16), 'dp', axis=0, tiled=True)  308 us
    all_to_all x1, blocking collectives, local(): lax.all_to_all(send_rows, 'dp', split_axis=0, concat_axis=0, tiled=True)  278 us
    all_to_all x1, waiting for transfers between devices, local(): lax.all_to_all(piece.astype(jnp.bfloat16), 'dp', split_axis=0, concat_axi...  252 us
    all_to_all x1, waiting for transfers between devices, local(): lax.all_to_all(send_grads, 'dp', split_axis=0, concat_axis=0, tiled=True)  250 us
    reduce_scatter x1, waiting for transfers between devices, local(): lax.psum_scatter(grad_proj_zx.astype(jnp.bfloat16), 'dp', scatter_dimensi...  98.5 us
    psum x1, waiting for transfers between devices, local(): lax.psum((shared_part + moe_part).astype(jnp.bfloat16), 'tensor')  73.1 us
    unnamed x328, local copies, waits for them, and re-layouts  56 us
    gather x2, local copies, waits for them, and re-layouts, local(): returned[local_slot] * weights_flat[:, None]  50.2 us
  transfers between devices with their start and end apart: 15, of which 8 were waited for; matrix products, arithmetic and copies ran while one was open for 29% of the time, Pallas kernels for 0%

commit v1 on v0

v1 whole, which is shorter than its diff:
```python
import jax
import jax.numpy as jnp
from jax import lax
from jax.sharding import PartitionSpec as P

BLOCK = 256


EPSILON = 1e-05
HIGHEST = lax.Precision.HIGHEST
BF = jnp.bfloat16
F32 = jnp.float32


def rms_scale(values):
    return lax.rsqrt(jnp.mean(values * values, axis=-1, keepdims=True) + EPSILON)


def silu_parts(values):
    sigmoid_val = jax.nn.sigmoid(values)
    return (values * sigmoid_val, sigmoid_val * (1.0 + values * (1.0 - sigmoid_val)))


def round_keep(values):
    return lax.optimization_barrier(values.astype(BF)).astype(F32)


def dotf(spec, a, b):
    return jnp.einsum(spec, a, b, preferred_element_type=F32)


def causal_conv(signal, kernel, offset):
    kernel_width = kernel.shape[0]
    seq_length = signal.shape[0]
    padded = jnp.concatenate(
        [jnp.zeros((kernel_width - 1, signal.shape[1]), signal.dtype), signal], axis=0
    )
    summed = offset[None, :] + kernel[0][None, :] * padded[0:seq_length]
    for tap_index in range(1, kernel_width):
        summed = summed + kernel[tap_index][None, :] * padded[tap_index : tap_index + seq_length]
    return summed


def ssd_scan(head_values, step_sizes, log_rates, b_rows, c_rows, skip_gain, block_rows):
    seq_length, n_heads, head_size = head_values.shape
    n_state = b_rows.shape[1]
    n_blocks = seq_length // block_rows
    decay_rates = -jnp.exp(log_rates)[None, :] * step_sizes
    scaled = (head_values * step_sizes[:, :, None]).reshape(
        n_blocks, block_rows, n_heads, head_size
    )
    cumulative = jnp.cumsum(decay_rates.reshape(n_blocks, block_rows, n_heads), axis=1)
    b_block = b_rows.reshape(n_blocks, block_rows, n_state)
    c_block = c_rows.reshape(n_blocks, block_rows, n_state)
    positions = jnp.arange(block_rows)
    causal = (positions[:, None] >= positions[None, :])[None, :, :, None]
    differences = cumulative[:, :, None, :] - cumulative[:, None, :, :]
    decay_mask = jnp.where(causal, jnp.exp(jnp.where(causal, differences, 0.0)), 0.0)
    intersection = jnp.einsum("kin,kjn->kij", c_block, b_block, precision=HIGHEST)
    within = jnp.einsum("kij,kijh,kjhp->kihp", intersection, decay_mask, scaled, precision=HIGHEST)
    block_end = cumulative[:, -1, :]
    to_end = jnp.exp(block_end[:, None, :] - cumulative)
    states = jnp.einsum("kjn,kjh,kjhp->khnp", b_block, to_end, scaled, precision=HIGHEST)

    def carry_state(previous, inputs):
        block_decay, block_state = inputs
        return (block_decay[:, None, None] * previous + block_state, previous)

    final_state, entering = lax.scan(
        carry_state,
        jnp.zeros((n_heads, n_state, head_size), head_values.dtype),
        (jnp.exp(block_end), states),
    )
    across = jnp.einsum(
        "kin,khnp,kih->kihp", c_block, entering, jnp.exp(cumulative), precision=HIGHEST
    )
    return (within + across).reshape(seq_length, n_heads, head_size) + skip_gain[
        None, :, None
    ] * head_values


def mixer_forward(
    zx, bc_proj, dt_proj, conv_x, conv_x_bias, conv_bc, conv_bc_bias, dt_bias, a_log, d_skip
):
    slots = zx.shape[0]
    inner = conv_x.shape[1]
    heads = dt_bias.shape[0]
    state = conv_bc.shape[1] // 2

    def conv_block(x_part, bc_part, kernel_x, offset_x, kernel_bc, offset_bc):
        return (
            jax.nn.silu(causal_conv(x_part, kernel_x, offset_x)),
            jax.nn.silu(causal_conv(bc_part, kernel_bc, offset_bc)),
        )

    (conv_values, conv_bc_values), conv_back = jax.vjp(
        conv_block, zx[:, inner:], bc_proj, conv_x, conv_x_bias, conv_bc, conv_bc_bias
    )
    head_input = round_keep(conv_values)
    bc_input = round_keep(conv_bc_values)

    def scan_block(head_flat, b_rows, c_rows, dt_part, z_part, dt_offset, log_rates, skip_gain):
        step_sizes = jax.nn.softplus(dt_part + dt_offset[None, :])
        output = ssd_scan(
            head_flat.reshape(slots, heads, inner // heads),
            step_sizes,
            log_rates,
            b_rows,
            c_rows,
            skip_gain,
            BLOCK,
        )
        return output.reshape(slots, inner) * jax.nn.silu(z_part)

    gated_mix, scan_back = jax.vjp(
        scan_block,
        head_input,
        bc_input[:, :state],
        bc_input[:, state:],
        dt_proj,
        zx[:, :inner],
        dt_bias,
        a_log,
        d_skip,
    )

    def mixer_back(grad_gated):
        g_head, g_b, g_c, g_dt, g_z, g_dt_bias, g_a_log, g_d_skip = scan_back(grad_gated)
        g_xs, g_bc, g_cx, g_cxb, g_cbc, g_cbcb = conv_back(
            (g_head, jnp.concatenate([g_b, g_c], axis=1))
        )
        g_zx = jnp.concatenate([g_z, g_xs], axis=1).astype(BF)
        return (
            g_zx, g_bc, g_dt.astype(BF), g_cx, g_cxb, g_cbc, g_cbcb, g_dt_bias, g_a_log, g_d_skip
        )

    return gated_mix, mixer_back


def local(
    x_in,
    lengths,
    routes,
    route_w,
    ln1_gain,
    w_zx,
    w_bc,
    w_dt,
    conv_x,
    conv_x_bias,
    conv_bc,
    conv_bc_bias,
    dt_bias,
    a_log,
    d_skip,
    gnorm_gain,
    w_out,
    ln2_gain,
    w_shared_gu,
    w_shared_down,
    w_exp_gu,
    w_exp_down,
    cotangent,
):
    slots, width = x_in.shape
    n_dp = lax.axis_size("dp")
    n_t = lax.axis_size("tensor")
    my_t = lax.axis_index("tensor")
    my_dp = lax.axis_index("dp")
    piece = slots // n_t
    n_local = w_exp_gu.shape[0]
    n_experts = n_dp * n_local
    cap = slots * routes.shape[1] * 4 // (3 * n_experts)
    if cap > slots:
        cap = slots
    heads = dt_bias.shape[0]
    inner = conv_x.shape[1]
    head_size = inner // heads
    state = conv_bc.shape[1] // 2
    full_inner = inner * n_t
    rows = w_zx.shape[0]
    n_sh = w_shared_gu.shape[2]
    everyone = ("dp", "tensor")

    first = jnp.concatenate(
        [w_zx.reshape(rows, 2 * inner), w_bc, w_dt], axis=1
    ).astype(BF)
    second = jnp.concatenate(
        [w_out, w_shared_gu.reshape(rows, 2 * n_sh), w_shared_down], axis=1
    ).astype(BF)
    first = lax.all_gather(first, "dp", axis=0, tiled=True)
    second = lax.all_gather(second, "dp", axis=0, tiled=True)
    proj_zx = first[:, : 2 * inner]
    proj_bc = first[:, 2 * inner : 2 * inner + 2 * state]
    proj_dt = first[:, 2 * inner + 2 * state :]
    proj_out = second[:, :inner]
    shared_gu = second[:, inner : inner + 2 * n_sh]
    shared_down = second[:, inner + 2 * n_sh :]

    live = (jnp.arange(slots, dtype=jnp.int32) < lengths[0]).astype(F32)
    g2 = cotangent.astype(F32) * live[:, None]
    g2_low = g2.astype(BF)
    expert_range = jnp.arange(n_experts, dtype=jnp.int32)
    chosen = routes[:, :, None] == expert_range[None, None, :]
    weights = jnp.sum(jnp.where(chosen, route_w[:, :, None], 0.0), axis=1)
    weights = lax.all_gather(weights, "dp", axis=0, tiled=True)
    weights = lax.dynamic_slice_in_dim(weights, my_dp * n_local, n_local, axis=1)
    weights = weights.reshape(n_dp, slots, n_local)
    member = (weights > 0.0).astype(BF)
    before = (
        jnp.arange(slots)[:, None] > jnp.arange(slots)[None, :]
    ).astype(BF)
    position = dotf("ut,ste->sue", before, member).astype(jnp.int32)
    position = jnp.where(weights > 0.0, position, -1)
    pick = (
        position.transpose(0, 2, 1)[:, :, None, :]
        == jnp.arange(cap, dtype=jnp.int32)[None, None, :, None]
    )
    slot_weight = jnp.sum(
        jnp.where(pick, weights.transpose(0, 2, 1)[:, :, None, :], 0.0), axis=-1
    )
    pick = pick.astype(BF).reshape(n_dp, n_local * cap, slots)

    g2_piece = lax.dynamic_slice_in_dim(g2_low, my_t * piece, piece, axis=0)
    g2_all = lax.all_gather(g2_piece, everyone, axis=0, tiled=True).reshape(n_dp, slots, width)

    gate_w = w_exp_gu.astype(BF).reshape(n_local, width, -1)
    down_w = w_exp_down.astype(BF)

    x_float = x_in.astype(F32)
    scale_one = rms_scale(x_float)
    normed_one = (x_float * scale_one * ln1_gain).astype(BF)
    zx = dotf("td,df->tf", normed_one, proj_zx)
    bc_proj = dotf("td,df->tf", normed_one, proj_bc)
    dt_proj = dotf("td,df->tf", normed_one, proj_dt)

    gated_mix, mixer_back = mixer_forward(
        zx, bc_proj, dt_proj, conv_x, conv_x_bias, conv_bc, conv_bc_bias, dt_bias, a_log, d_skip
    )
    squares = lax.psum(jnp.sum(gated_mix * gated_mix, axis=-1), "tensor")
    scale_mix = lax.rsqrt(squares / full_inner + EPSILON)[:, None]
    normed_mix = (gated_mix * scale_mix * gnorm_gain).astype(BF)
    mixer_part = dotf("tc,dc->td", normed_mix, proj_out).astype(BF)
    mixer_out = lax.psum_scatter(
        mixer_part, "tensor", scatter_dimension=0, tiled=True
    ).astype(F32)
    x_piece = lax.dynamic_slice_in_dim(x_float, my_t * piece, piece, axis=0)
    hidden_one = x_piece + mixer_out
    scale_two = rms_scale(hidden_one)
    normed_two = (hidden_one * scale_two * ln2_gain).astype(BF)
    all_rows = lax.all_gather(normed_two, everyone, axis=0, tiled=True)
    mine = lax.dynamic_slice_in_dim(all_rows, my_dp * slots, slots, axis=0)
    all_rows = all_rows.reshape(n_dp, slots, width)

    shared_pre = dotf("td,df->tf", mine, shared_gu)
    s_gate, s_up = shared_pre[:, :n_sh], shared_pre[:, n_sh:]
    shared_silu, shared_slope = silu_parts(s_gate)
    shared_act = (shared_silu * s_up).astype(BF)
    grad_shared_act = dotf("td,df->tf", g2_low, shared_down)
    grad_shared_pre = jnp.concatenate(
        [grad_shared_act * s_up * shared_slope, grad_shared_act * shared_silu], axis=1
    ).astype(BF)
    grad_normed_shared = dotf("tf,df->td", grad_shared_pre, shared_gu)
    shared_part = dotf("tf,df->td", shared_act, shared_down)

    def by_expert(v):
        return v.reshape(n_dp, n_local, cap, v.shape[-1]).transpose(1, 0, 2, 3).reshape(
            n_local, n_dp * cap, v.shape[-1]
        )

    def by_source(v):
        return v.reshape(n_local, n_dp, cap, v.shape[-1]).transpose(1, 0, 2, 3).reshape(
            n_dp, n_local * cap, v.shape[-1]
        )

    sw = slot_weight.transpose(1, 0, 2).reshape(n_local, n_dp * cap, 1)
    q = by_expert(dotf("sct,std->scd", pick, g2_all))
    q = (q * sw).astype(BF)
    grad_act = dotf("erd,efd->erf", q, down_w)
    xr = by_expert(dotf("sct,std->scd", pick, all_rows).astype(BF))
    pre = dotf("erd,edf->erf", xr, gate_w)
    n_f = pre.shape[-1] // 2
    p_gate, p_up = pre[..., :n_f], pre[..., n_f:]
    act_silu, act_slope = silu_parts(p_gate)
    act = (act_silu * p_up).astype(BF)
    grad_pre = jnp.concatenate(
        [grad_act * p_up * act_slope, grad_act * act_silu], axis=-1
    ).astype(BF)
    back = by_source(dotf("erf,edf->erd", grad_pre, gate_w).astype(BF))
    dxn_part = dotf("sct,scd->std", pick, back)
    own = (jnp.arange(n_dp) == my_dp).astype(F32)[:, None, None]
    dxn_part = (dxn_part + own * grad_normed_shared[None]).astype(BF)
    grad_normed_two = lax.psum_scatter(
        dxn_part.reshape(n_dp * slots, width), everyone, scatter_dimension=0, tiled=True
    ).astype(F32)

    forth = by_source((dotf("erf,efd->erd", act, down_w) * sw).astype(BF))
    out_part = dotf("sct,scd->std", pick, forth)
    out_part = (out_part + own * shared_part[None]).astype(BF)
    ffn_out = lax.psum_scatter(
        out_part.reshape(n_dp * slots, width), everyone, scatter_dimension=0, tiled=True
    ).astype(F32)
    layer_out = lax.all_gather(
        (hidden_one + ffn_out).astype(BF), "tensor", axis=0, tiled=True
    )
    grad_exp_down = dotf("erf,erd->efd", act, q)
    grad_exp_gu = dotf("erd,erf->edf", xr, grad_pre).reshape(w_exp_gu.shape)
    grad_shared_down = dotf("td,tf->df", g2_low, shared_act)
    grad_shared_gu = dotf("td,tf->df", mine, grad_shared_pre)

    weighted_two = ln2_gain * grad_normed_two
    grad_ln2 = jnp.sum(grad_normed_two * hidden_one * scale_two, axis=0)
    g2_own = g2_piece.astype(F32)
    grad_one = (
        g2_own
        + scale_two * weighted_two
        - hidden_one * scale_two**3 * jnp.mean(weighted_two * hidden_one, axis=-1, keepdims=True)
    )
    dm = lax.all_gather(grad_one.astype(BF), "tensor", axis=0, tiled=True)
    grad_out_proj = dotf("td,tc->dc", dm, normed_mix)
    grad_normed_mix = dotf("td,dc->tc", dm, proj_out)
    weighted_mix = gnorm_gain * grad_normed_mix
    grad_gnorm = jnp.sum(grad_normed_mix * gated_mix * scale_mix, axis=0)
    product_sum = lax.psum(jnp.sum(weighted_mix * gated_mix, axis=-1), "tensor")[:, None]
    grad_gated = scale_mix * weighted_mix - gated_mix * scale_mix**3 * product_sum / full_inner
    (
        grad_zx,
        grad_bc,
        grad_dt_low,
        grad_conv_x,
        grad_conv_x_bias,
        grad_conv_bc,
        grad_conv_bc_bias,
        grad_dt_bias,
        grad_a_log,
        grad_d_skip,
    ) = mixer_back(grad_gated)
    bc_low = grad_bc.astype(BF)
    grad_first = jnp.concatenate([grad_zx, bc_low, grad_dt_low], axis=1)
    grad_input_part = dotf("tf,df->td", grad_first, first)
    grad_input_piece = lax.psum_scatter(
        grad_input_part.astype(BF), "tensor", scatter_dimension=0, tiled=True
    ).astype(F32)
    grad_first_w = dotf("td,tf->df", normed_one, grad_first).astype(BF)
    grad_second_w = jnp.concatenate(
        [grad_out_proj, grad_shared_gu, grad_shared_down], axis=1
    ).astype(BF)
    grad_second_w = lax.psum_scatter(grad_second_w, "dp", scatter_dimension=0, tiled=True)
    grad_first_w = lax.psum_scatter(grad_first_w, "dp", scatter_dimension=0, tiled=True)
    grad_bc_w = lax.psum(grad_first_w[:, 2 * inner : 2 * inner + 2 * state], "tensor")

    scale_piece = lax.dynamic_slice_in_dim(scale_one, my_t * piece, piece, axis=0)
    weighted_one = ln1_gain * grad_input_piece
    grad_ln1 = jnp.sum(grad_input_piece * x_piece * scale_piece, axis=0)
    grad_x = (
        grad_one
        + scale_piece * weighted_one
        - x_piece * scale_piece**3 * jnp.mean(weighted_one * x_piece, axis=-1, keepdims=True)
    )
    grad_x = lax.all_gather(grad_x.astype(BF), "tensor", axis=0, tiled=True).astype(F32)

    wide = jnp.concatenate(
        [grad_ln1, grad_ln2, grad_conv_bc.reshape(-1), grad_conv_bc_bias]
    )
    wide = lax.psum(wide, everyone)
    narrow = jnp.concatenate(
        [grad_conv_x.reshape(-1), grad_conv_x_bias, grad_gnorm, grad_dt_bias, grad_a_log, grad_d_skip]
    )
    narrow = lax.psum(narrow, "dp")
    taps = conv_x.shape[0]
    at = [0]

    def take(vector, *shape):
        size = 1
        for s in shape:
            size *= s
        part = lax.slice_in_dim(vector, at[0], at[0] + size).reshape(shape)
        at[0] += size
        return part

    o_ln1 = take(wide, width)
    o_ln2 = take(wide, width)
    o_conv_bc = take(wide, taps, 2 * state)
    o_conv_bc_bias = take(wide, 2 * state)
    at[0] = 0
    o_conv_x = take(narrow, taps, inner)
    o_conv_x_bias = take(narrow, inner)
    o_gnorm = take(narrow, inner)
    o_dt_bias = take(narrow, heads)
    o_a_log = take(narrow, heads)
    o_d_skip = take(narrow, heads)
    first_f = grad_first_w.astype(F32)
    second_f = grad_second_w.astype(F32)
    return (
        layer_out,
        grad_x,
        o_ln1,
        first_f[:, : 2 * inner].reshape(rows, 2, inner),
        grad_bc_w.astype(F32),
        first_f[:, 2 * inner + 2 * state :],
        o_conv_x,
        o_conv_x_bias,
        o_conv_bc,
        o_conv_bc_bias,
        o_dt_bias,
        o_a_log,
        o_d_skip,
        o_gnorm,
        second_f[:, :inner],
        o_ln2,
        second_f[:, inner : inner + 2 * n_sh].reshape(rows, 2, n_sh),
        second_f[:, inner + 2 * n_sh :],
        grad_exp_gu,
        grad_exp_down,
    )


def solution(mesh):
    return jax.shard_map(
        local,
        mesh=mesh,
        in_specs=(
            P("dp", None),
            P("dp"),
            P("dp", None),
            P("dp", None),
            P(),
            P("dp", None, "tensor"),
            P("dp", None),
            P("dp", "tensor"),
            P(None, "tensor"),
            P("tensor"),
            P(),
            P(),
            P("tensor"),
            P("tensor"),
            P("tensor"),
            P("tensor"),
            P("dp", "tensor"),
            P(),
            P("dp", None, "tensor"),
            P("dp", "tensor"),
            P("dp", None, None, "tensor"),
            P("dp", "tensor", None),
            P("dp", None),
        ),
        out_specs=(
            P("dp", None),
            P("dp", None),
            P(),
            P("dp", None, "tensor"),
            P("dp", None),
            P("dp", "tensor"),
            P(None, "tensor"),
            P("tensor"),
            P(),
            P(),
            P("tensor"),
            P("tensor"),
            P("tensor"),
            P("tensor"),
            P("dp", "tensor"),
            P(),
            P("dp", None, "tensor"),
            P("dp", "tensor"),
            P("dp", None, None, "tensor"),
            P("dp", "tensor", None),
        ),
        check_vma=False,
    )
```

time: 2250 us -> 1340 us (0.60)
  blocking collectives: 698 us -> 88.4 us
  local copies, waits for them, and re-layouts: 329 us -> 151 us
  other arithmetic: 240 us -> 85.3 us
  matrix products: 166 us -> 217 us
    all_to_all x3 -> x0, waiting for transfers between devices: 502 us -> none  [the longest x1 252 us: local(): lax.all_to_all(piece.astype(jnp.bfloat16), 'dp', split_axis=0, concat_axi...]
    all_gather x3 -> x0, blocking collectives: 362 us -> none  [the longest x1 308 us: local(): lax.all_gather(w_shared_down.astype(jnp.bfloat16), 'dp', axis=0, tiled=True)]
    all_gather x3 -> x8, waiting for transfers between devices: 0.01 us -> 331 us  [the longest x1 95.5 us: local(): lax.all_gather(g2_piece, everyone, axis=0, tiled=True)]
    all_to_all x1 -> x0, blocking collectives: 278 us -> none  [local(): lax.all_to_all(send_rows, 'dp', split_axis=0, concat_axis=0, tiled=True)]
    reduce_scatter x5, waiting for transfers between devices: 148 us -> 316 us  [the longest x1 152 us: local(): lax.psum_scatter(dxn_part.reshape(n_dp * slots, width), everyone, scatter...]
    gather x6 -> x0, local copies, waits for them, and re-layouts: 150 us -> none  [the longest x2 50.2 us: local(): returned[local_slot] * weights_flat[:, None]]
    psum x3 -> x1, waiting for transfers between devices: 121 us -> 25.7 us  [local(): lax.psum(grad_first_w[:, 2 * inner:2 * inner + 2 * state], 'tensor')]
    unnamed x13 -> x16, waiting for transfers between devices: 2.49 us -> 95.9 us
  transfers between devices with their start and end apart: 15 -> 15, of which waited for: 8 -> 12; matrix products, arithmetic and copies ran while one was open for 29% -> 18% of each run, Pallas kernels for 0% -> 0%
where the time goes in v1:
time: 1340 us; the launch traced here: 1330 us
  waiting for transfers between devices  769 us (57%)
  matrix products  217 us (16%)
  local copies, waits for them, and re-layouts  151 us (11%)
  blocking collectives  88.4 us (7%)
  other arithmetic  85.3 us (6%)
  between operations  16.8 us (1%)
    dot_general x25, matrix products, dotf(): return jnp.einsum(spec, a, b, preferred_element_type=F32)  169 us
    reduce_scatter x1, waiting for transfers between devices, local(): lax.psum_scatter(dxn_part.reshape(n_dp * slots, width), everyone, scatter...  152 us
    reduce_scatter x1, waiting for transfers between devices, local(): lax.psum_scatter(out_part.reshape(n_dp * slots, width), everyone, scatter...  145 us
    unnamed x16, waiting for transfers between devices  95.9 us
    all_gather x1, waiting for transfers between devices, local(): lax.all_gather(g2_piece, everyone, axis=0, tiled=True)  95.5 us
    all_gather x1, waiting for transfers between devices, local(): first = lax.all_gather(first, 'dp', axis=0, tiled=True)  90.3 us
    all_gather x1, waiting for transfers between devices, local(): all_rows = lax.all_gather(normed_two, everyone, axis=0, tiled=True)  63.4 us
    unnamed x303, local copies, waits for them, and re-layouts  50.5 us
  transfers between devices with their start and end apart: 15, of which 12 were waited for; matrix products, arithmetic and copies ran while one was open for 18% of the time, Pallas kernels for 0%

profile of v1, /device:TPU:9, one launch (start us, length us, event | category | flops | bytes accessed | tf_op | source)
XLA Modules:
  0.0 1330.2 jit_solution(283489763582924508)
XLA Ops:
  14.7 90.3 %all-gather.9.cloned.1.call-done = bf16[1536,1804]{1,0:T(8,128)(2,1)} async-done(((bf16[192,1804]{1,0:T(8,128)(2,1)}), bf16[1536,1804]{1,0:T(8,128)(2,1)}) %all-gather.9.cloned.1.call-update) | async-done | bytes 5541904 | tf_op jit(solution)/shard_map/all_gather | solution.py:191
  157.0 29.2 %all-gather.11.cloned.1.call-done = bf16[1536,1536]{1,0:T(8,128)(2,1)} async-done(((bf16[192,1536]{1,0:T(8,128)(2,1)}), bf16[1536,1536]{1,0:T(8,128)(2,1)}) %all-gather.11.cloned.1.call-update) | async-done | bytes 4718608 | tf_op jit(solution)/shard_map/all_gather | solution.py:192
  199.5 19.9 %reduce-scatter.9.cloned.1.call-done = bf16[128,1536]{1,0:T(8,128)(2,1)} async-done(((bf16[512,1536]{1,0:T(8,128)(2,1)}), bf16[128,1536]{1,0:T(8,128)(2,1)}) %reduce-scatter.9.cloned.1.call-update) | async-done | bytes 393232 | tf_op jit(solution)/shard_map/reduce_scatter | solution.py:244
  222.8 9.4 convert_element_type.148
  232.2 10.8 reshape.369
  243.0 17.8 %all-gather.13.cloned.1.call-done = f32[4096,64]{0,1:T(8,128)} async-done(((f32[512,64]{0,1:T(8,128)}), f32[4096,64]{0,1:T(8,128)}) %all-gather.13.cloned.1.call-update) | async-done | bytes 1048592 | tf_op jit(solution)/shard_map/all_gather | solution.py:206
  265.3 95.5 %all-gather.19.cloned.1.call-done = bf16[4096,1536]{1,0:T(8,128)(2,1)} async-done(((bf16[128,1536]{1,0:T(8,128)(2,1)}), bf16[4096,1536]{1,0:T(8,128)(2,1)}) %all-gather.19.cloned.1.call-update) | async-done | bytes 12582928 | tf_op jit(solution)/shard_map/all_gather | solution.py:225
  360.8 16.9 %fusion.157 = f32[8,512,1536]{2,1,0:T(8,128)} fusion(pred[8,512,512]{2,1,0:T(32,128)(4,1)} %bitcast_compare_fusion, bf16[8,512,1536]{2,1,0:T(8,128)(2,1)} %bitcast.255), kind=kOutput, calls=%fused_computation.283 | convolution fusion | flops 6442450944 | bytes 39845888 | tf_op jit(solution)/shard_map/sct,std->scd/dot_general | solution.py:29
  377.6 10.6 copy.271
  395.4 63.4 %all-gather.15.cloned.1.call-done = bf16[4096,1536]{1,0:T(8,128)(2,1)} async-done(((bf16[128,1536]{1,0:T(8,128)(2,1)}), bf16[4096,1536]{1,0:T(8,128)(2,1)}) %all-gather.15.cloned.1.call-update) | async-done | bytes 12582928 | tf_op jit(solution)/shard_map/all_gather | solution.py:251
  458.8 14.5 %convolution_convert_fusion.1 = bf16[8,512,1536]{2,1,0:T(8,128)(2,1)} fusion(pred[8,512,512]{2,1,0:T(32,128)(4,1)} %bitcast_compare_fusion, bf16[8,512,1536]{2,1,0:T(8,128)(2,1)} %bitcast.308), kind=kOutput, calls=%fused_computation.19 | convolution fusion | flops 6448742400 | bytes 27262976 | tf_op jit(solution)/shard_map/sct,std->scd/dot_general | solution.py:29
  473.3 11.1 copy.263
  484.4 10.2 fusion.156
  494.6 11.0 multiply_convert_fusion.4
  514.0 10.8 copy.273
  534.6 15.1 %add_convert_fusion = bf16[8,512,1536]{2,1,0:T(8,128)(2,1)} fusion(pred[8,512,512]{2,1,0:T(32,128)(4,1)S(1)} %copy-done.21, bf16[8,512,1536]{2,1,0:T(8,128)(2,1)} %bitcast.258, f32[512,1536]{1,0:T(8,128)} %fusion.62, f32[8]{0:T(128)S(1)} %compare_convert_fusion), kind=kOutput, calls=%fused_computation.15 | convolution fusion | flops 6461325312 | bytes 30408736 | tf_op jit(solution)/shard_map/sct,scd->std/dot_general | solution.py:29
  549.8 151.9 %reduce-scatter.13.cloned.1.call-done = bf16[128,1536]{1,0:T(8,128)(2,1)} async-done(((bf16[4096,1536]{1,0:T(8,128)(2,1)}), bf16[128,1536]{1,0:T(8,128)(2,1)}) %reduce-scatter.13.cloned.1.call-update) | async-done | bytes 393232 | tf_op jit(solution)/shard_map/reduce_scatter | solution.py:293
  710.5 16.6 %all-gather.21.cloned.1.call-done = bf16[512,1536]{1,0:T(8,128)(2,1)} async-done(((bf16[128,1536]{1,0:T(8,128)(2,1)}), bf16[512,1536]{1,0:T(8,128)(2,1)}) %all-gather.21.cloned.1.call-update) | async-done | bytes 1572880 | tf_op jit(solution)/shard_map/all_gather | solution.py:319
  761.6 9.8 while.35
  781.5 10.1 fusion.17
  833.8 9.5 multiply_convert_fusion
  843.3 10.9 copy.267
  857.8 15.2 %add_convert_fusion.1 = bf16[8,512,1536]{2,1,0:T(8,128)(2,1)} fusion(pred[8,512,512]{2,1,0:T(32,128)(4,1)S(1)} %copy-done.22, bf16[8,512,1536]{2,1,0:T(8,128)(2,1)} %bitcast.259, f32[512,1536]{1,0:T(8,128)} %fusion.117, f32[8]{0:T(128)S(1)} %copy-done.140), kind=kOutput, calls=%fused_computation.16 | convolution fusion | flops 6461325312 | bytes 30408736 | tf_op jit(solution)/shard_map/sct,scd->std/dot_general | solution.py:29
  883.0 144.7 %reduce-scatter.11.cloned.1.call-done = bf16[128,1536]{1,0:T(8,128)(2,1)} async-done(((bf16[4096,1536]{1,0:T(8,128)(2,1)}), bf16[128,1536]{1,0:T(8,128)(2,1)}) %reduce-scatter.11.cloned.1.call-update) | async-done | bytes 393232 | tf_op jit(solution)/shard_map/reduce_scatter | solution.py:300
  1048.0 11.8 fusion.68
  1059.7 19.2 %copy.303 = f32[8,1536,2,128]{3,2,1,0:T(2,128)} copy(f32[8,1536,2,128]{1,3,2,0:T(8,128)} %bitcast.248) | data formatting | bytes 25165824
  1079.1 9.3 fusion.158
  1088.8 26.4 %psum.39 = f32[4644]{0:T(1024)S(1)} all-reduce(f32[4644]{0:T(1024)S(1)} %concatenate.50), channel_id=1, replica_groups=mesh['dp'=8,'tensor'=4] {'dp'}, use_global_device_ids=true, to_apply=%region_47.48 | all-reduce | flops 4644 | bytes 37152 | tf_op jit(solution)/shard_map/psum | solution.py:369
  1117.1 50.4 %psum.37 = f32[4352]{0:T(1024)S(1)} all-reduce(f32[4352]{0:T(1024)S(1)} %pad_maximum_fusion.13), channel_id=1, replica_groups=mesh['dp'=8,'tensor'=4] {'dp','tensor'}, use_global_device_ids=true, to_apply=%region_34.35 | all-reduce | flops 4352 | bytes 34816 | tf_op jit(solution)/shard_map/psum | solution.py:365
  1170.8 18.4 %all-gather.23.cloned.1.call-done = bf16[512,1536]{1,0:T(8,128)(2,1)} async-done(((bf16[128,1536]{1,0:T(8,128)(2,1)}), bf16[512,1536]{1,0:T(8,128)(2,1)}) %all-gather.23.cloned.1.call-update) | async-done | bytes 1572880 | tf_op jit(solution)/shard_map/all_gather | solution.py:360
  1192.7 95.0 %reduce-scatter.19.cloned.1.call-done = bf16[192,1536]{1,0:T(8,128)(2,1)} async-done(((bf16[1536,1536]{1,0:T(8,128)(2,1)}), bf16[192,1536]{1,0:T(8,128)(2,1)}) %reduce-scatter.19.cloned.1.call-update) | async-done | bytes 589840
  1294.8 25.7 %all-reduce.21.cloned.1.call-done = bf16[192,256]{1,0:T(8,128)(2,1)} async-done(((bf16[192,256]{1,0:T(8,128)(2,1)}), bf16[192,256]{1,0:T(8,128)(2,1)}) %all-reduce.21.cloned.1.call-update) | async-done | bytes 98320 | tf_op jit(solution)/shard_map/psum | solution.py:350
  (538 shorter events, 264.7 us)
Async XLA Ops:
  7.2 97.8 %all-gather.9.cloned.1.call-start = ((), (), s32[]{:S(2)}) async-start(), calls=%async_computation.6 | async-start | bytes 6635520 | tf_op jit(solution)/shard_map/all_gather | solution.py:191
  11.8 174.4 %all-gather.11.cloned.1.call-start = ((), (), s32[]{:S(2)}) async-start(), calls=%async_computation.7 | async-start | bytes 5308416 | tf_op jit(solution)/shard_map/all_gather | solution.py:192
  13.2 206.1 %reduce-scatter.9.cloned.1.call-start = ((), (), s32[]{:S(2)}) async-start(), calls=%async_computation.8 | async-start | bytes 1966080 | tf_op jit(solution)/shard_map/reduce_scatter | solution.py:244
  13.5 133.2 %copy-start.71 = (f32[768]{0:T(1024)}, f32[768]{0:T(1024)S(1)}, u32[]{:S(2)}) copy-start(f32[768]{0:T(1024)S(1)} %mul.670) | copy-start | bytes 9220
  14.2 103.0 %copy-start.74 = (f32[768]{0:T(1024)}, f32[768]{0:T(1024)S(1)}, u32[]{:S(2)}) copy-start(f32[768]{0:T(1024)S(1)} %get-tuple-element.428) | copy-start | bytes 9220
  14.2 103.0 %copy-start.76 = (f32[768]{0:T(1024)}, f32[768]{0:T(1024)S(1)}, u32[]{:S(2)}) copy-start(f32[768]{0:T(1024)S(1)} %get-tuple-element.429) | copy-start | bytes 9220
  14.2 103.0 %copy-start.78 = (f32[768]{0:T(1024)}, f32[768]{0:T(1024)S(1)}, u32[]{:S(2)}) copy-start(f32[768]{0:T(1024)S(1)} %get-tuple-element.430) | copy-start | bytes 9220
  14.2 103.0 %copy-start.80 = (f32[768]{0:T(1024)}, f32[768]{0:T(1024)S(1)}, u32[]{:S(2)}) copy-start(f32[768]{0:T(1024)S(1)} %get-tuple-element.431) | copy-start | bytes 9220
  157.0 581.0 %copy-start.106 = (f32[512]{0:T(512)}, f32[512]{0:T(512)S(1)}, u32[]{:S(2)}) copy-start(f32[512]{0:T(512)S(1)} %get-tuple-element.512) | copy-start | bytes 6148
  190.9 69.9 %all-gather.13.cloned.1.call-start = ((), (), s32[]{:S(2)}) async-start(), calls=%async_computation.9 | async-start | bytes 1179648 | tf_op jit(solution)/shard_map/all_gather | solution.py:206
  192.4 168.4 %all-gather.19.cloned.1.call-start = ((), (), s32[]{:S(2)}) async-start(), calls=%async_computation.13 | async-start | bytes 12976128 | tf_op jit(solution)/shard_map/all_gather | solution.py:225
  197.0 261.8 %all-gather.15.cloned.1.call-start = ((), (), s32[]{:S(2)}) async-start(), calls=%async_computation.10 | async-start | bytes 12976128 | tf_op jit(solution)/shard_map/all_gather | solution.py:251
  220.8 482.7 %copy-start.104 = (f32[128]{0:T(128)}, f32[128]{0:T(128)S(1)}, u32[]{:S(2)}) copy-start(f32[128]{0:T(128)S(1)} %get-tuple-element.514) | copy-start | bytes 1540
  220.9 482.7 %copy-start.120 = (f32[128]{0:T(128)}, f32[128]{0:T(128)S(1)}, u32[]{:S(2)}) copy-start(f32[128]{0:T(128)S(1)} %get-tuple-element.513) | copy-start | bytes 1540
  222.6 479.1 %reduce-scatter.13.cloned.1.call-start = ((), (), s32[]{:S(2)}) async-start(), calls=%async_computation.14 | async-start | bytes 12976128 | tf_op jit(solution)/shard_map/reduce_scatter | solution.py:293
  243.0 291.6 %copy-start.139 = (f32[8]{0:T(128)}, f32[8]{0:T(128)S(1)}, u32[]{:S(2)}) copy-start(f32[8]{0:T(128)S(1)} %compare_convert_fusion) | copy-start | bytes 100
  549.7 152.0 %copy-start.6 = (f32[128,1536]{1,0:T(8,128)S(1)}, f32[128,1536]{1,0:T(8,128)}, u32[]{:S(2)}) copy-start(f32[128,1536]{1,0:T(8,128)} %copy-done.5) | copy-start | bytes 2359300
  549.7 156.3 %copy-start.67 = (f32[512,12]{0,1:T(8,128)S(1)}, f32[512,12]{0,1:T(8,128)}, u32[]{:S(2)}) copy-start(f32[512,12]{0,1:T(8,128)} %copy-done.66) | copy-start | bytes 73732
  549.7 177.3 %all-gather.21.cloned.1.call-start = ((), (), s32[]{:S(2)}) async-start(), calls=%async_computation.15 | async-start | bytes 1966080 | tf_op jit(solution)/shard_map/all_gather | solution.py:319
  705.8 175.5 %reduce-scatter.15.cloned.1.call-start = ((), (), s32[]{:S(2)}) async-start(), calls=%async_computation.16 | async-start | bytes 1966080 | tf_op jit(solution)/shard_map/reduce_scatter | solution.py:341
  832.6 195.1 %reduce-scatter.11.cloned.1.call-start = ((), (), s32[]{:S(2)}) async-start(), calls=%async_computation.11 | async-start | bytes 12976128 | tf_op jit(solution)/shard_map/reduce_scatter | solution.py:300
  873.0 294.5 %reduce-scatter.17.cloned.1.call-start = ((), (), s32[]{:S(2)}) async-start(), calls=%async_computation.18 | async-start | bytes 6635520 | tf_op jit(solution)/shard_map/reduce_scatter | solution.py:349
  881.1 146.6 %copy-start.20 = (bf16[512,1536]{1,0:T(8,128)(2,1)S(1)}, bf16[512,1536]{1,0:T(8,128)(2,1)}, u32[]{:S(2)}) copy-start(bf16[512,1536]{1,0:T(8,128)(2,1)} %copy-done.18) | copy-start | bytes 4718596
  881.1 146.6 %copy-start.64 = (f32[1536]{0:T(1024)S(1)}, f32[1536]{0:T(1024)}, u32[]{:S(2)}) copy-start(f32[1536]{0:T(1024)} %param.44) | copy-start | bytes 18436
  881.1 146.6 %copy-start.105 = (f32[128]{0:T(128)S(1)}, f32[128]{0:T(128)}, u32[]{:S(2)}) copy-start(f32[128]{0:T(128)} %copy-done.104) | copy-start | bytes 1540
  881.1 146.6 %copy-start.121 = (f32[128]{0:T(128)S(1)}, f32[128]{0:T(128)}, u32[]{:S(2)}) copy-start(f32[128]{0:T(128)} %copy-done.120) | copy-start | bytes 1540
  881.1 146.6 %copy-start.123 = (f32[128]{0:T(128)S(1)}, f32[128]{0:T(128)}, u32[]{:S(2)}) copy-start(f32[128]{0:T(128)} %copy-done.122) | copy-start | bytes 1540
  881.1 146.6 %copy-start.7 = (f32[128,1536]{1,0:T(8,128)S(1)}, f32[128,1536]{1,0:T(8,128)}, u32[]{:S(2)}) copy-start(f32[128,1536]{1,0:T(8,128)} %copy-done.5) | copy-start | bytes 2359300
  881.1 289.7 %all-gather.17.cloned.1.call-start = ((), (), s32[]{:S(2)}) async-start(), calls=%async_computation.12 | async-start | bytes 1966080 | tf_op jit(solution)/shard_map/all_gather | solution.py:303
  1030.5 158.7 %all-gather.23.cloned.1.call-start = ((), (), s32[]{:S(2)}) async-start(), calls=%async_computation.17 | async-start | bytes 1966080 | tf_op jit(solution)/shard_map/all_gather | solution.py:360
  1031.3 256.4 %reduce-scatter.19.cloned.1.call-start = ((), (), s32[]{:S(2)}) async-start(), calls=%async_computation.20 | async-start | bytes 5308416
  1046.4 274.1 %all-reduce.21.cloned.1.call-start = ((), (), s32[]{:S(2)}) async-start(), calls=%async_computation.19 | async-start | bytes 196608 | tf_op jit(solution)/shard_map/psum | solution.py:350
  (131 other events, 1496.7 us)
Sparse Core Ops, SparseCore 0:
  11.9 93.0 all-gather.8
  107.8 78.3 all-gather.10
  191.1 28.2 reduce-scatter.8
  222.2 38.5 all-gather.12
  264.5 96.1 all-gather.18
  364.5 94.2 all-gather.14
  549.8 151.8 reduce-scatter.12
  705.9 21.1 all-gather.20
  832.7 29.4 reduce-scatter.14
  873.1 154.5 reduce-scatter.10
  1031.3 113.0 reduce-scatter.16
  1146.4 20.5 all-gather.16
  1169.2 19.9 all-gather.22
  1192.7 94.9 reduce-scatter.18
  1290.4 30.0 all-reduce.20

commit v2 on v1

--- a/solution.py
+++ b/solution.py
@@ -1,6 +1,10 @@
+import functools
+
 import jax
 import jax.numpy as jnp
 from jax import lax
+from jax.experimental import pallas as pl
+from jax.experimental.pallas import tpu as pltpu
 from jax.sharding import PartitionSpec as P
 
 BLOCK = 256
@@ -135,6 +139,329 @@
         )
 
     return gated_mix, mixer_back
+
+
+MESH = pl.DeviceIdType.MESH
+
+
+def place():
+    d = lax.axis_index("dp")
+    t = lax.axis_index("tensor")
+    return d // 2, d % 2, t // 2, t % 2
+
+
+def device(hi, lo, th, tl):
+    return (hi * 2 + lo, th * 2 + tl)
+
+
+def greet(n_hi):
+    hi, lo, th, tl = place()
+    barrier = pltpu.get_barrier_semaphore()
+    others = [device(lax.rem(hi + k, n_hi), lo, th, tl) for k in range(1, n_hi)]
+    others += [device(hi, 1 - lo, th, tl), device(hi, lo, 1 - th, tl), device(hi, lo, th, 1 - tl)]
+    for other in others:
+        pl.semaphore_signal(barrier, inc=1, device_id=other, device_id_type=MESH)
+    pl.semaphore_wait(barrier, len(others))
+
+
+def gather_kernel(n_hi, x_ref, o_ref, own_sem, send_sem, recv_sem):
+    hi, lo, th, tl = place()
+    rows = x_ref.shape[0]
+    half = rows // 2
+    greet(n_hi)
+    own_block = (hi * 2 + lo) * 4 + th * 2 + tl
+    own = pltpu.make_async_copy(x_ref, o_ref.at[pl.ds(own_block * rows, rows)], own_sem)
+    own.start()
+
+    def slot(k, f, s, c):
+        return ((c * 2 + s) * 2 + f) * n_hi + k
+
+    def where(h, k, f, s, c):
+        kk = lax.rem(hi + k, n_hi)
+        l = 1 - lo if (f if h == 0 else s) else lo
+        y = 1 - th if (s if h == 0 else f) else th
+        z = 1 - tl if c else tl
+        return ((kk * 2 + l) * 4 + y * 2 + z) * rows + h * half
+
+    sends = []
+
+    def push(h, k, f, s, c, step):
+        at = where(h, k, f, s, c)
+        if k == 0 and not (f or s or c):
+            src = x_ref.at[pl.ds(h * half, half)]
+        else:
+            src = o_ref.at[pl.ds(at, half)]
+        if step == "c":
+            to, rk, rf, rs, rc = device(hi, lo, th, 1 - tl), k, f, s, 1
+        elif step == "s":
+            to = device(hi, lo, 1 - th, tl) if h == 0 else device(hi, 1 - lo, th, tl)
+            rk, rf, rs, rc = k, f, 1, 0
+        elif step == "f":
+            to = device(hi, 1 - lo, th, tl) if h == 0 else device(hi, lo, 1 - th, tl)
+            rk, rf, rs, rc = k, 1, 0, 0
+        else:
+            to = device(lax.rem(hi + step, n_hi), lo, th, tl)
+            rk, rf, rs, rc = n_hi - step, 0, 0, 0
+        r = slot(rk, rf, rs, rc)
+        copy = pltpu.make_async_remote_copy(
+            src_ref=src,
+            dst_ref=o_ref.at[pl.ds(at, half)],
+            send_sem=send_sem.at[h, r],
+            recv_sem=recv_sem.at[h, r],
+            device_id=to,
+            device_id_type=MESH,
+        )
+        copy.start()
+        sends.append(copy)
+
+    def arrive(h, k, f, s, c):
+        at = where(h, k, f, s, c)
+        view = o_ref.at[pl.ds(at, half)]
+        r = slot(k, f, s, c)
+        pltpu.make_async_remote_copy(
+            src_ref=view,
+            dst_ref=view,
+            send_sem=send_sem.at[h, r],
+            recv_sem=recv_sem.at[h, r],
+            device_id=device(hi, lo, th, 1 - tl),
+            device_id_type=MESH,
+        ).wait_recv()
+
+    for k in range(1, n_hi):
+        for h in range(2):
+            push(h, 0, 0, 0, 0, k)
+    for k in range(n_hi):
+        for h in range(2):
+            if k:
+                arrive(h, k, 0, 0, 0)
+            for step in ("f", "s", "c"):
+                push(h, k, 0, 0, 0, step)
+        for h in range(2):
+            arrive(h, k, 1, 0, 0)
+            for step in ("s", "c"):
+                push(h, k, 1, 0, 0, step)
+    for k in range(n_hi):
+        for f in range(2):
+            for h in range(2):
+                arrive(h, k, f, 1, 0)
+                push(h, k, f, 1, 0, "c")
+    for k in range(n_hi):
+        for f in range(2):
+            for s in range(2):
+                for h in range(2):
+                    arrive(h, k, f, s, 1)
+    own.wait()
+    for copy in sends:
+        copy.wait_send()
+
+
+def gather_rows(x, n_dp, collective_id):
+    rows, width = x.shape
+    n_hi = n_dp // 2
+    return pl.pallas_call(
+        functools.partial(gather_kernel, n_hi),
+        out_shape=jax.ShapeDtypeStruct((n_dp * 4 * rows, width), x.dtype),
+        in_specs=[pl.BlockSpec(memory_space=pl.ANY)],
+        out_specs=pl.BlockSpec(memory_space=pl.ANY),
+        scratch_shapes=[
+            pltpu.SemaphoreType.DMA,
+            pltpu.SemaphoreType.DMA((2, 8 * n_hi)),
+            pltpu.SemaphoreType.DMA((2, 8 * n_hi)),
+        ],
+        compiler_params=pltpu.CompilerParams(collective_id=collective_id, has_side_effects=True),
+        name="gather_rows",
+    )(x)
+
+
+def scatter_kernel(
+    n_hi, depth, p_ref, o_ref, stage, from_c, from_f, from_s, from_h,
+    stage_sem, send_c, recv_c, send_f, recv_f, send_s, recv_s, send_h, recv_h,
+):
+    hi, lo, th, tl = place()
+    rows = o_ref.shape[0]
+    half = rows // 2
+    greet(n_hi)
+
+    def where(h, k, f, s, c):
+        kk = lax.rem(hi + k, n_hi)
+        l = 1 - lo if (f if h == 1 else s) else lo
+        y = 1 - th if (s if h == 1 else f) else th
+        z = 1 - tl if c else tl
+        return ((kk * 2 + l) * 4 + y * 2 + z) * rows + h * half
+
+    order = [(f, s, k, h) for f, s in ((1, 1), (1, 0), (0, 1), (0, 0)) for k in
+             list(range(1, n_hi)) + [0] for h in range(2)]
+
+    def slot(f, s, k):
+        return (f * 2 + s) * n_hi + k
+
+    def first(h):
+        return device(hi, lo, 1 - th, tl) if h == 0 else device(hi, 1 - lo, th, tl)
+
+    def second(h):
+        return device(hi, 1 - lo, th, tl) if h == 0 else device(hi, lo, 1 - th, tl)
+
+    sends = []
+
+    def push(src, dst, ssem, rsem, to):
+        copy = pltpu.make_async_remote_copy(
+            src_ref=src, dst_ref=dst, send_sem=ssem, recv_sem=rsem,
+            device_id=to, device_id_type=MESH,
+        )
+        copy.start()
+        sends.append(copy)
+
+    def arrive(dst, ssem, rsem):
+        pltpu.make_async_remote_copy(
+            src_ref=dst, dst_ref=dst, send_sem=ssem, recv_sem=rsem,
+            device_id=device(hi, lo, th, 1 - tl), device_id_type=MESH,
+        ).wait_recv()
+
+    for f, s, k, h in order:
+        n = slot(f, s, k)
+        push(
+            p_ref.at[pl.ds(where(h, k, f, s, 1), half)],
+            from_c.at[h, n],
+            send_c.at[h, n],
+            recv_c.at[h, n],
+            device(hi, lo, th, 1 - tl),
+        )
+
+    def load(i):
+        f, s, k, h = order[i]
+        return pltpu.make_async_copy(
+            p_ref.at[pl.ds(where(h, k, f, s, 0), half)], stage.at[i % depth], stage_sem.at[i % depth]
+        )
+
+    for i in range(depth - 1):
+        load(i).start()
+    for i, (f, s, k, h) in enumerate(order):
+        if i + depth - 1 < len(order):
+            load(i + depth - 1).start()
+        load(i).wait()
+        n = slot(f, s, k)
+        arrive(from_c.at[h, n], send_c.at[h, n], recv_c.at[h, n])
+        total = stage[i % depth].astype(F32) + from_c[h, n].astype(F32)
+        if f == 0:
+            m = s * n_hi + k
+            arrive(from_f.at[h, m], send_f.at[h, m], recv_f.at[h, m])
+            total = total + from_f[h, m].astype(F32)
+        if f == 0 and s == 0:
+            arrive(from_s.at[h, k], send_s.at[h, k], recv_s.at[h, k])
+            total = total + from_s[h, k].astype(F32)
+        if f == 0 and s == 0 and k == 0:
+            for j in range(1, n_hi):
+                arrive(from_h.at[h, j - 1], send_h.at[h, j - 1], recv_h.at[h, j - 1])
+                total = total + from_h[h, j - 1].astype(F32)
+            o_ref[pl.ds(h * half, half), :] = total.astype(o_ref.dtype)
+            continue
+        from_c[h, n] = total.astype(from_c.dtype)
+        src = from_c.at[h, n]
+        if f == 1:
+            m = s * n_hi + k
+            push(src, from_f.at[h, m], send_f.at[h, m], recv_f.at[h, m], first(h))
+        elif s == 1:
+            push(src, from_s.at[h, k], send_s.at[h, k], recv_s.at[h, k], second(h))
+        else:
+            j = n_hi - k
+            push(
+                src, from_h.at[h, j - 1], send_h.at[h, j - 1], recv_h.at[h, j - 1],
+                device(lax.rem(hi + k, n_hi), lo, th, tl),
+            )
+    for copy in sends:
+        copy.wait_send()
+
+
+def scatter_rows(p, n_dp, collective_id):
+    width = p.shape[1]
+    rows = p.shape[0] // (n_dp * 4)
+    half = rows // 2
+    n_hi = n_dp // 2
+    depth = 4
+    dma = pltpu.SemaphoreType.DMA
+    return pl.pallas_call(
+        functools.partial(scatter_kernel, n_hi, depth),
+        out_shape=jax.ShapeDtypeStruct((rows, width), F32),
+        in_specs=[pl.BlockSpec(memory_space=pl.ANY)],
+        out_specs=pl.BlockSpec(memory_space=pltpu.VMEM),
+        scratch_shapes=[
+            pltpu.VMEM((depth, half, width), p.dtype),
+            pltpu.VMEM((2, 4 * n_hi, half, width), p.dtype),
+            pltpu.VMEM((2, 2 * n_hi, half, width), p.dtype),
+            pltpu.VMEM((2, n_hi, half, width), p.dtype),
+            pltpu.VMEM((2, n_hi - 1, half, width), p.dtype),
+            dma((depth,)),
+            dma((2, 4 * n_hi)),
+            dma((2, 4 * n_hi)),
+            dma((2, 2 * n_hi)),
+            dma((2, 2 * n_hi)),
+            dma((2, n_hi)),
+            dma((2, n_hi)),
+            dma((2, n_hi - 1)),
+            dma((2, n_hi - 1)),
+        ],
+        compiler_params=pltpu.CompilerParams(
+            collective_id=collective_id, has_side_effects=True, vmem_limit_bytes=60 << 20
+        ),
+        name="scatter_rows",
+    )(p)
+
+
+def small_kernel(n_hi, wide, x_ref, o_ref, got_f, got_h, got_t, send_sem, recv_sem, send_h, recv_h):
+    hi, lo, th, tl = place()
+    greet(n_hi)
+
+    def trade(src, dst, i, to):
+        copy = pltpu.make_async_remote_copy(
+            src_ref=src, dst_ref=dst, send_sem=send_sem.at[i], recv_sem=recv_sem.at[i],
+            device_id=to, device_id_type=MESH,
+        )
+        copy.start()
+        copy.wait()
+
+    trade(x_ref, got_f, 0, device(hi, 1 - lo, th, tl))
+    got_h[hi] = x_ref[...] + got_f[...]
+    copies = []
+    for k in range(1, n_hi):
+        copy = pltpu.make_async_remote_copy(
+            src_ref=got_h.at[hi], dst_ref=got_h.at[hi],
+            send_sem=send_h.at[k - 1], recv_sem=recv_h.at[k - 1],
+            device_id=device(lax.rem(hi + k, n_hi), lo, th, tl), device_id_type=MESH,
+        )
+        copy.start()
+        copies.append(copy)
+    for copy in copies:
+        copy.wait()
+    total = got_h[0]
+    for k in range(1, n_hi):
+        total = total + got_h[k]
+    o_ref[...] = total
+    for i, to in enumerate((device(hi, lo, th, 1 - tl), device(hi, lo, 1 - th, tl))):
+        trade(o_ref.at[pl.ds(0, wide)], got_t.at[i], i + 1, to)
+        o_ref[pl.ds(0, wide), :] = o_ref[pl.ds(0, wide), :] + got_t[i]
+
+
+def sum_small(x, wide, n_dp, collective_id):
+    n_hi = n_dp // 2
+    dma = pltpu.SemaphoreType.DMA
+    vmem = pl.BlockSpec(memory_space=pltpu.VMEM)
+    return pl.pallas_call(
+        functools.partial(small_kernel, n_hi, wide),
+        out_shape=jax.ShapeDtypeStruct(x.shape, F32),
+        in_specs=[vmem],
+        out_specs=vmem,
+        scratch_shapes=[
+            pltpu.VMEM(x.shape, F32),
+            pltpu.VMEM((n_hi,) + x.shape, F32),
+            pltpu.VMEM((2, wide, x.shape[1]), F32),
+            dma((3,)),
+            dma((3,)),
+            dma((n_hi - 1,)),
+            dma((n_hi - 1,)),
+        ],
+        compiler_params=pltpu.CompilerParams(collective_id=collective_id, has_side_effects=True),
+        name="sum_small",
+    )(x)
 
 
 def local(
@@ -180,7 +507,6 @@
     full_inner = inner * n_t
     rows = w_zx.shape[0]
     n_sh = w_shared_gu.shape[2]
-    everyone = ("dp", "tensor")
 
     first = jnp.concatenate(
         [w_zx.reshape(rows, 2 * inner), w_bc, w_dt], axis=1
@@ -222,7 +548,7 @@
     pick = pick.astype(BF).reshape(n_dp, n_local * cap, slots)
 
     g2_piece = lax.dynamic_slice_in_dim(g2_low, my_t * piece, piece, axis=0)
-    g2_all = lax.all_gather(g2_piece, everyone, axis=0, tiled=True).reshape(n_dp, slots, width)
+    g2_all = gather_rows(g2_piece, n_dp, 1).reshape(n_dp, slots, width)
 
     gate_w = w_exp_gu.astype(BF).reshape(n_local, width, -1)
     down_w = w_exp_down.astype(BF)
@@ -248,7 +574,7 @@
     hidden_one = x_piece + mixer_out
     scale_two = rms_scale(hidden_one)
     normed_two = (hidden_one * scale_two * ln2_gain).astype(BF)
-    all_rows = lax.all_gather(normed_two, everyone, axis=0, tiled=True)
+    all_rows = gather_rows(normed_two, n_dp, 2)
     mine = lax.dynamic_slice_in_dim(all_rows, my_dp * slots, slots, axis=0)
     all_rows = all_rows.reshape(n_dp, slots, width)
 
@@ -290,16 +616,12 @@
     dxn_part = dotf("sct,scd->std", pick, back)
     own = (jnp.arange(n_dp) == my_dp).astype(F32)[:, None, None]
     dxn_part = (dxn_part + own * grad_normed_shared[None]).astype(BF)
-    grad_normed_two = lax.psum_scatter(
-        dxn_part.reshape(n_dp * slots, width), everyone, scatter_dimension=0, tiled=True
-    ).astype(F32)
+    grad_normed_two = scatter_rows(dxn_part.reshape(n_dp * slots, width), n_dp, 3)
 
     forth = by_source((dotf("erf,efd->erd", act, down_w) * sw).astype(BF))
     out_part = dotf("sct,scd->std", pick, forth)
     out_part = (out_part + own * shared_part[None]).astype(BF)
-    ffn_out = lax.psum_scatter(
-        out_part.reshape(n_dp * slots, width), everyone, scatter_dimension=0, tiled=True
-    ).astype(F32)
+    ffn_out = scatter_rows(out_part.reshape(n_dp * slots, width), n_dp, 4)
     layer_out = lax.all_gather(
         (hidden_one + ffn_out).astype(BF), "tensor", axis=0, tiled=True
     )
@@ -362,11 +684,17 @@
     wide = jnp.concatenate(
         [grad_ln1, grad_ln2, grad_conv_bc.reshape(-1), grad_conv_bc_bias]
     )
-    wide = lax.psum(wide, everyone)
     narrow = jnp.concatenate(
         [grad_conv_x.reshape(-1), grad_conv_x_bias, grad_gnorm, grad_dt_bias, grad_a_log, grad_d_skip]
     )
-    narrow = lax.psum(narrow, "dp")
+
+    def lanes(vector):
+        return jnp.pad(vector, (0, -vector.shape[0] % 1024)).reshape(-1, 128)
+
+    wide = lanes(wide)
+    n_wide = wide.shape[0]
+    sums = sum_small(jnp.concatenate([wide, lanes(narrow)], axis=0), n_wide, n_dp, 5)
+    wide, narrow = sums[:n_wide].reshape(-1), sums[n_wide:].reshape(-1)
     taps = conv_x.shape[0]
     at = [0]
 

time: 1340 us -> 1140 us (0.85)
  waiting for transfers between devices: 769 us -> 284 us
  Pallas kernels: 0 us -> 363 us
  blocking collectives: 88.4 us -> 10.8 us
    pallas_call x0 -> x5, Pallas kernels: none -> 363 us  [the longest x2 180 us: gather_rows(): pl.pallas_call(functools.partial(gather_kernel, n_hi), out_shape=jax.Shap...]
    reduce_scatter x2 -> x0, waiting for transfers between devices: 297 us -> none  [the longest x1 152 us: local(): lax.psum_scatter(dxn_part.reshape(n_dp * slots, width), everyone, scatter...]
    all_gather x2 -> x0, waiting for transfers between devices: 159 us -> none  [the longest x1 95.5 us: local(): lax.all_gather(g2_piece, everyone, axis=0, tiled=True)]
    psum x2 -> x0, blocking collectives: 76.8 us -> none  [the longest x1 50.4 us: local(): wide = lax.psum(wide, everyone)]
    all_gather x1, waiting for transfers between devices: 90.3 us -> 23.8 us  [local(): first = lax.all_gather(first, 'dp', axis=0, tiled=True)]
    reduce_scatter x1, waiting for transfers between devices: 0.01 us -> 55.6 us  [local(): lax.psum_scatter(grad_first_w, 'dp', scatter_dimension=0, tiled=True)]
    reduce_scatter x1, waiting for transfers between devices: 0.01 us -> 21.4 us  [local(): lax.psum_scatter(grad_input_part.astype(BF), 'tensor', scatter_dimension=...]
    reduce_scatter x1, waiting for transfers between devices: 19.9 us -> 0.01 us  [local(): lax.psum_scatter(mixer_part, 'tensor', scatter_dimension=0, tiled=True)]
  transfers between devices with their start and end apart: 15 -> 11, of which waited for: 12 -> 8; matrix products, arithmetic and copies ran while one was open for 18% -> 18% of each run, Pallas kernels for 0% -> 11%
where the time goes in v2:
time: 1140 us; the launch traced here: 1120 us
  Pallas kernels  363 us (32%)
  waiting for transfers between devices  284 us (25%)
  matrix products  215 us (19%)
  local copies, waits for them, and re-layouts  146 us (13%)
  other arithmetic  86.6 us (8%)
  between operations  16.6 us (1%)
    pallas_call x2, Pallas kernels, gather_rows(): pl.pallas_call(functools.partial(gather_kernel, n_hi), out_shape=jax.Shap...  180 us
    dot_general x25, matrix products, dotf(): return jnp.einsum(spec, a, b, preferred_element_type=F32)  166 us
    pallas_call x2, Pallas kernels, scatter_rows(): pl.pallas_call(functools.partial(scatter_kernel, n_hi, depth), out_shape=...  163 us
    unnamed x12, waiting for transfers between devices  95.8 us
    reduce_scatter x1, waiting for transfers between devices, local(): lax.psum_scatter(grad_first_w, 'dp', scatter_dimension=0, tiled=True)  55.6 us
    unnamed x293, local copies, waits for them, and re-layouts  48.4 us
    all_gather x1, waiting for transfers between devices, local(): second = lax.all_gather(second, 'dp', axis=0, tiled=True)  27.9 us
    psum x1, waiting for transfers between devices, local(): lax.psum(grad_first_w[:, 2 * inner:2 * inner + 2 * state], 'tensor')  25.9 us
  transfers between devices with their start and end apart: 11, of which 8 were waited for; matrix products, arithmetic and copies ran while one was open for 18% of the time, Pallas kernels for 11%

profile of v2, /device:TPU:9, one launch (start us, length us, event | category | flops | bytes accessed | tf_op | source)
XLA Modules:
  0.0 1122.9 jit_solution(16055896368266335998)
XLA Ops:
  18.6 9.4 convert_element_type.146
  28.0 10.9 reshape.382
  42.6 99.9 %gather_rows.3 = bf16[4096,1536]{1,0:T(8,128)(2,1)} custom-call(bf16[128,1536]{1,0:T(8,128)(2,1)} %constant_dynamic-slice_fusion.4.x_ref), custom_call_target="tpu_custom_call" | custom-call | tf_op jit(solution)/shard_map/gather_rows/pallas_call | solution.py:261
  148.1 23.8 %all-gather.7.cloned.1.call-done = bf16[1536,1804]{1,0:T(8,128)(2,1)} async-done(((bf16[192,1804]{1,0:T(8,128)(2,1)}), bf16[1536,1804]{1,0:T(8,128)(2,1)}) %all-gather.7.cloned.1.call-update) | async-done | bytes 5541904 | tf_op jit(solution)/shard_map/all_gather | solution.py:517
  202.6 7.6 fusion.46
  224.6 27.9 %all-gather.9.cloned.1.call-done = bf16[1536,1536]{1,0:T(8,128)(2,1)} async-done(((bf16[192,1536]{1,0:T(8,128)(2,1)}), bf16[1536,1536]{1,0:T(8,128)(2,1)}) %all-gather.9.cloned.1.call-update) | async-done | bytes 4718608 | tf_op jit(solution)/shard_map/all_gather | solution.py:518
  257.5 16.8 %fusion.149 = f32[8,512,1536]{2,1,0:T(8,128)} fusion(pred[8,512,512]{2,1,0:T(32,128)(4,1)S(1)} %copy-done.23, bf16[8,512,1536]{2,1,0:T(8,128)(2,1)} %bitcast.265), kind=kOutput, calls=%fused_computation.287 | convolution fusion | flops 6442450944 | bytes 39845888 | tf_op jit(solution)/shard_map/sct,std->scd/dot_general | solution.py:33
  275.3 10.6 copy.271
  295.4 79.8 %gather_rows.2 = bf16[4096,1536]{1,0:T(8,128)(2,1)} custom-call(bf16[128,1536]{1,0:T(8,128)(2,1)} %multiply_convert_fusion.8.x_ref), custom_call_target="tpu_custom_call" | custom-call | tf_op jit(solution)/shard_map/gather_rows/pallas_call | solution.py:261
  375.2 14.6 %convolution_convert_fusion.1 = bf16[8,512,1536]{2,1,0:T(8,128)(2,1)} fusion(pred[8,512,512]{2,1,0:T(32,128)(4,1)} %bitcast_compare_fusion, bf16[8,512,1536]{2,1,0:T(8,128)(2,1)} %bitcast.272), kind=kOutput, calls=%fused_computation.19 | convolution fusion | flops 6448742400 | bytes 27262976 | tf_op jit(solution)/shard_map/sct,std->scd/dot_general | solution.py:33
  389.8 10.8 copy.263
  400.7 8.9 fusion.148
  409.6 11.0 multiply_convert_fusion.4
  420.5 8.3 convolution_convert_fusion
  428.8 11.1 copy.273
  446.3 15.8 %add_convert_fusion = bf16[8,512,1536]{2,1,0:T(8,128)(2,1)} fusion(pred[8,512,512]{2,1,0:T(32,128)(4,1)} %bitcast_compare_fusion, bf16[8,512,1536]{2,1,0:T(8,128)(2,1)} %bitcast.273, f32[512,1536]{1,0:T(8,128)} %fusion.62, f32[8]{0:T(128)S(1)} %compare_convert_fusion), kind=kOutput, calls=%fused_computation.15 | convolution fusion | flops 6461325312 | bytes 30408736 | tf_op jit(solution)/shard_map/sct,scd->std/dot_general | solution.py:33
  462.1 80.5 %scatter_rows.3 = f32[128,1536]{1,0:T(8,128)} custom-call(bf16[4096,1536]{1,0:T(8,128)(2,1)} %bitcast.276), custom_call_target="tpu_custom_call" | custom-call | tf_op jit(solution)/shard_map/scatter_rows/pallas_call | solution.py:382
  544.5 11.5 %multiply_convert_fusion = bf16[8,512,1536]{2,1,0:T(8,128)(2,1)} fusion(bf16[8,512,128]{1,2,0:T(8,128)(2,1)} %get-tuple-element.481, f32[8,512]{1,0:T(8,128)S(1)} %mul.688, f32[8,128,1536]{2,1,0:T(8,128)} %param.48), kind=kOutput, calls=%fused_computation.17 | convolution fusion | flops 1624768512 | bytes 19939328 | tf_op jit(solution)/shard_map/erf,efd->erd/dot_general | solution.py:33
  556.0 10.8 copy.267
  570.2 15.5 %add_convert_fusion.1 = bf16[8,512,1536]{2,1,0:T(8,128)(2,1)} fusion(pred[8,512,512]{2,1,0:T(32,128)(4,1)} %bitcast_compare_fusion, bf16[8,512,1536]{2,1,0:T(8,128)(2,1)} %bitcast.274, f32[512,1536]{1,0:T(8,128)} %fusion.110, f32[8]{0:T(128)S(1)} %compare_convert_fusion), kind=kOutput, calls=%fused_computation.16 | convolution fusion | flops 6461325312 | bytes 30408736 | tf_op jit(solution)/shard_map/sct,scd->std/dot_general | solution.py:33
  585.8 82.2 %scatter_rows.2 = f32[128,1536]{1,0:T(8,128)} custom-call(bf16[4096,1536]{1,0:T(8,128)(2,1)} %bitcast.275), custom_call_target="tpu_custom_call" | custom-call | tf_op jit(solution)/shard_map/scatter_rows/pallas_call | solution.py:382
  672.8 16.2 %all-gather.15.cloned.1.call-done = bf16[512,1536]{1,0:T(8,128)(2,1)} async-done(((bf16[128,1536]{1,0:T(8,128)(2,1)}), bf16[512,1536]{1,0:T(8,128)(2,1)}) %all-gather.15.cloned.1.call-update) | async-done | bytes 1572880 | tf_op jit(solution)/shard_map/all_gather | solution.py:641
  737.5 10.3 fusion.17
  796.8 21.4 %reduce-scatter.9.cloned.1.call-done = bf16[128,1536]{1,0:T(8,128)(2,1)} async-done(((bf16[512,1536]{1,0:T(8,128)(2,1)}), bf16[128,1536]{1,0:T(8,128)(2,1)}) %reduce-scatter.9.cloned.1.call-update) | async-done | bytes 393232 | tf_op jit(solution)/shard_map/reduce_scatter | solution.py:663
  837.9 11.9 %fusion.68 = f32[8,1536,256]{1,2,0:T(8,128)} fusion(bf16[8,512,1536]{2,1,0:T(8,128)(2,1)} %bitcast.263, bf16[8,512,128]{1,2,0:T(8,128)(2,1)S(1)} %copy-done.31, bf16[8,512,128]{1,2,0:T(8,128)(2,1)S(1)} %copy-done.30), kind=kOutput, calls=%fused_computation.129 | convolution fusion | flops 3225419776 | bytes 27262976 | tf_op jit(solution)/shard_map/erd,erf->edf/dot_general | solution.py:33
  849.7 19.2 %copy.303 = f32[8,1536,2,128]{3,2,1,0:T(2,128)} copy(f32[8,1536,2,128]{1,3,2,0:T(8,128)} %bitcast.264) | data formatting | bytes 25165824
  869.1 9.4 fusion.150
  879.7 20.4 %sum_small.1 = f32[80,128]{1,0:T(8,128)} custom-call(f32[80,128]{1,0:T(8,128)} %pad_maximum_fusion.13.x_ref), custom_call_target="tpu_custom_call" | custom-call | tf_op jit(solution)/shard_map/sum_small/pallas_call | solution.py:448
  904.1 55.6 %reduce-scatter.11.cloned.1.call-done = bf16[192,1804]{1,0:T(8,128)(2,1)} async-done(((bf16[1536,1804]{1,0:T(8,128)(2,1)}), bf16[192,1804]{1,0:T(8,128)(2,1)}) %reduce-scatter.11.cloned.1.call-update) | async-done | bytes 692752 | tf_op jit(solution)/shard_map/reduce_scatter | solution.py:671
  965.1 16.8 %all-gather.17.cloned.1.call-done = bf16[512,1536]{1,0:T(8,128)(2,1)} async-done(((bf16[128,1536]{1,0:T(8,128)(2,1)}), bf16[512,1536]{1,0:T(8,128)(2,1)}) %all-gather.17.cloned.1.call-update) | async-done | bytes 1572880 | tf_op jit(solution)/shard_map/all_gather | solution.py:682
  985.4 95.0 %reduce-scatter.13.cloned.1.call-done = bf16[192,1536]{1,0:T(8,128)(2,1)} async-done(((bf16[1536,1536]{1,0:T(8,128)(2,1)}), bf16[192,1536]{1,0:T(8,128)(2,1)}) %reduce-scatter.13.cloned.1.call-update) | async-done | bytes 589840
  1087.5 25.9 %all-reduce.23.cloned.1.call-done = bf16[192,256]{1,0:T(8,128)(2,1)} async-done(((bf16[192,256]{1,0:T(8,128)(2,1)}), bf16[192,256]{1,0:T(8,128)(2,1)}) %all-reduce.23.cloned.1.call-update) | async-done | bytes 98320 | tf_op jit(solution)/shard_map/psum | solution.py:672
  (511 shorter events, 247.0 us)
Async XLA Ops:
  7.2 136.1 %all-gather.11.cloned.1.call-start = ((), (), s32[]{:S(2)}) async-start(), calls=%async_computation.7 | async-start | bytes 1179648 | tf_op jit(solution)/shard_map/all_gather | solution.py:532
  8.7 163.2 %all-gather.7.cloned.1.call-start = ((), (), s32[]{:S(2)}) async-start(), calls=%async_computation.4 | async-start | bytes 6635520 | tf_op jit(solution)/shard_map/all_gather | solution.py:517
  13.3 239.2 %all-gather.9.cloned.1.call-start = ((), (), s32[]{:S(2)}) async-start(), calls=%async_computation.5 | async-start | bytes 5308416 | tf_op jit(solution)/shard_map/all_gather | solution.py:518
  14.8 278.3 %reduce-scatter.7.cloned.1.call-start = ((), (), s32[]{:S(2)}) async-start(), calls=%async_computation.6 | async-start | bytes 1966080 | tf_op jit(solution)/shard_map/reduce_scatter | solution.py:570
  16.4 198.3 %copy-start.77 = (f32[768]{0:T(1024)}, f32[768]{0:T(1024)S(1)}, u32[]{:S(2)}) copy-start(f32[768]{0:T(1024)S(1)} %mul.670) | copy-start | bytes 9220
  16.4 167.7 %copy-start.79 = (f32[768]{0:T(1024)}, f32[768]{0:T(1024)S(1)}, u32[]{:S(2)}) copy-start(f32[768]{0:T(1024)S(1)} %get-tuple-element.428) | copy-start | bytes 9220
  16.4 167.7 %copy-start.81 = (f32[768]{0:T(1024)}, f32[768]{0:T(1024)S(1)}, u32[]{:S(2)}) copy-start(f32[768]{0:T(1024)S(1)} %get-tuple-element.429) | copy-start | bytes 9220
  16.4 167.7 %copy-start.83 = (f32[768]{0:T(1024)}, f32[768]{0:T(1024)S(1)}, u32[]{:S(2)}) copy-start(f32[768]{0:T(1024)S(1)} %get-tuple-element.430) | copy-start | bytes 9220
  16.5 167.7 %copy-start.85 = (f32[768]{0:T(1024)}, f32[768]{0:T(1024)S(1)}, u32[]{:S(2)}) copy-start(f32[768]{0:T(1024)S(1)} %get-tuple-element.431) | copy-start | bytes 9220
  143.1 28.8 %copy-start.87 = (f32[1536]{0:T(1024)S(1)}, f32[1536]{0:T(1024)}, u32[]{:S(2)}) copy-start(f32[1536]{0:T(1024)} %param.31) | copy-start | bytes 18436
  143.1 28.8 %copy-start.128 = (f32[12]{0:T(128)S(1)}, f32[12]{0:T(128)}, u32[]{:S(2)}) copy-start(f32[12]{0:T(128)} %param.39) | copy-start | bytes 148
  143.1 31.0 %copy-start.122 = (f32[12]{0:T(128)}, f32[12]{0:T(128)S(1)}, u32[]{:S(2)}) copy-start(f32[12]{0:T(128)S(1)} %exponential_negate_fusion) | copy-start | bytes 148
  143.2 36.6 %copy-start.118 = (f32[512]{0:T(512)}, f32[512]{0:T(512)S(1)}, u32[]{:S(2)}) copy-start(f32[512]{0:T(512)S(1)} %add_rsqrt_fusion.1) | copy-start | bytes 6148
  143.2 35.4 %copy-start.97 = (f32[1,256]{1,0:T(1,128)}, f32[1,256]{1,0:T(1,128)S(1)}, u32[]{:S(2)}) copy-start(f32[1,256]{1,0:T(1,128)S(1)} %get-tuple-element.508) | copy-start | bytes 3076
  143.2 35.4 %copy-start.99 = (f32[1,256]{1,0:T(1,128)}, f32[1,256]{1,0:T(1,128)S(1)}, u32[]{:S(2)}) copy-start(f32[1,256]{1,0:T(1,128)S(1)} %get-tuple-element.509) | copy-start | bytes 3076
  143.2 35.4 %copy-start.101 = (f32[1,256]{1,0:T(1,128)}, f32[1,256]{1,0:T(1,128)S(1)}, u32[]{:S(2)}) copy-start(f32[1,256]{1,0:T(1,128)S(1)} %get-tuple-element.510) | copy-start | bytes 3076
  143.2 35.4 %copy-start.103 = (f32[1,256]{1,0:T(1,128)}, f32[1,256]{1,0:T(1,128)S(1)}, u32[]{:S(2)}) copy-start(f32[1,256]{1,0:T(1,128)S(1)} %get-tuple-element.511) | copy-start | bytes 3076
  214.7 37.8 %copy-start.109 = (f32[768]{0:T(1024)S(1)}, f32[768]{0:T(1024)}, u32[]{:S(2)}) copy-start(f32[768]{0:T(1024)} %param.42) | copy-start | bytes 9220
  224.6 475.4 %copy-start.105 = (f32[512]{0:T(512)}, f32[512]{0:T(512)S(1)}, u32[]{:S(2)}) copy-start(f32[512]{0:T(512)S(1)} %get-tuple-element.513) | copy-start | bytes 6148
  257.4 431.6 %all-gather.15.cloned.1.call-start = ((), (), s32[]{:S(2)}) async-start(), calls=%async_computation.9 | async-start | bytes 1966080 | tf_op jit(solution)/shard_map/all_gather | solution.py:641
  295.4 105.3 %slice-start = ((s8[6291456]{0:T(1024)(128)(4,1)}), s8[2097152]{0:T(1024)(128)(4,1)S(1)}, s32[]{:S(2)}) async-start(s8[6291456]{0:T(1024)(128)(4,1)} %bitcast.267), calls=%async_computation.15 | async-start | bytes 4194304
  443.6 123.3 %copy-start.43 = (bf16[512,256]{1,0:T(8,128)(2,1)}, bf16[512,256]{1,0:T(8,128)(2,1)S(1)}, u32[]{:S(2)}) copy-start(bf16[512,256]{1,0:T(8,128)(2,1)S(1)} %get-tuple-element.488) | copy-start | bytes 786436
  670.9 147.3 %reduce-scatter.9.cloned.1.call-start = ((), (), s32[]{:S(2)}) async-start(), calls=%async_computation.10 | async-start | bytes 1966080 | tf_op jit(solution)/shard_map/reduce_scatter | solution.py:663
  672.8 27.2 %copy-start.18 = (bf16[512,768]{1,0:T(8,128)(2,1)S(1)}, bf16[512,768]{1,0:T(8,128)(2,1)}, u32[]{:S(2)}) copy-start(bf16[512,768]{1,0:T(8,128)(2,1)} %copy-done.16) | copy-start | bytes 2359300
  672.8 27.2 %copy-start.78 = (f32[768]{0:T(1024)S(1)}, f32[768]{0:T(1024)}, u32[]{:S(2)}) copy-start(f32[768]{0:T(1024)} %copy-done.77) | copy-start | bytes 9220
  672.8 27.2 %copy-start.107 = (f32[512]{0:T(512)S(1)}, f32[512]{0:T(512)}, u32[]{:S(2)}) copy-start(f32[512]{0:T(512)} %get-tuple-element.512) | copy-start | bytes 6148
  788.6 90.4 %all-gather.13.cloned.1.call-start = ((), (), s32[]{:S(2)}) async-start(), calls=%async_computation.8 | async-start | bytes 1966080 | tf_op jit(solution)/shard_map/all_gather | solution.py:625
  789.4 170.3 %reduce-scatter.11.cloned.1.call-start = ((), (), s32[]{:S(2)}) async-start(), calls=%async_computation.12 | async-start | bytes 6635520 | tf_op jit(solution)/shard_map/reduce_scatter | solution.py:671
  795.9 186.1 %all-gather.17.cloned.1.call-start = ((), (), s32[]{:S(2)}) async-start(), calls=%async_computation.11 | async-start | bytes 1966080 | tf_op jit(solution)/shard_map/all_gather | solution.py:682
  821.7 258.7 %reduce-scatter.13.cloned.1.call-start = ((), (), s32[]{:S(2)}) async-start(), calls=%async_computation.14 | async-start | bytes 5308416
  836.3 277.1 %all-reduce.23.cloned.1.call-start = ((), (), s32[]{:S(2)}) async-start(), calls=%async_computation.13 | async-start | bytes 196608 | tf_op jit(solution)/shard_map/psum | solution.py:672
  1085.7 29.3 %copy-start.41 = (bf16[512,1536]{1,0:T(8,128)(2,1)S(1)}, bf16[512,1536]{1,0:T(8,128)(2,1)}, u32[]{:S(2)}) copy-start(bf16[512,1536]{1,0:T(8,128)(2,1)} %all-gather.13.cloned.1.call-done) | copy-start | bytes 4718596
  (116 other events, 584.7 us)
Sparse Core Ops, SparseCore 0:
  10.8 42.3 all-gather.10
  56.0 115.9 all-gather.6
  174.7 77.7 all-gather.8
  257.5 28.2 reduce-scatter.6
  671.0 17.9 all-gather.14
  788.7 29.4 reduce-scatter.8
  820.4 20.0 all-gather.12
  844.1 115.5 reduce-scatter.10
  961.8 20.0 all-gather.16
  985.4 94.9 reduce-scatter.12
  1083.3 30.0 all-reduce.22

commit v3 on v1

--- a/solution.py
+++ b/solution.py
@@ -1,6 +1,10 @@
+import functools
+
 import jax
 import jax.numpy as jnp
 from jax import lax
+from jax.experimental import pallas as pl
+from jax.experimental.pallas import tpu as pltpu
 from jax.sharding import PartitionSpec as P
 
 BLOCK = 256
@@ -135,6 +139,525 @@
         )
 
     return gated_mix, mixer_back
+
+
+MESH = pl.DeviceIdType.MESH
+DMA = pltpu.SemaphoreType.DMA
+VMEM_SPEC = pl.BlockSpec(memory_space=pltpu.VMEM)
+ANY_SPEC = pl.BlockSpec(memory_space=pl.ANY)
+
+
+def place():
+    d = lax.axis_index("dp")
+    t = lax.axis_index("tensor")
+    return d // 2, d % 2, t // 2, t % 2
+
+
+def device(hi, lo, th, tl):
+    return (hi * 2 + lo, th * 2 + tl)
+
+
+def greet(n_hi):
+    hi, lo, th, tl = place()
+    barrier = pltpu.get_barrier_semaphore()
+    others = [device(lax.rem(hi + k, n_hi), lo, th, tl) for k in range(1, n_hi)]
+    others += [device(hi, 1 - lo, th, tl), device(hi, lo, 1 - th, tl), device(hi, lo, th, 1 - tl)]
+    for other in others:
+        pl.semaphore_signal(barrier, inc=1, device_id=other, device_id_type=MESH)
+    pl.semaphore_wait(barrier, len(others))
+
+
+def remote(src, dst, ssem, rsem, to):
+    return pltpu.make_async_remote_copy(
+        src_ref=src, dst_ref=dst, send_sem=ssem, recv_sem=rsem, device_id=to, device_id_type=MESH
+    )
+
+
+class Sends:
+    def __init__(self):
+        self.copies = []
+
+    def push(self, src, dst, ssem, rsem, to):
+        copy = remote(src, dst, ssem, rsem, to)
+        copy.start()
+        self.copies.append(copy)
+
+    def finish(self):
+        for copy in self.copies:
+            copy.wait_send()
+
+
+def arrive(dst, ssem, rsem, to):
+    remote(dst, dst, ssem, rsem, to).wait_recv()
+
+
+TENSOR_SUM_SCRATCH = lambda rows, width, dtype: [
+    pltpu.VMEM((2, rows, width), dtype),
+    pltpu.VMEM((rows, width), dtype),
+    DMA((3,)),
+    DMA((3,)),
+]
+
+
+def tensor_sum_start(sends, part_ref, got_c, ssem, rsem):
+    hi, lo, th, tl = place()
+    to_c = device(hi, lo, th, 1 - tl)
+    for j, y in enumerate((1 - th, th)):
+        sends.push(part_ref.at[y * 2 + 1 - tl], got_c.at[j], ssem.at[j], rsem.at[j], to_c)
+
+
+def tensor_sum_middle(sends, part_ref, got_c, got_y, ssem, rsem):
+    hi, lo, th, tl = place()
+    arrive(got_c.at[0], ssem.at[0], rsem.at[0], device(hi, lo, th, 1 - tl))
+    total = part_ref[(1 - th) * 2 + tl].astype(F32) + got_c[0].astype(F32)
+    got_c[0] = total.astype(got_c.dtype)
+    sends.push(got_c.at[0], got_y, ssem.at[2], rsem.at[2], device(hi, lo, 1 - th, tl))
+
+
+def tensor_sum_end(part_ref, got_c, got_y, ssem, rsem):
+    hi, lo, th, tl = place()
+    arrive(got_c.at[1], ssem.at[1], rsem.at[1], device(hi, lo, th, 1 - tl))
+    total = part_ref[th * 2 + tl].astype(F32) + got_c[1].astype(F32)
+    arrive(got_y, ssem.at[2], rsem.at[2], device(hi, lo, 1 - th, tl))
+    return total + got_y[...].astype(F32)
+
+
+def tensor_spread_start(sends, o_ref, ssem, rsem):
+    hi, lo, th, tl = place()
+    own = o_ref.at[th * 2 + tl]
+    sends.push(own, own, ssem.at[0], rsem.at[0], device(hi, lo, 1 - th, tl))
+    sends.push(own, own, ssem.at[1], rsem.at[1], device(hi, lo, th, 1 - tl))
+
+
+def tensor_spread_end(sends, o_ref, ssem, rsem):
+    hi, lo, th, tl = place()
+    other = o_ref.at[(1 - th) * 2 + tl]
+    to_c = device(hi, lo, th, 1 - tl)
+    arrive(other, ssem.at[0], rsem.at[0], device(hi, lo, 1 - th, tl))
+    sends.push(other, other, ssem.at[2], rsem.at[2], to_c)
+    arrive(o_ref.at[th * 2 + 1 - tl], ssem.at[1], rsem.at[1], to_c)
+    arrive(o_ref.at[(1 - th) * 2 + 1 - tl], ssem.at[2], rsem.at[2], to_c)
+
+
+def gather_steps(n_hi, x_ref, o_ref, own_sem, send_sem, recv_sem):
+    hi, lo, th, tl = place()
+    rows = x_ref.shape[0]
+    half = rows // 2
+    own_block = (hi * 2 + lo) * 4 + th * 2 + tl
+    own = pltpu.make_async_copy(x_ref, o_ref.at[pl.ds(own_block * rows, rows)], own_sem)
+    own.start()
+    sends = Sends()
+
+    def slot(k, f, s, c):
+        return ((c * 2 + s) * 2 + f) * n_hi + k
+
+    def where(h, k, f, s, c):
+        kk = lax.rem(hi + k, n_hi)
+        l = 1 - lo if (f if h == 0 else s) else lo
+        y = 1 - th if (s if h == 0 else f) else th
+        z = 1 - tl if c else tl
+        return ((kk * 2 + l) * 4 + y * 2 + z) * rows + h * half
+
+    def push(h, k, f, s, c, step):
+        at = where(h, k, f, s, c)
+        if k == 0 and not (f or s or c):
+            src = x_ref.at[pl.ds(h * half, half)]
+        else:
+            src = o_ref.at[pl.ds(at, half)]
+        if step == "c":
+            to, r = device(hi, lo, th, 1 - tl), slot(k, f, s, 1)
+        elif step == "s":
+            to = device(hi, lo, 1 - th, tl) if h == 0 else device(hi, 1 - lo, th, tl)
+            r = slot(k, f, 1, 0)
+        elif step == "f":
+            to = device(hi, 1 - lo, th, tl) if h == 0 else device(hi, lo, 1 - th, tl)
+            r = slot(k, 1, 0, 0)
+        else:
+            to, r = device(lax.rem(hi + step, n_hi), lo, th, tl), slot(n_hi - step, 0, 0, 0)
+        sends.push(src, o_ref.at[pl.ds(at, half)], send_sem.at[h, r], recv_sem.at[h, r], to)
+
+    def got(h, k, f, s, c):
+        r = slot(k, f, s, c)
+        arrive(
+            o_ref.at[pl.ds(where(h, k, f, s, c), half)],
+            send_sem.at[h, r], recv_sem.at[h, r], device(hi, lo, th, 1 - tl),
+        )
+
+    for k in range(1, n_hi):
+        for h in range(2):
+            push(h, 0, 0, 0, 0, k)
+    for k in range(n_hi):
+        for h in range(2):
+            if k:
+                got(h, k, 0, 0, 0)
+            for step in ("f", "s", "c"):
+                push(h, k, 0, 0, 0, step)
+        for h in range(2):
+            got(h, k, 1, 0, 0)
+            for step in ("s", "c"):
+                push(h, k, 1, 0, 0, step)
+    for k in range(n_hi):
+        for f in range(2):
+            for h in range(2):
+                got(h, k, f, 1, 0)
+                push(h, k, f, 1, 0, "c")
+    for k in range(n_hi):
+        for f in range(2):
+            for s in range(2):
+                for h in range(2):
+                    got(h, k, f, s, 1)
+    own.wait()
+    sends.finish()
+
+
+def gather_kernel(n_hi, x_ref, o_ref, own_sem, send_sem, recv_sem):
+    greet(n_hi)
+    gather_steps(n_hi, x_ref, o_ref, own_sem, send_sem, recv_sem)
+
+
+def gather_rows(x, n_dp, collective_id):
+    rows, width = x.shape
+    n_hi = n_dp // 2
+    return pl.pallas_call(
+        functools.partial(gather_kernel, n_hi),
+        out_shape=jax.ShapeDtypeStruct((n_dp * 4 * rows, width), x.dtype),
+        in_specs=[ANY_SPEC],
+        out_specs=ANY_SPEC,
+        scratch_shapes=[DMA, DMA((2, 8 * n_hi)), DMA((2, 8 * n_hi))],
+        compiler_params=pltpu.CompilerParams(collective_id=collective_id, has_side_effects=True),
+        name="gather_rows",
+    )(x)
+
+
+def middle_kernel(
+    n_hi, part_ref, x_ref, gain_ref, o_ref, hidden_ref, normed, got_c, got_y, t_send, t_recv,
+    own_sem, send_sem, recv_sem,
+):
+    greet(n_hi)
+    sends = Sends()
+    tensor_sum_start(sends, part_ref, got_c, t_send, t_recv)
+    tensor_sum_middle(sends, part_ref, got_c, got_y, t_send, t_recv)
+    hidden = x_ref[...].astype(F32) + tensor_sum_end(part_ref, got_c, got_y, t_send, t_recv)
+    hidden_ref[...] = hidden
+    normed[...] = (hidden * rms_scale(hidden) * gain_ref[...]).astype(normed.dtype)
+    gather_steps(n_hi, normed, o_ref, own_sem, send_sem, recv_sem)
+    sends.finish()
+
+
+def middle(part, x_piece, gain, n_dp, collective_id):
+    rows, width = x_piece.shape
+    n_hi = n_dp // 2
+    return pl.pallas_call(
+        functools.partial(middle_kernel, n_hi),
+        out_shape=(
+            jax.ShapeDtypeStruct((n_dp * 4 * rows, width), part.dtype),
+            jax.ShapeDtypeStruct((rows, width), F32),
+        ),
+        in_specs=[VMEM_SPEC] * 3,
+        out_specs=(ANY_SPEC, VMEM_SPEC),
+        scratch_shapes=[pltpu.VMEM((rows, width), part.dtype)]
+        + TENSOR_SUM_SCRATCH(rows, width, part.dtype)
+        + [DMA, DMA((2, 8 * n_hi)), DMA((2, 8 * n_hi))],
+        compiler_params=pltpu.CompilerParams(collective_id=collective_id, has_side_effects=True),
+        name="middle",
+    )(part.reshape(4, rows, width), x_piece, gain.reshape(1, width))
+
+
+def scatter_steps(n_hi, sends, p_ref, o_ref, bufs):
+    (stage, from_c, from_f, from_s, from_h,
+     stage_sem, send_c, recv_c, send_f, recv_f, send_s, recv_s, send_h, recv_h) = bufs
+    depth = stage.shape[0]
+    hi, lo, th, tl = place()
+    to_c = device(hi, lo, th, 1 - tl)
+    rows = o_ref.shape[0]
+    half = rows // 2
+
+    def where(h, k, f, s, c):
+        kk = lax.rem(hi + k, n_hi)
+        l = 1 - lo if (f if h == 1 else s) else lo
+        y = 1 - th if (s if h == 1 else f) else th
+        z = 1 - tl if c else tl
+        return ((kk * 2 + l) * 4 + y * 2 + z) * rows + h * half
+
+    order = [(f, s, k, h) for f, s in ((1, 1), (1, 0), (0, 1), (0, 0)) for k in
+             list(range(1, n_hi)) + [0] for h in range(2)]
+
+    def slot(f, s, k):
+        return (f * 2 + s) * n_hi + k
+
+    def first(h):
+        return device(hi, lo, 1 - th, tl) if h == 0 else device(hi, 1 - lo, th, tl)
+
+    def second(h):
+        return device(hi, 1 - lo, th, tl) if h == 0 else device(hi, lo, 1 - th, tl)
+
+    for f, s, k, h in order:
+        n = slot(f, s, k)
+        sends.push(
+            p_ref.at[pl.ds(where(h, k, f, s, 1), half)], from_c.at[h, n], send_c.at[h, n],
+            recv_c.at[h, n], to_c,
+        )
+
+    def load(i):
+        f, s, k, h = order[i]
+        return pltpu.make_async_copy(
+            p_ref.at[pl.ds(where(h, k, f, s, 0), half)], stage.at[i % depth], stage_sem.at[i % depth]
+        )
+
+    for i in range(depth - 1):
+        load(i).start()
+    for i, (f, s, k, h) in enumerate(order):
+        if i + depth - 1 < len(order):
+            load(i + depth - 1).start()
+        load(i).wait()
+        n = slot(f, s, k)
+        arrive(from_c.at[h, n], send_c.at[h, n], recv_c.at[h, n], to_c)
+        total = stage[i % depth].astype(F32) + from_c[h, n].astype(F32)
+        if f == 0:
+            m = s * n_hi + k
+            arrive(from_f.at[h, m], send_f.at[h, m], recv_f.at[h, m], to_c)
+            total = total + from_f[h, m].astype(F32)
+        if f == 0 and s == 0:
+            arrive(from_s.at[h, k], send_s.at[h, k], recv_s.at[h, k], to_c)
+            total = total + from_s[h, k].astype(F32)
+        if f == 0 and s == 0 and k == 0:
+            for j in range(n_hi - 1):
+                arrive(from_h.at[h, j], send_h.at[h, j], recv_h.at[h, j], to_c)
+                total = total + from_h[h, j].astype(F32)
+            o_ref[pl.ds(h * half, half), :] = total
+            continue
+        from_c[h, n] = total.astype(from_c.dtype)
+        src = from_c.at[h, n]
+        if f == 1:
+            m = s * n_hi + k
+            sends.push(src, from_f.at[h, m], send_f.at[h, m], recv_f.at[h, m], first(h))
+        elif s == 1:
+            sends.push(src, from_s.at[h, k], send_s.at[h, k], recv_s.at[h, k], second(h))
+        else:
+            j = n_hi - k - 1
+            sends.push(
+                src, from_h.at[h, j], send_h.at[h, j], recv_h.at[h, j],
+                device(lax.rem(hi + k, n_hi), lo, th, tl),
+            )
+
+
+def scatter_scratch(n_hi, half, width, dtype, depth=4):
+    return [
+        pltpu.VMEM((depth, half, width), dtype),
+        pltpu.VMEM((2, 4 * n_hi, half, width), dtype),
+        pltpu.VMEM((2, 2 * n_hi, half, width), dtype),
+        pltpu.VMEM((2, n_hi, half, width), dtype),
+        pltpu.VMEM((2, n_hi - 1, half, width), dtype),
+        DMA((depth,)),
+        DMA((2, 4 * n_hi)), DMA((2, 4 * n_hi)),
+        DMA((2, 2 * n_hi)), DMA((2, 2 * n_hi)),
+        DMA((2, n_hi)), DMA((2, n_hi)),
+        DMA((2, n_hi - 1)), DMA((2, n_hi - 1)),
+    ]
+
+
+def scatter_kernel(n_hi, p_ref, o_ref, *bufs):
+    greet(n_hi)
+    sends = Sends()
+    scatter_steps(n_hi, sends, p_ref, o_ref, bufs)
+    sends.finish()
+
+
+def scatter_rows(p, n_dp, collective_id):
+    width = p.shape[1]
+    rows = p.shape[0] // (n_dp * 4)
+    n_hi = n_dp // 2
+    return pl.pallas_call(
+        functools.partial(scatter_kernel, n_hi),
+        out_shape=jax.ShapeDtypeStruct((rows, width), F32),
+        in_specs=[ANY_SPEC],
+        out_specs=VMEM_SPEC,
+        scratch_shapes=scatter_scratch(n_hi, rows // 2, width, p.dtype),
+        compiler_params=pltpu.CompilerParams(
+            collective_id=collective_id, has_side_effects=True, vmem_limit_bytes=60 << 20
+        ),
+        name="scatter_rows",
+    )(p)
+
+
+def turn_kernel(
+    n_hi, p_ref, hidden_ref, g2_ref, gain_ref, grad_ref, sum_ref, dm_ref, total_ref, sp_send, sp_recv, *bufs
+):
+    hi, lo, th, tl = place()
+    greet(n_hi)
+    sends = Sends()
+    scatter_steps(n_hi, sends, p_ref, total_ref, bufs)
+    grad = total_ref[...]
+    hidden = hidden_ref[...]
+    scale = rms_scale(hidden)
+    weighted = gain_ref[...] * grad
+    sum_ref[...] = jnp.sum(grad * hidden * scale, axis=0, keepdims=True)
+    mean = jnp.mean(weighted * hidden, axis=-1, keepdims=True)
+    grad = g2_ref[...].astype(F32) + scale * weighted - hidden * (scale * scale * scale) * mean
+    grad_ref[...] = grad
+    dm_ref[th * 2 + tl] = grad.astype(dm_ref.dtype)
+    tensor_spread_start(sends, dm_ref, sp_send, sp_recv)
+    tensor_spread_end(sends, dm_ref, sp_send, sp_recv)
+    sends.finish()
+
+
+def turn(p, hidden, g2_piece, gain, n_dp, collective_id):
+    rows, width = hidden.shape
+    n_hi = n_dp // 2
+    return pl.pallas_call(
+        functools.partial(turn_kernel, n_hi),
+        out_shape=(
+            jax.ShapeDtypeStruct((rows, width), F32),
+            jax.ShapeDtypeStruct((1, width), F32),
+            jax.ShapeDtypeStruct((4, rows, width), p.dtype),
+        ),
+        in_specs=[ANY_SPEC] + [VMEM_SPEC] * 3,
+        out_specs=(VMEM_SPEC,) * 3,
+        scratch_shapes=[pltpu.VMEM((rows, width), F32), DMA((3,)), DMA((3,))]
+        + scatter_scratch(n_hi, rows // 2, width, p.dtype),
+        compiler_params=pltpu.CompilerParams(
+            collective_id=collective_id, has_side_effects=True, vmem_limit_bytes=60 << 20
+        ),
+        name="turn",
+    )(p, hidden, g2_piece, gain.reshape(1, width))
+
+
+def tail_kernel(
+    n_hi, wide, bc_at, w_ref, part_ref, grad_ref, x_ref, gain_ref, small_ref,
+    ow_ref, ox_ref, os_ref,
+    stage, from_f, from_h, stage_sem, send_f, recv_f, send_h, recv_h,
+    got_c, got_y, t_send, t_recv, sp_send, sp_recv,
+    small, small_f, small_h, small_t, sm_send, sm_recv, smh_send, smh_recv,
+    bc_own, bc_got, bc_send, bc_recv,
+):
+    hi, lo, th, tl = place()
+    to_f, to_y, to_c = device(hi, 1 - lo, th, tl), device(hi, lo, 1 - th, tl), device(hi, lo, th, 1 - tl)
+    half = w_ref.shape[2]
+    greet(n_hi)
+    sends = Sends()
+    order = [(k, h) for k in list(range(1, n_hi)) + [0] for h in range(2)]
+
+    def owner(k, l):
+        return lax.rem(hi + k, n_hi) * 2 + l
+
+    for k, h in order:
+        sends.push(w_ref.at[owner(k, 1 - lo), h], from_f.at[h, k], send_f.at[h, k], recv_f.at[h, k], to_f)
+    loads = [
+        pltpu.make_async_copy(w_ref.at[owner(k, lo), h], stage.at[h, k], stage_sem.at[h, k])
+        for k, h in order
+    ]
+    for copy in loads:
+        copy.start()
+    tensor_sum_start(sends, part_ref, got_c, t_send, t_recv)
+    tensor_sum_middle(sends, part_ref, got_c, got_y, t_send, t_recv)
+    grad = tensor_sum_end(part_ref, got_c, got_y, t_send, t_recv)
+    x = x_ref[...].astype(F32)
+    scale = rms_scale(x)
+    weighted = gain_ref[...] * grad
+    mean = jnp.mean(weighted * x, axis=-1, keepdims=True)
+    ox_ref[th * 2 + tl] = (
+        grad_ref[...] + scale * weighted - x * (scale * scale * scale) * mean
+    ).astype(ox_ref.dtype)
+    tensor_spread_start(sends, ox_ref, sp_send, sp_recv)
+    small[...] = small_ref[...]
+    small[0:1, :] = jnp.sum(grad * x * scale, axis=0, keepdims=True)
+    sends.push(small, small_f, sm_send.at[0], sm_recv.at[0], to_f)
+
+    finals = []
+    for i, (k, h) in enumerate(order):
+        loads[i].wait()
+        arrive(from_f.at[h, k], send_f.at[h, k], recv_f.at[h, k], to_c)
+        if k == 0:
+            continue
+        from_f[h, k] = (stage[h, k].astype(F32) + from_f[h, k].astype(F32)).astype(from_f.dtype)
+        j = n_hi - k - 1
+        sends.push(
+            from_f.at[h, k], from_h.at[h, j], send_h.at[h, j], recv_h.at[h, j],
+            device(lax.rem(hi + k, n_hi), lo, th, tl),
+        )
+        if i == 0:
+            tensor_spread_end(sends, ox_ref, sp_send, sp_recv)
+        if i == 1:
+            arrive(small_f, sm_send.at[0], sm_recv.at[0], to_c)
+            small_h[hi] = small[...] + small_f[...]
+            for q in range(1, n_hi):
+                sends.push(
+                    small_h.at[hi], small_h.at[hi], smh_send.at[q - 1], smh_recv.at[q - 1],
+                    device(lax.rem(hi + q, n_hi), lo, th, tl),
+                )
+    for q in range(1, n_hi):
+        arrive(small_h.at[lax.rem(hi - q + n_hi, n_hi)], smh_send.at[q - 1], smh_recv.at[q - 1], to_c)
+    total = small_h[0]
+    for q in range(1, n_hi):
+        total = total + small_h[q]
+    os_ref[...] = total
+    sends.push(os_ref.at[pl.ds(0, wide)], small_t.at[0], sm_send.at[1], sm_recv.at[1], to_c)
+    for h in range(2):
+        total = stage[h, 0].astype(F32) + from_f[h, 0].astype(F32)
+        for j in range(n_hi - 1):
+            arrive(from_h.at[h, j], send_h.at[h, j], recv_h.at[h, j], to_c)
+            total = total + from_h[h, j].astype(F32)
+        ow_ref[h] = total
+        bc_own[0, h] = total[:, bc_at : bc_at + bc_own.shape[3]].astype(bc_own.dtype)
+    sends.push(bc_own.at[0], bc_got.at[0], bc_send.at[0], bc_recv.at[0], to_c)
+    arrive(small_t.at[0], sm_send.at[1], sm_recv.at[1], to_c)
+    small_t[2] = os_ref[pl.ds(0, wide), :] + small_t[0]
+    sends.push(small_t.at[2], small_t.at[1], sm_send.at[2], sm_recv.at[2], to_y)
+    arrive(bc_got.at[0], bc_send.at[0], bc_recv.at[0], to_c)
+    bc_own[1] = (bc_own[0].astype(F32) + bc_got[0].astype(F32)).astype(bc_own.dtype)
+    sends.push(bc_own.at[1], bc_got.at[1], bc_send.at[1], bc_recv.at[1], to_y)
+    arrive(small_t.at[1], sm_send.at[2], sm_recv.at[2], to_c)
+    arrive(bc_got.at[1], bc_send.at[1], bc_recv.at[1], to_c)
+    for h in range(2):
+        ow_ref[h, :, bc_at : bc_at + bc_own.shape[3]] = bc_own[1, h].astype(F32) + bc_got[1, h].astype(F32)
+    sends.finish()
+    os_ref[pl.ds(0, wide), :] = small_t[2] + small_t[1]
+
+
+def tail(w, part, grad_one, x_piece, gain, small, wide, bc_at, bc_width, n_dp, collective_id):
+    rows, width = x_piece.shape
+    n_hi = n_dp // 2
+    half = w.shape[0] // (2 * n_dp)
+    w_width = w.shape[1]
+    dt = w.dtype
+    return pl.pallas_call(
+        functools.partial(tail_kernel, n_hi, wide, bc_at),
+        out_shape=(
+            jax.ShapeDtypeStruct((2, half, w_width), F32),
+            jax.ShapeDtypeStruct((4, rows, width), dt),
+            jax.ShapeDtypeStruct(small.shape, F32),
+        ),
+        in_specs=[ANY_SPEC] + [VMEM_SPEC] * 5,
+        out_specs=(VMEM_SPEC,) * 3,
+        scratch_shapes=[
+            pltpu.VMEM((2, n_hi, half, w_width), dt),
+            pltpu.VMEM((2, n_hi, half, w_width), dt),
+            pltpu.VMEM((2, n_hi - 1, half, w_width), dt),
+            DMA((2, n_hi)),
+            DMA((2, n_hi)), DMA((2, n_hi)),
+            DMA((2, n_hi - 1)), DMA((2, n_hi - 1)),
+        ]
+        + TENSOR_SUM_SCRATCH(rows, width, part.dtype)
+        + [
+            DMA((3,)), DMA((3,)),
+            pltpu.VMEM(small.shape, F32),
+            pltpu.VMEM(small.shape, F32),
+            pltpu.VMEM((n_hi,) + small.shape, F32),
+            pltpu.VMEM((3, wide, small.shape[1]), F32),
+            DMA((3,)), DMA((3,)),
+            DMA((n_hi - 1,)), DMA((n_hi - 1,)),
+            pltpu.VMEM((2, 2, half, bc_width), dt),
+            pltpu.VMEM((2, 2, half, bc_width), dt),
+            DMA((2,)), DMA((2,)),
+        ],
+        compiler_params=pltpu.CompilerParams(
+            collective_id=collective_id, has_side_effects=True, vmem_limit_bytes=60 << 20
+        ),
+        name="tail",
+    )(
+        w.reshape(n_dp, 2, half, w_width), part.reshape(4, rows, width), grad_one, x_piece,
+        gain.reshape(1, width), small,
+    )
 
 
 def local(
@@ -180,22 +703,24 @@
     full_inner = inner * n_t
     rows = w_zx.shape[0]
     n_sh = w_shared_gu.shape[2]
-    everyone = ("dp", "tensor")
-
+
+    dt_at = 2 * inner + 2 * state
+    first_width = dt_at + heads + -(dt_at + heads) % 128
     first = jnp.concatenate(
-        [w_zx.reshape(rows, 2 * inner), w_bc, w_dt], axis=1
-    ).astype(BF)
-    second = jnp.concatenate(
-        [w_out, w_shared_gu.reshape(rows, 2 * n_sh), w_shared_down], axis=1
+        [
+            w_zx.reshape(rows, 2 * inner),
+            w_bc,
+            w_dt,
+            jnp.zeros((rows, first_width - dt_at - heads), F32),
+        ],
+        axis=1,
     ).astype(BF)
     first = lax.all_gather(first, "dp", axis=0, tiled=True)
-    second = lax.all_gather(second, "dp", axis=0, tiled=True)
-    proj_zx = first[:, : 2 * inner]
-    proj_bc = first[:, 2 * inner : 2 * inner + 2 * state]
-    proj_dt = first[:, 2 * inner + 2 * state :]
-    proj_out = second[:, :inner]
-    shared_gu = second[:, inner : inner + 2 * n_sh]
-    shared_down = second[:, inner + 2 * n_sh :]
+    proj_out = lax.all_gather(w_out.astype(BF), "dp", axis=0, tiled=True)
+    shared = jnp.concatenate([w_shared_gu.reshape(rows, 2 * n_sh), w_shared_down], axis=1)
+    shared = lax.all_gather(shared.astype(BF), "dp", axis=0, tiled=True)
+    shared_gu = shared[:, : 2 * n_sh]
+    shared_down = shared[:, 2 * n_sh :]
 
     live = (jnp.arange(slots, dtype=jnp.int32) < lengths[0]).astype(F32)
     g2 = cotangent.astype(F32) * live[:, None]
@@ -203,9 +728,16 @@
     expert_range = jnp.arange(n_experts, dtype=jnp.int32)
     chosen = routes[:, :, None] == expert_range[None, None, :]
     weights = jnp.sum(jnp.where(chosen, route_w[:, :, None], 0.0), axis=1)
-    weights = lax.all_gather(weights, "dp", axis=0, tiled=True)
-    weights = lax.dynamic_slice_in_dim(weights, my_dp * n_local, n_local, axis=1)
-    weights = weights.reshape(n_dp, slots, n_local)
+    high = weights.astype(BF)
+    low = (weights - high.astype(F32)).astype(BF)
+    table = jnp.concatenate([g2_low, high, low], axis=1)
+    table = lax.dynamic_slice_in_dim(table, my_t * piece, piece, axis=0)
+    table = gather_rows(table, n_dp, 1)
+    g2_all = table[:, :width].reshape(n_dp, slots, width)
+    g2_piece = lax.dynamic_slice_in_dim(g2_low, my_t * piece, piece, axis=0)
+    high = lax.dynamic_slice_in_dim(table, width + my_dp * n_local, n_local, axis=1)
+    low = lax.dynamic_slice_in_dim(table, width + n_experts + my_dp * n_local, n_local, axis=1)
+    weights = (high.astype(F32) + low.astype(F32)).reshape(n_dp, slots, n_local)
     member = (weights > 0.0).astype(BF)
     before = (
         jnp.arange(slots)[:, None] > jnp.arange(slots)[None, :]
@@ -221,18 +753,16 @@
     )
     pick = pick.astype(BF).reshape(n_dp, n_local * cap, slots)
 
-    g2_piece = lax.dynamic_slice_in_dim(g2_low, my_t * piece, piece, axis=0)
-    g2_all = lax.all_gather(g2_piece, everyone, axis=0, tiled=True).reshape(n_dp, slots, width)
-
     gate_w = w_exp_gu.astype(BF).reshape(n_local, width, -1)
     down_w = w_exp_down.astype(BF)
 
     x_float = x_in.astype(F32)
     scale_one = rms_scale(x_float)
     normed_one = (x_float * scale_one * ln1_gain).astype(BF)
-    zx = dotf("td,df->tf", normed_one, proj_zx)
-    bc_proj = dotf("td,df->tf", normed_one, proj_bc)
-    dt_proj = dotf("td,df->tf", normed_one, proj_dt)
+    firsts = dotf("td,df->tf", normed_one, first)
+    zx = firsts[:, : 2 * inner]
+    bc_proj = firsts[:, 2 * inner : dt_at]
+    dt_proj = firsts[:, dt_at : dt_at + heads]
 
     gated_mix, mixer_back = mixer_forward(
         zx, bc_proj, dt_proj, conv_x, conv_x_bias, conv_bc, conv_bc_bias, dt_bias, a_log, d_skip
@@ -241,14 +771,8 @@
     scale_mix = lax.rsqrt(squares / full_inner + EPSILON)[:, None]
     normed_mix = (gated_mix * scale_mix * gnorm_gain).astype(BF)
     mixer_part = dotf("tc,dc->td", normed_mix, proj_out).astype(BF)
-    mixer_out = lax.psum_scatter(
-        mixer_part, "tensor", scatter_dimension=0, tiled=True
-    ).astype(F32)
-    x_piece = lax.dynamic_slice_in_dim(x_float, my_t * piece, piece, axis=0)
-    hidden_one = x_piece + mixer_out
-    scale_two = rms_scale(hidden_one)
-    normed_two = (hidden_one * scale_two * ln2_gain).astype(BF)
-    all_rows = lax.all_gather(normed_two, everyone, axis=0, tiled=True)
+    x_piece = lax.dynamic_slice_in_dim(x_in, my_t * piece, piece, axis=0)
+    all_rows, hidden_one = middle(mixer_part, x_piece, ln2_gain, n_dp, 2)
     mine = lax.dynamic_slice_in_dim(all_rows, my_dp * slots, slots, axis=0)
     all_rows = all_rows.reshape(n_dp, slots, width)
 
@@ -290,16 +814,15 @@
     dxn_part = dotf("sct,scd->std", pick, back)
     own = (jnp.arange(n_dp) == my_dp).astype(F32)[:, None, None]
     dxn_part = (dxn_part + own * grad_normed_shared[None]).astype(BF)
-    grad_normed_two = lax.psum_scatter(
-        dxn_part.reshape(n_dp * slots, width), everyone, scatter_dimension=0, tiled=True
-    ).astype(F32)
+    grad_one, sum_ln2, dm = turn(
+        dxn_part.reshape(n_dp * slots, width), hidden_one, g2_piece, ln2_gain, n_dp, 3
+    )
+    dm = dm.reshape(slots, width)
 
     forth = by_source((dotf("erf,efd->erd", act, down_w) * sw).astype(BF))
     out_part = dotf("sct,scd->std", pick, forth)
     out_part = (out_part + own * shared_part[None]).astype(BF)
-    ffn_out = lax.psum_scatter(
-        out_part.reshape(n_dp * slots, width), everyone, scatter_dimension=0, tiled=True
-    ).astype(F32)
+    ffn_out = scatter_rows(out_part.reshape(n_dp * slots, width), n_dp, 4)
     layer_out = lax.all_gather(
         (hidden_one + ffn_out).astype(BF), "tensor", axis=0, tiled=True
     )
@@ -308,15 +831,6 @@
     grad_shared_down = dotf("td,tf->df", g2_low, shared_act)
     grad_shared_gu = dotf("td,tf->df", mine, grad_shared_pre)
 
-    weighted_two = ln2_gain * grad_normed_two
-    grad_ln2 = jnp.sum(grad_normed_two * hidden_one * scale_two, axis=0)
-    g2_own = g2_piece.astype(F32)
-    grad_one = (
-        g2_own
-        + scale_two * weighted_two
-        - hidden_one * scale_two**3 * jnp.mean(weighted_two * hidden_one, axis=-1, keepdims=True)
-    )
-    dm = lax.all_gather(grad_one.astype(BF), "tensor", axis=0, tiled=True)
     grad_out_proj = dotf("td,tc->dc", dm, normed_mix)
     grad_normed_mix = dotf("td,dc->tc", dm, proj_out)
     weighted_mix = gnorm_gain * grad_normed_mix
@@ -335,39 +849,49 @@
         grad_a_log,
         grad_d_skip,
     ) = mixer_back(grad_gated)
-    bc_low = grad_bc.astype(BF)
-    grad_first = jnp.concatenate([grad_zx, bc_low, grad_dt_low], axis=1)
-    grad_input_part = dotf("tf,df->td", grad_first, first)
-    grad_input_piece = lax.psum_scatter(
-        grad_input_part.astype(BF), "tensor", scatter_dimension=0, tiled=True
-    ).astype(F32)
+    grad_first = jnp.concatenate(
+        [
+            grad_zx,
+            grad_bc.astype(BF),
+            grad_dt_low,
+            jnp.zeros((slots, first_width - dt_at - heads), BF),
+        ],
+        axis=1,
+    )
+    grad_input_part = dotf("tf,df->td", grad_first, first).astype(BF)
     grad_first_w = dotf("td,tf->df", normed_one, grad_first).astype(BF)
-    grad_second_w = jnp.concatenate(
-        [grad_out_proj, grad_shared_gu, grad_shared_down], axis=1
-    ).astype(BF)
-    grad_second_w = lax.psum_scatter(grad_second_w, "dp", scatter_dimension=0, tiled=True)
-    grad_first_w = lax.psum_scatter(grad_first_w, "dp", scatter_dimension=0, tiled=True)
-    grad_bc_w = lax.psum(grad_first_w[:, 2 * inner : 2 * inner + 2 * state], "tensor")
-
-    scale_piece = lax.dynamic_slice_in_dim(scale_one, my_t * piece, piece, axis=0)
-    weighted_one = ln1_gain * grad_input_piece
-    grad_ln1 = jnp.sum(grad_input_piece * x_piece * scale_piece, axis=0)
-    grad_x = (
-        grad_one
-        + scale_piece * weighted_one
-        - x_piece * scale_piece**3 * jnp.mean(weighted_one * x_piece, axis=-1, keepdims=True)
-    )
-    grad_x = lax.all_gather(grad_x.astype(BF), "tensor", axis=0, tiled=True).astype(F32)
-
-    wide = jnp.concatenate(
-        [grad_ln1, grad_ln2, grad_conv_bc.reshape(-1), grad_conv_bc_bias]
-    )
-    wide = lax.psum(wide, everyone)
-    narrow = jnp.concatenate(
-        [grad_conv_x.reshape(-1), grad_conv_x_bias, grad_gnorm, grad_dt_bias, grad_a_log, grad_d_skip]
-    )
-    narrow = lax.psum(narrow, "dp")
+    grad_shared_w = jnp.concatenate([grad_shared_gu, grad_shared_down], axis=1).astype(BF)
+    grad_shared_w = lax.psum_scatter(grad_shared_w, "dp", scatter_dimension=0, tiled=True)
+    grad_out_w = lax.psum_scatter(
+        grad_out_proj.astype(BF), "dp", scatter_dimension=0, tiled=True
+    )
+
+    def lanes(*vectors):
+        vector = jnp.concatenate([v.reshape(-1) for v in vectors])
+        return jnp.pad(vector, (0, -vector.shape[0] % (8 * width))).reshape(-1, width)
+
     taps = conv_x.shape[0]
+    wide = lanes(jnp.zeros((width,), F32), sum_ln2, grad_conv_bc, grad_conv_bc_bias)
+    n_wide = wide.shape[0]
+    narrow = lanes(
+        grad_conv_x, grad_conv_x_bias, grad_gnorm, grad_dt_bias, grad_a_log, grad_d_skip
+    )
+    first_f, grad_x, sums = tail(
+        grad_first_w,
+        grad_input_part,
+        grad_one,
+        x_piece,
+        ln1_gain,
+        jnp.concatenate([wide, narrow], axis=0),
+        n_wide,
+        2 * inner,
+        2 * state,
+        n_dp,
+        5,
+    )
+    first_f = first_f.reshape(rows, first_width)
+    grad_x = grad_x.reshape(slots, width).astype(F32)
+    wide, narrow = sums[:n_wide].reshape(-1), sums[n_wide:].reshape(-1)
     at = [0]
 
     def take(vector, *shape):
@@ -389,15 +913,14 @@
     o_dt_bias = take(narrow, heads)
     o_a_log = take(narrow, heads)
     o_d_skip = take(narrow, heads)
-    first_f = grad_first_w.astype(F32)
-    second_f = grad_second_w.astype(F32)
+    shared_f = grad_shared_w.astype(F32)
     return (
         layer_out,
         grad_x,
         o_ln1,
         first_f[:, : 2 * inner].reshape(rows, 2, inner),
-        grad_bc_w.astype(F32),
-        first_f[:, 2 * inner + 2 * state :],
+        first_f[:, 2 * inner : dt_at],
+        first_f[:, dt_at : dt_at + heads],
         o_conv_x,
         o_conv_x_bias,
         o_conv_bc,
@@ -406,10 +929,10 @@
         o_a_log,
         o_d_skip,
         o_gnorm,
-        second_f[:, :inner],
+        grad_out_w.astype(F32),
         o_ln2,
-        second_f[:, inner : inner + 2 * n_sh].reshape(rows, 2, n_sh),
-        second_f[:, inner + 2 * n_sh :],
+        shared_f[:, : 2 * n_sh].reshape(rows, 2, n_sh),
+        shared_f[:, 2 * n_sh :],
         grad_exp_gu,
         grad_exp_down,
     )

time: 1340 us -> 1080 us (0.81)
  waiting for transfers between devices: 769 us -> 0.14 us
  Pallas kernels: 0 us -> 549 us
  blocking collectives: 88.4 us -> 10.5 us
  local copies, waits for them, and re-layouts: 151 us -> 179 us
    pallas_call x0 -> x5, Pallas kernels: none -> 549 us  [the longest x1 151 us: tail(): pl.pallas_call(functools.partial(tail_kernel, n_hi, wide, bc_at), out_sha...]
    reduce_scatter x5 -> x1, waiting for transfers between devices: 316 us -> 0.01 us  [local(): lax.psum_scatter(grad_out_proj.astype(BF), 'dp', scatter_dimension=0, til...]
    all_gather x6 -> x2, waiting for transfers between devices: 241 us -> 0.04 us  [the longest x1 0.02 us: local(): shared = lax.all_gather(shared.astype(BF), 'dp', axis=0, tiled=True)]
    unnamed x16 -> x7, waiting for transfers between devices: 95.9 us -> 0.1 us
    all_gather x1, waiting for transfers between devices: 90.3 us -> 0.01 us  [local(): first = lax.all_gather(first, 'dp', axis=0, tiled=True)]
    psum x2 -> x0, blocking collectives: 76.8 us -> none  [the longest x1 50.4 us: local(): wide = lax.psum(wide, everyone)]
    psum x1 -> x0, waiting for transfers between devices: 25.7 us -> none  [local(): lax.psum(grad_first_w[:, 2 * inner:2 * inner + 2 * state], 'tensor')]
    unnamed x303 -> x259, local copies, waits for them, and re-layouts: 50.5 us -> 37.9 us
  transfers between devices with their start and end apart: 15 -> 6, of which waited for: 12 -> 0; matrix products, arithmetic and copies ran while one was open for 18% -> 29% of each run, Pallas kernels for 0% -> 35%
where the time goes in v3:
time: 1080 us; the launch traced here: 1070 us
  Pallas kernels  549 us (51%)
  matrix products  223 us (21%)
  local copies, waits for them, and re-layouts  179 us (17%)
  other arithmetic  92 us (9%)
  between operations  16.7 us (2%)
    dot_general x23, matrix products, dotf(): return jnp.einsum(spec, a, b, preferred_element_type=F32)  174 us
    pallas_call x1, Pallas kernels, tail(): pl.pallas_call(functools.partial(tail_kernel, n_hi, wide, bc_at), out_sha...  151 us
    pallas_call x1, Pallas kernels, gather_rows(): pl.pallas_call(functools.partial(gather_kernel, n_hi), out_shape=jax.Shap...  127 us
    pallas_call x1, Pallas kernels, turn(): pl.pallas_call(functools.partial(turn_kernel, n_hi), out_shape=(jax.Shape...  95.9 us
    pallas_call x1, Pallas kernels, middle(): pl.pallas_call(functools.partial(middle_kernel, n_hi), out_shape=(jax.Sha...  92.2 us
    pallas_call x1, Pallas kernels, scatter_rows(): pl.pallas_call(functools.partial(scatter_kernel, n_hi), out_shape=jax.Sha...  82.6 us
    unnamed x259, local copies, waits for them, and re-layouts  37.9 us
    dot_general x3, matrix products, ssd_scan(): jnp.einsum('kij,kijh,kjhp->kihp', intersection, decay_mask, scaled, preci...  24.3 us
  transfers between devices with their start and end apart: 6, of which 0 were waited for; matrix products, arithmetic and copies ran while one was open for 29% of the time, Pallas kernels for 35%

profile of v3, /device:TPU:9, one launch (start us, length us, event | category | flops | bytes accessed | tf_op | source)
XLA Modules:
  0.0 1070.5 jit_solution(18106744405436422055)
XLA Ops:
  26.7 9.4 convert_element_type.156
  36.2 10.9 %reshape.368 = bf16[8,1536,256]{2,1,0:T(8,128)(2,1)} reshape(bf16[8,1536,2,128]{3,2,1,0:T(2,128)(2,1)} %convert_element_type.156) | data formatting | bytes 12582912 | tf_op jit(solution)/shard_map/reshape | solution.py:756
  47.0 127.0 %gather_rows.1 = bf16[4096,1664]{1,0:T(8,128)(2,1)} custom-call(bf16[128,1664]{1,0:T(8,128)(2,1)} %constant_dynamic-slice_fusion.5.x_ref), custom_call_target="tpu_custom_call" | custom-call | tf_op jit(solution)/shard_map/gather_rows/pallas_call | solution.py:321
  174.0 10.5 slice.192
  190.6 17.1 %fusion.138 = f32[8,512,1536]{2,1,0:T(8,128)} fusion(pred[8,512,512]{2,1,0:T(32,128)(4,1)S(1)} %bitcast_compare_fusion, bf16[8,512,1536]{2,1,0:T(8,128)(2,1)} %bitcast.261), kind=kOutput, calls=%fused_computation.259 | convolution fusion | flops 6442450944 | bytes 39845888 | tf_op jit(solution)/shard_map/sct,std->scd/dot_general | solution.py:33
  207.8 18.3 %copy.345 = f32[8,8,64,1536]{3,2,0,1:T(8,128)} copy(f32[8,8,64,1536]{3,2,1,0:T(8,128)} %bitcast.256) | data formatting | bytes 50331648 | tf_op jit(solution)/shard_map/reshape | solution.py:791
  226.1 13.8 %fusion.3 = bf16[8,512,1536]{2,1,0:T(8,128)(2,1)} fusion(f32[8,8,64,1536]{3,2,0,1:T(8,128)} %copy.345, f32[8,512]{1,0:T(8,128)S(1)} %mul.581), kind=kLoop, calls=%fused_computation.14 | loop fusion | flops 12582912 | bytes 37765120 | tf_op jit(solution)/shard_map/convert_element_type | solution.py:802
  239.9 5.7 fusion.105
  265.2 7.4 while.34
  275.2 7.6 fusion.44
  301.1 92.2 %middle.1 = (bf16[4096,1536]{1,0:T(8,128)(2,1)}, f32[128,1536]{1,0:T(8,128)}) custom-call(bf16[4,128,1536]{2,1,0:T(8,128)(2,1)} %bitcast.295, bf16[128,1536]{1,0:T(8,128)(2,1)} %constant_dynamic-slice_fusion.6.x_ref, f32[1,1536]{1,0:T(1,128)} %reshape.363.gain_ref), custom_call_target="tpu_custom_call" | custom-call | tf_op jit(solution)/shard_map/middle/pallas_call | solution.py:350
  400.6 14.6 %convolution_convert_fusion.1 = bf16[8,512,1536]{2,1,0:T(8,128)(2,1)} fusion(pred[8,512,512]{2,1,0:T(32,128)(4,1)} %copy-done.16, bf16[8,512,1536]{2,1,0:T(8,128)(2,1)} %bitcast.326), kind=kOutput, calls=%fused_computation.19 | convolution fusion | flops 6448742400 | bytes 27262976 | tf_op jit(solution)/shard_map/sct,std->scd/dot_general | solution.py:33
  415.2 10.8 %copy.336 = bf16[8,8,64,1536]{3,2,1,0:T(8,128)(2,1)} copy(bf16[8,8,64,1536]{3,2,0,1:T(8,128)(2,1)} %bitcast.273) | data formatting | bytes 25165824 | tf_op jit(solution)/shard_map/transpose | solution.py:791
  426.1 8.6 fusion.137
  434.7 11.0 %multiply_convert_fusion.3 = (bf16[8,512,128]{1,2,0:T(8,128)(2,1)}, bf16[8,512,128]{1,2,0:T(8,128)(2,1)}, bf16[8,512,128]{1,2,0:T(8,128)(2,1)}) fusion(f32[8,512,256]{1,2,0:T(8,128)} %fusion.137, bf16[8,512,1536]{2,1,0:T(8,128)(2,1)} %fusion.3, f32[8,128,1536]{2,1,0:T(8,128)} %param.48), kind=kOutput, calls=%fused_computation.63 | convolution fusion | flops 1620049920 | bytes 26214400 | tf_op jit(solution)/shard_map/erd,efd->erf/dot_general | solution.py:33
  445.6 8.8 convolution_convert_fusion
  454.4 10.8 %copy.347 = bf16[8,8,64,1536]{3,2,1,0:T(8,128)(2,1)} copy(bf16[8,8,64,1536]{3,2,0,1:T(8,128)(2,1)} %bitcast.257) | data formatting | bytes 25165824 | tf_op jit(solution)/shard_map/transpose | solution.py:796
  471.7 15.1 %add_convert_fusion = bf16[8,512,1536]{2,1,0:T(8,128)(2,1)} fusion(pred[8,512,512]{2,1,0:T(32,128)(4,1)S(1)} %copy-done.17, bf16[8,512,1536]{2,1,0:T(8,128)(2,1)} %bitcast.270, f32[512,1536]{1,0:T(8,128)} %fusion.60, f32[8]{0:T(128)S(1)} %copy-done.123), kind=kOutput, calls=%fused_computation.15 | convolution fusion | flops 6461325312 | bytes 30408736 | tf_op jit(solution)/shard_map/sct,scd->std/dot_general | solution.py:33
  486.8 95.9 %turn.1 = (f32[128,1536]{1,0:T(8,128)}, f32[1,1536]{1,0:T(1,128)}, bf16[4,128,1536]{2,1,0:T(8,128)(2,1)}) custom-call(bf16[4096,1536]{1,0:T(8,128)(2,1)} %bitcast.274, f32[128,1536]{1,0:T(8,128)} %get-tuple-element.204.hidden_ref, bf16[128,1536]{1,0:T(8,128)(2,1)} %constant_dynamic-slice_fusion.4.g2_ref, f32[1,1536]{1,0:T(1,128)} %reshape.363.gain_ref), custom_call_target="tpu_custom_call" | custom-call | tf_op jit(solution)/shard_map/turn/pallas_call | solution.py:507
  608.3 9.4 while.35
  617.7 11.5 %multiply_convert_fusion = bf16[8,512,1536]{2,1,0:T(8,128)(2,1)} fusion(bf16[8,512,128]{1,2,0:T(8,128)(2,1)} %get-tuple-element.527, f32[8,512]{1,0:T(8,128)S(1)} %mul.581, f32[8,128,1536]{2,1,0:T(8,128)} %param.48), kind=kOutput, calls=%fused_computation.17 | convolution fusion | flops 1624768512 | bytes 19939328 | tf_op jit(solution)/shard_map/erf,efd->erd/dot_general | solution.py:33
  629.2 10.9 %copy.341 = bf16[8,8,64,1536]{3,2,1,0:T(8,128)(2,1)} copy(bf16[8,8,64,1536]{3,2,0,1:T(8,128)(2,1)} %bitcast.262) | data formatting | bytes 25165824 | tf_op jit(solution)/shard_map/transpose | solution.py:796
  643.6 15.5 %add_convert_fusion.1 = bf16[8,512,1536]{2,1,0:T(8,128)(2,1)} fusion(pred[8,512,512]{2,1,0:T(32,128)(4,1)S(1)} %copy-done.18, bf16[8,512,1536]{2,1,0:T(8,128)(2,1)} %bitcast.271, f32[512,1536]{1,0:T(8,128)} %fusion.98, f32[8]{0:T(128)S(1)} %copy-done.124), kind=kOutput, calls=%fused_computation.16 | convolution fusion | flops 6461325312 | bytes 30408736 | tf_op jit(solution)/shard_map/sct,scd->std/dot_general | solution.py:33
  659.1 82.6 %scatter_rows.1 = f32[128,1536]{1,0:T(8,128)} custom-call(bf16[4096,1536]{1,0:T(8,128)(2,1)} %bitcast.272), custom_call_target="tpu_custom_call" | custom-call | tf_op jit(solution)/shard_map/scatter_rows/pallas_call | solution.py:470
  754.0 6.7 fusion.73
  766.0 10.1 fusion.15
  797.4 6.5 bitcast_add_fusion.2
  837.6 7.4 convolution_convert_fusion.5
  851.1 151.3 %tail.1 = (f32[2,96,1920]{2,1,0:T(8,128)}, bf16[4,128,1536]{2,1,0:T(8,128)(2,1)}, f32[16,1536]{1,0:T(8,128)}) custom-call(bf16[8,2,96,1920]{3,2,1,0:T(8,128)(2,1)} %bitcast.282, bf16[4,128,1536]{2,1,0:T(8,128)(2,1)} %bitcast.296, f32[128,1536]{1,0:T(8,128)} %get-tuple-element.210.grad_ref, bf16[128,1536]{1,0:T(8,128)(2,1)} %constant_dynamic-slice_fusion.6.x_ref, ...), custom_call_target="tpu_custom_call" | custom-call | tf_op jit(solution)/shard_map/tail/pallas_call | solution.py:623
  1008.1 11.8 %fusion.66 = f32[8,1536,256]{1,2,0:T(8,128)} fusion(bf16[8,512,1536]{2,1,0:T(8,128)(2,1)} %bitcast.259, bf16[8,512,128]{1,2,0:T(8,128)(2,1)S(1)} %copy-done.31, bf16[8,512,128]{1,2,0:T(8,128)(2,1)S(1)} %copy-done.30), kind=kOutput, calls=%fused_computation.128 | convolution fusion | flops 3225419776 | bytes 27262976 | tf_op jit(solution)/shard_map/erd,erf->edf/dot_general | solution.py:33
  1019.8 19.2 %copy.378 = f32[8,1536,2,128]{3,2,1,0:T(2,128)} copy(f32[8,1536,2,128]{1,3,2,0:T(8,128)} %bitcast.260) | data formatting | bytes 25165824
  1048.2 9.1 fusion.139
  (491 shorter events, 223.2 us)
Async XLA Ops:
  7.2 232.7 %all-gather.5.cloned.1.call-start = ((), (), s32[]{:S(2)}) async-start(), calls=%async_computation.2 | async-start | bytes 6635520 | tf_op jit(solution)/shard_map/all_gather | solution.py:718
  11.9 284.5 %all-gather.7.cloned.1.call-start = ((), (), s32[]{:S(2)}) async-start(), calls=%async_computation.3 | async-start | bytes 2654208 | tf_op jit(solution)/shard_map/all_gather | solution.py:719
  12.8 380.5 %all-gather.9.cloned.1.call-start = ((), (), s32[]{:S(2)}) async-start(), calls=%async_computation.4 | async-start | bytes 2654208 | tf_op jit(solution)/shard_map/all_gather | solution.py:721
  13.9 1043.4 %all-gather.11.cloned.1.call-start = ((), (), s32[]{:S(2)}) async-start(), calls=%async_computation.5 | async-start | bytes 1966080 | tf_op jit(solution)/shard_map/all_gather | solution.py:826
  16.0 229.7 %copy-start.112 = (f32[12]{0:T(128)}, f32[12]{0:T(128)S(1)}, u32[]{:S(2)}) copy-start(f32[12]{0:T(128)S(1)} %exponential_negate_fusion) | copy-start | bytes 148
  16.5 223.4 %copy-start.113 = (f32[512]{0:T(512)}, f32[512]{0:T(512)S(1)}, u32[]{:S(2)}) copy-start(f32[512]{0:T(512)S(1)} %add_rsqrt_fusion.1) | copy-start | bytes 6148
  16.6 233.7 %copy-start.95 = (f32[1,256]{1,0:T(1,128)}, f32[1,256]{1,0:T(1,128)S(1)}, u32[]{:S(2)}) copy-start(f32[1,256]{1,0:T(1,128)S(1)} %get-tuple-element.551) | copy-start | bytes 3076
  16.6 233.7 %copy-start.97 = (f32[1,256]{1,0:T(1,128)}, f32[1,256]{1,0:T(1,128)S(1)}, u32[]{:S(2)}) copy-start(f32[1,256]{1,0:T(1,128)S(1)} %get-tuple-element.552) | copy-start | bytes 3076
  16.6 233.7 %copy-start.99 = (f32[1,256]{1,0:T(1,128)}, f32[1,256]{1,0:T(1,128)S(1)}, u32[]{:S(2)}) copy-start(f32[1,256]{1,0:T(1,128)S(1)} %get-tuple-element.553) | copy-start | bytes 3076
  16.6 233.6 %copy-start.101 = (f32[1,256]{1,0:T(1,128)}, f32[1,256]{1,0:T(1,128)S(1)}, u32[]{:S(2)}) copy-start(f32[1,256]{1,0:T(1,128)S(1)} %get-tuple-element.554) | copy-start | bytes 3076
  190.6 17.1 %copy-start.16 = (pred[8,512,512]{2,1,0:T(32,128)(4,1)}, pred[8,512,512]{2,1,0:T(32,128)(4,1)S(1)}, u32[]{:S(2)}) copy-start(pred[8,512,512]{2,1,0:T(32,128)(4,1)S(1)} %bitcast_compare_fusion) | copy-start | bytes 6291460
  226.1 13.8 %copy-start.40 = (bf16[512,1536]{1,0:T(8,128)(2,1)S(1)}, bf16[512,1536]{1,0:T(8,128)(2,1)}, u32[]{:S(2)}) copy-start(bf16[512,1536]{1,0:T(8,128)(2,1)} %param.27) | copy-start | bytes 4718596
  247.6 10.0 copy-start.28
  251.4 10.6 copy-start.32
  287.2 9.2 copy-start.108
  296.4 296.9 %copy-start.106 = (f32[512]{0:T(512)}, f32[512]{0:T(512)S(1)}, u32[]{:S(2)}) copy-start(f32[512]{0:T(512)S(1)} %get-tuple-element.556) | copy-start | bytes 6148
  396.3 29.7 %slice-start = ((s8[6291456]{0:T(1024)(128)(4,1)}), s8[4194304]{0:T(1024)(128)(4,1)S(1)}, s32[]{:S(2)}) async-start(s8[6291456]{0:T(1024)(128)(4,1)} %bitcast.263), calls=%async_computation.8 | async-start | bytes 8388608
  400.6 25.4 %slice-start.1 = ((s8[6291456]{0:T(1024)(128)(4,1)}), s8[2097152]{0:T(1024)(128)(4,1)S(1)}, s32[]{:S(2)}) async-start(s8[6291456]{0:T(1024)(128)(4,1)} %bitcast.263), calls=%async_computation.9 | async-start | bytes 4194304
  454.4 10.8 %copy-start.71 = (bf16[512,256]{1,0:T(8,128)(2,1)S(1)}, bf16[512,256]{1,0:T(8,128)(2,1)}, u32[]{:S(2)}) copy-start(bf16[512,256]{1,0:T(8,128)(2,1)} %get-tuple-element.532) | copy-start | bytes 786436
  454.4 10.8 %copy-start.72 = (bf16[512,256]{1,0:T(8,128)(2,1)S(1)}, bf16[512,256]{1,0:T(8,128)(2,1)}, u32[]{:S(2)}) copy-start(bf16[512,256]{1,0:T(8,128)(2,1)} %get-tuple-element.533) | copy-start | bytes 786436
  486.8 95.9 %copy-start.23 = (f32[512,768]{1,0:T(8,128)S(1)}, f32[512,768]{1,0:T(8,128)}, u32[]{:S(2)}) copy-start(f32[512,768]{1,0:T(8,128)} %get-tuple-element.515) | copy-start | bytes 4718596
  629.2 10.9 %copy-start.50 = (bf16[512,256]{1,0:T(8,128)(2,1)S(1)}, bf16[512,256]{1,0:T(8,128)(2,1)}, u32[]{:S(2)}) copy-start(bf16[512,256]{1,0:T(8,128)(2,1)} %copy-done.49) | copy-start | bytes 786436
  659.1 82.6 %copy-start.38 = (f32[128,1536]{1,0:T(8,128)S(1)}, f32[128,1536]{1,0:T(8,128)}, u32[]{:S(2)}) copy-start(f32[128,1536]{1,0:T(8,128)} %get-tuple-element.204.hidden_ref) | copy-start | bytes 2359300
  743.8 313.5 %reduce-scatter.7.cloned.1.call-start = ((), (), s32[]{:S(2)}) async-start(), calls=%async_computation.7 | async-start | bytes 2654208
  766.0 10.2 copy-start.33
  766.0 10.6 copy-start.36
  780.8 279.6 %reduce-scatter.5.cloned.1.call-start = ((), (), s32[]{:S(2)}) async-start(), calls=%async_computation.6 | async-start | bytes 2654208 | tf_op jit(solution)/shard_map/reduce_scatter | solution.py:865
  785.9 11.5 %copy-start.46 = (f32[2,256,12,64]{1,3,2,0:T(8,128)S(1)}, f32[2,256,12,64]{1,3,2,0:T(8,128)}, u32[]{:S(2)}) copy-start(f32[2,256,12,64]{1,3,2,0:T(8,128)} %get-tuple-element.559) | copy-start | bytes 4718596
  812.3 8.5 copy-start.96
  812.3 8.4 copy-start.98
  812.3 8.4 copy-start.100
  837.5 8.1 copy-start.41
  (106 other events, 358.5 us)
Sparse Core Ops, SparseCore 0:
  12.0 122.1 all-gather.4
  136.4 54.1 all-gather.6
  192.8 50.5 all-gather.8
  743.9 18.9 all-gather.10
  780.9 65.9 reduce-scatter.6
  850.3 88.1 reduce-scatter.4

commit v4 on v3

--- a/solution.py
+++ b/solution.py
@@ -660,6 +660,139 @@
     )
 
 
+def dot_mm(a, b):
+    return lax.dot_general(a, b, (((1,), (0,)), ((), ())), preferred_element_type=F32)
+
+
+def dot_nt(a, b):
+    return lax.dot_general(a, b, (((1,), (1,)), ((), ())), preferred_element_type=F32)
+
+
+def dot_tn(a, b):
+    return lax.dot_general(a, b, (((0,), (0,)), ((), ())), preferred_element_type=F32)
+
+
+def experts_kernel(
+    n_dp, n_local, cap, chunk, pos_ref, wt_ref, x_ref, g_ref, gu_ref, dn_ref,
+    dxn_ref, out_ref, ggu_ref, gdn_ref, pick, xr, q, sw, gu,
+):
+    step = pl.program_id(0)
+    width = x_ref.shape[1]
+    hidden = dn_ref.shape[1]
+    slots = x_ref.shape[0]
+    columns = [pl.ds(c, chunk) for c in range(0, width, chunk)]
+
+    @pl.when(step < n_dp)
+    def _():
+        s = step
+        lane = lax.broadcasted_iota(jnp.int32, (cap, slots), 0)
+        for e in range(n_local):
+            hit = lane == pos_ref[0, e : e + 1, :]
+            pick[s, e * cap : (e + 1) * cap, :] = jnp.where(hit, 1.0, 0.0).astype(BF)
+            sw[e, s] = jnp.sum(jnp.where(hit, wt_ref[0, e : e + 1, :], 0.0), axis=1, keepdims=True)
+        chosen = pick[s]
+        for c in columns:
+            rows = dot_mm(chosen, x_ref[:, c]).astype(BF)
+            grads = dot_mm(chosen, g_ref[:, c])
+            for e in range(n_local):
+                xr[e, s, :, c] = rows[e * cap : (e + 1) * cap]
+                q[e, s, :, c] = (grads[e * cap : (e + 1) * cap] * sw[e, s]).astype(BF)
+
+    @pl.when(jnp.logical_and(step >= n_dp, step < n_dp + n_local))
+    def _():
+        e = step - n_dp
+        gu[:, :hidden] = gu_ref[pl.ds(0, width, stride=2), :].astype(BF)
+        gu[:, hidden:] = gu_ref[pl.ds(1, width, stride=2), :].astype(BF)
+        down = dn_ref[0].astype(BF)
+        x = xr[e].reshape(n_dp * cap, width)
+        qe = q[e].reshape(n_dp * cap, width)
+        pre = dot_mm(x, gu[...])
+        grad_act = dot_nt(qe, down)
+        gate, up = pre[:, :hidden], pre[:, hidden:]
+        sig = 1.0 / (1.0 + jnp.exp(-gate))
+        act_silu = gate * sig
+        slope = sig * (1.0 + gate * (1.0 - sig))
+        value = act_silu * up
+        act = value.astype(BF)
+        scaled = (value * sw[e].reshape(n_dp * cap, 1)).astype(BF)
+        grad_pre = jnp.concatenate([grad_act * up * slope, grad_act * act_silu], axis=1).astype(BF)
+        ggu = dot_tn(x, grad_pre)
+        ggu_ref[pl.ds(0, width, stride=2), :] = ggu[:, :hidden]
+        ggu_ref[pl.ds(1, width, stride=2), :] = ggu[:, hidden:]
+        gdn_ref[0] = dot_tn(act, qe)
+        for c in columns:
+            xr[e, :, :, c] = dot_nt(grad_pre, gu[c, :]).astype(BF).reshape(n_dp, cap, chunk)
+            q[e, :, :, c] = dot_mm(scaled, down[:, c.start : c.start + chunk]).astype(BF).reshape(n_dp, cap, chunk)
+
+    @pl.when(step >= n_dp + n_local)
+    def _():
+        s = step - n_dp - n_local
+        chosen = pick[s]
+        for c in columns:
+            dxn_ref[:, c] = dot_tn(chosen, xr[:, s, :, c].reshape(n_local * cap, chunk)).astype(BF)
+            out_ref[:, c] = dot_tn(chosen, q[:, s, :, c].reshape(n_local * cap, chunk)).astype(BF)
+
+
+def experts(position, weights, rows, table, w_gu, w_down, cap):
+    n_dp, n_local, slots = position.shape
+    width = rows.shape[1]
+    hidden = w_down.shape[1]
+    chunk = width // 3 if width % 384 == 0 else width
+    by_source = lambda i: (jnp.clip(i, 0, n_dp - 1), 0, 0)
+    rows_in = lambda i: (jnp.clip(i, 0, n_dp - 1), 0)
+    rows_out = lambda i: (jnp.clip(i - n_dp - n_local, 0, n_dp - 1), 0)
+    flat = lambda i: (jnp.clip(i - n_dp, 0, n_local - 1), 0)
+    deep = lambda i: (jnp.clip(i - n_dp, 0, n_local - 1), 0, 0)
+    total = n_dp * n_local * cap
+    return pl.pallas_call(
+        functools.partial(experts_kernel, n_dp, n_local, cap, chunk),
+        grid=(2 * n_dp + n_local,),
+        out_shape=(
+            jax.ShapeDtypeStruct((n_dp * slots, width), BF),
+            jax.ShapeDtypeStruct((n_dp * slots, width), BF),
+            jax.ShapeDtypeStruct((n_local * width * 2, hidden), F32),
+            jax.ShapeDtypeStruct((n_local, hidden, width), F32),
+        ),
+        in_specs=[
+            pl.BlockSpec((1, n_local, slots), by_source),
+            pl.BlockSpec((1, n_local, slots), by_source),
+            pl.BlockSpec((slots, width), rows_in),
+            pl.BlockSpec((slots, width), rows_in),
+            pl.BlockSpec((width * 2, hidden), flat),
+            pl.BlockSpec((1, hidden, width), deep),
+        ],
+        out_specs=(
+            pl.BlockSpec((slots, width), rows_out),
+            pl.BlockSpec((slots, width), rows_out),
+            pl.BlockSpec((width * 2, hidden), flat),
+            pl.BlockSpec((1, hidden, width), deep),
+        ),
+        scratch_shapes=[
+            pltpu.VMEM((n_dp, n_local * cap, slots), BF),
+            pltpu.VMEM((n_local, n_dp, cap, width), BF),
+            pltpu.VMEM((n_local, n_dp, cap, width), BF),
+            pltpu.VMEM((n_local, n_dp, cap, 1), F32),
+            pltpu.VMEM((width, 2 * hidden), BF),
+        ],
+        compiler_params=pltpu.CompilerParams(
+            dimension_semantics=("arbitrary",), vmem_limit_bytes=60 << 20
+        ),
+        cost_estimate=pl.CostEstimate(
+            flops=8 * total * slots * width + 18 * total * width * hidden,
+            bytes_accessed=8 * n_dp * slots * width + 24 * n_local * width * hidden,
+            transcendentals=total * hidden,
+        ),
+        name="experts",
+    )(
+        position,
+        weights,
+        rows,
+        table,
+        w_gu.reshape(n_local * width * 2, hidden),
+        w_down,
+    )
+
+
 def local(
     x_in,
     lengths,
@@ -733,7 +866,6 @@
     table = jnp.concatenate([g2_low, high, low], axis=1)
     table = lax.dynamic_slice_in_dim(table, my_t * piece, piece, axis=0)
     table = gather_rows(table, n_dp, 1)
-    g2_all = table[:, :width].reshape(n_dp, slots, width)
     g2_piece = lax.dynamic_slice_in_dim(g2_low, my_t * piece, piece, axis=0)
     high = lax.dynamic_slice_in_dim(table, width + my_dp * n_local, n_local, axis=1)
     low = lax.dynamic_slice_in_dim(table, width + n_experts + my_dp * n_local, n_local, axis=1)
@@ -742,19 +874,9 @@
     before = (
         jnp.arange(slots)[:, None] > jnp.arange(slots)[None, :]
     ).astype(BF)
-    position = dotf("ut,ste->sue", before, member).astype(jnp.int32)
+    position = dotf("ut,ste->seu", before, member).astype(jnp.int32)
+    weights = weights.transpose(0, 2, 1)
     position = jnp.where(weights > 0.0, position, -1)
-    pick = (
-        position.transpose(0, 2, 1)[:, :, None, :]
-        == jnp.arange(cap, dtype=jnp.int32)[None, None, :, None]
-    )
-    slot_weight = jnp.sum(
-        jnp.where(pick, weights.transpose(0, 2, 1)[:, :, None, :], 0.0), axis=-1
-    )
-    pick = pick.astype(BF).reshape(n_dp, n_local * cap, slots)
-
-    gate_w = w_exp_gu.astype(BF).reshape(n_local, width, -1)
-    down_w = w_exp_down.astype(BF)
 
     x_float = x_in.astype(F32)
     scale_one = rms_scale(x_float)
@@ -774,7 +896,6 @@
     x_piece = lax.dynamic_slice_in_dim(x_in, my_t * piece, piece, axis=0)
     all_rows, hidden_one = middle(mixer_part, x_piece, ln2_gain, n_dp, 2)
     mine = lax.dynamic_slice_in_dim(all_rows, my_dp * slots, slots, axis=0)
-    all_rows = all_rows.reshape(n_dp, slots, width)
 
     shared_pre = dotf("td,df->tf", mine, shared_gu)
     s_gate, s_up = shared_pre[:, :n_sh], shared_pre[:, n_sh:]
@@ -787,47 +908,27 @@
     grad_normed_shared = dotf("tf,df->td", grad_shared_pre, shared_gu)
     shared_part = dotf("tf,df->td", shared_act, shared_down)
 
-    def by_expert(v):
-        return v.reshape(n_dp, n_local, cap, v.shape[-1]).transpose(1, 0, 2, 3).reshape(
-            n_local, n_dp * cap, v.shape[-1]
-        )
-
-    def by_source(v):
-        return v.reshape(n_local, n_dp, cap, v.shape[-1]).transpose(1, 0, 2, 3).reshape(
-            n_dp, n_local * cap, v.shape[-1]
-        )
-
-    sw = slot_weight.transpose(1, 0, 2).reshape(n_local, n_dp * cap, 1)
-    q = by_expert(dotf("sct,std->scd", pick, g2_all))
-    q = (q * sw).astype(BF)
-    grad_act = dotf("erd,efd->erf", q, down_w)
-    xr = by_expert(dotf("sct,std->scd", pick, all_rows).astype(BF))
-    pre = dotf("erd,edf->erf", xr, gate_w)
-    n_f = pre.shape[-1] // 2
-    p_gate, p_up = pre[..., :n_f], pre[..., n_f:]
-    act_silu, act_slope = silu_parts(p_gate)
-    act = (act_silu * p_up).astype(BF)
-    grad_pre = jnp.concatenate(
-        [grad_act * p_up * act_slope, grad_act * act_silu], axis=-1
-    ).astype(BF)
-    back = by_source(dotf("erf,edf->erd", grad_pre, gate_w).astype(BF))
-    dxn_part = dotf("sct,scd->std", pick, back)
-    own = (jnp.arange(n_dp) == my_dp).astype(F32)[:, None, None]
-    dxn_part = (dxn_part + own * grad_normed_shared[None]).astype(BF)
+    dxn_part, out_part, grad_exp_gu, grad_exp_down = experts(
+        position, weights, all_rows, table, w_exp_gu, w_exp_down, cap
+    )
+    grad_exp_gu = grad_exp_gu.reshape(w_exp_gu.shape)
+
+    def add_own(total, own):
+        at = my_dp * slots
+        own = own + lax.dynamic_slice_in_dim(total, at, slots, axis=0).astype(F32)
+        return lax.dynamic_update_slice_in_dim(total, own.astype(BF), at, axis=0)
+
+    dxn_part = add_own(dxn_part, grad_normed_shared)
+    out_part = add_own(out_part, shared_part)
     grad_one, sum_ln2, dm = turn(
-        dxn_part.reshape(n_dp * slots, width), hidden_one, g2_piece, ln2_gain, n_dp, 3
+        dxn_part, hidden_one, g2_piece, ln2_gain, n_dp, 3
     )
     dm = dm.reshape(slots, width)
 
-    forth = by_source((dotf("erf,efd->erd", act, down_w) * sw).astype(BF))
-    out_part = dotf("sct,scd->std", pick, forth)
-    out_part = (out_part + own * shared_part[None]).astype(BF)
-    ffn_out = scatter_rows(out_part.reshape(n_dp * slots, width), n_dp, 4)
+    ffn_out = scatter_rows(out_part, n_dp, 4)
     layer_out = lax.all_gather(
         (hidden_one + ffn_out).astype(BF), "tensor", axis=0, tiled=True
     )
-    grad_exp_down = dotf("erf,erd->efd", act, q)
-    grad_exp_gu = dotf("erd,erf->edf", xr, grad_pre).reshape(w_exp_gu.shape)
     grad_shared_down = dotf("td,tf->df", g2_low, shared_act)
     grad_shared_gu = dotf("td,tf->df", mine, grad_shared_pre)
 

time: 1080 us -> 922 us (0.85)
  matrix products: 223 us -> 96.5 us
  local copies, waits for them, and re-layouts: 179 us -> 92.5 us
  Pallas kernels: 549 us -> 626 us
  other arithmetic: 92 us -> 67.5 us
    dot_general x23 -> x13, matrix products: 174 us -> 49.6 us  [dotf(): return jnp.einsum(spec, a, b, preferred_element_type=F32)]
    pallas_call x0 -> x1, Pallas kernels: none -> 58.9 us  [experts(): pl.pallas_call(functools.partial(experts_kernel, n_dp, n_local, cap, chun...]
    transpose x5 -> x0, local copies, waits for them, and re-layouts: 33.1 us -> none  [the longest x2 21.7 us: by_source(): v.reshape(n_local, n_dp, cap, v.shape[-1]).transpose(1, 0, 2, 3)]
    reshape x5 -> x2, local copies, waits for them, and re-layouts: 29.8 us -> 0.04 us  [the longest x1 18.3 us: by_expert(): v.reshape(n_dp, n_local, cap, v.shape[-1]).transpose(1, 0, 2, 3)]
    convert_element_type x3 -> x0, other arithmetic: 23.7 us -> none  [the longest x1 13.8 us: local(): q = (q * sw).astype(BF)]
    unnamed x259 -> x202, local copies, waits for them, and re-layouts: 37.9 us -> 16.5 us
    pallas_call x1, Pallas kernels: 92.2 us -> 112 us  [middle(): pl.pallas_call(functools.partial(middle_kernel, n_hi), out_shape=(jax.Sha...]
  transfers between devices with their start and end apart: 6 -> 6, of which waited for: 0 -> 0; matrix products, arithmetic and copies ran while one was open for 29% -> 26% of each run, Pallas kernels for 35% -> 60%
where the time goes in v4:
time: 922 us; the launch traced here: 911 us
  Pallas kernels  626 us (68%)
  matrix products  96.5 us (10%)
  local copies, waits for them, and re-layouts  92.5 us (10%)
  other arithmetic  67.5 us (7%)
  between operations  16.6 us (2%)
  blocking collectives  10.3 us (1%)
    pallas_call x1, Pallas kernels, tail(): pl.pallas_call(functools.partial(tail_kernel, n_hi, wide, bc_at), out_sha...  151 us
    pallas_call x1, Pallas kernels, gather_rows(): pl.pallas_call(functools.partial(gather_kernel, n_hi), out_shape=jax.Shap...  127 us
    pallas_call x1, Pallas kernels, middle(): pl.pallas_call(functools.partial(middle_kernel, n_hi), out_shape=(jax.Sha...  112 us
    pallas_call x1, Pallas kernels, turn(): pl.pallas_call(functools.partial(turn_kernel, n_hi), out_shape=(jax.Shape...  96.5 us
    pallas_call x1, Pallas kernels, scatter_rows(): pl.pallas_call(functools.partial(scatter_kernel, n_hi), out_shape=jax.Sha...  80.7 us
    pallas_call x1, Pallas kernels, experts(): pl.pallas_call(functools.partial(experts_kernel, n_dp, n_local, cap, chun...  58.9 us
    dot_general x13, matrix products, dotf(): return jnp.einsum(spec, a, b, preferred_element_type=F32)  49.6 us
    dot_general x3, matrix products, ssd_scan(): jnp.einsum('kij,kijh,kjhp->kihp', intersection, decay_mask, scaled, preci...  22 us
  transfers between devices with their start and end apart: 6, of which 0 were waited for; matrix products, arithmetic and copies ran while one was open for 26% of the time, Pallas kernels for 60%

profile of v4, /device:TPU:9, one launch (start us, length us, event | category | flops | bytes accessed | tf_op | source)
XLA Modules:
  0.0 910.9 jit_solution(12200238772924230982)
XLA Ops:
  23.2 3.3 concatenate.46
  28.3 127.4 %gather_rows.1.g_ref = bf16[4096,1664]{1,0:T(8,128)(2,1)} custom-call(bf16[128,1664]{1,0:T(8,128)(2,1)} %constant_dynamic-slice_fusion.5.x_ref), custom_call_target="tpu_custom_call" | custom-call | tf_op jit(solution)/shard_map/gather_rows/pallas_call | solution.py:321
  155.7 3.7 convert_add_fusion
  163.3 5.6 fusion.99
  180.1 3.2 multiply_convert_fusion.2
  192.9 6.8 while.34
  203.1 7.6 fusion.46
  216.4 3.6 multiply_reduce_fusion.9
  220.0 5.3 psum.14
  225.3 4.7 convolution_convert_fusion.4
  230.0 111.5 %middle.1 = (bf16[4096,1536]{1,0:T(8,128)(2,1)}, f32[128,1536]{1,0:T(8,128)}) custom-call(bf16[4,128,1536]{2,1,0:T(8,128)(2,1)} %bitcast.230, bf16[128,1536]{1,0:T(8,128)(2,1)} %constant_dynamic-slice_fusion.6.x_ref, f32[1,1536]{1,0:T(1,128)} %reshape.313.gain_ref), custom_call_target="tpu_custom_call" | custom-call | tf_op jit(solution)/shard_map/middle/pallas_call | solution.py:350
  341.6 58.9 %experts.1 = (bf16[4096,1536]{1,0:T(8,128)(2,1)}, bf16[4096,1536]{1,0:T(8,128)(2,1)}, f32[24576,128]{1,0:T(8,128)}, f32[8,128,1536]{2,1,0:T(8,128)}) custom-call(s32[8,8,512]{2,1,0:T(8,128)} %fusion.78.pos_ref, f32[8,8,512]{2,1,0:T(8,128)} %bitcast.246, bf16[4096,1536]{1,0:T(8,128)(2,1)} %get-tuple-element.209.x_ref, bf16[4096,1664]{1,0:T(8,128)(2,1)} %gather_rows.1.g_ref, ...), custom_call_target="tpu_custom_call" | custom-call | flops 40265318400 | bytes 88080384 | tf_op jit(solution)/shard_map/experts/pallas_call | solution.py:747
  405.7 3.2 fusion.29.p_ref
  408.9 80.7 %scatter_rows.1 = f32[128,1536]{1,0:T(8,128)} custom-call(bf16[4096,1536]{1,0:T(8,128)(2,1)} %fusion.29.p_ref), custom_call_target="tpu_custom_call" | custom-call | tf_op jit(solution)/shard_map/scatter_rows/pallas_call | solution.py:470
  492.3 4.2 fusion.31.p_ref
  496.6 96.5 %turn.1 = (f32[128,1536]{1,0:T(8,128)}, f32[1,1536]{1,0:T(1,128)}, bf16[4,128,1536]{2,1,0:T(8,128)(2,1)}) custom-call(bf16[4096,1536]{1,0:T(8,128)(2,1)} %fusion.31.p_ref, f32[128,1536]{1,0:T(8,128)} %get-tuple-element.208.hidden_ref, bf16[128,1536]{1,0:T(8,128)(2,1)} %constant_dynamic-slice_fusion.4.g2_ref, f32[1,1536]{1,0:T(1,128)} %reshape.313.gain_ref), custom_call_target="tpu_custom_call" | custom-call | tf_op jit(solution)/shard_map/turn/pallas_call | solution.py:507
  593.1 5.8 multiply_reduce_fusion.2
  598.8 5.1 psum.15
  603.9 5.1 multiply_reduce_fusion.1
  615.1 3.2 fusion.67
  620.2 11.1 %while.35 = (s32[]{:T(128)}, f32[12,128,64]{2,1,0:T(8,128)S(1)}, f32[2,12]{1,0:T(2,128)}, f32[2,12,128,64]{3,2,1,0:T(8,128)}, f32[2,12,128,64]{2,3,1,0:T(8,128)}...) while((s32[]{:T(128)}, f32[12,128,64]{2,1,0:T(8,128)S(1)}, ...), condition=%wide.region_12.13_spmd.clone, body=%wide.region_10.12_spmd.clone.sunk | while | flops 589816 | bytes 4326632 | solution.py:73
  635.4 5.4 bitcast_add_fusion.2
  658.4 4.3 copy.339
  668.1 9.0 fusion.14
  677.2 5.0 reduce-window.16
  682.7 7.1 multiply_reduce_fusion.5
  691.1 6.7 fusion.70
  697.8 5.1 fusion.73
  715.2 3.4 concatenate.50
  720.1 7.2 convolution_convert_fusion
  727.3 7.3 convolution_convert_fusion.3
  734.6 150.9 %tail.1 = (f32[2,96,1920]{2,1,0:T(8,128)}, bf16[4,128,1536]{2,1,0:T(8,128)(2,1)}, f32[16,1536]{1,0:T(8,128)}) custom-call(bf16[8,2,96,1920]{3,2,1,0:T(8,128)(2,1)} %bitcast.217, bf16[4,128,1536]{2,1,0:T(8,128)(2,1)} %bitcast.231, f32[128,1536]{1,0:T(8,128)} %get-tuple-element.216.grad_ref, bf16[128,1536]{1,0:T(8,128)(2,1)} %constant_dynamic-slice_fusion.6.x_ref, ...), custom_call_target="tpu_custom_call" | custom-call | tf_op jit(solution)/shard_map/tail/pallas_call | solution.py:623
  (412 shorter events, 143.5 us)
Async XLA Ops:
  7.2 156.0 %all-gather.5.cloned.1.call-start = ((), (), s32[]{:S(2)}) async-start(), calls=%async_computation.2 | async-start | bytes 6635520 | tf_op jit(solution)/shard_map/all_gather | solution.py:851
  10.4 214.9 %all-gather.7.cloned.1.call-start = ((), (), s32[]{:S(2)}) async-start(), calls=%async_computation.3 | async-start | bytes 2654208 | tf_op jit(solution)/shard_map/all_gather | solution.py:852
  11.2 389.3 %all-gather.9.cloned.1.call-start = ((), (), s32[]{:S(2)}) async-start(), calls=%async_computation.4 | async-start | bytes 2654208 | tf_op jit(solution)/shard_map/all_gather | solution.py:854
  11.5 5.1 copy-start.91
  12.3 885.5 %all-gather.11.cloned.1.call-start = ((), (), s32[]{:S(2)}) async-start(), calls=%async_computation.5 | async-start | bytes 1966080 | tf_op jit(solution)/shard_map/all_gather | solution.py:929
  161.7 7.2 copy-start.51
  171.0 9.1 copy-start.9
  171.0 5.4 copy-start.62
  171.0 5.4 copy-start.64
  171.0 5.4 copy-start.66
  171.0 5.4 copy-start.68
  171.1 5.4 copy-start.90
  172.1 16.0 %copy-start.18 = (f32[512,12]{1,0:T(8,128)}, f32[512,12]{1,0:T(8,128)S(1)}, u32[]{:S(2)}) copy-start(f32[512,12]{1,0:T(8,128)S(1)} %get-tuple-element.529) | copy-start | bytes 73732
  180.1 8.9 copy-start.22
  202.8 7.9 copy-start.13
  203.1 7.7 copy-start.38
  216.4 8.9 copy-start.76
  225.3 378.7 %copy-start.73 = (f32[512]{0:T(512)}, f32[512]{0:T(512)S(1)}, u32[]{:S(2)}) copy-start(f32[512]{0:T(512)S(1)} %get-tuple-element.561) | copy-start | bytes 6148
  491.9 405.9 %reduce-scatter.7.cloned.1.call-start = ((), (), s32[]{:S(2)}) async-start(), calls=%async_computation.7 | async-start | bytes 2654208
  662.8 238.1 %reduce-scatter.5.cloned.1.call-start = ((), (), s32[]{:S(2)}) async-start(), calls=%async_computation.6 | async-start | bytes 2654208 | tf_op jit(solution)/shard_map/reduce_scatter | solution.py:966
  682.7 7.2 copy-start.19
  682.7 7.2 copy-start.81
  682.7 7.2 copy-start.83
  682.7 8.4 copy-start.95
  682.7 8.4 copy-start.4
  682.7 8.4 copy-start.45
  691.1 6.7 copy-start.10
  697.8 5.2 copy-start.24
  697.8 5.6 copy-start.21
  697.8 6.3 copy-start.93
  720.1 7.2 copy-start.30
  889.4 6.2 copy-start.32
  (80 other events, 202.9 us)
Sparse Core Ops, SparseCore 0:
  10.8 148.2 all-gather.4
  161.8 52.4 all-gather.6
  216.5 75.5 all-gather.8
  492.0 24.7 all-gather.10
  662.9 67.4 reduce-scatter.6
  733.7 87.7 reduce-scatter.4

commit v5 on v4

--- a/solution.py
+++ b/solution.py
@@ -157,11 +157,13 @@
     return (hi * 2 + lo, th * 2 + tl)
 
 
-def greet(n_hi):
+def greet(n_hi, tensor=True):
     hi, lo, th, tl = place()
     barrier = pltpu.get_barrier_semaphore()
     others = [device(lax.rem(hi + k, n_hi), lo, th, tl) for k in range(1, n_hi)]
-    others += [device(hi, 1 - lo, th, tl), device(hi, lo, 1 - th, tl), device(hi, lo, th, 1 - tl)]
+    others += [device(hi, 1 - lo, th, tl)]
+    if tensor:
+        others += [device(hi, lo, 1 - th, tl), device(hi, lo, th, 1 - tl)]
     for other in others:
         pl.semaphore_signal(barrier, inc=1, device_id=other, device_id_type=MESH)
     pl.semaphore_wait(barrier, len(others))
@@ -292,15 +294,18 @@
                 got(h, k, 0, 0, 0)
             for step in ("f", "s", "c"):
                 push(h, k, 0, 0, 0, step)
+        yield
         for h in range(2):
             got(h, k, 1, 0, 0)
             for step in ("s", "c"):
                 push(h, k, 1, 0, 0, step)
+        yield
     for k in range(n_hi):
         for f in range(2):
             for h in range(2):
                 got(h, k, f, 1, 0)
                 push(h, k, f, 1, 0, "c")
+        yield
     for k in range(n_hi):
         for f in range(2):
             for s in range(2):
@@ -310,57 +315,114 @@
     sends.finish()
 
 
-def gather_kernel(n_hi, x_ref, o_ref, own_sem, send_sem, recv_sem):
-    greet(n_hi)
-    gather_steps(n_hi, x_ref, o_ref, own_sem, send_sem, recv_sem)
-
-
-def gather_rows(x, n_dp, collective_id):
-    rows, width = x.shape
-    n_hi = n_dp // 2
-    return pl.pallas_call(
-        functools.partial(gather_kernel, n_hi),
-        out_shape=jax.ShapeDtypeStruct((n_dp * 4 * rows, width), x.dtype),
-        in_specs=[ANY_SPEC],
-        out_specs=ANY_SPEC,
-        scratch_shapes=[DMA, DMA((2, 8 * n_hi)), DMA((2, 8 * n_hi))],
-        compiler_params=pltpu.CompilerParams(collective_id=collective_id, has_side_effects=True),
-        name="gather_rows",
-    )(x)
+def in_turns(*streams):
+    live = list(streams)
+    while live:
+        for stream in list(live):
+            if next(stream, True) is True:
+                live.remove(stream)
 
 
 def middle_kernel(
-    n_hi, part_ref, x_ref, gain_ref, o_ref, hidden_ref, normed, got_c, got_y, t_send, t_recv,
-    own_sem, send_sem, recv_sem,
+    n_hi, part_ref, x_ref, gain_ref, table_ref, o_ref, all_table_ref, hidden_ref,
+    normed, got_c, got_y, t_send, t_recv, *sems,
 ):
     greet(n_hi)
     sends = Sends()
     tensor_sum_start(sends, part_ref, got_c, t_send, t_recv)
+    tables = gather_steps(n_hi, table_ref, all_table_ref, *sems[:3])
+    next(tables)
     tensor_sum_middle(sends, part_ref, got_c, got_y, t_send, t_recv)
     hidden = x_ref[...].astype(F32) + tensor_sum_end(part_ref, got_c, got_y, t_send, t_recv)
     hidden_ref[...] = hidden
     normed[...] = (hidden * rms_scale(hidden) * gain_ref[...]).astype(normed.dtype)
-    gather_steps(n_hi, normed, o_ref, own_sem, send_sem, recv_sem)
+    in_turns(gather_steps(n_hi, normed, o_ref, *sems[3:]), tables)
     sends.finish()
 
 
-def middle(part, x_piece, gain, n_dp, collective_id):
+def middle(part, x_piece, gain, table, n_dp, collective_id):
     rows, width = x_piece.shape
     n_hi = n_dp // 2
+    gather_sems = [DMA, DMA((2, 8 * n_hi)), DMA((2, 8 * n_hi))]
     return pl.pallas_call(
         functools.partial(middle_kernel, n_hi),
         out_shape=(
             jax.ShapeDtypeStruct((n_dp * 4 * rows, width), part.dtype),
+            jax.ShapeDtypeStruct((n_dp * 4 * rows, table.shape[1]), table.dtype),
             jax.ShapeDtypeStruct((rows, width), F32),
         ),
-        in_specs=[VMEM_SPEC] * 3,
-        out_specs=(ANY_SPEC, VMEM_SPEC),
+        in_specs=[VMEM_SPEC] * 3 + [ANY_SPEC],
+        out_specs=(ANY_SPEC, ANY_SPEC, VMEM_SPEC),
         scratch_shapes=[pltpu.VMEM((rows, width), part.dtype)]
         + TENSOR_SUM_SCRATCH(rows, width, part.dtype)
-        + [DMA, DMA((2, 8 * n_hi)), DMA((2, 8 * n_hi))],
+        + gather_sems
+        + gather_sems,
         compiler_params=pltpu.CompilerParams(collective_id=collective_id, has_side_effects=True),
         name="middle",
-    )(part.reshape(4, rows, width), x_piece, gain.reshape(1, width))
+    )(part.reshape(4, rows, width), x_piece, gain.reshape(1, width), table)
+
+
+def start_kernel(n_hi, n, *refs):
+    ins, outs, sems = refs[:n], refs[n : 2 * n], refs[2 * n :]
+    hi, lo, th, tl = place()
+    to_f = device(hi, 1 - lo, th, tl)
+    greet(n_hi, tensor=False)
+    sends = Sends()
+    own = []
+
+    def at(k, l):
+        return lax.rem(hi + k, n_hi) * 2 + l
+
+    for w_ref, o_ref, (own_sem, send_h, recv_h, send_f, recv_f) in zip(
+        ins, outs, [sems[5 * i : 5 * i + 5] for i in range(n)]
+    ):
+        for h in range(2):
+            for k in range(1, n_hi):
+                sends.push(
+                    w_ref.at[h], o_ref.at[at(0, lo), h], send_h.at[h, k - 1], recv_h.at[h, n_hi - k - 1],
+                    device(lax.rem(hi + k, n_hi), lo, th, tl),
+                )
+            sends.push(w_ref.at[h], o_ref.at[at(0, lo), h], send_f.at[h, 0], recv_f.at[h, 0], to_f)
+        copy = pltpu.make_async_copy(w_ref, o_ref.at[at(0, lo)], own_sem)
+        copy.start()
+        own.append(copy)
+    for o_ref, (own_sem, send_h, recv_h, send_f, recv_f) in zip(
+        outs, [sems[5 * i : 5 * i + 5] for i in range(n)]
+    ):
+        for k in range(1, n_hi):
+            for h in range(2):
+                view = o_ref.at[at(k, lo), h]
+                arrive(view, send_h.at[h, k - 1], recv_h.at[h, k - 1], to_f)
+                sends.push(view, view, send_f.at[h, k], recv_f.at[h, k], to_f)
+    for o_ref, (own_sem, send_h, recv_h, send_f, recv_f) in zip(
+        outs, [sems[5 * i : 5 * i + 5] for i in range(n)]
+    ):
+        for k in range(n_hi):
+            for h in range(2):
+                arrive(o_ref.at[at(k, 1 - lo), h], send_f.at[h, k], recv_f.at[h, k], to_f)
+    for copy in own:
+        copy.wait()
+    sends.finish()
+
+
+def start(weights, n_dp, collective_id):
+    n_hi = n_dp // 2
+    n = len(weights)
+    half = weights[0].shape[0] // 2
+    outs = pl.pallas_call(
+        functools.partial(start_kernel, n_hi, n),
+        out_shape=[jax.ShapeDtypeStruct((n_dp, 2, half, w.shape[1]), w.dtype) for w in weights],
+        in_specs=[ANY_SPEC] * n,
+        out_specs=[ANY_SPEC] * n,
+        scratch_shapes=[
+            DMA,
+            DMA((2, n_hi - 1)), DMA((2, n_hi - 1)),
+            DMA((2, n_hi)), DMA((2, n_hi)),
+        ] * n,
+        compiler_params=pltpu.CompilerParams(collective_id=collective_id, has_side_effects=True),
+        name="start",
+    )(*[w.reshape(2, half, w.shape[1]) for w in weights])
+    return [o.reshape(n_dp * 2 * half, o.shape[3]) for o in outs]
 
 
 def scatter_steps(n_hi, sends, p_ref, o_ref, bufs):
@@ -379,8 +441,12 @@
         z = 1 - tl if c else tl
         return ((kk * 2 + l) * 4 + y * 2 + z) * rows + h * half
 
-    order = [(f, s, k, h) for f, s in ((1, 1), (1, 0), (0, 1), (0, 0)) for k in
-             list(range(1, n_hi)) + [0] for h in range(2)]
+    ks = list(range(1, n_hi)) + [0]
+    order = []
+    for i in range(n_hi + 2):
+        for lag, groups in ((0, ((1, 1), (1, 0))), (1, ((0, 1),)), (2, ((0, 0),))):
+            if 0 <= i - lag < n_hi:
+                order += [(f, s, ks[i - lag], h) for f, s in groups for h in range(2)]
 
     def slot(f, s, k):
         return (f * 2 + s) * n_hi + k
@@ -522,17 +588,18 @@
     )(p, hidden, g2_piece, gain.reshape(1, width))
 
 
-def tail_kernel(
-    n_hi, wide, bc_at, w_ref, part_ref, grad_ref, x_ref, gain_ref, small_ref,
-    ow_ref, ox_ref, os_ref,
-    stage, from_f, from_h, stage_sem, send_f, recv_f, send_h, recv_h,
-    got_c, got_y, t_send, t_recv, sp_send, sp_recv,
-    small, small_f, small_h, small_t, sm_send, sm_recv, smh_send, smh_recv,
-    bc_own, bc_got, bc_send, bc_recv,
-):
+def tail_kernel(n_hi, wide, bc_at, n, *refs):
+    part_ref, grad_ref, x_ref, gain_ref, small_ref = refs[:5]
+    w_refs = refs[5 : 5 + n]
+    ox_ref, os_ref = refs[5 + n : 7 + n]
+    ow_refs = refs[7 + n : 7 + 2 * n]
+    (got_c, got_y, t_send, t_recv, sp_send, sp_recv,
+     small, small_f, small_h, small_t, sm_send, sm_recv, smh_send, smh_recv,
+     bc_own, bc_got, bc_send, bc_recv) = refs[7 + 2 * n : 25 + 2 * n]
+    rest = refs[25 + 2 * n :]
+    bufs = [rest[8 * i : 8 * i + 8] for i in range(n)]
     hi, lo, th, tl = place()
     to_f, to_y, to_c = device(hi, 1 - lo, th, tl), device(hi, lo, 1 - th, tl), device(hi, lo, th, 1 - tl)
-    half = w_ref.shape[2]
     greet(n_hi)
     sends = Sends()
     order = [(k, h) for k in list(range(1, n_hi)) + [0] for h in range(2)]
@@ -540,14 +607,17 @@
     def owner(k, l):
         return lax.rem(hi + k, n_hi) * 2 + l
 
-    for k, h in order:
-        sends.push(w_ref.at[owner(k, 1 - lo), h], from_f.at[h, k], send_f.at[h, k], recv_f.at[h, k], to_f)
-    loads = [
-        pltpu.make_async_copy(w_ref.at[owner(k, lo), h], stage.at[h, k], stage_sem.at[h, k])
-        for k, h in order
-    ]
-    for copy in loads:
-        copy.start()
+    for w_ref, (stage, from_f, from_h, stage_sem, send_f, recv_f, send_h, recv_h) in zip(w_refs, bufs):
+        for k, h in order:
+            sends.push(
+                w_ref.at[owner(k, 1 - lo), h], from_f.at[h, k], send_f.at[h, k], recv_f.at[h, k], to_f
+            )
+    loads = []
+    for w_ref, (stage, from_f, from_h, stage_sem, send_f, recv_f, send_h, recv_h) in zip(w_refs, bufs):
+        for k, h in order:
+            copy = pltpu.make_async_copy(w_ref.at[owner(k, lo), h], stage.at[h, k], stage_sem.at[h, k])
+            copy.start()
+            loads.append(copy)
     tensor_sum_start(sends, part_ref, got_c, t_send, t_recv)
     tensor_sum_middle(sends, part_ref, got_c, got_y, t_send, t_recv)
     grad = tensor_sum_end(part_ref, got_c, got_y, t_send, t_recv)
@@ -563,12 +633,13 @@
     small[0:1, :] = jnp.sum(grad * x * scale, axis=0, keepdims=True)
     sends.push(small, small_f, sm_send.at[0], sm_recv.at[0], to_f)
 
-    finals = []
-    for i, (k, h) in enumerate(order):
+    events = [(w, k, h) for w in range(n) for k, h in order]
+    for i, (w, k, h) in enumerate(events):
+        if k == 0:
+            continue
+        stage, from_f, from_h, stage_sem, send_f, recv_f, send_h, recv_h = bufs[w]
         loads[i].wait()
         arrive(from_f.at[h, k], send_f.at[h, k], recv_f.at[h, k], to_c)
-        if k == 0:
-            continue
         from_f[h, k] = (stage[h, k].astype(F32) + from_f[h, k].astype(F32)).astype(from_f.dtype)
         j = n_hi - k - 1
         sends.push(
@@ -592,72 +663,82 @@
         total = total + small_h[q]
     os_ref[...] = total
     sends.push(os_ref.at[pl.ds(0, wide)], small_t.at[0], sm_send.at[1], sm_recv.at[1], to_c)
-    for h in range(2):
+    for i, (w, k, h) in enumerate(events):
+        if k:
+            continue
+        stage, from_f, from_h, stage_sem, send_f, recv_f, send_h, recv_h = bufs[w]
+        loads[i].wait()
+        arrive(from_f.at[h, 0], send_f.at[h, 0], recv_f.at[h, 0], to_c)
         total = stage[h, 0].astype(F32) + from_f[h, 0].astype(F32)
         for j in range(n_hi - 1):
             arrive(from_h.at[h, j], send_h.at[h, j], recv_h.at[h, j], to_c)
             total = total + from_h[h, j].astype(F32)
-        ow_ref[h] = total
-        bc_own[0, h] = total[:, bc_at : bc_at + bc_own.shape[3]].astype(bc_own.dtype)
-    sends.push(bc_own.at[0], bc_got.at[0], bc_send.at[0], bc_recv.at[0], to_c)
-    arrive(small_t.at[0], sm_send.at[1], sm_recv.at[1], to_c)
-    small_t[2] = os_ref[pl.ds(0, wide), :] + small_t[0]
-    sends.push(small_t.at[2], small_t.at[1], sm_send.at[2], sm_recv.at[2], to_y)
-    arrive(bc_got.at[0], bc_send.at[0], bc_recv.at[0], to_c)
-    bc_own[1] = (bc_own[0].astype(F32) + bc_got[0].astype(F32)).astype(bc_own.dtype)
-    sends.push(bc_own.at[1], bc_got.at[1], bc_send.at[1], bc_recv.at[1], to_y)
+        ow_refs[w][h] = total
+        if w == 0:
+            bc_own[0, h] = total[:, bc_at : bc_at + bc_own.shape[3]].astype(bc_own.dtype)
+            if h == 1:
+                sends.push(bc_own.at[0], bc_got.at[0], bc_send.at[0], bc_recv.at[0], to_c)
+                arrive(small_t.at[0], sm_send.at[1], sm_recv.at[1], to_c)
+                small_t[2] = os_ref[pl.ds(0, wide), :] + small_t[0]
+                sends.push(small_t.at[2], small_t.at[1], sm_send.at[2], sm_recv.at[2], to_y)
+                arrive(bc_got.at[0], bc_send.at[0], bc_recv.at[0], to_c)
+                bc_own[1] = (bc_own[0].astype(F32) + bc_got[0].astype(F32)).astype(bc_own.dtype)
+                sends.push(bc_own.at[1], bc_got.at[1], bc_send.at[1], bc_recv.at[1], to_y)
     arrive(small_t.at[1], sm_send.at[2], sm_recv.at[2], to_c)
     arrive(bc_got.at[1], bc_send.at[1], bc_recv.at[1], to_c)
     for h in range(2):
-        ow_ref[h, :, bc_at : bc_at + bc_own.shape[3]] = bc_own[1, h].astype(F32) + bc_got[1, h].astype(F32)
+        ow_refs[0][h, :, bc_at : bc_at + bc_own.shape[3]] = (
+            bc_own[1, h].astype(F32) + bc_got[1, h].astype(F32)
+        )
     sends.finish()
     os_ref[pl.ds(0, wide), :] = small_t[2] + small_t[1]
 
 
-def tail(w, part, grad_one, x_piece, gain, small, wide, bc_at, bc_width, n_dp, collective_id):
+def tail(weights, part, grad_one, x_piece, gain, small, wide, bc_at, bc_width, n_dp, collective_id):
     rows, width = x_piece.shape
     n_hi = n_dp // 2
-    half = w.shape[0] // (2 * n_dp)
-    w_width = w.shape[1]
-    dt = w.dtype
-    return pl.pallas_call(
-        functools.partial(tail_kernel, n_hi, wide, bc_at),
-        out_shape=(
-            jax.ShapeDtypeStruct((2, half, w_width), F32),
-            jax.ShapeDtypeStruct((4, rows, width), dt),
-            jax.ShapeDtypeStruct(small.shape, F32),
-        ),
-        in_specs=[ANY_SPEC] + [VMEM_SPEC] * 5,
-        out_specs=(VMEM_SPEC,) * 3,
-        scratch_shapes=[
-            pltpu.VMEM((2, n_hi, half, w_width), dt),
-            pltpu.VMEM((2, n_hi, half, w_width), dt),
-            pltpu.VMEM((2, n_hi - 1, half, w_width), dt),
+    n = len(weights)
+    half = weights[0].shape[0] // (2 * n_dp)
+    dt = weights[0].dtype
+    scratch = TENSOR_SUM_SCRATCH(rows, width, part.dtype) + [
+        DMA((3,)), DMA((3,)),
+        pltpu.VMEM(small.shape, F32),
+        pltpu.VMEM(small.shape, F32),
+        pltpu.VMEM((n_hi,) + small.shape, F32),
+        pltpu.VMEM((3, wide, small.shape[1]), F32),
+        DMA((3,)), DMA((3,)),
+        DMA((n_hi - 1,)), DMA((n_hi - 1,)),
+        pltpu.VMEM((2, 2, half, bc_width), dt),
+        pltpu.VMEM((2, 2, half, bc_width), dt),
+        DMA((2,)), DMA((2,)),
+    ]
+    for w in weights:
+        scratch += [
+            pltpu.VMEM((2, n_hi, half, w.shape[1]), dt),
+            pltpu.VMEM((2, n_hi, half, w.shape[1]), dt),
+            pltpu.VMEM((2, n_hi - 1, half, w.shape[1]), dt),
             DMA((2, n_hi)),
             DMA((2, n_hi)), DMA((2, n_hi)),
             DMA((2, n_hi - 1)), DMA((2, n_hi - 1)),
         ]
-        + TENSOR_SUM_SCRATCH(rows, width, part.dtype)
-        + [
-            DMA((3,)), DMA((3,)),
-            pltpu.VMEM(small.shape, F32),
-            pltpu.VMEM(small.shape, F32),
-            pltpu.VMEM((n_hi,) + small.shape, F32),
-            pltpu.VMEM((3, wide, small.shape[1]), F32),
-            DMA((3,)), DMA((3,)),
-            DMA((n_hi - 1,)), DMA((n_hi - 1,)),
-            pltpu.VMEM((2, 2, half, bc_width), dt),
-            pltpu.VMEM((2, 2, half, bc_width), dt),
-            DMA((2,)), DMA((2,)),
-        ],
+    outs = pl.pallas_call(
+        functools.partial(tail_kernel, n_hi, wide, bc_at, n),
+        out_shape=[
+            jax.ShapeDtypeStruct((4, rows, width), dt),
+            jax.ShapeDtypeStruct(small.shape, F32),
+        ] + [jax.ShapeDtypeStruct((2, half, w.shape[1]), F32) for w in weights],
+        in_specs=[VMEM_SPEC] * 5 + [ANY_SPEC] * n,
+        out_specs=[VMEM_SPEC] * (2 + n),
+        scratch_shapes=scratch,
         compiler_params=pltpu.CompilerParams(
             collective_id=collective_id, has_side_effects=True, vmem_limit_bytes=60 << 20
         ),
         name="tail",
     )(
-        w.reshape(n_dp, 2, half, w_width), part.reshape(4, rows, width), grad_one, x_piece,
-        gain.reshape(1, width), small,
-    )
+        part.reshape(4, rows, width), grad_one, x_piece, gain.reshape(1, width), small,
+        *[w.reshape(n_dp, 2, half, w.shape[1]) for w in weights],
+    )
+    return outs[0], outs[1], [o.reshape(2 * half, o.shape[2]) for o in outs[2:]]
 
 
 def dot_mm(a, b):
@@ -848,10 +929,10 @@
         ],
         axis=1,
     ).astype(BF)
-    first = lax.all_gather(first, "dp", axis=0, tiled=True)
-    proj_out = lax.all_gather(w_out.astype(BF), "dp", axis=0, tiled=True)
+    first, proj_out = start([first, w_out.astype(BF)], n_dp, 1)
     shared = jnp.concatenate([w_shared_gu.reshape(rows, 2 * n_sh), w_shared_down], axis=1)
-    shared = lax.all_gather(shared.astype(BF), "dp", axis=0, tiled=True)
+    shared, first = lax.optimization_barrier((shared.astype(BF), first))
+    shared = lax.all_gather(shared, "dp", axis=0, tiled=True)
     shared_gu = shared[:, : 2 * n_sh]
     shared_down = shared[:, 2 * n_sh :]
 
@@ -865,8 +946,38 @@
     low = (weights - high.astype(F32)).astype(BF)
     table = jnp.concatenate([g2_low, high, low], axis=1)
     table = lax.dynamic_slice_in_dim(table, my_t * piece, piece, axis=0)
-    table = gather_rows(table, n_dp, 1)
     g2_piece = lax.dynamic_slice_in_dim(g2_low, my_t * piece, piece, axis=0)
+
+    x_float = x_in.astype(F32)
+    scale_one = rms_scale(x_float)
+    normed_one = (x_float * scale_one * ln1_gain).astype(BF)
+    firsts = dotf("td,df->tf", normed_one, first)
+    zx = firsts[:, : 2 * inner]
+    bc_proj = firsts[:, 2 * inner : dt_at]
+    dt_proj = firsts[:, dt_at : dt_at + heads]
+
+    gated_mix, mixer_back = mixer_forward(
+        zx, bc_proj, dt_proj, conv_x, conv_x_bias, conv_bc, conv_bc_bias, dt_bias, a_log, d_skip
+    )
+    squares = lax.psum(jnp.sum(gated_mix * gated_mix, axis=-1), "tensor")
+    scale_mix = lax.rsqrt(squares / full_inner + EPSILON)[:, None]
+    normed_mix = (gated_mix * scale_mix * gnorm_gain).astype(BF)
+    mixer_part = dotf("tc,dc->td", normed_mix, proj_out).astype(BF)
+    x_piece = lax.dynamic_slice_in_dim(x_in, my_t * piece, piece, axis=0)
+    all_rows, table, hidden_one = middle(mixer_part, x_piece, ln2_gain, table, n_dp, 2)
+    mine = lax.dynamic_slice_in_dim(all_rows, my_dp * slots, slots, axis=0)
+
+    shared_pre = dotf("td,df->tf", mine, shared_gu)
+    s_gate, s_up = shared_pre[:, :n_sh], shared_pre[:, n_sh:]
+    shared_silu, shared_slope = silu_parts(s_gate)
+    shared_act = (shared_silu * s_up).astype(BF)
+    grad_shared_act = dotf("td,df->tf", g2_low, shared_down)
+    grad_shared_pre = jnp.concatenate(
+        [grad_shared_act * s_up * shared_slope, grad_shared_act * shared_silu], axis=1
+    ).astype(BF)
+    grad_normed_shared = dotf("tf,df->td", grad_shared_pre, shared_gu)
+    shared_part = dotf("tf,df->td", shared_act, shared_down)
+
     high = lax.dynamic_slice_in_dim(table, width + my_dp * n_local, n_local, axis=1)
     low = lax.dynamic_slice_in_dim(table, width + n_experts + my_dp * n_local, n_local, axis=1)
     weights = (high.astype(F32) + low.astype(F32)).reshape(n_dp, slots, n_local)
@@ -878,36 +989,6 @@
     weights = weights.transpose(0, 2, 1)
     position = jnp.where(weights > 0.0, position, -1)
 
-    x_float = x_in.astype(F32)
-    scale_one = rms_scale(x_float)
-    normed_one = (x_float * scale_one * ln1_gain).astype(BF)
-    firsts = dotf("td,df->tf", normed_one, first)
-    zx = firsts[:, : 2 * inner]
-    bc_proj = firsts[:, 2 * inner : dt_at]
-    dt_proj = firsts[:, dt_at : dt_at + heads]
-
-    gated_mix, mixer_back = mixer_forward(
-        zx, bc_proj, dt_proj, conv_x, conv_x_bias, conv_bc, conv_bc_bias, dt_bias, a_log, d_skip
-    )
-    squares = lax.psum(jnp.sum(gated_mix * gated_mix, axis=-1), "tensor")
-    scale_mix = lax.rsqrt(squares / full_inner + EPSILON)[:, None]
-    normed_mix = (gated_mix * scale_mix * gnorm_gain).astype(BF)
-    mixer_part = dotf("tc,dc->td", normed_mix, proj_out).astype(BF)
-    x_piece = lax.dynamic_slice_in_dim(x_in, my_t * piece, piece, axis=0)
-    all_rows, hidden_one = middle(mixer_part, x_piece, ln2_gain, n_dp, 2)
-    mine = lax.dynamic_slice_in_dim(all_rows, my_dp * slots, slots, axis=0)
-
-    shared_pre = dotf("td,df->tf", mine, shared_gu)
-    s_gate, s_up = shared_pre[:, :n_sh], shared_pre[:, n_sh:]
-    shared_silu, shared_slope = silu_parts(s_gate)
-    shared_act = (shared_silu * s_up).astype(BF)
-    grad_shared_act = dotf("td,df->tf", g2_low, shared_down)
-    grad_shared_pre = jnp.concatenate(
-        [grad_shared_act * s_up * shared_slope, grad_shared_act * shared_silu], axis=1
-    ).astype(BF)
-    grad_normed_shared = dotf("tf,df->td", grad_shared_pre, shared_gu)
-    shared_part = dotf("tf,df->td", shared_act, shared_down)
-
     dxn_part, out_part, grad_exp_gu, grad_exp_down = experts(
         position, weights, all_rows, table, w_exp_gu, w_exp_down, cap
     )
@@ -920,18 +1001,22 @@
 
     dxn_part = add_own(dxn_part, grad_normed_shared)
     out_part = add_own(out_part, shared_part)
+    ffn_out = scatter_rows(out_part, n_dp, 4)
+    dxn_part, ffn_out = lax.optimization_barrier((dxn_part, ffn_out))
     grad_one, sum_ln2, dm = turn(
         dxn_part, hidden_one, g2_piece, ln2_gain, n_dp, 3
     )
     dm = dm.reshape(slots, width)
 
-    ffn_out = scatter_rows(out_part, n_dp, 4)
     layer_out = lax.all_gather(
         (hidden_one + ffn_out).astype(BF), "tensor", axis=0, tiled=True
     )
     grad_shared_down = dotf("td,tf->df", g2_low, shared_act)
     grad_shared_gu = dotf("td,tf->df", mine, grad_shared_pre)
 
+    grad_shared_w = jnp.concatenate([grad_shared_gu, grad_shared_down], axis=1).astype(BF)
+    grad_shared_w, dm = lax.optimization_barrier((grad_shared_w, dm))
+    grad_shared_w = lax.psum_scatter(grad_shared_w, "dp", scatter_dimension=0, tiled=True)
     grad_out_proj = dotf("td,tc->dc", dm, normed_mix)
     grad_normed_mix = dotf("td,dc->tc", dm, proj_out)
     weighted_mix = gnorm_gain * grad_normed_mix
@@ -961,12 +1046,6 @@
     )
     grad_input_part = dotf("tf,df->td", grad_first, first).astype(BF)
     grad_first_w = dotf("td,tf->df", normed_one, grad_first).astype(BF)
-    grad_shared_w = jnp.concatenate([grad_shared_gu, grad_shared_down], axis=1).astype(BF)
-    grad_shared_w = lax.psum_scatter(grad_shared_w, "dp", scatter_dimension=0, tiled=True)
-    grad_out_w = lax.psum_scatter(
-        grad_out_proj.astype(BF), "dp", scatter_dimension=0, tiled=True
-    )
-
     def lanes(*vectors):
         vector = jnp.concatenate([v.reshape(-1) for v in vectors])
         return jnp.pad(vector, (0, -vector.shape[0] % (8 * width))).reshape(-1, width)
@@ -977,8 +1056,8 @@
     narrow = lanes(
         grad_conv_x, grad_conv_x_bias, grad_gnorm, grad_dt_bias, grad_a_log, grad_d_skip
     )
-    first_f, grad_x, sums = tail(
-        grad_first_w,
+    grad_x, sums, (first_f, grad_out_w) = tail(
+        [grad_first_w, grad_out_proj.astype(BF)],
         grad_input_part,
         grad_one,
         x_piece,
@@ -990,7 +1069,6 @@
         n_dp,
         5,
     )
-    first_f = first_f.reshape(rows, first_width)
     grad_x = grad_x.reshape(slots, width).astype(F32)
     wide, narrow = sums[:n_wide].reshape(-1), sums[n_wide:].reshape(-1)
     at = [0]
@@ -1030,7 +1108,7 @@
         o_a_log,
         o_d_skip,
         o_gnorm,
-        grad_out_w.astype(F32),
+        grad_out_w,
         o_ln2,
         shared_f[:, : 2 * n_sh].reshape(rows, 2, n_sh),
         shared_f[:, 2 * n_sh :],

time: 922 us -> 978 us (1.061)
  Pallas kernels: 626 us -> 686 us
    pallas_call x2, Pallas kernels: 278 us -> 327 us  [the longest x1 186 us: tail(): pl.pallas_call(functools.partial(tail_kernel, n_hi, wide, bc_at, n), out_...]
    pallas_call x1, Pallas kernels: 112 us -> 150 us  [middle(): pl.pallas_call(functools.partial(middle_kernel, n_hi), out_shape=(jax.Sha...]
    pallas_call x1, Pallas kernels: 80.7 us -> 64.9 us  [scatter_rows(): pl.pallas_call(functools.partial(scatter_kernel, n_hi), out_shape=jax.Sha...]
    pallas_call x1, Pallas kernels: 96.5 us -> 85.2 us  [turn(): pl.pallas_call(functools.partial(turn_kernel, n_hi), out_shape=(jax.Shape...]
  transfers between devices with their start and end apart: 6 -> 3, of which waited for: 0 -> 0; matrix products, arithmetic and copies ran while one was open for 26% -> 20% of each run, Pallas kernels for 60% -> 41%
where the time goes in v5:
time: 978 us; the launch traced here: 965 us
  Pallas kernels  686 us (70%)
  local copies, waits for them, and re-layouts  93.7 us (10%)
  matrix products  93.3 us (10%)
  other arithmetic  63 us (6%)
  between operations  16.2 us (2%)
  blocking collectives  11.5 us (1%)
    pallas_call x1, Pallas kernels, tail(): pl.pallas_call(functools.partial(tail_kernel, n_hi, wide, bc_at, n), out_...  186 us
    pallas_call x1, Pallas kernels, middle(): pl.pallas_call(functools.partial(middle_kernel, n_hi), out_shape=(jax.Sha...  150 us
    pallas_call x1, Pallas kernels, start(): pl.pallas_call(functools.partial(start_kernel, n_hi, n), out_shape=[jax.S...  141 us
    pallas_call x1, Pallas kernels, turn(): pl.pallas_call(functools.partial(turn_kernel, n_hi), out_shape=(jax.Shape...  85.2 us
    pallas_call x1, Pallas kernels, scatter_rows(): pl.pallas_call(functools.partial(scatter_kernel, n_hi), out_shape=jax.Sha...  64.9 us
    pallas_call x1, Pallas kernels, experts(): pl.pallas_call(functools.partial(experts_kernel, n_dp, n_local, cap, chun...  59.1 us
    dot_general x13, matrix products, dotf(): return jnp.einsum(spec, a, b, preferred_element_type=F32)  46.3 us
    dot_general x3, matrix products, ssd_scan(): jnp.einsum('kij,kijh,kjhp->kihp', intersection, decay_mask, scaled, preci...  22.1 us
  transfers between devices with their start and end apart: 3, of which 0 were waited for; matrix products, arithmetic and copies ran while one was open for 20% of the time, Pallas kernels for 41%

profile of v5, /device:TPU:9, one launch (start us, length us, event | category | flops | bytes accessed | tf_op | source)
XLA Modules:
  0.0 964.9 jit_solution(17717633482240797225)
XLA Ops:
  11.6 141.0 %start.1 = (bf16[8,2,96,1920]{3,2,1,0:T(8,128)(2,1)}, bf16[8,2,96,768]{3,2,1,0:T(8,128)(2,1)}) custom-call(bf16[2,96,1920]{2,1,0:T(8,128)(2,1)} %concatenate.54.refs_0_, bf16[2,96,768]{2,1,0:T(8,128)(2,1)} %bitcast.239), custom_call_target="tpu_custom_call" | custom-call | tf_op jit(solution)/shard_map/start/pallas_call | solution.py:412
  153.9 5.7 fusion.99
  186.4 6.7 while.34
  196.4 7.6 fusion.46
  206.6 3.1 copy.273
  209.9 3.7 multiply_reduce_fusion.9
  213.5 6.4 psum.14
  226.7 3.7 concatenate.57
  232.2 4.7 convolution_convert_fusion.4
  237.0 149.7 %middle.1 = (bf16[4096,1536]{1,0:T(8,128)(2,1)}, bf16[4096,1664]{1,0:T(8,128)(2,1)}, f32[128,1536]{1,0:T(8,128)}) custom-call(bf16[4,128,1536]{2,1,0:T(8,128)(2,1)} %bitcast.234, bf16[128,1536]{1,0:T(8,128)(2,1)} %constant_dynamic-slice_fusion.6.x_ref.refs_2_, f32[1,1536]{1,0:T(1,128)} %reshape.337.gain_ref, ...), custom_call_target="tpu_custom_call" | custom-call | tf_op jit(solution)/shard_map/middle/pallas_call | solution.py:347
  386.7 3.6 convert_add_fusion
  399.5 59.1 %experts.1 = (bf16[4096,1536]{1,0:T(8,128)(2,1)}, bf16[4096,1536]{1,0:T(8,128)(2,1)}, f32[24576,128]{1,0:T(8,128)}, f32[8,128,1536]{2,1,0:T(8,128)}) custom-call(s32[8,8,512]{2,1,0:T(8,128)} %fusion.78.pos_ref, f32[8,8,512]{2,1,0:T(8,128)} %bitcast.254, bf16[4096,1536]{1,0:T(8,128)(2,1)} %get-tuple-element.223.x_ref, ...), custom_call_target="tpu_custom_call" | custom-call | flops 40265318400 | bytes 88080384 | tf_op jit(solution)/shard_map/experts/pallas_call | solution.py:828
  464.0 3.2 fusion.29.p_ref
  467.1 64.9 %scatter_rows.1 = f32[128,1536]{1,0:T(8,128)} custom-call(bf16[4096,1536]{1,0:T(8,128)(2,1)} %fusion.29.p_ref), custom_call_target="tpu_custom_call" | custom-call | tf_op jit(solution)/shard_map/scatter_rows/pallas_call | solution.py:536
  534.7 3.7 fusion.31.p_ref
  540.0 85.2 %turn.1 = (f32[128,1536]{1,0:T(8,128)}, f32[1,1536]{1,0:T(1,128)}, bf16[4,128,1536]{2,1,0:T(8,128)(2,1)}) custom-call(bf16[4096,1536]{1,0:T(8,128)(2,1)} %fusion.31.p_ref, f32[128,1536]{1,0:T(8,128)} %get-tuple-element.221.hidden_ref, bf16[128,1536]{1,0:T(8,128)(2,1)} %constant_dynamic-slice_fusion.4.g2_ref, f32[1,1536]{1,0:T(1,128)} %reshape.337.gain_ref), custom_call_target="tpu_custom_call" | custom-call | tf_op jit(solution)/shard_map/turn/pallas_call | solution.py:573
  625.2 5.8 multiply_reduce_fusion.2
  630.9 5.1 psum.15
  636.0 5.1 multiply_reduce_fusion.1
  647.3 3.3 fusion.67
  655.7 10.9 %while.35 = (s32[]{:T(128)}, f32[12,128,64]{2,1,0:T(8,128)S(1)}, f32[2,12]{1,0:T(2,128)}, f32[2,12,128,64]{3,2,1,0:T(8,128)}, f32[2,12,128,64]{2,3,1,0:T(8,128)}...) while((s32[]{:T(128)}, f32[12,128,64]{2,1,0:T(8,128)S(1)}, ...), condition=%wide.region_12.13_spmd.clone, body=%wide.region_10.12_spmd.clone.sunk | while | flops 589816 | bytes 4326632 | solution.py:73
  669.8 9.0 fusion.14
  678.8 5.5 bitcast_add_fusion.2
  693.7 5.4 reduce-window.16
  700.2 7.3 multiply_reduce_fusion.5
  709.8 6.6 fusion.70
  716.5 5.1 fusion.73
  734.4 3.5 concatenate.61
  739.4 4.5 convolution_convert_fusion.1
  743.9 5.5 convolution_convert_fusion
  749.4 4.6 convolution_convert_fusion.3
  754.0 186.5 %tail.1 = (bf16[4,128,1536]{2,1,0:T(8,128)(2,1)}, f32[16,1536]{1,0:T(8,128)}, f32[2,96,1920]{2,1,0:T(8,128)}, f32[2,96,768]{2,1,0:T(8,128)}) custom-call(bf16[4,128,1536]{2,1,0:T(8,128)(2,1)} %bitcast.235, f32[128,1536]{1,0:T(8,128)} %get-tuple-element.234.refs_1_, bf16[128,1536]{1,0:T(8,128)(2,1)} %constant_dynamic-slice_fusion.6.x_ref.refs_2_, ...), custom_call_target="tpu_custom_call" | custom-call | tf_op jit(solution)/shard_map/tail/pallas_call | solution.py:724
  (430 shorter events, 140.1 us)
Async XLA Ops:
  7.2 451.5 %all-gather.3.cloned.1.call-start = ((), (), s32[]{:S(2)}) async-start(), calls=%async_computation.1 | async-start | bytes 2654208 | tf_op jit(solution)/shard_map/all_gather | solution.py:935
  10.6 142.9 %copy-start.29 = (bf16[512,1536]{1,0:T(8,128)(2,1)S(1)}, bf16[512,1536]{1,0:T(8,128)(2,1)}, u32[]{:S(2)}) copy-start(bf16[512,1536]{1,0:T(8,128)(2,1)} %param.27) | copy-start | bytes 4718596
  11.6 142.3 %copy-start.87 = (f32[1536]{0:T(1024)S(1)}, f32[1536]{0:T(1024)}, u32[]{:S(2)}) copy-start(f32[1536]{0:T(1024)} %param.31) | copy-start | bytes 18436
  153.4 799.3 %all-gather.5.cloned.1.call-start = ((), (), s32[]{:S(2)}) async-start(), calls=%async_computation.2 | async-start | bytes 1966080 | tf_op jit(solution)/shard_map/all_gather | solution.py:1011
  153.9 5.7 copy-start.101
  161.1 11.8 %copy-start.7 = (f32[512,768]{1,0:T(8,128)}, f32[512,768]{1,0:T(8,128)S(1)}, u32[]{:S(2)}) copy-start(f32[512,768]{1,0:T(8,128)S(1)} %slice.209) | copy-start | bytes 4718596
  161.2 7.1 copy-start.95
  161.2 7.2 copy-start.107
  161.8 19.9 %copy-start.18 = (f32[512,12]{1,0:T(8,128)}, f32[512,12]{1,0:T(8,128)S(1)}, u32[]{:S(2)}) copy-start(f32[512,12]{1,0:T(8,128)S(1)} %get-tuple-element.549) | copy-start | bytes 73732
  172.0 10.4 %copy-start.22 = (bf16[512,128]{1,0:T(8,128)(2,1)}, bf16[512,128]{1,0:T(8,128)(2,1)S(1)}, u32[]{:S(2)}) copy-start(bf16[512,128]{1,0:T(8,128)(2,1)S(1)} %get-tuple-element.566) | copy-start | bytes 393220
  196.1 8.0 copy-start.13
  196.4 7.7 copy-start.45
  209.9 12.5 %copy-start.86 = (f32[1536]{0:T(1024)S(1)}, f32[1536]{0:T(1024)}, u32[]{:S(2)}) copy-start(f32[1536]{0:T(1024)} %param.44) | copy-start | bytes 18436
  209.9 13.7 %copy-start.54 = (bf16[512,64]{0,1:T(8,128)(2,1)S(1)}, bf16[512,64]{0,1:T(8,128)(2,1)}, u32[]{:S(2)}) copy-start(bf16[512,64]{0,1:T(8,128)(2,1)} %convert_element_type.119) | copy-start | bytes 196612
  540.0 85.2 %copy-start.89 = (f32[512]{0:T(512)S(1)}, f32[512]{0:T(512)}, u32[]{:S(2)}) copy-start(f32[512]{0:T(512)} %get-tuple-element.581) | copy-start | bytes 6148
  540.0 85.2 %copy-start.93 = (f32[768]{0:T(1024)S(1)}, f32[768]{0:T(1024)}, u32[]{:S(2)}) copy-start(f32[768]{0:T(1024)} %param.42) | copy-start | bytes 9220
  625.1 10.9 %copy-start.91 = (f32[512]{0:T(512)S(1)}, f32[512]{0:T(512)}, u32[]{:S(2)}) copy-start(f32[512]{0:T(512)} %get-tuple-element.580) | copy-start | bytes 6148
  653.8 299.0 %reduce-scatter.4.cloned.1.call-start = ((), (), s32[]{:S(2)}) async-start(), calls=%async_computation.3 | async-start | bytes 2654208
  669.8 9.0 copy-start.40
  700.2 9.6 copy-start.4
  700.2 9.6 copy-start.53
  709.8 6.7 copy-start.9
  716.5 5.2 copy-start.24
  716.5 5.6 copy-start.21
  734.4 5.0 copy-start.16
  734.4 5.0 copy-start.90
  734.4 5.0 copy-start.94
  739.4 4.5 copy-start.30
  739.4 4.5 copy-start.33
  739.4 10.0 %slice-start = ((s8[5898240]{0:T(1024)(128)(4,1)}), s8[4194304]{0:T(1024)(128)(4,1)S(1)}, s32[]{:S(2)}) async-start(s8[5898240]{0:T(1024)(128)(4,1)} %bitcast.273), calls=%async_computation.4 | async-start | bytes 8388608
  743.9 5.5 slice-start.1
  944.4 6.2 copy-start.35
  (90 other events, 212.7 us)
Sparse Core Ops, SparseCore 0:
  153.5 49.6 all-gather.2
  653.9 20.3 all-gather.4
  729.6 75.2 reduce-scatter.3

commit v6 on v5

--- a/solution.py
+++ b/solution.py
@@ -157,10 +157,25 @@
     return (hi * 2 + lo, th * 2 + tl)
 
 
+def peer(hi, k, n_hi):
+    if n_hi & (n_hi - 1):
+        return lax.rem(hi + k, n_hi)
+    other, bit = hi, 1
+    while bit <= k:
+        if k & bit:
+            other = other + bit * (1 - 2 * lax.rem(hi // bit, 2))
+        bit *= 2
+    return other
+
+
+def back(k, n_hi):
+    return n_hi - k if n_hi & (n_hi - 1) else k
+
+
 def greet(n_hi, tensor=True):
     hi, lo, th, tl = place()
     barrier = pltpu.get_barrier_semaphore()
-    others = [device(lax.rem(hi + k, n_hi), lo, th, tl) for k in range(1, n_hi)]
+    others = [device(peer(hi, k, n_hi), lo, th, tl) for k in range(1, n_hi)]
     others += [device(hi, 1 - lo, th, tl)]
     if tensor:
         others += [device(hi, lo, 1 - th, tl), device(hi, lo, th, 1 - tl)]
@@ -241,7 +256,7 @@
     arrive(o_ref.at[(1 - th) * 2 + 1 - tl], ssem.at[2], rsem.at[2], to_c)
 
 
-def gather_steps(n_hi, x_ref, o_ref, own_sem, send_sem, recv_sem):
+def gather_steps(n_hi, x_ref, o_ref, own_sem, send_sem, recv_sem, lo_first=(True, False)):
     hi, lo, th, tl = place()
     rows = x_ref.shape[0]
     half = rows // 2
@@ -254,9 +269,9 @@
         return ((c * 2 + s) * 2 + f) * n_hi + k
 
     def where(h, k, f, s, c):
-        kk = lax.rem(hi + k, n_hi)
-        l = 1 - lo if (f if h == 0 else s) else lo
-        y = 1 - th if (s if h == 0 else f) else th
+        kk = peer(hi, k, n_hi)
+        l = 1 - lo if (f if lo_first[h] else s) else lo
+        y = 1 - th if (s if lo_first[h] else f) else th
         z = 1 - tl if c else tl
         return ((kk * 2 + l) * 4 + y * 2 + z) * rows + h * half
 
@@ -269,13 +284,13 @@
         if step == "c":
             to, r = device(hi, lo, th, 1 - tl), slot(k, f, s, 1)
         elif step == "s":
-            to = device(hi, lo, 1 - th, tl) if h == 0 else device(hi, 1 - lo, th, tl)
+            to = device(hi, lo, 1 - th, tl) if lo_first[h] else device(hi, 1 - lo, th, tl)
             r = slot(k, f, 1, 0)
         elif step == "f":
-            to = device(hi, 1 - lo, th, tl) if h == 0 else device(hi, lo, 1 - th, tl)
+            to = device(hi, 1 - lo, th, tl) if lo_first[h] else device(hi, lo, 1 - th, tl)
             r = slot(k, 1, 0, 0)
         else:
-            to, r = device(lax.rem(hi + step, n_hi), lo, th, tl), slot(n_hi - step, 0, 0, 0)
+            to, r = device(peer(hi, step, n_hi), lo, th, tl), slot(back(step, n_hi), 0, 0, 0)
         sends.push(src, o_ref.at[pl.ds(at, half)], send_sem.at[h, r], recv_sem.at[h, r], to)
 
     def got(h, k, f, s, c):
@@ -324,105 +339,98 @@
 
 
 def middle_kernel(
-    n_hi, part_ref, x_ref, gain_ref, table_ref, o_ref, all_table_ref, hidden_ref,
+    n_hi, part_ref, x_ref, gain_ref, o_ref, hidden_ref,
     normed, got_c, got_y, t_send, t_recv, *sems,
 ):
     greet(n_hi)
     sends = Sends()
     tensor_sum_start(sends, part_ref, got_c, t_send, t_recv)
-    tables = gather_steps(n_hi, table_ref, all_table_ref, *sems[:3])
-    next(tables)
     tensor_sum_middle(sends, part_ref, got_c, got_y, t_send, t_recv)
     hidden = x_ref[...].astype(F32) + tensor_sum_end(part_ref, got_c, got_y, t_send, t_recv)
     hidden_ref[...] = hidden
     normed[...] = (hidden * rms_scale(hidden) * gain_ref[...]).astype(normed.dtype)
-    in_turns(gather_steps(n_hi, normed, o_ref, *sems[3:]), tables)
+    in_turns(gather_steps(n_hi, normed, o_ref, *sems))
     sends.finish()
 
 
-def middle(part, x_piece, gain, table, n_dp, collective_id):
+def middle(part, x_piece, gain, n_dp, collective_id):
     rows, width = x_piece.shape
     n_hi = n_dp // 2
-    gather_sems = [DMA, DMA((2, 8 * n_hi)), DMA((2, 8 * n_hi))]
     return pl.pallas_call(
         functools.partial(middle_kernel, n_hi),
         out_shape=(
             jax.ShapeDtypeStruct((n_dp * 4 * rows, width), part.dtype),
-            jax.ShapeDtypeStruct((n_dp * 4 * rows, table.shape[1]), table.dtype),
             jax.ShapeDtypeStruct((rows, width), F32),
         ),
-        in_specs=[VMEM_SPEC] * 3 + [ANY_SPEC],
-        out_specs=(ANY_SPEC, ANY_SPEC, VMEM_SPEC),
+        in_specs=[VMEM_SPEC] * 3,
+        out_specs=(ANY_SPEC, VMEM_SPEC),
         scratch_shapes=[pltpu.VMEM((rows, width), part.dtype)]
         + TENSOR_SUM_SCRATCH(rows, width, part.dtype)
-        + gather_sems
-        + gather_sems,
+        + [DMA, DMA((2, 8 * n_hi)), DMA((2, 8 * n_hi))],
         compiler_params=pltpu.CompilerParams(collective_id=collective_id, has_side_effects=True),
         name="middle",
-    )(part.reshape(4, rows, width), x_piece, gain.reshape(1, width), table)
-
-
-def start_kernel(n_hi, n, *refs):
-    ins, outs, sems = refs[:n], refs[n : 2 * n], refs[2 * n :]
+    )(part.reshape(4, rows, width), x_piece, gain.reshape(1, width))
+
+
+def weight_steps(n_hi, w_ref, o_ref, own_sem, send_h, recv_h, send_f, recv_f):
     hi, lo, th, tl = place()
     to_f = device(hi, 1 - lo, th, tl)
-    greet(n_hi, tensor=False)
     sends = Sends()
-    own = []
 
     def at(k, l):
-        return lax.rem(hi + k, n_hi) * 2 + l
-
-    for w_ref, o_ref, (own_sem, send_h, recv_h, send_f, recv_f) in zip(
-        ins, outs, [sems[5 * i : 5 * i + 5] for i in range(n)]
-    ):
+        return peer(hi, k, n_hi) * 2 + l
+
+    for h in range(2):
+        for k in range(1, n_hi):
+            sends.push(
+                w_ref.at[h], o_ref.at[at(0, lo), h], send_h.at[h, k - 1], recv_h.at[h, back(k, n_hi) - 1],
+                device(peer(hi, k, n_hi), lo, th, tl),
+            )
+        sends.push(w_ref.at[h], o_ref.at[at(0, lo), h], send_f.at[h, 0], recv_f.at[h, 0], to_f)
+    own = pltpu.make_async_copy(w_ref, o_ref.at[at(0, lo)], own_sem)
+    own.start()
+    yield
+    for k in range(1, n_hi):
         for h in range(2):
-            for k in range(1, n_hi):
-                sends.push(
-                    w_ref.at[h], o_ref.at[at(0, lo), h], send_h.at[h, k - 1], recv_h.at[h, n_hi - k - 1],
-                    device(lax.rem(hi + k, n_hi), lo, th, tl),
-                )
-            sends.push(w_ref.at[h], o_ref.at[at(0, lo), h], send_f.at[h, 0], recv_f.at[h, 0], to_f)
-        copy = pltpu.make_async_copy(w_ref, o_ref.at[at(0, lo)], own_sem)
-        copy.start()
-        own.append(copy)
-    for o_ref, (own_sem, send_h, recv_h, send_f, recv_f) in zip(
-        outs, [sems[5 * i : 5 * i + 5] for i in range(n)]
-    ):
-        for k in range(1, n_hi):
-            for h in range(2):
-                view = o_ref.at[at(k, lo), h]
-                arrive(view, send_h.at[h, k - 1], recv_h.at[h, k - 1], to_f)
-                sends.push(view, view, send_f.at[h, k], recv_f.at[h, k], to_f)
-    for o_ref, (own_sem, send_h, recv_h, send_f, recv_f) in zip(
-        outs, [sems[5 * i : 5 * i + 5] for i in range(n)]
-    ):
-        for k in range(n_hi):
-            for h in range(2):
-                arrive(o_ref.at[at(k, 1 - lo), h], send_f.at[h, k], recv_f.at[h, k], to_f)
-    for copy in own:
-        copy.wait()
+            view = o_ref.at[at(k, lo), h]
+            arrive(view, send_h.at[h, k - 1], recv_h.at[h, k - 1], to_f)
+            sends.push(view, view, send_f.at[h, k], recv_f.at[h, k], to_f)
+        yield
+    for k in range(n_hi):
+        for h in range(2):
+            arrive(o_ref.at[at(k, 1 - lo), h], send_f.at[h, k], recv_f.at[h, k], to_f)
+    own.wait()
     sends.finish()
 
 
-def start(weights, n_dp, collective_id):
+def start_kernel(n_hi, n, *refs):
+    ins, outs, sems = refs[: n + 1], refs[n + 1 : 2 * n + 2], refs[2 * n + 2 :]
+    greet(n_hi)
+    streams = [
+        weight_steps(n_hi, ins[i], outs[i], *sems[5 * i : 5 * i + 5]) for i in range(n)
+    ] + [gather_steps(n_hi, ins[n], outs[n], *sems[5 * n :], lo_first=(True, True))]
+    in_turns(*streams)
+
+
+def start(weights, table, n_dp, collective_id):
     n_hi = n_dp // 2
     n = len(weights)
     half = weights[0].shape[0] // 2
     outs = pl.pallas_call(
         functools.partial(start_kernel, n_hi, n),
-        out_shape=[jax.ShapeDtypeStruct((n_dp, 2, half, w.shape[1]), w.dtype) for w in weights],
-        in_specs=[ANY_SPEC] * n,
-        out_specs=[ANY_SPEC] * n,
+        out_shape=[jax.ShapeDtypeStruct((n_dp, 2, half, w.shape[1]), w.dtype) for w in weights]
+        + [jax.ShapeDtypeStruct((n_dp * 4 * table.shape[0], table.shape[1]), table.dtype)],
+        in_specs=[ANY_SPEC] * (n + 1),
+        out_specs=[ANY_SPEC] * (n + 1),
         scratch_shapes=[
             DMA,
             DMA((2, n_hi - 1)), DMA((2, n_hi - 1)),
             DMA((2, n_hi)), DMA((2, n_hi)),
-        ] * n,
+        ] * n + [DMA, DMA((2, 8 * n_hi)), DMA((2, 8 * n_hi))],
         compiler_params=pltpu.CompilerParams(collective_id=collective_id, has_side_effects=True),
         name="start",
-    )(*[w.reshape(2, half, w.shape[1]) for w in weights])
-    return [o.reshape(n_dp * 2 * half, o.shape[3]) for o in outs]
+    )(*[w.reshape(2, half, w.shape[1]) for w in weights], table)
+    return [o.reshape(n_dp * 2 * half, o.shape[3]) for o in outs[:n]] + [outs[n]]
 
 
 def scatter_steps(n_hi, sends, p_ref, o_ref, bufs):
@@ -435,7 +443,7 @@
     half = rows // 2
 
     def where(h, k, f, s, c):
-        kk = lax.rem(hi + k, n_hi)
+        kk = peer(hi, k, n_hi)
         l = 1 - lo if (f if h == 1 else s) else lo
         y = 1 - th if (s if h == 1 else f) else th
         z = 1 - tl if c else tl
@@ -500,10 +508,10 @@
         elif s == 1:
             sends.push(src, from_s.at[h, k], send_s.at[h, k], recv_s.at[h, k], second(h))
         else:
-            j = n_hi - k - 1
+            j = back(k, n_hi) - 1
             sends.push(
                 src, from_h.at[h, j], send_h.at[h, j], recv_h.at[h, j],
-                device(lax.rem(hi + k, n_hi), lo, th, tl),
+                device(peer(hi, k, n_hi), lo, th, tl),
             )
 
 
@@ -605,7 +613,7 @@
     order = [(k, h) for k in list(range(1, n_hi)) + [0] for h in range(2)]
 
     def owner(k, l):
-        return lax.rem(hi + k, n_hi) * 2 + l
+        return peer(hi, k, n_hi) * 2 + l
 
     for w_ref, (stage, from_f, from_h, stage_sem, send_f, recv_f, send_h, recv_h) in zip(w_refs, bufs):
         for k, h in order:
@@ -641,10 +649,10 @@
         loads[i].wait()
         arrive(from_f.at[h, k], send_f.at[h, k], recv_f.at[h, k], to_c)
         from_f[h, k] = (stage[h, k].astype(F32) + from_f[h, k].astype(F32)).astype(from_f.dtype)
-        j = n_hi - k - 1
+        j = back(k, n_hi) - 1
         sends.push(
             from_f.at[h, k], from_h.at[h, j], send_h.at[h, j], recv_h.at[h, j],
-            device(lax.rem(hi + k, n_hi), lo, th, tl),
+            device(peer(hi, k, n_hi), lo, th, tl),
         )
         if i == 0:
             tensor_spread_end(sends, ox_ref, sp_send, sp_recv)
@@ -653,11 +661,11 @@
             small_h[hi] = small[...] + small_f[...]
             for q in range(1, n_hi):
                 sends.push(
-                    small_h.at[hi], small_h.at[hi], smh_send.at[q - 1], smh_recv.at[q - 1],
-                    device(lax.rem(hi + q, n_hi), lo, th, tl),
+                    small_h.at[hi], small_h.at[hi], smh_send.at[q - 1], smh_recv.at[back(q, n_hi) - 1],
+                    device(peer(hi, q, n_hi), lo, th, tl),
                 )
     for q in range(1, n_hi):
-        arrive(small_h.at[lax.rem(hi - q + n_hi, n_hi)], smh_send.at[q - 1], smh_recv.at[q - 1], to_c)
+        arrive(small_h.at[peer(hi, q, n_hi)], smh_send.at[q - 1], smh_recv.at[q - 1], to_c)
     total = small_h[0]
     for q in range(1, n_hi):
         total = total + small_h[q]
@@ -929,12 +937,7 @@
         ],
         axis=1,
     ).astype(BF)
-    first, proj_out = start([first, w_out.astype(BF)], n_dp, 1)
     shared = jnp.concatenate([w_shared_gu.reshape(rows, 2 * n_sh), w_shared_down], axis=1)
-    shared, first = lax.optimization_barrier((shared.astype(BF), first))
-    shared = lax.all_gather(shared, "dp", axis=0, tiled=True)
-    shared_gu = shared[:, : 2 * n_sh]
-    shared_down = shared[:, 2 * n_sh :]
 
     live = (jnp.arange(slots, dtype=jnp.int32) < lengths[0]).astype(F32)
     g2 = cotangent.astype(F32) * live[:, None]
@@ -948,6 +951,12 @@
     table = lax.dynamic_slice_in_dim(table, my_t * piece, piece, axis=0)
     g2_piece = lax.dynamic_slice_in_dim(g2_low, my_t * piece, piece, axis=0)
 
+    first, proj_out, table = start([first, w_out.astype(BF)], table, n_dp, 1)
+    shared, first = lax.optimization_barrier((shared.astype(BF), first))
+    shared = lax.all_gather(shared, "dp", axis=0, tiled=True)
+    shared_gu = shared[:, : 2 * n_sh]
+    shared_down = shared[:, 2 * n_sh :]
+
     x_float = x_in.astype(F32)
     scale_one = rms_scale(x_float)
     normed_one = (x_float * scale_one * ln1_gain).astype(BF)
@@ -964,7 +973,7 @@
     normed_mix = (gated_mix * scale_mix * gnorm_gain).astype(BF)
     mixer_part = dotf("tc,dc->td", normed_mix, proj_out).astype(BF)
     x_piece = lax.dynamic_slice_in_dim(x_in, my_t * piece, piece, axis=0)
-    all_rows, table, hidden_one = middle(mixer_part, x_piece, ln2_gain, table, n_dp, 2)
+    all_rows, hidden_one = middle(mixer_part, x_piece, ln2_gain, n_dp, 2)
     mine = lax.dynamic_slice_in_dim(all_rows, my_dp * slots, slots, axis=0)
 
     shared_pre = dotf("td,df->tf", mine, shared_gu)
@@ -1015,9 +1024,9 @@
     grad_shared_gu = dotf("td,tf->df", mine, grad_shared_pre)
 
     grad_shared_w = jnp.concatenate([grad_shared_gu, grad_shared_down], axis=1).astype(BF)
-    grad_shared_w, dm = lax.optimization_barrier((grad_shared_w, dm))
     grad_shared_w = lax.psum_scatter(grad_shared_w, "dp", scatter_dimension=0, tiled=True)
-    grad_out_proj = dotf("td,tc->dc", dm, normed_mix)
+    grad_out_w = dotf("td,tc->dc", dm, normed_mix).astype(BF)
+    grad_out_w = lax.psum_scatter(grad_out_w, "dp", scatter_dimension=0, tiled=True)
     grad_normed_mix = dotf("td,dc->tc", dm, proj_out)
     weighted_mix = gnorm_gain * grad_normed_mix
     grad_gnorm = jnp.sum(grad_normed_mix * gated_mix * scale_mix, axis=0)
@@ -1056,8 +1065,11 @@
     narrow = lanes(
         grad_conv_x, grad_conv_x_bias, grad_gnorm, grad_dt_bias, grad_a_log, grad_d_skip
     )
-    grad_x, sums, (first_f, grad_out_w) = tail(
-        [grad_first_w, grad_out_proj.astype(BF)],
+    grad_first_w, grad_out_w, grad_shared_w = lax.optimization_barrier(
+        (grad_first_w, grad_out_w, grad_shared_w)
+    )
+    grad_x, sums, (first_f,) = tail(
+        [grad_first_w],
         grad_input_part,
         grad_one,
         x_piece,
@@ -1108,7 +1120,7 @@
         o_a_log,
         o_d_skip,
         o_gnorm,
-        grad_out_w,
+        grad_out_w.astype(F32),
         o_ln2,
         shared_f[:, : 2 * n_sh].reshape(rows, 2, n_sh),
         shared_f[:, 2 * n_sh :],

time: 978 us -> 966 us (0.988)
  Pallas kernels: 686 us -> 639 us
  waiting for transfers between devices: 0.07 us -> 32.5 us
    pallas_call x1, Pallas kernels: 150 us -> 95.3 us  [middle(): pl.pallas_call(functools.partial(middle_kernel, n_hi), out_shape=(jax.Sha...]
    pallas_call x1, Pallas kernels: 186 us -> 152 us  [tail(): pl.pallas_call(functools.partial(tail_kernel, n_hi, wide, bc_at, n), out_...]
    reduce_scatter x0 -> x1, waiting for transfers between devices: none -> 32.4 us  [local(): lax.psum_scatter(grad_out_w, 'dp', scatter_dimension=0, tiled=True)]
    pallas_call x1, Pallas kernels: 141 us -> 163 us  [start(): pl.pallas_call(functools.partial(start_kernel, n_hi, n), out_shape=[jax.S...]
    pallas_call x1, Pallas kernels: 64.9 us -> 77.3 us  [scatter_rows(): pl.pallas_call(functools.partial(scatter_kernel, n_hi), out_shape=jax.Sha...]
  transfers between devices with their start and end apart: 3 -> 4, of which waited for: 0 -> 1; matrix products, arithmetic and copies ran while one was open for 20% -> 22% of each run, Pallas kernels for 41% -> 26%
where the time goes in v6:
time: 966 us; the launch traced here: 956 us
  Pallas kernels  639 us (66%)
  matrix products  98.9 us (10%)
  local copies, waits for them, and re-layouts  93 us (10%)
  other arithmetic  64.9 us (7%)
  waiting for transfers between devices  32.5 us (3%)
  between operations  16 us (2%)
  blocking collectives  10.4 us (1%)
    pallas_call x1, Pallas kernels, start(): pl.pallas_call(functools.partial(start_kernel, n_hi, n), out_shape=[jax.S...  163 us
    pallas_call x1, Pallas kernels, tail(): pl.pallas_call(functools.partial(tail_kernel, n_hi, wide, bc_at, n), out_...  152 us
    pallas_call x1, Pallas kernels, middle(): pl.pallas_call(functools.partial(middle_kernel, n_hi), out_shape=(jax.Sha...  95.3 us
    pallas_call x1, Pallas kernels, turn(): pl.pallas_call(functools.partial(turn_kernel, n_hi), out_shape=(jax.Shape...  91.9 us
    pallas_call x1, Pallas kernels, scatter_rows(): pl.pallas_call(functools.partial(scatter_kernel, n_hi), out_shape=jax.Sha...  77.3 us
    pallas_call x1, Pallas kernels, experts(): pl.pallas_call(functools.partial(experts_kernel, n_dp, n_local, cap, chun...  59.1 us
    dot_general x13, matrix products, dotf(): return jnp.einsum(spec, a, b, preferred_element_type=F32)  50.6 us
    reduce_scatter x1, waiting for transfers between devices, local(): lax.psum_scatter(grad_out_w, 'dp', scatter_dimension=0, tiled=True)  32.4 us
  transfers between devices with their start and end apart: 4, of which 1 were waited for; matrix products, arithmetic and copies ran while one was open for 22% of the time, Pallas kernels for 26%

profile of v6, /device:TPU:9, one launch (start us, length us, event | category | flops | bytes accessed | tf_op | source)
XLA Modules:
  0.0 955.9 jit_solution(4623628875715585157)
XLA Ops:
  23.5 163.4 %start.1 = (bf16[8,2,96,1920]{3,2,1,0:T(8,128)(2,1)}, bf16[8,2,96,768]{3,2,1,0:T(8,128)(2,1)}, bf16[4096,1664]{1,0:T(8,128)(2,1)}) custom-call(bf16[2,96,1920]{2,1,0:T(8,128)(2,1)} %concatenate.54.refs_0_, bf16[2,96,768]{2,1,0:T(8,128)(2,1)} %bitcast.236, bf16[128,1664]{1,0:T(8,128)(2,1)} %constant_dynamic-slice_fusion.6.refs_2_), custom_call_target="tpu_custom_call" | custom-call | tf_op jit(solution)/shard_map/start/pallas_call | solution.py:419
  187.3 5.7 fusion.99
  217.8 6.4 while.34
  227.6 7.6 fusion.46
  241.0 3.6 multiply_reduce_fusion.9
  244.6 5.3 psum.14
  250.5 3.6 convert_add_fusion
  260.7 4.7 convolution_convert_fusion.4
  267.2 95.3 %middle.1 = (bf16[4096,1536]{1,0:T(8,128)(2,1)}, f32[128,1536]{1,0:T(8,128)}) custom-call(bf16[4,128,1536]{2,1,0:T(8,128)(2,1)} %bitcast.231, bf16[128,1536]{1,0:T(8,128)(2,1)} %constant_dynamic-slice_fusion.5.x_ref.refs_2_, f32[1,1536]{1,0:T(1,128)} %reshape.331.gain_ref), custom_call_target="tpu_custom_call" | custom-call | tf_op jit(solution)/shard_map/middle/pallas_call | solution.py:359
  363.5 59.1 %experts.1 = (bf16[4096,1536]{1,0:T(8,128)(2,1)}, bf16[4096,1536]{1,0:T(8,128)(2,1)}, f32[24576,128]{1,0:T(8,128)}, f32[8,128,1536]{2,1,0:T(8,128)}) custom-call(s32[8,8,512]{2,1,0:T(8,128)} %fusion.78.pos_ref, f32[8,8,512]{2,1,0:T(8,128)} %bitcast.250, bf16[4096,1536]{1,0:T(8,128)(2,1)} %get-tuple-element.223.x_ref, ...), custom_call_target="tpu_custom_call" | custom-call | flops 40265318400 | bytes 88080384 | tf_op jit(solution)/shard_map/experts/pallas_call | solution.py:836
  430.2 77.3 %scatter_rows.1 = f32[128,1536]{1,0:T(8,128)} custom-call(bf16[4096,1536]{1,0:T(8,128)(2,1)} %fusion.29.p_ref), custom_call_target="tpu_custom_call" | custom-call | tf_op jit(solution)/shard_map/scatter_rows/pallas_call | solution.py:544
  507.6 4.2 fusion.31.p_ref
  514.6 91.9 %turn.1 = (f32[128,1536]{1,0:T(8,128)}, f32[1,1536]{1,0:T(1,128)}, bf16[4,128,1536]{2,1,0:T(8,128)(2,1)}) custom-call(bf16[4096,1536]{1,0:T(8,128)(2,1)} %fusion.31.p_ref, f32[128,1536]{1,0:T(8,128)} %get-tuple-element.221.hidden_ref, bf16[128,1536]{1,0:T(8,128)(2,1)} %constant_dynamic-slice_fusion.4.g2_ref, f32[1,1536]{1,0:T(1,128)} %reshape.331.gain_ref), custom_call_target="tpu_custom_call" | custom-call | tf_op jit(solution)/shard_map/turn/pallas_call | solution.py:581
  606.5 5.8 multiply_reduce_fusion.2
  612.2 5.1 psum.15
  617.3 5.1 multiply_reduce_fusion.1
  625.5 3.2 reshape.335
  633.4 4.3 copy.339
  642.9 11.3 %while.35 = (s32[]{:T(128)}, f32[12,128,64]{2,1,0:T(8,128)S(1)}, f32[2,12]{1,0:T(2,128)}, f32[2,12,128,64]{3,2,1,0:T(8,128)}, f32[2,12,128,64]{2,3,1,0:T(8,128)}...) while((s32[]{:T(128)}, f32[12,128,64]{2,1,0:T(8,128)S(1)}, ...), condition=%wide.region_12.13_spmd.clone, body=%wide.region_10.12_spmd.clone.sunk | while | flops 589816 | bytes 4326632 | solution.py:73
  657.3 5.5 bitcast_add_fusion.2
  673.8 10.1 %fusion.14 = (f32[2,256,12]{1,2,0:T(8,128)S(1)}, f32[2,256,12]{1,2,0:T(8,128)S(1)}, f32[2,256,256]{2,1,0:T(8,128)}) fusion(f32[2,256,12]{1,2,0:T(8,128)S(1)} %bitcast.245, f32[2,256,256]{2,1,0:T(8,128)S(1)} %copy-done.41, pred[256,256]{1,0:T(8,128)(4,1)S(1)} %copy-done.56, f32[2,256,12,64]{1,0,3,2:T(2,128)S(1)} %copy-done.1, ...), kind=kOutput, calls=%fused_computation.28 | convolution fusion | flops 1225510912 | bytes 4358144 | tf_op jit(solution)/shard_map/transpose(jvp(kij,kijh,kjhp->kihp))/dot_general | solution.py:64
  684.0 5.0 reduce-window.16
  690.1 7.2 multiply_reduce_fusion.5
  698.1 4.8 convolution_convert_fusion.1
  707.7 6.6 fusion.70
  714.3 5.1 fusion.73
  726.4 3.5 concatenate.60
  731.4 7.3 convolution_convert_fusion
  738.7 7.3 convolution_convert_fusion.3
  747.1 32.4 %reduce-scatter.5.cloned.1.call-done = bf16[192,768]{1,0:T(8,128)(2,1)} async-done(((bf16[1536,768]{1,0:T(8,128)(2,1)}), bf16[192,768]{1,0:T(8,128)(2,1)}) %reduce-scatter.5.cloned.1.call-update) | async-done | bytes 294928 | tf_op jit(solution)/shard_map/reduce_scatter | solution.py:1029
  779.5 152.3 %tail.1 = (bf16[4,128,1536]{2,1,0:T(8,128)(2,1)}, f32[16,1536]{1,0:T(8,128)}, f32[2,96,1920]{2,1,0:T(8,128)}) custom-call(bf16[4,128,1536]{2,1,0:T(8,128)(2,1)} %bitcast.232, f32[128,1536]{1,0:T(8,128)} %get-tuple-element.233.refs_1_, bf16[128,1536]{1,0:T(8,128)(2,1)} %constant_dynamic-slice_fusion.5.x_ref.refs_2_, f32[1,1536]{1,0:T(1,128)} %broadcast_in_dim.124.refs_3_, ...), custom_call_target="tpu_custom_call" | custom-call | tf_op jit(solution)/shard_map/tail/pallas_call | solution.py:732
  937.7 3.5 bitcast_convert_fusion
  (407 shorter events, 143.7 us)
Async XLA Ops:
  7.2 415.4 %all-gather.3.cloned.1.call-start = ((), (), s32[]{:S(2)}) async-start(), calls=%async_computation.2 | async-start | bytes 2654208 | tf_op jit(solution)/shard_map/all_gather | solution.py:956
  10.7 5.7 copy-start.45
  11.9 5.4 copy-start.32
  18.2 168.7 %copy-start.3 = (bf16[512,1536]{1,0:T(8,128)(2,1)}, bf16[512,1536]{1,0:T(8,128)(2,1)S(1)}, u32[]{:S(2)}) copy-start(bf16[512,1536]{1,0:T(8,128)(2,1)S(1)} %multiply_convert_fusion) | copy-start | bytes 4718596
  21.4 165.6 %copy-start.26 = (bf16[512,1536]{1,0:T(8,128)(2,1)S(1)}, bf16[512,1536]{1,0:T(8,128)(2,1)}, u32[]{:S(2)}) copy-start(bf16[512,1536]{1,0:T(8,128)(2,1)} %param.27) | copy-start | bytes 4718596
  23.5 163.9 %copy-start.75 = (f32[1536]{0:T(1024)S(1)}, f32[1536]{0:T(1024)}, u32[]{:S(2)}) copy-start(f32[1536]{0:T(1024)} %param.31) | copy-start | bytes 18436
  186.8 559.1 %all-gather.5.cloned.1.call-start = ((), (), s32[]{:S(2)}) async-start(), calls=%async_computation.3 | async-start | bytes 1966080 | tf_op jit(solution)/shard_map/all_gather | solution.py:1020
  187.3 5.7 copy-start.88
  194.6 9.8 %copy-start.7 = (f32[512,768]{1,0:T(8,128)}, f32[512,768]{1,0:T(8,128)S(1)}, u32[]{:S(2)}) copy-start(f32[512,768]{1,0:T(8,128)S(1)} %slice.209) | copy-start | bytes 4718596
  194.6 5.2 copy-start.82
  194.6 5.2 copy-start.94
  195.2 18.0 %copy-start.16 = (f32[512,12]{1,0:T(8,128)}, f32[512,12]{1,0:T(8,128)S(1)}, u32[]{:S(2)}) copy-start(f32[512,12]{1,0:T(8,128)S(1)} %get-tuple-element.549) | copy-start | bytes 73732
  203.5 10.4 %copy-start.20 = (bf16[512,128]{1,0:T(8,128)(2,1)}, bf16[512,128]{1,0:T(8,128)(2,1)S(1)}, u32[]{:S(2)}) copy-start(bf16[512,128]{1,0:T(8,128)(2,1)S(1)} %get-tuple-element.566) | copy-start | bytes 393220
  227.3 7.9 copy-start.12
  227.6 7.7 copy-start.39
  241.0 8.9 copy-start.74
  249.9 367.4 %copy-start.77 = (f32[512]{0:T(512)}, f32[512]{0:T(512)S(1)}, u32[]{:S(2)}) copy-start(f32[512]{0:T(512)S(1)} %get-tuple-element.581) | copy-start | bytes 6148
  256.3 106.3 %copy-start.53 = (f32[4096,8]{0,1:T(8,128)}, f32[4096,8]{0,1:T(8,128)S(1)}, u32[]{:S(2)}) copy-start(f32[4096,8]{0,1:T(8,128)S(1)} %copy.277) | copy-start | bytes 393220
  426.4 81.1 %copy-start.99 = (bf16[512,256]{1,0:T(8,128)(2,1)}, bf16[512,256]{1,0:T(8,128)(2,1)S(1)}, u32[]{:S(2)}) copy-start(bf16[512,256]{1,0:T(8,128)(2,1)S(1)} %get-tuple-element.557) | copy-start | bytes 786436
  426.4 81.1 %copy-start.101 = (bf16[512,256]{1,0:T(8,128)(2,1)}, bf16[512,256]{1,0:T(8,128)(2,1)S(1)}, u32[]{:S(2)}) copy-start(bf16[512,256]{1,0:T(8,128)(2,1)S(1)} %get-tuple-element.558) | copy-start | bytes 786436
  512.6 233.4 %reduce-scatter.7.cloned.1.call-start = ((), (), s32[]{:S(2)}) async-start(), calls=%async_computation.5 | async-start | bytes 2654208
  640.9 138.6 %reduce-scatter.5.cloned.1.call-start = ((), (), s32[]{:S(2)}) async-start(), calls=%async_computation.4 | async-start | bytes 2654208 | tf_op jit(solution)/shard_map/reduce_scatter | solution.py:1029
  690.1 7.2 copy-start.63
  690.1 8.0 copy-start.78
  690.1 8.0 copy-start.81
  707.7 6.7 copy-start.9
  714.3 5.2 copy-start.22
  714.3 5.2 copy-start.29
  714.3 5.6 copy-start.19
  726.4 5.0 copy-start.76
  731.4 7.3 copy-start.30
  942.9 5.0 copy-start.31
  (79 other events, 198.3 us)
Sparse Core Ops, SparseCore 0:
  187.0 70.1 all-gather.2
  512.7 28.0 all-gather.4
  641.0 66.4 reduce-scatter.6
  711.5 67.9 reduce-scatter.4

commit v7 on v6

--- a/solution.py
+++ b/solution.py
@@ -300,13 +300,12 @@
             send_sem.at[h, r], recv_sem.at[h, r], device(hi, lo, th, 1 - tl),
         )
 
-    for k in range(1, n_hi):
-        for h in range(2):
-            push(h, 0, 0, 0, 0, k)
     for k in range(n_hi):
         for h in range(2):
             if k:
                 got(h, k, 0, 0, 0)
+            if k < n_hi - 1:
+                push(h, 0, 0, 0, 0, k + 1)
             for step in ("f", "s", "c"):
                 push(h, k, 0, 0, 0, step)
         yield
@@ -372,43 +371,73 @@
     )(part.reshape(4, rows, width), x_piece, gain.reshape(1, width))
 
 
-def weight_steps(n_hi, w_ref, o_ref, own_sem, send_h, recv_h, send_f, recv_f):
+def weight_steps(n_hi, w_ref, o_ref, own_sem, send_b, recv_b, send_a, recv_a, send_f, recv_f):
     hi, lo, th, tl = place()
     to_f = device(hi, 1 - lo, th, tl)
-    sends = Sends()
-
-    def at(k, l):
-        return peer(hi, k, n_hi) * 2 + l
+    above = device(lax.rem(hi + 1, n_hi), lo, th, tl)
+    below = device(lax.rem(hi + n_hi - 1, n_hi), lo, th, tl)
+    sends = []
+
+    def push(cond, src, at, h, ssem, rsem, to):
+        copy = remote(src, o_ref.at[at, h], ssem, rsem, to)
+        sends.append((cond, copy))
+        if cond is None:
+            copy.start()
+        else:
+            pl.when(cond)(copy.start)
+
+    def block(j, l):
+        return lax.rem(hi + j + n_hi, n_hi) * 2 + l
 
     for h in range(2):
-        for k in range(1, n_hi):
-            sends.push(
-                w_ref.at[h], o_ref.at[at(0, lo), h], send_h.at[h, k - 1], recv_h.at[h, back(k, n_hi) - 1],
-                device(peer(hi, k, n_hi), lo, th, tl),
-            )
-        sends.push(w_ref.at[h], o_ref.at[at(0, lo), h], send_f.at[h, 0], recv_f.at[h, 0], to_f)
-    own = pltpu.make_async_copy(w_ref, o_ref.at[at(0, lo)], own_sem)
+        at = block(0, lo)
+        push(hi < n_hi - 1, w_ref.at[h], at, h, send_b.at[h, 0], recv_b.at[h, 0], above)
+        push(hi > 0, w_ref.at[h], at, h, send_a.at[h, 0], recv_a.at[h, 0], below)
+        push(None, w_ref.at[h], at, h, send_f.at[h, 0], recv_f.at[h, 0], to_f)
+    own = pltpu.make_async_copy(w_ref, o_ref.at[block(0, lo)], own_sem)
     own.start()
     yield
-    for k in range(1, n_hi):
+    for j in range(1, n_hi):
         for h in range(2):
-            view = o_ref.at[at(k, lo), h]
-            arrive(view, send_h.at[h, k - 1], recv_h.at[h, k - 1], to_f)
-            sends.push(view, view, send_f.at[h, k], recv_f.at[h, k], to_f)
+            for down in (0, 1):
+                valid = hi + j < n_hi if down else hi - j >= 0
+                at = block(j if down else -j, lo)
+                view = o_ref.at[at, h]
+                sem = (send_a if down else send_b).at[h, j - 1], (recv_a if down else recv_b).at[h, j - 1]
+                pl.when(valid)(remote(view, view, *sem, to_f).wait_recv)
+                if j < n_hi - 1:
+                    on = jnp.logical_and(valid, hi > 0 if down else hi < n_hi - 1)
+                    push(
+                        on, view, at, h, (send_a if down else send_b).at[h, j],
+                        (recv_a if down else recv_b).at[h, j], below if down else above,
+                    )
+                f = 1 + down * (n_hi - 1) + j - 1
+                push(valid, view, at, h, send_f.at[h, f], recv_f.at[h, f], to_f)
         yield
-    for k in range(n_hi):
+    for h in range(2):
+        view = o_ref.at[block(0, 1 - lo), h]
+        arrive(view, send_f.at[h, 0], recv_f.at[h, 0], to_f)
+    for j in range(1, n_hi):
         for h in range(2):
-            arrive(o_ref.at[at(k, 1 - lo), h], send_f.at[h, k], recv_f.at[h, k], to_f)
+            for down in (0, 1):
+                valid = hi + j < n_hi if down else hi - j >= 0
+                view = o_ref.at[block(j if down else -j, 1 - lo), h]
+                f = 1 + down * (n_hi - 1) + j - 1
+                pl.when(valid)(remote(view, view, send_f.at[h, f], recv_f.at[h, f], to_f).wait_recv)
     own.wait()
-    sends.finish()
+    for cond, copy in sends:
+        if cond is None:
+            copy.wait_send()
+        else:
+            pl.when(cond)(copy.wait_send)
 
 
 def start_kernel(n_hi, n, *refs):
     ins, outs, sems = refs[: n + 1], refs[n + 1 : 2 * n + 2], refs[2 * n + 2 :]
     greet(n_hi)
     streams = [
-        weight_steps(n_hi, ins[i], outs[i], *sems[5 * i : 5 * i + 5]) for i in range(n)
-    ] + [gather_steps(n_hi, ins[n], outs[n], *sems[5 * n :], lo_first=(True, True))]
+        weight_steps(n_hi, ins[i], outs[i], *sems[7 * i : 7 * i + 7]) for i in range(n)
+    ] + [gather_steps(n_hi, ins[n], outs[n], *sems[7 * n :], lo_first=(True, True))]
     in_turns(*streams)
 
 
@@ -425,7 +454,8 @@
         scratch_shapes=[
             DMA,
             DMA((2, n_hi - 1)), DMA((2, n_hi - 1)),
-            DMA((2, n_hi)), DMA((2, n_hi)),
+            DMA((2, n_hi - 1)), DMA((2, n_hi - 1)),
+            DMA((2, 2 * n_hi - 1)), DMA((2, 2 * n_hi - 1)),
         ] * n + [DMA, DMA((2, 8 * n_hi)), DMA((2, 8 * n_hi))],
         compiler_params=pltpu.CompilerParams(collective_id=collective_id, has_side_effects=True),
         name="start",
@@ -610,22 +640,31 @@
     to_f, to_y, to_c = device(hi, 1 - lo, th, tl), device(hi, lo, 1 - th, tl), device(hi, lo, th, 1 - tl)
     greet(n_hi)
     sends = Sends()
-    order = [(k, h) for k in list(range(1, n_hi)) + [0] for h in range(2)]
+    order = [(k, h) for k in reversed(range(n_hi)) for h in range(2)]
+    events = [(w, k, h) for w in range(n) for k, h in order]
+    events = [e for e in events if e[1]] + [e for e in events if not e[1]]
 
     def owner(k, l):
         return peer(hi, k, n_hi) * 2 + l
 
-    for w_ref, (stage, from_f, from_h, stage_sem, send_f, recv_f, send_h, recv_h) in zip(w_refs, bufs):
-        for k, h in order:
+    def forward(i):
+        if i < len(events):
+            w, k, h = events[i]
+            stage, from_f, from_h, stage_sem, send_f, recv_f, send_h, recv_h = bufs[w]
             sends.push(
-                w_ref.at[owner(k, 1 - lo), h], from_f.at[h, k], send_f.at[h, k], recv_f.at[h, k], to_f
+                w_refs[w].at[owner(k, 1 - lo), h], from_f.at[h, k], send_f.at[h, k], recv_f.at[h, k], to_f
             )
+
+    window = 4
+    for i in range(window):
+        forward(i)
     loads = []
-    for w_ref, (stage, from_f, from_h, stage_sem, send_f, recv_f, send_h, recv_h) in zip(w_refs, bufs):
-        for k, h in order:
-            copy = pltpu.make_async_copy(w_ref.at[owner(k, lo), h], stage.at[h, k], stage_sem.at[h, k])
-            copy.start()
-            loads.append(copy)
+    for w, k, h in events:
+        copy = pltpu.make_async_copy(
+            w_refs[w].at[owner(k, lo), h], bufs[w][0].at[h, k], bufs[w][3].at[h, k]
+        )
+        copy.start()
+        loads.append(copy)
     tensor_sum_start(sends, part_ref, got_c, t_send, t_recv)
     tensor_sum_middle(sends, part_ref, got_c, got_y, t_send, t_recv)
     grad = tensor_sum_end(part_ref, got_c, got_y, t_send, t_recv)
@@ -641,13 +680,13 @@
     small[0:1, :] = jnp.sum(grad * x * scale, axis=0, keepdims=True)
     sends.push(small, small_f, sm_send.at[0], sm_recv.at[0], to_f)
 
-    events = [(w, k, h) for w in range(n) for k, h in order]
     for i, (w, k, h) in enumerate(events):
         if k == 0:
-            continue
+            break
         stage, from_f, from_h, stage_sem, send_f, recv_f, send_h, recv_h = bufs[w]
         loads[i].wait()
         arrive(from_f.at[h, k], send_f.at[h, k], recv_f.at[h, k], to_c)
+        forward(i + window)
         from_f[h, k] = (stage[h, k].astype(F32) + from_f[h, k].astype(F32)).astype(from_f.dtype)
         j = back(k, n_hi) - 1
         sends.push(
@@ -674,6 +713,7 @@
     for i, (w, k, h) in enumerate(events):
         if k:
             continue
+        forward(i + window)
         stage, from_f, from_h, stage_sem, send_f, recv_f, send_h, recv_h = bufs[w]
         loads[i].wait()
         arrive(from_f.at[h, 0], send_f.at[h, 0], recv_f.at[h, 0], to_c)
@@ -1026,7 +1066,6 @@
     grad_shared_w = jnp.concatenate([grad_shared_gu, grad_shared_down], axis=1).astype(BF)
     grad_shared_w = lax.psum_scatter(grad_shared_w, "dp", scatter_dimension=0, tiled=True)
     grad_out_w = dotf("td,tc->dc", dm, normed_mix).astype(BF)
-    grad_out_w = lax.psum_scatter(grad_out_w, "dp", scatter_dimension=0, tiled=True)
     grad_normed_mix = dotf("td,dc->tc", dm, proj_out)
     weighted_mix = gnorm_gain * grad_normed_mix
     grad_gnorm = jnp.sum(grad_normed_mix * gated_mix * scale_mix, axis=0)
@@ -1065,11 +1104,9 @@
     narrow = lanes(
         grad_conv_x, grad_conv_x_bias, grad_gnorm, grad_dt_bias, grad_a_log, grad_d_skip
     )
-    grad_first_w, grad_out_w, grad_shared_w = lax.optimization_barrier(
-        (grad_first_w, grad_out_w, grad_shared_w)
-    )
-    grad_x, sums, (first_f,) = tail(
-        [grad_first_w],
+    grad_first_w, grad_shared_w = lax.optimization_barrier((grad_first_w, grad_shared_w))
+    grad_x, sums, (first_f, grad_out_w) = tail(
+        [grad_first_w, grad_out_w],
         grad_input_part,
         grad_one,
         x_piece,
@@ -1120,7 +1157,7 @@
         o_a_log,
         o_d_skip,
         o_gnorm,
-        grad_out_w.astype(F32),
+        grad_out_w,
         o_ln2,
         shared_f[:, : 2 * n_sh].reshape(rows, 2, n_sh),
         shared_f[:, 2 * n_sh :],

time: 966 us -> 904 us (0.936)
  Pallas kernels: 639 us -> 580 us
    pallas_call x1, Pallas kernels: 152 us -> 117 us  [tail(): pl.pallas_call(functools.partial(tail_kernel, n_hi, wide, bc_at, n), out_...]
    reduce_scatter x1 -> x0, waiting for transfers between devices: 32.4 us -> none  [local(): lax.psum_scatter(grad_out_w, 'dp', scatter_dimension=0, tiled=True)]
    unnamed x5 -> x4, waiting for transfers between devices: 0.07 us -> 27.8 us
    pallas_call x1, Pallas kernels: 95.3 us -> 76.8 us  [middle(): pl.pallas_call(functools.partial(middle_kernel, n_hi), out_shape=(jax.Sha...]
  transfers between devices with their start and end apart: 4 -> 3, of which waited for: 1 -> 1; matrix products, arithmetic and copies ran while one was open for 22% -> 20% of each run, Pallas kernels for 26% -> 15%
where the time goes in v7:
time: 904 us; the launch traced here: 890 us
  Pallas kernels  580 us (64%)
  local copies, waits for them, and re-layouts  94.1 us (10%)
  matrix products  93.9 us (10%)
  other arithmetic  66.4 us (7%)
  waiting for transfers between devices  27.8 us (3%)
  between operations  16.4 us (2%)
  blocking collectives  11 us (1%)
    pallas_call x1, Pallas kernels, start(): pl.pallas_call(functools.partial(start_kernel, n_hi, n), out_shape=[jax.S...  159 us
    pallas_call x1, Pallas kernels, tail(): pl.pallas_call(functools.partial(tail_kernel, n_hi, wide, bc_at, n), out_...  117 us
    pallas_call x1, Pallas kernels, turn(): pl.pallas_call(functools.partial(turn_kernel, n_hi), out_shape=(jax.Shape...  91.6 us
    pallas_call x1, Pallas kernels, middle(): pl.pallas_call(functools.partial(middle_kernel, n_hi), out_shape=(jax.Sha...  76.8 us
    pallas_call x1, Pallas kernels, scatter_rows(): pl.pallas_call(functools.partial(scatter_kernel, n_hi), out_shape=jax.Sha...  76.8 us
    pallas_call x1, Pallas kernels, experts(): pl.pallas_call(functools.partial(experts_kernel, n_dp, n_local, cap, chun...  58.9 us
    dot_general x13, matrix products, dotf(): return jnp.einsum(spec, a, b, preferred_element_type=F32)  45.7 us
    unnamed x4, waiting for transfers between devices  27.8 us
  transfers between devices with their start and end apart: 3, of which 1 were waited for; matrix products, arithmetic and copies ran while one was open for 20% of the time, Pallas kernels for 15%

profile of v7, /device:TPU:9, one launch (start us, length us, event | category | flops | bytes accessed | tf_op | source)
XLA Modules:
  0.0 890.5 jit_solution(15024546292947503305)
XLA Ops:
  23.4 159.1 %start.1 = (bf16[8,2,96,1920]{3,2,1,0:T(8,128)(2,1)}, bf16[8,2,96,768]{3,2,1,0:T(8,128)(2,1)}, bf16[4096,1664]{1,0:T(8,128)(2,1)}) custom-call(bf16[2,96,1920]{2,1,0:T(8,128)(2,1)} %concatenate.54.refs_0_, bf16[2,96,768]{2,1,0:T(8,128)(2,1)} %bitcast.239, bf16[128,1664]{1,0:T(8,128)(2,1)} %constant_dynamic-slice_fusion.6.refs_2_), custom_call_target="tpu_custom_call" | custom-call | tf_op jit(solution)/shard_map/start/pallas_call | solution.py:448
  183.1 5.7 fusion.99
  215.4 6.4 while.34
  225.3 7.6 fusion.46
  238.6 3.6 multiply_reduce_fusion.9
  242.3 5.5 psum.14
  248.4 3.7 convert_add_fusion
  258.6 4.7 convolution_convert_fusion.4
  263.4 76.8 %middle.1 = (bf16[4096,1536]{1,0:T(8,128)(2,1)}, f32[128,1536]{1,0:T(8,128)}) custom-call(bf16[4,128,1536]{2,1,0:T(8,128)(2,1)} %bitcast.234, bf16[128,1536]{1,0:T(8,128)(2,1)} %constant_dynamic-slice_fusion.5.x_ref.refs_2_, f32[1,1536]{1,0:T(1,128)} %reshape.337.gain_ref), custom_call_target="tpu_custom_call" | custom-call | tf_op jit(solution)/shard_map/middle/pallas_call | solution.py:358
  342.9 58.9 %experts.1 = (bf16[4096,1536]{1,0:T(8,128)(2,1)}, bf16[4096,1536]{1,0:T(8,128)(2,1)}, f32[24576,128]{1,0:T(8,128)}, f32[8,128,1536]{2,1,0:T(8,128)}) custom-call(s32[8,8,512]{2,1,0:T(8,128)} %fusion.78.pos_ref, f32[8,8,512]{2,1,0:T(8,128)} %bitcast.254, bf16[4096,1536]{1,0:T(8,128)(2,1)} %get-tuple-element.223.x_ref, ...), custom_call_target="tpu_custom_call" | custom-call | flops 40265318400 | bytes 88080384 | tf_op jit(solution)/shard_map/experts/pallas_call | solution.py:876
  409.5 76.8 %scatter_rows.1 = f32[128,1536]{1,0:T(8,128)} custom-call(bf16[4096,1536]{1,0:T(8,128)(2,1)} %fusion.29.p_ref), custom_call_target="tpu_custom_call" | custom-call | tf_op jit(solution)/shard_map/scatter_rows/pallas_call | solution.py:574
  486.3 4.1 fusion.31.p_ref
  490.4 91.6 %turn.1 = (f32[128,1536]{1,0:T(8,128)}, f32[1,1536]{1,0:T(1,128)}, bf16[4,128,1536]{2,1,0:T(8,128)(2,1)}) custom-call(bf16[4096,1536]{1,0:T(8,128)(2,1)} %fusion.31.p_ref, f32[128,1536]{1,0:T(8,128)} %get-tuple-element.221.hidden_ref, bf16[128,1536]{1,0:T(8,128)(2,1)} %constant_dynamic-slice_fusion.4.g2_ref, f32[1,1536]{1,0:T(1,128)} %reshape.337.gain_ref), custom_call_target="tpu_custom_call" | custom-call | tf_op jit(solution)/shard_map/turn/pallas_call | solution.py:611
  582.0 5.8 multiply_reduce_fusion.2
  587.7 5.5 psum.15
  593.2 5.1 multiply_reduce_fusion.1
  604.4 3.3 fusion.67
  612.9 10.9 %while.35 = (s32[]{:T(128)}, f32[12,128,64]{2,1,0:T(8,128)S(1)}, f32[2,12]{1,0:T(2,128)}, f32[2,12,128,64]{3,2,1,0:T(8,128)}, f32[2,12,128,64]{2,3,1,0:T(8,128)}...) while((s32[]{:T(128)}, f32[12,128,64]{2,1,0:T(8,128)S(1)}, ...), condition=%wide.region_12.13_spmd.clone, body=%wide.region_10.12_spmd.clone.sunk | while | flops 589816 | bytes 4326632 | solution.py:73
  627.0 10.1 %fusion.14 = (f32[2,256,12]{1,2,0:T(8,128)S(1)}, f32[2,256,12]{1,2,0:T(8,128)S(1)}, f32[2,256,256]{2,1,0:T(8,128)}) fusion(f32[2,256,12]{1,2,0:T(8,128)S(1)} %bitcast.248, f32[2,256,256]{2,1,0:T(8,128)S(1)} %copy-done.42, pred[256,256]{1,0:T(8,128)(4,1)S(1)} %copy-done.57, f32[2,256,12,64]{1,0,3,2:T(2,128)S(1)} %copy-done.1, ...), kind=kOutput, calls=%fused_computation.28 | convolution fusion | flops 1225510912 | bytes 4358144 | tf_op jit(solution)/shard_map/transpose(jvp(kij,kijh,kjhp->kihp))/dot_general | solution.py:64
  637.1 5.5 bitcast_add_fusion.2
  653.7 5.2 reduce-window.16
  660.0 7.1 multiply_reduce_fusion.5
  671.9 4.4 copy.339
  680.2 6.6 fusion.70
  686.9 5.1 fusion.73
  699.0 3.4 concatenate.60
  704.0 4.5 convolution_convert_fusion.1
  708.5 5.5 convolution_convert_fusion
  714.0 4.6 convolution_convert_fusion.3
  718.5 27.8 %reduce-scatter.4.cloned.1.call-done = bf16[192,768]{1,0:T(8,128)(2,1)} async-done(((bf16[1536,768]{1,0:T(8,128)(2,1)}), bf16[192,768]{1,0:T(8,128)(2,1)}) %reduce-scatter.4.cloned.1.call-update) | async-done | bytes 294928
  747.5 117.2 %tail.1 = (bf16[4,128,1536]{2,1,0:T(8,128)(2,1)}, f32[16,1536]{1,0:T(8,128)}, f32[2,96,1920]{2,1,0:T(8,128)}, f32[2,96,768]{2,1,0:T(8,128)}) custom-call(bf16[4,128,1536]{2,1,0:T(8,128)(2,1)} %bitcast.235, f32[128,1536]{1,0:T(8,128)} %get-tuple-element.233.refs_1_, bf16[128,1536]{1,0:T(8,128)(2,1)} %constant_dynamic-slice_fusion.5.x_ref.refs_2_, ...), custom_call_target="tpu_custom_call" | custom-call | tf_op jit(solution)/shard_map/tail/pallas_call | solution.py:772
  870.5 3.5 bitcast_convert_fusion
  (413 shorter events, 145.7 us)
Async XLA Ops:
  7.2 394.7 %all-gather.3.cloned.1.call-start = ((), (), s32[]{:S(2)}) async-start(), calls=%async_computation.1 | async-start | bytes 2654208 | tf_op jit(solution)/shard_map/all_gather | solution.py:996
  10.7 5.7 copy-start.46
  11.9 5.4 copy-start.33
  18.2 164.4 %copy-start.4 = (bf16[512,1536]{1,0:T(8,128)(2,1)}, bf16[512,1536]{1,0:T(8,128)(2,1)S(1)}, u32[]{:S(2)}) copy-start(bf16[512,1536]{1,0:T(8,128)(2,1)S(1)} %multiply_convert_fusion) | copy-start | bytes 4718596
  21.3 161.3 %copy-start.28 = (bf16[512,1536]{1,0:T(8,128)(2,1)S(1)}, bf16[512,1536]{1,0:T(8,128)(2,1)}, u32[]{:S(2)}) copy-start(bf16[512,1536]{1,0:T(8,128)(2,1)} %param.27) | copy-start | bytes 4718596
  23.4 159.6 %copy-start.76 = (f32[1536]{0:T(1024)S(1)}, f32[1536]{0:T(1024)}, u32[]{:S(2)}) copy-start(f32[1536]{0:T(1024)} %param.31) | copy-start | bytes 18436
  182.6 536.0 %all-gather.5.cloned.1.call-start = ((), (), s32[]{:S(2)}) async-start(), calls=%async_computation.2 | async-start | bytes 1966080 | tf_op jit(solution)/shard_map/all_gather | solution.py:1060
  183.0 5.7 copy-start.90
  190.3 11.6 %copy-start.8 = (f32[512,768]{1,0:T(8,128)}, f32[512,768]{1,0:T(8,128)S(1)}, u32[]{:S(2)}) copy-start(f32[512,768]{1,0:T(8,128)S(1)} %slice.209) | copy-start | bytes 4718596
  190.3 7.0 copy-start.83
  190.3 7.0 copy-start.96
  190.8 5.8 copy-start.87
  191.0 19.8 %copy-start.18 = (f32[512,12]{1,0:T(8,128)}, f32[512,12]{1,0:T(8,128)S(1)}, u32[]{:S(2)}) copy-start(f32[512,12]{1,0:T(8,128)S(1)} %get-tuple-element.549) | copy-start | bytes 73732
  201.0 10.5 %copy-start.22 = (bf16[512,128]{1,0:T(8,128)(2,1)}, bf16[512,128]{1,0:T(8,128)(2,1)S(1)}, u32[]{:S(2)}) copy-start(bf16[512,128]{1,0:T(8,128)(2,1)S(1)} %get-tuple-element.566) | copy-start | bytes 393220
  225.0 7.9 copy-start.12
  225.2 7.7 copy-start.41
  238.6 9.1 %copy-start.75 = (f32[1536]{0:T(1024)S(1)}, f32[1536]{0:T(1024)}, u32[]{:S(2)}) copy-start(f32[1536]{0:T(1024)} %param.44) | copy-start | bytes 18436
  247.8 345.4 %copy-start.78 = (f32[512]{0:T(512)}, f32[512]{0:T(512)S(1)}, u32[]{:S(2)}) copy-start(f32[512]{0:T(512)S(1)} %get-tuple-element.581) | copy-start | bytes 6148
  254.2 86.0 %copy-start.54 = (f32[4096,8]{0,1:T(8,128)}, f32[4096,8]{0,1:T(8,128)S(1)}, u32[]{:S(2)}) copy-start(f32[4096,8]{0,1:T(8,128)S(1)} %copy.277) | copy-start | bytes 393220
  405.6 80.6 %copy-start.101 = (bf16[512,256]{1,0:T(8,128)(2,1)}, bf16[512,256]{1,0:T(8,128)(2,1)S(1)}, u32[]{:S(2)}) copy-start(bf16[512,256]{1,0:T(8,128)(2,1)S(1)} %get-tuple-element.557) | copy-start | bytes 786436
  405.6 80.6 %copy-start.103 = (bf16[512,256]{1,0:T(8,128)(2,1)}, bf16[512,256]{1,0:T(8,128)(2,1)S(1)}, u32[]{:S(2)}) copy-start(bf16[512,256]{1,0:T(8,128)(2,1)S(1)} %get-tuple-element.558) | copy-start | bytes 786436
  611.0 135.3 %reduce-scatter.4.cloned.1.call-start = ((), (), s32[]{:S(2)}) async-start(), calls=%async_computation.3 | async-start | bytes 2654208
  627.0 10.1 %copy-start.35 = (f32[2,256,12]{1,2,0:T(8,128)S(1)}, f32[2,256,12]{1,2,0:T(8,128)}, u32[]{:S(2)}) copy-start(f32[2,256,12]{1,2,0:T(8,128)} %get-tuple-element.575) | copy-start | bytes 73732
  660.0 7.1 copy-start.102
  660.0 7.1 copy-start.104
  671.9 6.8 copy-start.100
  680.2 6.7 copy-start.9
  686.8 5.2 copy-start.24
  686.8 5.2 copy-start.31
  686.9 5.6 copy-start.21
  704.0 10.0 %slice-start = ((s8[5898240]{0:T(1024)(128)(4,1)}), s8[4194304]{0:T(1024)(128)(4,1)S(1)}, s32[]{:S(2)}) async-start(s8[5898240]{0:T(1024)(128)(4,1)} %bitcast.273), calls=%async_computation.4 | async-start | bytes 8388608
  708.5 5.5 slice-start.1
  (82 other events, 212.6 us)
Sparse Core Ops, SparseCore 0:
  182.7 47.7 all-gather.2
  611.1 20.2 all-gather.4
  678.9 67.3 reduce-scatter.3

commit v8 on v7

--- a/solution.py
+++ b/solution.py
@@ -25,120 +25,8 @@
     return (values * sigmoid_val, sigmoid_val * (1.0 + values * (1.0 - sigmoid_val)))
 
 
-def round_keep(values):
-    return lax.optimization_barrier(values.astype(BF)).astype(F32)
-
-
 def dotf(spec, a, b):
     return jnp.einsum(spec, a, b, preferred_element_type=F32)
-
-
-def causal_conv(signal, kernel, offset):
-    kernel_width = kernel.shape[0]
-    seq_length = signal.shape[0]
-    padded = jnp.concatenate(
-        [jnp.zeros((kernel_width - 1, signal.shape[1]), signal.dtype), signal], axis=0
-    )
-    summed = offset[None, :] + kernel[0][None, :] * padded[0:seq_length]
-    for tap_index in range(1, kernel_width):
-        summed = summed + kernel[tap_index][None, :] * padded[tap_index : tap_index + seq_length]
-    return summed
-
-
-def ssd_scan(head_values, step_sizes, log_rates, b_rows, c_rows, skip_gain, block_rows):
-    seq_length, n_heads, head_size = head_values.shape
-    n_state = b_rows.shape[1]
-    n_blocks = seq_length // block_rows
-    decay_rates = -jnp.exp(log_rates)[None, :] * step_sizes
-    scaled = (head_values * step_sizes[:, :, None]).reshape(
-        n_blocks, block_rows, n_heads, head_size
-    )
-    cumulative = jnp.cumsum(decay_rates.reshape(n_blocks, block_rows, n_heads), axis=1)
-    b_block = b_rows.reshape(n_blocks, block_rows, n_state)
-    c_block = c_rows.reshape(n_blocks, block_rows, n_state)
-    positions = jnp.arange(block_rows)
-    causal = (positions[:, None] >= positions[None, :])[None, :, :, None]
-    differences = cumulative[:, :, None, :] - cumulative[:, None, :, :]
-    decay_mask = jnp.where(causal, jnp.exp(jnp.where(causal, differences, 0.0)), 0.0)
-    intersection = jnp.einsum("kin,kjn->kij", c_block, b_block, precision=HIGHEST)
-    within = jnp.einsum("kij,kijh,kjhp->kihp", intersection, decay_mask, scaled, precision=HIGHEST)
-    block_end = cumulative[:, -1, :]
-    to_end = jnp.exp(block_end[:, None, :] - cumulative)
-    states = jnp.einsum("kjn,kjh,kjhp->khnp", b_block, to_end, scaled, precision=HIGHEST)
-
-    def carry_state(previous, inputs):
-        block_decay, block_state = inputs
-        return (block_decay[:, None, None] * previous + block_state, previous)
-
-    final_state, entering = lax.scan(
-        carry_state,
-        jnp.zeros((n_heads, n_state, head_size), head_values.dtype),
-        (jnp.exp(block_end), states),
-    )
-    across = jnp.einsum(
-        "kin,khnp,kih->kihp", c_block, entering, jnp.exp(cumulative), precision=HIGHEST
-    )
-    return (within + across).reshape(seq_length, n_heads, head_size) + skip_gain[
-        None, :, None
-    ] * head_values
-
-
-def mixer_forward(
-    zx, bc_proj, dt_proj, conv_x, conv_x_bias, conv_bc, conv_bc_bias, dt_bias, a_log, d_skip
-):
-    slots = zx.shape[0]
-    inner = conv_x.shape[1]
-    heads = dt_bias.shape[0]
-    state = conv_bc.shape[1] // 2
-
-    def conv_block(x_part, bc_part, kernel_x, offset_x, kernel_bc, offset_bc):
-        return (
-            jax.nn.silu(causal_conv(x_part, kernel_x, offset_x)),
-            jax.nn.silu(causal_conv(bc_part, kernel_bc, offset_bc)),
-        )
-
-    (conv_values, conv_bc_values), conv_back = jax.vjp(
-        conv_block, zx[:, inner:], bc_proj, conv_x, conv_x_bias, conv_bc, conv_bc_bias
-    )
-    head_input = round_keep(conv_values)
-    bc_input = round_keep(conv_bc_values)
-
-    def scan_block(head_flat, b_rows, c_rows, dt_part, z_part, dt_offset, log_rates, skip_gain):
-        step_sizes = jax.nn.softplus(dt_part + dt_offset[None, :])
-        output = ssd_scan(
-            head_flat.reshape(slots, heads, inner // heads),
-            step_sizes,
-            log_rates,
-            b_rows,
-            c_rows,
-            skip_gain,
-            BLOCK,
-        )
-        return output.reshape(slots, inner) * jax.nn.silu(z_part)
-
-    gated_mix, scan_back = jax.vjp(
-        scan_block,
-        head_input,
-        bc_input[:, :state],
-        bc_input[:, state:],
-        dt_proj,
-        zx[:, :inner],
-        dt_bias,
-        a_log,
-        d_skip,
-    )
-
-    def mixer_back(grad_gated):
-        g_head, g_b, g_c, g_dt, g_z, g_dt_bias, g_a_log, g_d_skip = scan_back(grad_gated)
-        g_xs, g_bc, g_cx, g_cxb, g_cbc, g_cbcb = conv_back(
-            (g_head, jnp.concatenate([g_b, g_c], axis=1))
-        )
-        g_zx = jnp.concatenate([g_z, g_xs], axis=1).astype(BF)
-        return (
-            g_zx, g_bc, g_dt.astype(BF), g_cx, g_cxb, g_cbc, g_cbcb, g_dt_bias, g_a_log, g_d_skip
-        )
-
-    return gated_mix, mixer_back
 
 
 MESH = pl.DeviceIdType.MESH
@@ -922,6 +810,321 @@
     )
 
 
+def conv_pre(pad, values, taps, bias):
+    n = values.shape[0]
+    pad[pl.ds(8, n), :] = values
+    count = taps.shape[0]
+    total = bias + taps[count - 1 : count] * values
+    for k in range(count - 1):
+        total = total + taps[k : k + 1] * pad[pl.ds(8 - (count - 1) + k, n), :]
+    return total
+
+
+def sigmoid(v):
+    return 1.0 / (1.0 + jnp.exp(-v))
+
+
+def dot_exact(a, b):
+    return lax.dot_general(
+        a, b, (((1,), (0,)), ((), ())), precision=HIGHEST, preferred_element_type=F32
+    )
+
+
+def step_parts(first_ref, at, dtb_ref, alog_ref):
+    raw = first_ref[:, at : at + 128] + dtb_ref[...]
+    delta = jnp.maximum(raw, 0.0) + jnp.log(1.0 + jnp.exp(-jnp.abs(raw)))
+    return raw, delta, -jnp.exp(alog_ref[...])
+
+
+def lower_mask():
+    t = lax.broadcasted_iota(jnp.int32, (BLOCK, BLOCK), 0)
+    s = lax.broadcasted_iota(jnp.int32, (BLOCK, BLOCK), 1)
+    return t >= s
+
+
+def by_head(left, a, b):
+    return jnp.where(left, a, b)
+
+
+def mixer_forward_kernel(
+    first_ref, cx_ref, cxb_ref, cbc_ref, cbcb_ref, dtb_ref, alog_ref, skip_ref,
+    y_ref, gated_ref, square_ref, state_ref, pad,
+):
+    slots = first_ref.shape[0]
+    inner = cx_ref.shape[1]
+    n_blocks = slots // BLOCK
+    bc_at = 2 * inner
+    pad[0:8, :] = jnp.zeros((8, 128), F32)
+    mask = lower_mask()
+    tri = mask.astype(F32)
+    left = lax.broadcasted_iota(jnp.int32, (BLOCK, 128), 1) < 64
+    left_row = left[0:1]
+
+    parts = []
+    for c in (0, 128):
+        pre = conv_pre(pad, first_ref[:, bc_at + c : bc_at + c + 128], cbc_ref[:, c : c + 128], cbcb_ref[:, c : c + 128])
+        parts.append((pre * sigmoid(pre)).astype(BF))
+    b_rows, c_rows = parts
+    raw, delta, rate = step_parts(first_ref, bc_at + 256, dtb_ref, alog_ref)
+    blocks = []
+    for b in range(n_blocks):
+        r = slice(b * BLOCK, (b + 1) * BLOCK)
+        d = delta[r]
+        cum = dot_exact(tri, rate * d)
+        blocks.append((d, cum, d.T, cum.T, dot_nt(c_rows[r], b_rows[r])))
+    squares = jnp.zeros((slots, 1), F32)
+    for p in range(inner // 128):
+        lanes = slice(p * 128, (p + 1) * 128)
+        pre = conv_pre(pad, first_ref[:, inner + p * 128 : inner + (p + 1) * 128], cx_ref[:, lanes], cxb_ref[:, lanes])
+        heads_in = (pre * sigmoid(pre)).astype(BF)
+        state = None
+        outs = []
+        for b in range(n_blocks):
+            d, cum, d_t, cum_t, inter = blocks[b]
+            r = slice(b * BLOCK, (b + 1) * BLOCK)
+            x = heads_in[r]
+            ys = []
+            for h in (2 * p, 2 * p + 1):
+                decay = jnp.exp(jnp.where(mask, cum[:, h : h + 1] - cum_t[h : h + 1, :], -1e30))
+                ys.append(dot_mm((inter * decay * d_t[h : h + 1, :]).astype(BF), x))
+            y = by_head(left, ys[0], ys[1]) + skip_ref[:, lanes] * x.astype(F32)
+            cum_p = by_head(left, cum[:, 2 * p : 2 * p + 1], cum[:, 2 * p + 1 : 2 * p + 2])
+            d_p = by_head(left, d[:, 2 * p : 2 * p + 1], d[:, 2 * p + 1 : 2 * p + 2])
+            if state is not None:
+                state_ref[p, b - 1] = state
+                y = y + jnp.exp(cum_p) * dot_mm(c_rows[r], state.astype(BF))
+            if b + 1 < n_blocks:
+                end = cum_p[BLOCK - 1 :]
+                z_rows = x.astype(F32) * d_p * jnp.exp(end - cum_p)
+                fresh = dot_tn(b_rows[r], z_rows.astype(BF))
+                state = fresh if state is None else jnp.exp(end) * state + fresh
+            outs.append(y)
+        y = jnp.concatenate(outs, axis=0)
+        z = first_ref[:, lanes]
+        gated = y * (z * sigmoid(z))
+        y_ref[:, lanes] = y
+        gated_ref[:, lanes] = gated
+        squares = squares + jnp.sum(gated * gated, axis=1, keepdims=True)
+    square_ref[...] = squares
+
+
+def mixer_backward_kernel(
+    full_inner, first_ref, y_ref, gated_ref, dyn_ref, scale_ref, product_ref, gain_ref, state_ref,
+    cx_ref, cxb_ref, cbc_ref, cbcb_ref, dtb_ref, alog_ref, skip_ref,
+    grad_ref, small_ref, pad, after, cols, sums_t,
+):
+    slots = first_ref.shape[0]
+    inner = cx_ref.shape[1]
+    n_blocks = slots // BLOCK
+    bc_at = 2 * inner
+    taps = cx_ref.shape[0]
+    pad[0:8, :] = jnp.zeros((8, 128), F32)
+    after[pl.ds(slots, 8), :] = jnp.zeros((8, 128), F32)
+    small_ref[...] = jnp.zeros_like(small_ref)
+    cols[...] = jnp.zeros_like(cols)
+    sums_t[...] = jnp.zeros_like(sums_t)
+    mask = lower_mask()
+    tri = mask.astype(F32)
+    lane = lax.broadcasted_iota(jnp.int32, (BLOCK, 128), 1)
+    left = lane < 64
+
+    parts, bc_pre = [], []
+    for c in (0, 128):
+        pre = conv_pre(pad, first_ref[:, bc_at + c : bc_at + c + 128], cbc_ref[:, c : c + 128], cbcb_ref[:, c : c + 128])
+        bc_pre.append(pre)
+        parts.append((pre * sigmoid(pre)).astype(BF))
+    b_rows, c_rows = parts
+    raw, delta, rate = step_parts(first_ref, bc_at + 256, dtb_ref, alog_ref)
+    scale = scale_ref[...]
+    cube = scale * scale * scale * product_ref[...] * (1.0 / full_inner)
+    blocks = []
+    for b in range(n_blocks):
+        r = slice(b * BLOCK, (b + 1) * BLOCK)
+        d = delta[r]
+        cum = dot_exact(tri, rate * d)
+        blocks.append((d, cum, d.T, cum.T, dot_nt(c_rows[r], b_rows[r])))
+    grad_inter = [jnp.zeros((BLOCK, BLOCK), F32) for _ in range(n_blocks)]
+    grad_b = [jnp.zeros((BLOCK, 128), F32) for _ in range(n_blocks)]
+    grad_c = [jnp.zeros((BLOCK, 128), F32) for _ in range(n_blocks)]
+
+    def conv_back(grad_out, pre, values, taps_v, row, bias_row, lanes, at):
+        sig = sigmoid(pre)
+        a = grad_out * (sig * (1.0 + pre * (1.0 - sig)))
+        after[pl.ds(0, slots), :] = a
+        pad[pl.ds(8, slots), :] = values
+        total = taps_v[taps - 1 : taps] * a
+        small_ref[row + taps - 1 : row + taps, lanes] = jnp.sum(a * values, axis=0, keepdims=True)
+        for k in range(taps - 1):
+            total = total + taps_v[k : k + 1] * after[pl.ds(taps - 1 - k, slots), :]
+            small_ref[row + k : row + k + 1, lanes] = jnp.sum(
+                a * pad[pl.ds(8 - (taps - 1) + k, slots), :], axis=0, keepdims=True
+            )
+        small_ref[bias_row : bias_row + 1, lanes] = jnp.sum(a, axis=0, keepdims=True)
+        grad_ref[:, at : at + 128] = total.astype(grad_ref.dtype)
+
+    for p in range(inner // 128):
+        lanes = slice(p * 128, (p + 1) * 128)
+        values = first_ref[:, inner + p * 128 : inner + (p + 1) * 128]
+        pre = conv_pre(pad, values, cx_ref[:, lanes], cxb_ref[:, lanes])
+        heads_in = (pre * sigmoid(pre)).astype(BF)
+        z = first_ref[:, lanes]
+        sig = sigmoid(z)
+        grad_gated = scale * gain_ref[:, lanes] * dyn_ref[:, lanes] - gated_ref[:, lanes] * cube
+        grad_y = grad_gated * (z * sig)
+        grad_ref[:, lanes] = (
+            grad_gated * y_ref[:, lanes] * (sig * (1.0 + z * (1.0 - sig)))
+        ).astype(grad_ref.dtype)
+        skip = skip_ref[:, lanes]
+        x_f = heads_in.astype(F32)
+        small_ref[5:6, lanes] = jnp.sum(grad_y * x_f, axis=0, keepdims=True)
+        grad_y_low = grad_y.astype(BF)
+        grad_x = [None] * n_blocks
+        grad_state = None
+        for b in reversed(range(n_blocks)):
+            d, cum, d_t, cum_t, inter = blocks[b]
+            r = slice(b * BLOCK, (b + 1) * BLOCK)
+            x, xf, dy, dyl = heads_in[r], x_f[r], grad_y[r], grad_y_low[r]
+            cum_p = by_head(left, cum[:, 2 * p : 2 * p + 1], cum[:, 2 * p + 1 : 2 * p + 2])
+            d_p = by_head(left, d[:, 2 * p : 2 * p + 1], d[:, 2 * p + 1 : 2 * p + 2])
+            dxs = []
+            for i, h in enumerate((2 * p, 2 * p + 1)):
+                own = left if i == 0 else jnp.logical_not(left)
+                q = dot_nt(jnp.where(own, dy, 0.0).astype(BF), x)
+                decay = jnp.exp(jnp.where(mask, cum[:, h : h + 1] - cum_t[h : h + 1, :], -1e30))
+                scaled = decay * d_t[h : h + 1, :]
+                dxs.append(dot_tn((inter * scaled).astype(BF), dyl))
+                grad_inter[b] = grad_inter[b] + scaled * q
+                moved = inter * decay * q
+                sums_t[b, h : h + 1, :] = jnp.sum(moved, axis=0, keepdims=True)
+                rows = jnp.sum(moved * d_t[h : h + 1, :], axis=1, keepdims=True)
+                cols[0, r, :] += jnp.where(lane == h, rows, 0.0)
+            dx = by_head(left, dxs[0], dxs[1]) + skip * dy
+            extra = None
+            if b > 0:
+                state = state_ref[p, b - 1]
+                grown = dy * jnp.exp(cum_p)
+                grown_low = grown.astype(BF)
+                extra = grown * dot_mm(c_rows[r], state.astype(BF))
+                grad_c[b] = grad_c[b] + dot_nt(grown_low, state.astype(BF))
+                back_state = dot_tn(c_rows[r], grown_low)
+            end = cum_p[BLOCK - 1 :]
+            end_sum = None
+            if grad_state is not None:
+                weight = jnp.exp(end - cum_p)
+                low_state = grad_state.astype(BF)
+                dz_rows = dot_mm(b_rows[r], low_state)
+                grad_b[b] = grad_b[b] + dot_nt((xf * d_p * weight).astype(BF), low_state)
+                dx = dx + dz_rows * d_p * weight
+                direct = dz_rows * xf * weight
+                through = direct * d_p
+                end_sum = jnp.sum(through, axis=0, keepdims=True)
+                if b > 0:
+                    end_sum = end_sum + jnp.exp(end) * jnp.sum(grad_state * state, axis=0, keepdims=True)
+                extra = -through if extra is None else extra - through
+            for i, h in enumerate((2 * p, 2 * p + 1)):
+                own = left if i == 0 else jnp.logical_not(left)
+                if extra is not None:
+                    column = jnp.sum(jnp.where(own, extra, 0.0), axis=1, keepdims=True)
+                    cols[0, r, :] += jnp.where(lane == h, column, 0.0)
+                if end_sum is not None:
+                    column = jnp.sum(jnp.where(own, direct, 0.0), axis=1, keepdims=True)
+                    cols[1, r, :] += jnp.where(lane == h, column, 0.0)
+                    last = jnp.sum(jnp.where(own[0:1], end_sum, 0.0), axis=1, keepdims=True)
+                    at = slice((b + 1) * BLOCK - 1, (b + 1) * BLOCK)
+                    cols[0, at, :] += jnp.where(lane[0:1] == h, last, 0.0)
+            if b > 0:
+                grad_state = back_state if grad_state is None else jnp.exp(end) * grad_state + back_state
+            grad_x[b] = dx
+        conv_back(
+            jnp.concatenate(grad_x, axis=0), pre, values, cx_ref[:, lanes], 0, 4, lanes, inner + p * 128
+        )
+    upper = jnp.logical_not(mask).astype(F32) + (
+        lax.broadcasted_iota(jnp.int32, (BLOCK, BLOCK), 0)
+        == lax.broadcasted_iota(jnp.int32, (BLOCK, BLOCK), 1)
+    ).astype(F32)
+    ddts, logs = [], jnp.zeros((1, 128), F32)
+    for b in range(n_blocks):
+        d, cum, d_t, cum_t, inter = blocks[b]
+        r = slice(b * BLOCK, (b + 1) * BLOCK)
+        low = grad_inter[b].astype(BF)
+        grad_c[b] = grad_c[b] + dot_mm(low, b_rows[r])
+        grad_b[b] = grad_b[b] + dot_tn(low, c_rows[r])
+        direct = sums_t[b].T
+        reach = dot_exact(upper, cols[0, r, :] - direct * d)
+        logs = logs + jnp.sum(rate * d * reach, axis=0, keepdims=True)
+        ddts.append((direct + cols[1, r, :] + rate * reach) * sigmoid(raw[r]))
+    ddt = jnp.concatenate(ddts, axis=0)
+    grad_ref[:, bc_at + 256 : bc_at + 384] = ddt.astype(grad_ref.dtype)
+    small_ref[11:12, 0:128] = logs
+    small_ref[12:13, 0:128] = jnp.sum(ddt, axis=0, keepdims=True)
+    for i, (c, grads) in enumerate(((0, grad_b), (128, grad_c))):
+        conv_back(
+            jnp.concatenate(grads, axis=0), bc_pre[i], first_ref[:, bc_at + c : bc_at + c + 128],
+            cbc_ref[:, c : c + 128], 6, 10, slice(c, c + 128), bc_at + c,
+        )
+
+
+def pad_lanes(v):
+    return jnp.pad(v, (0, -v.shape[0] % 128)).reshape(1, -1)
+
+
+def mixer_params(conv_x, conv_x_bias, conv_bc, conv_bc_bias, dt_bias, a_log, d_skip):
+    size = conv_x.shape[1] // d_skip.shape[0]
+    return (
+        conv_x, conv_x_bias.reshape(1, -1), conv_bc, conv_bc_bias.reshape(1, -1),
+        pad_lanes(dt_bias), pad_lanes(a_log), jnp.repeat(d_skip, size).reshape(1, -1),
+    )
+
+
+def mixer_forward(firsts, params):
+    slots = firsts.shape[0]
+    inner = params[0].shape[1]
+    pairs, n_blocks = inner // 128, slots // BLOCK
+    shape = lambda *s: jax.ShapeDtypeStruct(s, F32)
+    return pl.pallas_call(
+        mixer_forward_kernel,
+        out_shape=(
+            shape(slots, inner), shape(slots, inner), shape(slots, 1),
+            shape(pairs, n_blocks - 1, 128, 128),
+        ),
+        in_specs=[VMEM_SPEC] * 8,
+        out_specs=(VMEM_SPEC,) * 4,
+        scratch_shapes=[pltpu.VMEM((slots + 8, 128), F32)],
+        compiler_params=pltpu.CompilerParams(vmem_limit_bytes=48 << 20),
+        cost_estimate=pl.CostEstimate(
+            flops=8 * slots * BLOCK * inner, bytes_accessed=24 * slots * inner,
+            transcendentals=slots * BLOCK * inner // 32,
+        ),
+        name="mixer_forward",
+    )(firsts, *params)
+
+
+def mixer_backward(full_inner, firsts, y, gated, dyn, scale, product, gain, state, params):
+    slots, width = firsts.shape
+    inner = params[0].shape[1]
+    return pl.pallas_call(
+        functools.partial(mixer_backward_kernel, full_inner),
+        out_shape=(
+            jax.ShapeDtypeStruct((slots, width), BF),
+            jax.ShapeDtypeStruct((16, inner), F32),
+        ),
+        in_specs=[VMEM_SPEC] * 15,
+        out_specs=(VMEM_SPEC,) * 2,
+        scratch_shapes=[
+            pltpu.VMEM((slots + 8, 128), F32),
+            pltpu.VMEM((slots + 8, 128), F32),
+            pltpu.VMEM((2, slots, 128), F32),
+            pltpu.VMEM((slots // BLOCK, 128, BLOCK), F32),
+        ],
+        compiler_params=pltpu.CompilerParams(vmem_limit_bytes=56 << 20),
+        cost_estimate=pl.CostEstimate(
+            flops=24 * slots * BLOCK * inner, bytes_accessed=40 * slots * inner,
+            transcendentals=slots * BLOCK * inner // 32,
+        ),
+        name="mixer_backward",
+    )(firsts, y, gated, dyn, scale, product, gain.reshape(1, -1), state, *params)
+
+
 def local(
     x_in,
     lengths,
@@ -1001,15 +1204,10 @@
     scale_one = rms_scale(x_float)
     normed_one = (x_float * scale_one * ln1_gain).astype(BF)
     firsts = dotf("td,df->tf", normed_one, first)
-    zx = firsts[:, : 2 * inner]
-    bc_proj = firsts[:, 2 * inner : dt_at]
-    dt_proj = firsts[:, dt_at : dt_at + heads]
-
-    gated_mix, mixer_back = mixer_forward(
-        zx, bc_proj, dt_proj, conv_x, conv_x_bias, conv_bc, conv_bc_bias, dt_bias, a_log, d_skip
-    )
-    squares = lax.psum(jnp.sum(gated_mix * gated_mix, axis=-1), "tensor")
-    scale_mix = lax.rsqrt(squares / full_inner + EPSILON)[:, None]
+    params = mixer_params(conv_x, conv_x_bias, conv_bc, conv_bc_bias, dt_bias, a_log, d_skip)
+    y, gated_mix, squares, states = mixer_forward(firsts, params)
+    squares = lax.psum(squares.reshape(slots), "tensor")[:, None]
+    scale_mix = lax.rsqrt(squares / full_inner + EPSILON)
     normed_mix = (gated_mix * scale_mix * gnorm_gain).astype(BF)
     mixer_part = dotf("tc,dc->td", normed_mix, proj_out).astype(BF)
     x_piece = lax.dynamic_slice_in_dim(x_in, my_t * piece, piece, axis=0)
@@ -1051,7 +1249,10 @@
     dxn_part = add_own(dxn_part, grad_normed_shared)
     out_part = add_own(out_part, shared_part)
     ffn_out = scatter_rows(out_part, n_dp, 4)
-    dxn_part, ffn_out = lax.optimization_barrier((dxn_part, ffn_out))
+    grad_shared_down = dotf("td,tf->df", g2_low, shared_act)
+    grad_shared_gu = dotf("td,tf->df", mine, grad_shared_pre)
+    grad_shared_w = jnp.concatenate([grad_shared_gu, grad_shared_down], axis=1).astype(BF)
+    dxn_part, ffn_out, grad_shared_w = lax.optimization_barrier((dxn_part, ffn_out, grad_shared_w))
     grad_one, sum_ln2, dm = turn(
         dxn_part, hidden_one, g2_piece, ln2_gain, n_dp, 3
     )
@@ -1060,45 +1261,28 @@
     layer_out = lax.all_gather(
         (hidden_one + ffn_out).astype(BF), "tensor", axis=0, tiled=True
     )
-    grad_shared_down = dotf("td,tf->df", g2_low, shared_act)
-    grad_shared_gu = dotf("td,tf->df", mine, grad_shared_pre)
-
-    grad_shared_w = jnp.concatenate([grad_shared_gu, grad_shared_down], axis=1).astype(BF)
+    grad_shared_w, dm = lax.optimization_barrier((grad_shared_w, dm))
     grad_shared_w = lax.psum_scatter(grad_shared_w, "dp", scatter_dimension=0, tiled=True)
     grad_out_w = dotf("td,tc->dc", dm, normed_mix).astype(BF)
     grad_normed_mix = dotf("td,dc->tc", dm, proj_out)
     weighted_mix = gnorm_gain * grad_normed_mix
     grad_gnorm = jnp.sum(grad_normed_mix * gated_mix * scale_mix, axis=0)
     product_sum = lax.psum(jnp.sum(weighted_mix * gated_mix, axis=-1), "tensor")[:, None]
-    grad_gated = scale_mix * weighted_mix - gated_mix * scale_mix**3 * product_sum / full_inner
-    (
-        grad_zx,
-        grad_bc,
-        grad_dt_low,
-        grad_conv_x,
-        grad_conv_x_bias,
-        grad_conv_bc,
-        grad_conv_bc_bias,
-        grad_dt_bias,
-        grad_a_log,
-        grad_d_skip,
-    ) = mixer_back(grad_gated)
-    grad_first = jnp.concatenate(
-        [
-            grad_zx,
-            grad_bc.astype(BF),
-            grad_dt_low,
-            jnp.zeros((slots, first_width - dt_at - heads), BF),
-        ],
-        axis=1,
+    grad_first, mixer_sums = mixer_backward(
+        full_inner, firsts, y, gated_mix, grad_normed_mix, scale_mix, product_sum, gnorm_gain,
+        states, params,
     )
+    taps = conv_x.shape[0]
+    grad_conv_x, grad_conv_x_bias = mixer_sums[:taps], mixer_sums[4]
+    grad_d_skip = jnp.sum(mixer_sums[5].reshape(heads, head_size), axis=1)
+    grad_conv_bc, grad_conv_bc_bias = mixer_sums[6 : 6 + taps, : 2 * state], mixer_sums[10, : 2 * state]
+    grad_a_log, grad_dt_bias = mixer_sums[11, :heads], mixer_sums[12, :heads]
     grad_input_part = dotf("tf,df->td", grad_first, first).astype(BF)
     grad_first_w = dotf("td,tf->df", normed_one, grad_first).astype(BF)
     def lanes(*vectors):
         vector = jnp.concatenate([v.reshape(-1) for v in vectors])
         return jnp.pad(vector, (0, -vector.shape[0] % (8 * width))).reshape(-1, width)
 
-    taps = conv_x.shape[0]
     wide = lanes(jnp.zeros((width,), F32), sum_ln2, grad_conv_bc, grad_conv_bc_bias)
     n_wide = wide.shape[0]
     narrow = lanes(

time: 904 us -> 767 us (0.85)
  local copies, waits for them, and re-layouts: 94.1 us -> 43.3 us
  matrix products: 93.9 us -> 45.3 us
  other arithmetic: 66.4 us -> 18.1 us
  Pallas kernels: 580 us -> 605 us
  waiting for transfers between devices: 27.8 us -> 8.36 us
    dot_general x12 -> x0, matrix products: 48.2 us -> none  [the longest x3 23.2 us: ssd_scan(): jnp.einsum('kij,kijh,kjhp->kihp', intersection, decay_mask, scaled, preci...]
    reduce_sum x10 -> x1, other arithmetic: 25.2 us -> 0.12 us  [local(): grad_d_skip = jnp.sum(mixer_sums[5].reshape(heads, head_size), axis=1)]
    pallas_call x0 -> x2, Pallas kernels: none -> 24.5 us  [the longest x1 17.2 us: mixer_backward(): pl.pallas_call(functools.partial(mixer_backward_kernel, full_inner), out_...]
    unnamed x4, waiting for transfers between devices: 27.8 us -> 8.34 us
    reshape x12 -> x2, local copies, waits for them, and re-layouts: 13.2 us -> 0.01 us  [the longest x1 0.01 us: pad_lanes(): return jnp.pad(v, (0, -v.shape[0] % 128)).reshape(1, -1)]
    mul x10 -> x0, local copies, waits for them, and re-layouts: 12 us -> none  [the longest x3 5.14 us: ssd_scan(): head_values * step_sizes[:, :, None]]
    unnamed x218 -> x93, local copies, waits for them, and re-layouts: 18.9 us -> 14.7 us
  transfers between devices with their start and end apart: 3 -> 3, of which waited for: 1 -> 1; matrix products, arithmetic and copies ran while one was open for 20% -> 7% of each run, Pallas kernels for 15% -> 33%
where the time goes in v8:
time: 767 us; the launch traced here: 754 us
  Pallas kernels  605 us (79%)
  matrix products  45.3 us (6%)
  local copies, waits for them, and re-layouts  43.3 us (6%)
  blocking collectives  19.3 us (3%)
  other arithmetic  18.1 us (2%)
  between operations  15.2 us (2%)
  waiting for transfers between devices  8.36 us (1%)
    pallas_call x1, Pallas kernels, start(): pl.pallas_call(functools.partial(start_kernel, n_hi, n), out_shape=[jax.S...  159 us
    pallas_call x1, Pallas kernels, tail(): pl.pallas_call(functools.partial(tail_kernel, n_hi, wide, bc_at, n), out_...  117 us
    pallas_call x1, Pallas kernels, turn(): pl.pallas_call(functools.partial(turn_kernel, n_hi), out_shape=(jax.Shape...  91.3 us
    pallas_call x1, Pallas kernels, scatter_rows(): pl.pallas_call(functools.partial(scatter_kernel, n_hi), out_shape=jax.Sha...  76.9 us
    pallas_call x1, Pallas kernels, middle(): pl.pallas_call(functools.partial(middle_kernel, n_hi), out_shape=(jax.Sha...  76.7 us
    pallas_call x1, Pallas kernels, experts(): pl.pallas_call(functools.partial(experts_kernel, n_dp, n_local, cap, chun...  58.9 us
    dot_general x13, matrix products, dotf(): return jnp.einsum(spec, a, b, preferred_element_type=F32)  45.3 us
    pallas_call x1, Pallas kernels, mixer_backward(): pl.pallas_call(functools.partial(mixer_backward_kernel, full_inner), out_...  17.2 us
  transfers between devices with their start and end apart: 3, of which 1 were waited for; matrix products, arithmetic and copies ran while one was open for 7% of the time, Pallas kernels for 33%

profile of v8, /device:TPU:9, one launch (start us, length us, event | category | flops | bytes accessed | tf_op | source)
XLA Modules:
  0.0 754.3 jit_solution(17476103165081980915)
XLA Ops:
  16.1 1.9 concatenate.40
  18.0 1.8 constant_dynamic-slice_fusion.2.refs_2_
  19.8 1.8 pad_maximum_fusion.4
  21.6 1.9 concatenate.39.refs_0_
  23.6 159.2 %start.1 = (bf16[8,2,96,1920]{3,2,1,0:T(8,128)(2,1)}, bf16[8,2,96,768]{3,2,1,0:T(8,128)(2,1)}, bf16[4096,1664]{1,0:T(8,128)(2,1)}) custom-call(bf16[2,96,1920]{2,1,0:T(8,128)(2,1)} %concatenate.39.refs_0_, bf16[2,96,768]{2,1,0:T(8,128)(2,1)} %bitcast.66, bf16[128,1664]{1,0:T(8,128)(2,1)} %constant_dynamic-slice_fusion.2.refs_2_), custom_call_target="tpu_custom_call" | custom-call | tf_op jit(solution)/shard_map/start/pallas_call | solution.py:336
  183.5 8.1 %fusion.20.first_ref = f32[512,1920]{1,0:T(8,128)} fusion(bf16[1536,1920]{1,0:T(8,128)(2,1)} %bitcast.80, bf16[512,1536]{1,0:T(8,128)(2,1)S(1)} %copy-done.14, f32[1536]{0:T(1024)S(1)} %copy-done.28, f32[512]{0:T(512)S(1)} %add_rsqrt_fusion.1), kind=kOutput, calls=%fused_computation.45 | convolution fusion | flops 3023044608 | bytes 11411456 | tf_op jit(solution)/shard_map/td,df->tf/dot_general | solution.py:29
  191.6 7.4 mixer_forward.1
  201.0 5.6 psum.14
  206.7 3.9 convert_add_fusion
  210.6 2.6 convolution_convert_fusion.4
  213.2 1.9 constant_dynamic-slice_fusion
  215.7 2.2 copy.80
  217.9 76.7 %middle.1 = (bf16[4096,1536]{1,0:T(8,128)(2,1)}, f32[128,1536]{1,0:T(8,128)}) custom-call(bf16[4,128,1536]{2,1,0:T(8,128)(2,1)} %bitcast.61, bf16[128,1536]{1,0:T(8,128)(2,1)} %get-tuple-element.202.x_ref.refs_2_, f32[1,1536]{1,0:T(1,128)} %reshape.185.gain_ref), custom_call_target="tpu_custom_call" | custom-call | tf_op jit(solution)/shard_map/middle/pallas_call | solution.py:246
  295.5 58.9 %experts.1 = (bf16[4096,1536]{1,0:T(8,128)(2,1)}, bf16[4096,1536]{1,0:T(8,128)(2,1)}, f32[24576,128]{1,0:T(8,128)}, f32[8,128,1536]{2,1,0:T(8,128)}) custom-call(s32[8,8,512]{2,1,0:T(8,128)} %fusion.12.pos_ref, f32[8,8,512]{2,1,0:T(8,128)} %bitcast.74, bf16[4096,1536]{1,0:T(8,128)(2,1)} %get-tuple-element.58.x_ref, ...), custom_call_target="tpu_custom_call" | custom-call | flops 40265318400 | bytes 88080384 | tf_op jit(solution)/shard_map/experts/pallas_call | solution.py:764
  354.5 3.1 fusion.8
  359.8 3.2 fusion.4.p_ref
  363.0 76.9 %scatter_rows.1 = f32[128,1536]{1,0:T(8,128)} custom-call(bf16[4096,1536]{1,0:T(8,128)(2,1)} %fusion.4.p_ref), custom_call_target="tpu_custom_call" | custom-call | tf_op jit(solution)/shard_map/scatter_rows/pallas_call | solution.py:462
  439.9 2.5 convolution_convert_fusion.2
  444.9 3.7 fusion.6.p_ref
  449.6 91.3 %turn.1 = (f32[128,1536]{1,0:T(8,128)}, f32[1,1536]{1,0:T(1,128)}, bf16[4,128,1536]{2,1,0:T(8,128)(2,1)}) custom-call(bf16[4096,1536]{1,0:T(8,128)(2,1)} %fusion.6.p_ref, f32[128,1536]{1,0:T(8,128)} %get-tuple-element.56.hidden_ref, bf16[128,1536]{1,0:T(8,128)(2,1)} %get-tuple-element.201.g2_ref, f32[1,1536]{1,0:T(1,128)} %reshape.185.gain_ref), custom_call_target="tpu_custom_call" | custom-call | tf_op jit(solution)/shard_map/turn/pallas_call | solution.py:499
  540.8 4.4 copy.86
  547.3 4.3 multiply_reduce_fusion
  551.7 13.7 %psum.15.product_ref = f32[512,1]{1,0:T(8,128)} all-reduce(f32[512,1]{1,0:T(8,128)S(1)} %copy.81), channel_id=1, replica_groups=mesh['dp'=8,'tensor'=4] {'tensor'}, use_global_device_ids=true, to_apply=%region_4.5 | all-reduce | flops 512 | bytes 4096 | tf_op jit(solution)/shard_map/psum | solution.py:1270
  565.4 17.2 %mixer_backward.1 = (bf16[512,1920]{1,0:T(8,128)(2,1)}, f32[16,768]{1,0:T(8,128)}) custom-call(f32[512,1920]{1,0:T(8,128)} %fusion.20.first_ref, f32[512,768]{1,0:T(8,128)} %copy-done.2, f32[512,768]{1,0:T(8,128)} %copy-done, f32[512,768]{1,0:T(8,128)} %get-tuple-element.200.dyn_ref, f32[512,1]{1,0:T(8,128)} %copy.82.scale_ref, f32[512,1]{1,0:T(8,128)} %psum.15.product_ref, ...), custom_call_target="tpu_custom_call" | custom-call | flops 2415919104 | bytes 15728640 | tf_op jit(solution)/shard_map/mixer_backward/pallas_call | solution.py:1105
  587.4 4.7 convolution_convert_fusion.1
  592.0 5.5 convolution_convert_fusion
  597.6 4.6 convolution_convert_fusion.3
  602.1 8.3 %reduce-scatter.4.cloned.1.call-done = bf16[192,768]{1,0:T(8,128)(2,1)} async-done(((bf16[1536,768]{1,0:T(8,128)(2,1)}), bf16[192,768]{1,0:T(8,128)(2,1)}) %reduce-scatter.4.cloned.1.call-update) | async-done | bytes 294928
  611.6 117.2 %tail.1 = (bf16[4,128,1536]{2,1,0:T(8,128)(2,1)}, f32[16,1536]{1,0:T(8,128)}, f32[2,96,1920]{2,1,0:T(8,128)}, f32[2,96,768]{2,1,0:T(8,128)}) custom-call(bf16[4,128,1536]{2,1,0:T(8,128)(2,1)} %bitcast.62, f32[128,1536]{1,0:T(8,128)} %get-tuple-element.70.refs_1_, bf16[128,1536]{1,0:T(8,128)(2,1)} %get-tuple-element.202.x_ref.refs_2_, ...), custom_call_target="tpu_custom_call" | custom-call | tf_op jit(solution)/shard_map/tail/pallas_call | solution.py:660
  734.6 3.5 bitcast_convert_fusion
  738.1 1.8 reshape.198
  744.1 2.7 copy.96
  (166 shorter events, 37.0 us)
Async XLA Ops:
  7.2 4.1 copy-start.22
  7.2 4.7 copy-start.26
  7.2 347.2 %all-gather.3.cloned.1.call-start = ((), (), s32[]{:S(2)}) async-start(), calls=%async_computation.1 | async-start | bytes 2654208 | tf_op jit(solution)/shard_map/all_gather | solution.py:1199
  8.1 4.5 copy-start.18
  8.3 5.9 copy-start.23
  8.3 6.5 copy-start.20
  11.2 4.4 copy-start.16
  16.1 5.5 copy-start.21
  19.8 163.0 %copy-start.14 = (bf16[512,1536]{1,0:T(8,128)(2,1)S(1)}, bf16[512,1536]{1,0:T(8,128)(2,1)}, u32[]{:S(2)}) copy-start(bf16[512,1536]{1,0:T(8,128)(2,1)} %param.23) | copy-start | bytes 4718596
  23.5 159.7 %copy-start.30 = (f32[768]{0:T(1024)S(1)}, f32[768]{0:T(1024)}, u32[]{:S(2)}) copy-start(f32[768]{0:T(1024)} %param.32) | copy-start | bytes 9220
  23.5 159.7 %copy-start.32 = (f32[12]{0:T(128)S(1)}, f32[12]{0:T(128)}, u32[]{:S(2)}) copy-start(f32[12]{0:T(128)} %param.37) | copy-start | bytes 148
  23.5 159.9 %copy-start.33 = (f32[12]{0:T(128)S(1)}, f32[12]{0:T(128)}, u32[]{:S(2)}) copy-start(f32[12]{0:T(128)} %param.36) | copy-start | bytes 148
  23.5 159.9 %copy-start.34 = (f32[12]{0:T(128)S(1)}, f32[12]{0:T(128)}, u32[]{:S(2)}) copy-start(f32[12]{0:T(128)} %param.35) | copy-start | bytes 148
  23.5 159.9 %copy-start.28 = (f32[1536]{0:T(1024)S(1)}, f32[1536]{0:T(1024)}, u32[]{:S(2)}) copy-start(f32[1536]{0:T(1024)} %param.27) | copy-start | bytes 18436
  182.7 419.4 %all-gather.5.cloned.1.call-start = ((), (), s32[]{:S(2)}) async-start(), calls=%async_computation.2 | async-start | bytes 1966080 | tf_op jit(solution)/shard_map/all_gather | solution.py:1261
  183.2 8.3 %copy-start.4 = (f32[1,768]{1,0:T(1,128)}, f32[1,768]{1,0:T(1,128)S(1)}, u32[]{:S(2)}) copy-start(f32[1,768]{1,0:T(1,128)S(1)} %reshape.178.cxb_ref) | copy-start | bytes 9220
  183.4 8.1 %copy-start.5 = (f32[1,768]{1,0:T(1,128)}, f32[1,768]{1,0:T(1,128)S(1)}, u32[]{:S(2)}) copy-start(f32[1,768]{1,0:T(1,128)S(1)} %reshape_reshape.3.skip_ref) | copy-start | bytes 9220
  183.4 8.1 %copy-start.8 = (f32[1,128]{1,0:T(1,128)}, f32[1,128]{1,0:T(1,128)S(1)}, u32[]{:S(2)}) copy-start(f32[1,128]{1,0:T(1,128)S(1)} %get-tuple-element.203.alog_ref) | copy-start | bytes 1540
  183.4 8.1 %copy-start.9 = (f32[1,128]{1,0:T(1,128)}, f32[1,128]{1,0:T(1,128)S(1)}, u32[]{:S(2)}) copy-start(f32[1,128]{1,0:T(1,128)S(1)} %get-tuple-element.204.dtb_ref) | copy-start | bytes 1540
  183.5 8.1 %copy-start.6 = (f32[4,768]{1,0:T(4,128)S(1)}, f32[4,768]{1,0:T(4,128)}, u32[]{:S(2)}) copy-start(f32[4,768]{1,0:T(4,128)} %cx_ref.3) | copy-start | bytes 36868
  183.5 8.1 %copy-start.7 = (f32[4,256]{1,0:T(4,128)S(1)}, f32[4,256]{1,0:T(4,128)}, u32[]{:S(2)}) copy-start(f32[4,256]{1,0:T(4,128)} %cbc_ref.3) | copy-start | bytes 12292
  183.5 8.1 %copy-start.10 = (f32[256]{0:T(256)S(1)}, f32[256]{0:T(256)}, u32[]{:S(2)}) copy-start(f32[256]{0:T(256)} %param.34) | copy-start | bytes 3076
  200.9 346.4 %copy-start = (f32[512,768]{1,0:T(8,128)}, f32[512,768]{1,0:T(8,128)S(1)}, u32[]{:S(2)}) copy-start(f32[512,768]{1,0:T(8,128)S(1)} %get-tuple-element.53.gated_ref) | copy-start | bytes 4718596
  210.6 4.5 copy-start.27
  217.9 77.6 %copy-start.25 = (f32[4096,8]{0,1:T(8,128)}, f32[4096,8]{0,1:T(8,128)S(1)}, u32[]{:S(2)}) copy-start(f32[4096,8]{0,1:T(8,128)S(1)} %copy.80) | copy-start | bytes 393220
  449.5 160.9 %reduce-scatter.4.cloned.1.call-start = ((), (), s32[]{:S(2)}) async-start(), calls=%async_computation.3 | async-start | bytes 2654208
  565.4 21.3 %copy-start.29 = (f32[1,1536]{1,0:T(1,128)S(1)}, f32[1,1536]{1,0:T(1,128)}, u32[]{:S(2)}) copy-start(f32[1,1536]{1,0:T(1,128)} %get-tuple-element.71) | copy-start | bytes 18436
  565.4 22.0 %copy-start.1 = (f32[512,768]{1,0:T(8,128)S(1)}, f32[512,768]{1,0:T(8,128)}, u32[]{:S(2)}) copy-start(f32[512,768]{1,0:T(8,128)} %copy-done) | copy-start | bytes 4718596
  587.4 4.7 copy-start.15
  587.4 4.7 copy-start.38
  587.4 10.2 %slice-start = ((s8[5898240]{0:T(1024)(128)(4,1)}), s8[4194304]{0:T(1024)(128)(4,1)S(1)}, s32[]{:S(2)}) async-start(s8[5898240]{0:T(1024)(128)(4,1)} %bitcast.81), calls=%async_computation.4 | async-start | bytes 8388608
  592.0 5.5 slice-start.1
  (13 other events, 38.6 us)
Sparse Core Ops, SparseCore 0:
  182.9 47.7 all-gather.2
  449.6 26.7 all-gather.4
  545.3 65.0 reduce-scatter.3

commit v9 on v8

--- a/solution.py
+++ b/solution.py
@@ -351,7 +351,7 @@
     return [o.reshape(n_dp * 2 * half, o.shape[3]) for o in outs[:n]] + [outs[n]]
 
 
-def scatter_steps(n_hi, sends, p_ref, o_ref, bufs):
+def scatter_steps(n_hi, sends, p_ref, o_ref, bufs, lo_first=(False, True)):
     (stage, from_c, from_f, from_s, from_h,
      stage_sem, send_c, recv_c, send_f, recv_f, send_s, recv_s, send_h, recv_h) = bufs
     depth = stage.shape[0]
@@ -362,8 +362,8 @@
 
     def where(h, k, f, s, c):
         kk = peer(hi, k, n_hi)
-        l = 1 - lo if (f if h == 1 else s) else lo
-        y = 1 - th if (s if h == 1 else f) else th
+        l = 1 - lo if (f if lo_first[h] else s) else lo
+        y = 1 - th if (s if lo_first[h] else f) else th
         z = 1 - tl if c else tl
         return ((kk * 2 + l) * 4 + y * 2 + z) * rows + h * half
 
@@ -378,10 +378,10 @@
         return (f * 2 + s) * n_hi + k
 
     def first(h):
-        return device(hi, lo, 1 - th, tl) if h == 0 else device(hi, 1 - lo, th, tl)
+        return device(hi, 1 - lo, th, tl) if lo_first[h] else device(hi, lo, 1 - th, tl)
 
     def second(h):
-        return device(hi, 1 - lo, th, tl) if h == 0 else device(hi, lo, 1 - th, tl)
+        return device(hi, lo, 1 - th, tl) if lo_first[h] else device(hi, 1 - lo, th, tl)
 
     for f, s, k, h in order:
         n = slot(f, s, k)
@@ -401,6 +401,8 @@
     for i, (f, s, k, h) in enumerate(order):
         if i + depth - 1 < len(order):
             load(i + depth - 1).start()
+        if i % 4 == 0:
+            yield
         load(i).wait()
         n = slot(f, s, k)
         arrive(from_c.at[h, n], send_c.at[h, n], recv_c.at[h, n], to_c)
@@ -451,7 +453,7 @@
 def scatter_kernel(n_hi, p_ref, o_ref, *bufs):
     greet(n_hi)
     sends = Sends()
-    scatter_steps(n_hi, sends, p_ref, o_ref, bufs)
+    in_turns(scatter_steps(n_hi, sends, p_ref, o_ref, bufs))
     sends.finish()
 
 
@@ -478,7 +480,7 @@
     hi, lo, th, tl = place()
     greet(n_hi)
     sends = Sends()
-    scatter_steps(n_hi, sends, p_ref, total_ref, bufs)
+    in_turns(scatter_steps(n_hi, sends, p_ref, total_ref, bufs))
     grad = total_ref[...]
     hidden = hidden_ref[...]
     scale = rms_scale(hidden)
@@ -514,9 +516,15 @@
     )(p, hidden, g2_piece, gain.reshape(1, width))
 
 
-def tail_kernel(n_hi, wide, bc_at, n, *refs):
+def tail_kernel(n_hi, wide, bc_at, n, merged, *refs):
+    if merged:
+        p_ref, hidden_ref, refs = refs[0], refs[1], refs[2:]
     part_ref, grad_ref, x_ref, gain_ref, small_ref = refs[:5]
     w_refs = refs[5 : 5 + n]
+    if merged:
+        oy_ref, refs = refs[5 + n], refs[: 5 + n] + refs[6 + n :]
+        o_total, y_send, y_recv = refs[-17:-14]
+        p_bufs, refs = refs[-14:], refs[:-17]
     ox_ref, os_ref = refs[5 + n : 7 + n]
     ow_refs = refs[7 + n : 7 + 2 * n]
     (got_c, got_y, t_send, t_recv, sp_send, sp_recv,
@@ -534,6 +542,12 @@
 
     def owner(k, l):
         return peer(hi, k, n_hi) * 2 + l
+
+    if merged:
+        others = scatter_steps(n_hi, sends, p_ref, o_total, p_bufs, lo_first=(False, False))
+    else:
+        others = iter(())
+    next(others, None)
 
     def forward(i):
         if i < len(events):
@@ -572,6 +586,7 @@
         if k == 0:
             break
         stage, from_f, from_h, stage_sem, send_f, recv_f, send_h, recv_h = bufs[w]
+        next(others, None)
         loads[i].wait()
         arrive(from_f.at[h, k], send_f.at[h, k], recv_f.at[h, k], to_c)
         forward(i + window)
@@ -591,6 +606,10 @@
                     small_h.at[hi], small_h.at[hi], smh_send.at[q - 1], smh_recv.at[back(q, n_hi) - 1],
                     device(peer(hi, q, n_hi), lo, th, tl),
                 )
+    if merged:
+        in_turns(others)
+        oy_ref[th * 2 + tl] = (hidden_ref[...] + o_total[...]).astype(oy_ref.dtype)
+        tensor_spread_start(sends, oy_ref, y_send, y_recv)
     for q in range(1, n_hi):
         arrive(small_h.at[peer(hi, q, n_hi)], smh_send.at[q - 1], smh_recv.at[q - 1], to_c)
     total = small_h[0]
@@ -620,6 +639,8 @@
                 arrive(bc_got.at[0], bc_send.at[0], bc_recv.at[0], to_c)
                 bc_own[1] = (bc_own[0].astype(F32) + bc_got[0].astype(F32)).astype(bc_own.dtype)
                 sends.push(bc_own.at[1], bc_got.at[1], bc_send.at[1], bc_recv.at[1], to_y)
+    if merged:
+        tensor_spread_end(sends, oy_ref, y_send, y_recv)
     arrive(small_t.at[1], sm_send.at[2], sm_recv.at[2], to_c)
     arrive(bc_got.at[1], bc_send.at[1], bc_recv.at[1], to_c)
     for h in range(2):
@@ -630,7 +651,11 @@
     os_ref[pl.ds(0, wide), :] = small_t[2] + small_t[1]
 
 
-def tail(weights, part, grad_one, x_piece, gain, small, wide, bc_at, bc_width, n_dp, collective_id):
+def tail(
+    weights, part, grad_one, x_piece, gain, small, wide, bc_at, bc_width, n_dp, collective_id,
+    out_part=None, hidden=None,
+):
+    merged = out_part is not None
     rows, width = x_piece.shape
     n_hi = n_dp // 2
     n = len(weights)
@@ -657,24 +682,29 @@
             DMA((2, n_hi)), DMA((2, n_hi)),
             DMA((2, n_hi - 1)), DMA((2, n_hi - 1)),
         ]
+    if merged:
+        scratch += [pltpu.VMEM((rows, width), F32), DMA((3,)), DMA((3,))]
+        scratch += scatter_scratch(n_hi, rows // 2, width, out_part.dtype)
     outs = pl.pallas_call(
-        functools.partial(tail_kernel, n_hi, wide, bc_at, n),
-        out_shape=[
+        functools.partial(tail_kernel, n_hi, wide, bc_at, n, merged),
+        out_shape=[jax.ShapeDtypeStruct((4, rows, width), dt)] * merged + [
             jax.ShapeDtypeStruct((4, rows, width), dt),
             jax.ShapeDtypeStruct(small.shape, F32),
         ] + [jax.ShapeDtypeStruct((2, half, w.shape[1]), F32) for w in weights],
-        in_specs=[VMEM_SPEC] * 5 + [ANY_SPEC] * n,
-        out_specs=[VMEM_SPEC] * (2 + n),
+        in_specs=[ANY_SPEC, VMEM_SPEC] * merged + [VMEM_SPEC] * 5 + [ANY_SPEC] * n,
+        out_specs=[VMEM_SPEC] * (2 + n + merged),
         scratch_shapes=scratch,
         compiler_params=pltpu.CompilerParams(
             collective_id=collective_id, has_side_effects=True, vmem_limit_bytes=60 << 20
         ),
         name="tail",
     )(
-        part.reshape(4, rows, width), grad_one, x_piece, gain.reshape(1, width), small,
+        *([out_part, hidden] if merged else []), part.reshape(4, rows, width), grad_one, x_piece, gain.reshape(1, width), small,
         *[w.reshape(n_dp, 2, half, w.shape[1]) for w in weights],
     )
-    return outs[0], outs[1], [o.reshape(2 * half, o.shape[2]) for o in outs[2:]]
+    out = outs[0].reshape(4 * rows, width) if merged else None
+    outs = outs[merged:]
+    return outs[0], outs[1], [o.reshape(2 * half, o.shape[2]) for o in outs[2:]], out
 
 
 def dot_mm(a, b):
@@ -1248,26 +1278,22 @@
 
     dxn_part = add_own(dxn_part, grad_normed_shared)
     out_part = add_own(out_part, shared_part)
-    ffn_out = scatter_rows(out_part, n_dp, 4)
     grad_shared_down = dotf("td,tf->df", g2_low, shared_act)
     grad_shared_gu = dotf("td,tf->df", mine, grad_shared_pre)
     grad_shared_w = jnp.concatenate([grad_shared_gu, grad_shared_down], axis=1).astype(BF)
-    dxn_part, ffn_out, grad_shared_w = lax.optimization_barrier((dxn_part, ffn_out, grad_shared_w))
+    dxn_part, grad_shared_w = lax.optimization_barrier((dxn_part, grad_shared_w))
     grad_one, sum_ln2, dm = turn(
         dxn_part, hidden_one, g2_piece, ln2_gain, n_dp, 3
     )
     dm = dm.reshape(slots, width)
 
-    layer_out = lax.all_gather(
-        (hidden_one + ffn_out).astype(BF), "tensor", axis=0, tiled=True
-    )
-    grad_shared_w, dm = lax.optimization_barrier((grad_shared_w, dm))
     grad_shared_w = lax.psum_scatter(grad_shared_w, "dp", scatter_dimension=0, tiled=True)
     grad_out_w = dotf("td,tc->dc", dm, normed_mix).astype(BF)
     grad_normed_mix = dotf("td,dc->tc", dm, proj_out)
     weighted_mix = gnorm_gain * grad_normed_mix
     grad_gnorm = jnp.sum(grad_normed_mix * gated_mix * scale_mix, axis=0)
-    product_sum = lax.psum(jnp.sum(weighted_mix * gated_mix, axis=-1), "tensor")[:, None]
+    product_sum = jnp.sum(weighted_mix * gated_mix, axis=-1).reshape(-1, 128)
+    product_sum = lax.psum(product_sum, "tensor").reshape(slots, 1)
     grad_first, mixer_sums = mixer_backward(
         full_inner, firsts, y, gated_mix, grad_normed_mix, scale_mix, product_sum, gnorm_gain,
         states, params,
@@ -1289,7 +1315,8 @@
         grad_conv_x, grad_conv_x_bias, grad_gnorm, grad_dt_bias, grad_a_log, grad_d_skip
     )
     grad_first_w, grad_shared_w = lax.optimization_barrier((grad_first_w, grad_shared_w))
-    grad_x, sums, (first_f, grad_out_w) = tail(
+    merged = n_dp <= 8
+    grad_x, sums, (first_f, grad_out_w), layer_out = tail(
         [grad_first_w, grad_out_w],
         grad_input_part,
         grad_one,
@@ -1301,7 +1328,11 @@
         2 * state,
         n_dp,
         5,
+        *((out_part, hidden_one) if merged else ()),
     )
+    if not merged:
+        ffn_out = scatter_rows(out_part, n_dp, 4)
+        layer_out = lax.all_gather((hidden_one + ffn_out).astype(BF), "tensor", axis=0, tiled=True)
     grad_x = grad_x.reshape(slots, width).astype(F32)
     wide, narrow = sums[:n_wide].reshape(-1), sums[n_wide:].reshape(-1)
     at = [0]

time: 767 us -> 753 us (0.982)
  waiting for transfers between devices: 8.36 us -> 0.05 us
    pallas_call x1, Pallas kernels: 91.3 us -> 115 us  [turn(): pl.pallas_call(functools.partial(turn_kernel, n_hi), out_shape=(jax.Shape...]
    pallas_call x2 -> x1, Pallas kernels: 194 us -> 172 us  [tail(): pl.pallas_call(functools.partial(tail_kernel, n_hi, wide, bc_at, n, merge...]
    unnamed x4 -> x3, waiting for transfers between devices: 8.34 us -> 0.03 us
  transfers between devices with their start and end apart: 3 -> 2, of which waited for: 1 -> 0; matrix products, arithmetic and copies ran while one was open for 7% -> 7% of each run, Pallas kernels for 33% -> 37%
where the time goes in v9:
time: 753 us; the launch traced here: 748 us
  Pallas kernels  607 us (81%)
  matrix products  45.2 us (6%)
  local copies, waits for them, and re-layouts  42.3 us (6%)
  blocking collectives  19.6 us (3%)
  other arithmetic  17.9 us (2%)
  between operations  15.7 us (2%)
    pallas_call x1, Pallas kernels, tail(): pl.pallas_call(functools.partial(tail_kernel, n_hi, wide, bc_at, n, merge...  172 us
    pallas_call x1, Pallas kernels, start(): pl.pallas_call(functools.partial(start_kernel, n_hi, n), out_shape=[jax.S...  159 us
    pallas_call x1, Pallas kernels, turn(): pl.pallas_call(functools.partial(turn_kernel, n_hi), out_shape=(jax.Shape...  115 us
    pallas_call x1, Pallas kernels, middle(): pl.pallas_call(functools.partial(middle_kernel, n_hi), out_shape=(jax.Sha...  76.8 us
    pallas_call x1, Pallas kernels, experts(): pl.pallas_call(functools.partial(experts_kernel, n_dp, n_local, cap, chun...  58.7 us
    dot_general x13, matrix products, dotf(): return jnp.einsum(spec, a, b, preferred_element_type=F32)  45.2 us
    pallas_call x1, Pallas kernels, mixer_backward(): pl.pallas_call(functools.partial(mixer_backward_kernel, full_inner), out_...  17 us
  transfers between devices with their start and end apart: 2, of which 0 were waited for; matrix products, arithmetic and copies ran while one was open for 7% of the time, Pallas kernels for 37%

profile of v9, /device:TPU:9, one launch (start us, length us, event | category | flops | bytes accessed | tf_op | source)
XLA Modules:
  0.0 747.7 jit_solution(11489809628105558960)
XLA Ops:
  9.0 1.7 convert.34
  14.9 1.6 convert.38
  19.0 1.7 pad_maximum_fusion.4
  20.8 2.0 concatenate.38.refs_0_
  22.7 159.1 %start.1 = (bf16[8,2,96,1920]{3,2,1,0:T(8,128)(2,1)}, bf16[8,2,96,768]{3,2,1,0:T(8,128)(2,1)}, bf16[4096,1664]{1,0:T(8,128)(2,1)}) custom-call(bf16[2,96,1920]{2,1,0:T(8,128)(2,1)} %concatenate.38.refs_0_, bf16[2,96,768]{2,1,0:T(8,128)(2,1)} %bitcast.68, bf16[128,1664]{1,0:T(8,128)(2,1)} %constant_dynamic-slice_fusion.2.refs_2_), custom_call_target="tpu_custom_call" | custom-call | tf_op jit(solution)/shard_map/start/pallas_call | solution.py:336
  182.1 3.7 convert_add_fusion
  185.9 2.4 copy.80
  188.9 8.0 %fusion.20.first_ref = f32[512,1920]{1,0:T(8,128)} fusion(bf16[1536,1920]{1,0:T(8,128)(2,1)} %bitcast.82, bf16[512,1536]{1,0:T(8,128)(2,1)S(1)} %copy-done.11, f32[1536]{0:T(1024)S(1)} %copy-done.23, f32[512]{0:T(512)S(1)} %add_rsqrt_fusion.1), kind=kOutput, calls=%fused_computation.44 | convolution fusion | flops 3023044608 | bytes 11411456 | tf_op jit(solution)/shard_map/td,df->tf/dot_general | solution.py:29
  197.0 7.4 mixer_forward.1
  206.5 6.0 psum.14
  213.1 4.3 convolution_convert_fusion.4
  217.3 1.8 constant_dynamic-slice_fusion.1.x_ref.refs_4_
  219.1 76.8 %middle.1 = (bf16[4096,1536]{1,0:T(8,128)(2,1)}, f32[128,1536]{1,0:T(8,128)}) custom-call(bf16[4,128,1536]{2,1,0:T(8,128)(2,1)} %bitcast.63, bf16[128,1536]{1,0:T(8,128)(2,1)} %constant_dynamic-slice_fusion.1.x_ref.refs_4_, f32[1,1536]{1,0:T(1,128)} %reshape.195.gain_ref), custom_call_target="tpu_custom_call" | custom-call | tf_op jit(solution)/shard_map/middle/pallas_call | solution.py:246
  296.8 58.7 %experts.1 = (bf16[4096,1536]{1,0:T(8,128)(2,1)}, bf16[4096,1536]{1,0:T(8,128)(2,1)}, f32[24576,128]{1,0:T(8,128)}, f32[8,128,1536]{2,1,0:T(8,128)}) custom-call(s32[8,8,512]{2,1,0:T(8,128)} %fusion.12.pos_ref, f32[8,8,512]{2,1,0:T(8,128)} %bitcast.76, bf16[4096,1536]{1,0:T(8,128)(2,1)} %get-tuple-element.55.x_ref, ...), custom_call_target="tpu_custom_call" | custom-call | flops 40265318400 | bytes 88080384 | tf_op jit(solution)/shard_map/experts/pallas_call | solution.py:794
  355.6 3.1 fusion.8
  360.0 2.4 convolution_convert_fusion.2
  362.4 1.6 pad_maximum_fusion
  364.0 3.6 fusion.6.p_ref
  367.6 4.5 copy.86
  375.6 115.2 %turn.1 = (f32[128,1536]{1,0:T(8,128)}, f32[1,1536]{1,0:T(1,128)}, bf16[4,128,1536]{2,1,0:T(8,128)(2,1)}) custom-call(bf16[4096,1536]{1,0:T(8,128)(2,1)} %fusion.6.p_ref, f32[128,1536]{1,0:T(8,128)} %get-tuple-element.58.hidden_ref.refs_1_, bf16[128,1536]{1,0:T(8,128)(2,1)} %constant_dynamic-slice_fusion.g2_ref, f32[1,1536]{1,0:T(1,128)} %reshape.195.gain_ref), custom_call_target="tpu_custom_call" | custom-call | tf_op jit(solution)/shard_map/turn/pallas_call | solution.py:501
  490.8 4.8 multiply_reduce_fusion
  495.7 13.6 %psum.15.product_ref = f32[512,1]{1,0:T(8,128)} all-reduce(f32[512,1]{1,0:T(8,128)S(1)} %copy.81), channel_id=1, replica_groups=mesh['dp'=8,'tensor'=4] {'tensor'}, use_global_device_ids=true, to_apply=%region_4.5 | all-reduce | flops 512 | bytes 4096 | tf_op jit(solution)/shard_map/psum | solution.py:1296
  509.3 17.0 %mixer_backward.1 = (bf16[512,1920]{1,0:T(8,128)(2,1)}, f32[16,768]{1,0:T(8,128)}) custom-call(f32[512,1920]{1,0:T(8,128)} %fusion.20.first_ref, f32[512,768]{1,0:T(8,128)} %copy-done.2, f32[512,768]{1,0:T(8,128)} %copy-done, f32[512,768]{1,0:T(8,128)} %get-tuple-element.196.dyn_ref, f32[512,1]{1,0:T(8,128)} %copy.82.scale_ref, f32[512,1]{1,0:T(8,128)} %psum.15.product_ref, ...), custom_call_target="tpu_custom_call" | custom-call | flops 2415919104 | bytes 15728640 | tf_op jit(solution)/shard_map/mixer_backward/pallas_call | solution.py:1135
  531.2 3.8 fusion.4.refs_0_
  535.0 2.9 convolution_convert_fusion.1
  538.0 5.5 convolution_convert_fusion
  543.5 4.6 convolution_convert_fusion.3
  549.2 172.5 %tail.1 = (bf16[4,128,1536]{2,1,0:T(8,128)(2,1)}, bf16[4,128,1536]{2,1,0:T(8,128)(2,1)}, f32[16,1536]{1,0:T(8,128)}, f32[2,96,1920]{2,1,0:T(8,128)}, f32[2,96,768]{2,1,0:T(8,128)}) custom-call(bf16[4096,1536]{1,0:T(8,128)(2,1)} %fusion.4.refs_0_, f32[128,1536]{1,0:T(8,128)} %get-tuple-element.58.hidden_ref.refs_1_, bf16[4,128,1536]{2,1,0:T(8,128)(2,1)} %bitcast.64, ...), custom_call_target="tpu_custom_call" | custom-call | tf_op jit(solution)/shard_map/tail/pallas_call | solution.py:688
  723.1 1.6 slice.133
  727.5 3.5 bitcast_convert_fusion
  731.0 1.8 reshape.210
  737.0 2.7 copy.96
  (154 shorter events, 32.4 us)
Async XLA Ops:
  7.2 4.7 copy-start.18
  7.2 5.4 copy-start.21
  7.2 348.4 %all-gather.2.cloned.1.call-start = ((), (), s32[]{:S(2)}) async-start(), calls=%async_computation.1 | async-start | bytes 2654208 | tf_op jit(solution)/shard_map/all_gather | solution.py:1229
  8.1 5.2 copy-start.15
  9.0 7.5 copy-start.17
  10.7 6.6 copy-start.13
  181.9 366.2 %reduce-scatter.4.cloned.1.call-start = ((), (), s32[]{:S(2)}) async-start(), calls=%async_computation.2 | async-start | bytes 2654208
  185.8 3.0 copy-start.31
  185.8 3.0 copy-start.32
  185.9 3.0 copy-start.23
  188.2 107.7 %copy-start.20 = (f32[4096,8]{0,1:T(8,128)}, f32[4096,8]{0,1:T(8,128)S(1)}, u32[]{:S(2)}) copy-start(f32[4096,8]{0,1:T(8,128)S(1)} %copy.80) | copy-start | bytes 393220
  188.6 8.3 %copy-start.28 = (f32[512]{0:T(512)}, f32[512]{0:T(512)S(1)}, u32[]{:S(2)}) copy-start(f32[512]{0:T(512)S(1)} %add_rsqrt_fusion.1) | copy-start | bytes 6148
  188.7 8.3 %copy-start.4 = (f32[1,768]{1,0:T(1,128)}, f32[1,768]{1,0:T(1,128)S(1)}, u32[]{:S(2)}) copy-start(f32[1,768]{1,0:T(1,128)S(1)} %reshape.188.cxb_ref) | copy-start | bytes 9220
  188.8 8.1 %copy-start.5 = (f32[1,768]{1,0:T(1,128)}, f32[1,768]{1,0:T(1,128)S(1)}, u32[]{:S(2)}) copy-start(f32[1,768]{1,0:T(1,128)S(1)} %reshape_reshape.3.skip_ref) | copy-start | bytes 9220
  188.9 8.1 %copy-start.8 = (f32[1,128]{1,0:T(1,128)}, f32[1,128]{1,0:T(1,128)S(1)}, u32[]{:S(2)}) copy-start(f32[1,128]{1,0:T(1,128)S(1)} %get-tuple-element.197.alog_ref) | copy-start | bytes 1540
  188.9 8.1 %copy-start.9 = (f32[1,128]{1,0:T(1,128)}, f32[1,128]{1,0:T(1,128)S(1)}, u32[]{:S(2)}) copy-start(f32[1,128]{1,0:T(1,128)S(1)} %get-tuple-element.198.dtb_ref) | copy-start | bytes 1540
  188.9 8.1 %copy-start.6 = (f32[4,768]{1,0:T(4,128)S(1)}, f32[4,768]{1,0:T(4,128)}, u32[]{:S(2)}) copy-start(f32[4,768]{1,0:T(4,128)} %cx_ref.3) | copy-start | bytes 36868
  188.9 8.1 %copy-start.7 = (f32[4,256]{1,0:T(4,128)S(1)}, f32[4,256]{1,0:T(4,128)}, u32[]{:S(2)}) copy-start(f32[4,256]{1,0:T(4,128)} %cbc_ref.3) | copy-start | bytes 12292
  188.9 8.1 %copy-start.10 = (f32[256]{0:T(256)S(1)}, f32[256]{0:T(256)}, u32[]{:S(2)}) copy-start(f32[256]{0:T(256)} %param.34) | copy-start | bytes 3076
  197.0 15.4 %copy-start.22 = (f32[1536]{0:T(1024)S(1)}, f32[1536]{0:T(1024)}, u32[]{:S(2)}) copy-start(f32[1536]{0:T(1024)} %param.40) | copy-start | bytes 18436
  206.3 284.4 %copy-start = (f32[512,768]{1,0:T(8,128)}, f32[512,768]{1,0:T(8,128)S(1)}, u32[]{:S(2)}) copy-start(f32[512,768]{1,0:T(8,128)S(1)} %get-tuple-element.52.gated_ref) | copy-start | bytes 4718596
  355.6 3.1 copy-start.33
  509.3 21.1 %copy-start.25 = (f32[1,1536]{1,0:T(1,128)S(1)}, f32[1,1536]{1,0:T(1,128)}, u32[]{:S(2)}) copy-start(f32[1,1536]{1,0:T(1,128)} %get-tuple-element.66) | copy-start | bytes 18436
  531.2 3.8 copy-start.1
  531.2 3.8 copy-start.35
  535.0 2.9 copy-start.12
  535.0 2.9 copy-start.29
  535.0 2.9 copy-start.34
  535.0 8.5 %slice-start = ((s8[5898240]{0:T(1024)(128)(4,1)}), s8[4194304]{0:T(1024)(128)(4,1)S(1)}, s32[]{:S(2)}) async-start(s8[5898240]{0:T(1024)(128)(4,1)} %bitcast.83), calls=%async_computation.3 | async-start | bytes 8388608
  537.9 5.6 slice-start.1
  721.7 3.9 copy-start.19
  736.2 3.4 copy-start.16
  (8 other events, 13.1 us)
Sparse Core Ops, SparseCore 0:
  182.0 47.5 all-gather.1
  372.2 90.3 reduce-scatter.3

commit v10 on v9

--- a/solution.py
+++ b/solution.py
@@ -557,7 +557,7 @@
                 w_refs[w].at[owner(k, 1 - lo), h], from_f.at[h, k], send_f.at[h, k], recv_f.at[h, k], to_f
             )
 
-    window = 4
+    window = 6
     for i in range(window):
         forward(i)
     loads = []
@@ -1292,8 +1292,8 @@
     grad_normed_mix = dotf("td,dc->tc", dm, proj_out)
     weighted_mix = gnorm_gain * grad_normed_mix
     grad_gnorm = jnp.sum(grad_normed_mix * gated_mix * scale_mix, axis=0)
-    product_sum = jnp.sum(weighted_mix * gated_mix, axis=-1).reshape(-1, 128)
-    product_sum = lax.psum(product_sum, "tensor").reshape(slots, 1)
+    product_sum = lax.optimization_barrier(jnp.sum(weighted_mix * gated_mix, axis=-1))
+    product_sum = lax.optimization_barrier(lax.psum(product_sum, "tensor")).reshape(slots, 1)
     grad_first, mixer_sums = mixer_backward(
         full_inner, firsts, y, gated_mix, grad_normed_mix, scale_mix, product_sum, gnorm_gain,
         states, params,

time: 753 us -> 739 us (0.981)
  blocking collectives: 19.6 us -> 11.1 us
    psum x1, blocking collectives: 13.6 us -> 5.09 us  [local(): lax.psum(product_sum, 'tensor')]
  transfers between devices with their start and end apart: 2 -> 2, of which waited for: 0 -> 0; matrix products, arithmetic and copies ran while one was open for 7% -> 7% of each run, Pallas kernels for 37% -> 38%
where the time goes in v10:
time: 739 us; the launch traced here: 733 us
  Pallas kernels  600 us (81%)
  matrix products  45.2 us (6%)
  local copies, waits for them, and re-layouts  43 us (6%)
  other arithmetic  17.9 us (2%)
  between operations  15.7 us (2%)
  blocking collectives  11.1 us (2%)
    pallas_call x1, Pallas kernels, tail(): pl.pallas_call(functools.partial(tail_kernel, n_hi, wide, bc_at, n, merge...  165 us
    pallas_call x1, Pallas kernels, start(): pl.pallas_call(functools.partial(start_kernel, n_hi, n), out_shape=[jax.S...  159 us
    pallas_call x1, Pallas kernels, turn(): pl.pallas_call(functools.partial(turn_kernel, n_hi), out_shape=(jax.Shape...  115 us
    pallas_call x1, Pallas kernels, middle(): pl.pallas_call(functools.partial(middle_kernel, n_hi), out_shape=(jax.Sha...  76.8 us
    pallas_call x1, Pallas kernels, experts(): pl.pallas_call(functools.partial(experts_kernel, n_dp, n_local, cap, chun...  58.7 us
    dot_general x13, matrix products, dotf(): return jnp.einsum(spec, a, b, preferred_element_type=F32)  45.2 us
    pallas_call x1, Pallas kernels, mixer_backward(): pl.pallas_call(functools.partial(mixer_backward_kernel, full_inner), out_...  17 us
  transfers between devices with their start and end apart: 2, of which 0 were waited for; matrix products, arithmetic and copies ran while one was open for 7% of the time, Pallas kernels for 38%

profile of v10, /device:TPU:9, one launch (start us, length us, event | category | flops | bytes accessed | tf_op | source)
XLA Modules:
  0.0 732.9 jit_solution(3517357746806482711)
XLA Ops:
  9.0 1.7 convert.34
  14.9 1.6 convert.38
  19.0 1.7 pad_maximum_fusion.4
  20.8 2.0 concatenate.38.refs_0_
  22.7 159.1 %start.1 = (bf16[8,2,96,1920]{3,2,1,0:T(8,128)(2,1)}, bf16[8,2,96,768]{3,2,1,0:T(8,128)(2,1)}, bf16[4096,1664]{1,0:T(8,128)(2,1)}) custom-call(bf16[2,96,1920]{2,1,0:T(8,128)(2,1)} %concatenate.38.refs_0_, bf16[2,96,768]{2,1,0:T(8,128)(2,1)} %bitcast.68, bf16[128,1664]{1,0:T(8,128)(2,1)} %constant_dynamic-slice_fusion.2.refs_2_), custom_call_target="tpu_custom_call" | custom-call | tf_op jit(solution)/shard_map/start/pallas_call | solution.py:336
  182.1 3.7 convert_add_fusion
  185.9 2.4 copy.80
  188.9 8.0 %fusion.20.first_ref = f32[512,1920]{1,0:T(8,128)} fusion(bf16[1536,1920]{1,0:T(8,128)(2,1)} %bitcast.82, bf16[512,1536]{1,0:T(8,128)(2,1)S(1)} %copy-done.11, f32[1536]{0:T(1024)S(1)} %copy-done.23, f32[512]{0:T(512)S(1)} %add_rsqrt_fusion.1), kind=kOutput, calls=%fused_computation.44 | convolution fusion | flops 3023044608 | bytes 11411456 | tf_op jit(solution)/shard_map/td,df->tf/dot_general | solution.py:29
  197.0 7.4 %mixer_forward.1 = (f32[512,768]{1,0:T(8,128)S(1)}, f32[512,768]{1,0:T(8,128)S(1)}, f32[512,1]{1,0:T(8,128)S(1)}, f32[6,1,128,128]{3,2,1,0:T(8,128)S(1)}) custom-call(f32[512,1920]{1,0:T(8,128)} %fusion.20.first_ref, f32[4,768]{1,0:T(4,128)S(1)} %copy-done.6, f32[1,768]{1,0:T(1,128)S(1)} %reshape.185.cxb_ref, f32[4,256]{1,0:T(4,128)S(1)} %copy-done.7, ...), custom_call_target="tpu_custom_call" | custom-call | flops 805306368 | bytes 9437184 | tf_op jit(solution)/shard_map/mixer_forward/pallas_call | solution.py:1114
  206.5 6.0 psum.14
  213.1 4.3 convolution_convert_fusion.4
  217.3 1.8 constant_dynamic-slice_fusion.1.x_ref.refs_4_
  219.1 76.8 %middle.1 = (bf16[4096,1536]{1,0:T(8,128)(2,1)}, f32[128,1536]{1,0:T(8,128)}) custom-call(bf16[4,128,1536]{2,1,0:T(8,128)(2,1)} %bitcast.63, bf16[128,1536]{1,0:T(8,128)(2,1)} %constant_dynamic-slice_fusion.1.x_ref.refs_4_, f32[1,1536]{1,0:T(1,128)} %reshape.192.gain_ref), custom_call_target="tpu_custom_call" | custom-call | tf_op jit(solution)/shard_map/middle/pallas_call | solution.py:246
  296.8 58.7 %experts.1 = (bf16[4096,1536]{1,0:T(8,128)(2,1)}, bf16[4096,1536]{1,0:T(8,128)(2,1)}, f32[24576,128]{1,0:T(8,128)}, f32[8,128,1536]{2,1,0:T(8,128)}) custom-call(s32[8,8,512]{2,1,0:T(8,128)} %fusion.12.pos_ref, f32[8,8,512]{2,1,0:T(8,128)} %bitcast.76, bf16[4096,1536]{1,0:T(8,128)(2,1)} %get-tuple-element.55.x_ref, ...), custom_call_target="tpu_custom_call" | custom-call | flops 40265318400 | bytes 88080384 | tf_op jit(solution)/shard_map/experts/pallas_call | solution.py:794
  355.6 3.1 fusion.8
  360.0 2.4 convolution_convert_fusion.2
  362.4 1.6 pad_maximum_fusion
  364.0 3.6 fusion.6.p_ref
  367.6 4.5 copy.86
  375.6 115.2 %turn.1 = (f32[128,1536]{1,0:T(8,128)}, f32[1,1536]{1,0:T(1,128)}, bf16[4,128,1536]{2,1,0:T(8,128)(2,1)}) custom-call(bf16[4096,1536]{1,0:T(8,128)(2,1)} %fusion.6.p_ref, f32[128,1536]{1,0:T(8,128)} %get-tuple-element.58.hidden_ref.refs_1_, bf16[128,1536]{1,0:T(8,128)(2,1)} %constant_dynamic-slice_fusion.g2_ref, f32[1,1536]{1,0:T(1,128)} %reshape.192.gain_ref), custom_call_target="tpu_custom_call" | custom-call | tf_op jit(solution)/shard_map/turn/pallas_call | solution.py:501
  490.8 4.8 multiply_reduce_fusion
  495.5 5.1 psum.15
  501.5 17.0 %mixer_backward.1 = (bf16[512,1920]{1,0:T(8,128)(2,1)}, f32[16,768]{1,0:T(8,128)}) custom-call(f32[512,1920]{1,0:T(8,128)} %fusion.20.first_ref, f32[512,768]{1,0:T(8,128)} %copy-done.2, f32[512,768]{1,0:T(8,128)} %copy-done, f32[512,768]{1,0:T(8,128)} %get-tuple-element.196.dyn_ref, f32[512,1]{1,0:T(8,128)} %copy.81.scale_ref, f32[512,1]{1,0:T(8,128)} %copy.82.product_ref, ...), custom_call_target="tpu_custom_call" | custom-call | flops 2415919104 | bytes 15728640 | tf_op jit(solution)/shard_map/mixer_backward/pallas_call | solution.py:1135
  523.3 3.8 fusion.4.refs_0_
  527.2 2.9 convolution_convert_fusion.1
  530.1 5.5 convolution_convert_fusion
  535.7 4.6 convolution_convert_fusion.3
  541.4 165.5 %tail.1 = (bf16[4,128,1536]{2,1,0:T(8,128)(2,1)}, bf16[4,128,1536]{2,1,0:T(8,128)(2,1)}, f32[16,1536]{1,0:T(8,128)}, f32[2,96,1920]{2,1,0:T(8,128)}, f32[2,96,768]{2,1,0:T(8,128)}) custom-call(bf16[4096,1536]{1,0:T(8,128)(2,1)} %fusion.4.refs_0_, f32[128,1536]{1,0:T(8,128)} %get-tuple-element.58.hidden_ref.refs_1_, bf16[4,128,1536]{2,1,0:T(8,128)(2,1)} %bitcast.64, ...), custom_call_target="tpu_custom_call" | custom-call | tf_op jit(solution)/shard_map/tail/pallas_call | solution.py:688
  708.2 1.6 slice.133
  712.7 3.5 bitcast_convert_fusion
  716.2 1.8 reshape.206
  722.2 2.7 copy.96
  (154 shorter events, 33.1 us)
Async XLA Ops:
  7.2 4.7 copy-start.18
  7.2 5.4 copy-start.21
  7.2 348.4 %all-gather.2.cloned.1.call-start = ((), (), s32[]{:S(2)}) async-start(), calls=%async_computation.1 | async-start | bytes 2654208 | tf_op jit(solution)/shard_map/all_gather | solution.py:1229
  8.1 5.2 copy-start.15
  9.0 7.5 %copy-start.17 = (f32[192,2,256]{2,1,0:T(2,128)S(1)}, f32[192,2,256]{2,1,0:T(2,128)}, u32[]{:S(2)}) copy-start(f32[192,2,256]{2,1,0:T(2,128)} %param.41) | copy-start | bytes 1179652
  10.7 6.6 copy-start.13
  181.9 358.4 %reduce-scatter.4.cloned.1.call-start = ((), (), s32[]{:S(2)}) async-start(), calls=%async_computation.2 | async-start | bytes 2654208
  185.8 3.0 copy-start.31
  185.8 3.0 copy-start.32
  185.9 3.0 copy-start.23
  188.2 107.7 %copy-start.20 = (f32[4096,8]{0,1:T(8,128)}, f32[4096,8]{0,1:T(8,128)S(1)}, u32[]{:S(2)}) copy-start(f32[4096,8]{0,1:T(8,128)S(1)} %copy.80) | copy-start | bytes 393220
  188.6 8.3 %copy-start.28 = (f32[512]{0:T(512)}, f32[512]{0:T(512)S(1)}, u32[]{:S(2)}) copy-start(f32[512]{0:T(512)S(1)} %add_rsqrt_fusion.1) | copy-start | bytes 6148
  188.7 8.3 %copy-start.4 = (f32[1,768]{1,0:T(1,128)}, f32[1,768]{1,0:T(1,128)S(1)}, u32[]{:S(2)}) copy-start(f32[1,768]{1,0:T(1,128)S(1)} %reshape.185.cxb_ref) | copy-start | bytes 9220
  188.8 8.1 %copy-start.5 = (f32[1,768]{1,0:T(1,128)}, f32[1,768]{1,0:T(1,128)S(1)}, u32[]{:S(2)}) copy-start(f32[1,768]{1,0:T(1,128)S(1)} %reshape_reshape.3.skip_ref) | copy-start | bytes 9220
  188.9 8.1 %copy-start.8 = (f32[1,128]{1,0:T(1,128)}, f32[1,128]{1,0:T(1,128)S(1)}, u32[]{:S(2)}) copy-start(f32[1,128]{1,0:T(1,128)S(1)} %get-tuple-element.197.alog_ref) | copy-start | bytes 1540
  188.9 8.1 %copy-start.9 = (f32[1,128]{1,0:T(1,128)}, f32[1,128]{1,0:T(1,128)S(1)}, u32[]{:S(2)}) copy-start(f32[1,128]{1,0:T(1,128)S(1)} %get-tuple-element.198.dtb_ref) | copy-start | bytes 1540
  188.9 8.1 %copy-start.6 = (f32[4,768]{1,0:T(4,128)S(1)}, f32[4,768]{1,0:T(4,128)}, u32[]{:S(2)}) copy-start(f32[4,768]{1,0:T(4,128)} %cx_ref.3) | copy-start | bytes 36868
  188.9 8.1 %copy-start.7 = (f32[4,256]{1,0:T(4,128)S(1)}, f32[4,256]{1,0:T(4,128)}, u32[]{:S(2)}) copy-start(f32[4,256]{1,0:T(4,128)} %cbc_ref.3) | copy-start | bytes 12292
  188.9 8.1 %copy-start.10 = (f32[256]{0:T(256)S(1)}, f32[256]{0:T(256)}, u32[]{:S(2)}) copy-start(f32[256]{0:T(256)} %param.34) | copy-start | bytes 3076
  197.0 15.4 %copy-start.22 = (f32[1536]{0:T(1024)S(1)}, f32[1536]{0:T(1024)}, u32[]{:S(2)}) copy-start(f32[1536]{0:T(1024)} %param.40) | copy-start | bytes 18436
  206.3 284.4 %copy-start = (f32[512,768]{1,0:T(8,128)}, f32[512,768]{1,0:T(8,128)S(1)}, u32[]{:S(2)}) copy-start(f32[512,768]{1,0:T(8,128)S(1)} %get-tuple-element.52.gated_ref) | copy-start | bytes 4718596
  355.6 3.1 copy-start.33
  501.5 21.1 %copy-start.25 = (f32[1,1536]{1,0:T(1,128)S(1)}, f32[1,1536]{1,0:T(1,128)}, u32[]{:S(2)}) copy-start(f32[1,1536]{1,0:T(1,128)} %get-tuple-element.66) | copy-start | bytes 18436
  523.3 3.8 copy-start.1
  523.3 3.8 copy-start.35
  527.2 2.9 copy-start.12
  527.2 2.9 copy-start.29
  527.2 2.9 copy-start.34
  527.2 8.5 %slice-start = ((s8[5898240]{0:T(1024)(128)(4,1)}), s8[4194304]{0:T(1024)(128)(4,1)S(1)}, s32[]{:S(2)}) async-start(s8[5898240]{0:T(1024)(128)(4,1)} %bitcast.83), calls=%async_computation.3 | async-start | bytes 8388608
  530.1 5.5 slice-start.1
  706.9 3.9 copy-start.19
  721.4 3.4 copy-start.16
  (8 other events, 13.1 us)
Sparse Core Ops, SparseCore 0:
  182.0 47.5 all-gather.1
  372.2 90.3 reduce-scatter.3

commit v11 on v10

--- a/solution.py
+++ b/solution.py
@@ -325,7 +325,7 @@
     greet(n_hi)
     streams = [
         weight_steps(n_hi, ins[i], outs[i], *sems[7 * i : 7 * i + 7]) for i in range(n)
-    ] + [gather_steps(n_hi, ins[n], outs[n], *sems[7 * n :], lo_first=(True, True))]
+    ] + [gather_steps(n_hi, ins[n], outs[n], *sems[7 * n :], lo_first=(True, False))]
     in_turns(*streams)
 
 
@@ -544,7 +544,7 @@
         return peer(hi, k, n_hi) * 2 + l
 
     if merged:
-        others = scatter_steps(n_hi, sends, p_ref, o_total, p_bufs, lo_first=(False, False))
+        others = scatter_steps(n_hi, sends, p_ref, o_total, p_bufs, lo_first=(False, True))
     else:
         others = iter(())
     next(others, None)

time: 739 us -> 735 us (level)
  no operation moved by 1% of the time
where the time goes in v11:
time: 735 us; the launch traced here: 729 us
  Pallas kernels  595 us (81%)
  matrix products  45.4 us (6%)
  local copies, waits for them, and re-layouts  42.9 us (6%)
  other arithmetic  17.9 us (2%)
  between operations  15.7 us (2%)
  blocking collectives  11.1 us (2%)
    pallas_call x1, Pallas kernels, tail(): pl.pallas_call(functools.partial(tail_kernel, n_hi, wide, bc_at, n, merge...  169 us
    pallas_call x1, Pallas kernels, start(): pl.pallas_call(functools.partial(start_kernel, n_hi, n), out_shape=[jax.S...  152 us
    pallas_call x1, Pallas kernels, turn(): pl.pallas_call(functools.partial(turn_kernel, n_hi), out_shape=(jax.Shape...  113 us
    pallas_call x1, Pallas kernels, middle(): pl.pallas_call(functools.partial(middle_kernel, n_hi), out_shape=(jax.Sha...  77.6 us
    pallas_call x1, Pallas kernels, experts(): pl.pallas_call(functools.partial(experts_kernel, n_dp, n_local, cap, chun...  58.7 us
    dot_general x13, matrix products, dotf(): return jnp.einsum(spec, a, b, preferred_element_type=F32)  45.4 us
    pallas_call x1, Pallas kernels, mixer_backward(): pl.pallas_call(functools.partial(mixer_backward_kernel, full_inner), out_...  17 us
  transfers between devices with their start and end apart: 2, of which 0 were waited for; matrix products, arithmetic and copies ran while one was open for 7% of the time, Pallas kernels for 38%

profile of v11, /device:TPU:9, one launch (start us, length us, event | category | flops | bytes accessed | tf_op | source)
XLA Modules:
  0.0 728.6 jit_solution(17545251116898314027)
XLA Ops:
  9.0 1.7 convert.34
  14.9 1.6 convert.38
  19.0 1.7 pad_maximum_fusion.4
  20.8 2.0 concatenate.38.refs_0_
  22.7 152.3 %start.1 = (bf16[8,2,96,1920]{3,2,1,0:T(8,128)(2,1)}, bf16[8,2,96,768]{3,2,1,0:T(8,128)(2,1)}, bf16[4096,1664]{1,0:T(8,128)(2,1)}) custom-call(bf16[2,96,1920]{2,1,0:T(8,128)(2,1)} %concatenate.38.refs_0_, bf16[2,96,768]{2,1,0:T(8,128)(2,1)} %bitcast.68, bf16[128,1664]{1,0:T(8,128)(2,1)} %constant_dynamic-slice_fusion.2.refs_2_), custom_call_target="tpu_custom_call" | custom-call | tf_op jit(solution)/shard_map/start/pallas_call | solution.py:336
  175.3 3.7 convert_add_fusion
  179.1 2.3 copy.80
  182.0 8.2 %fusion.20.first_ref = f32[512,1920]{1,0:T(8,128)} fusion(bf16[1536,1920]{1,0:T(8,128)(2,1)} %bitcast.82, bf16[512,1536]{1,0:T(8,128)(2,1)S(1)} %copy-done.11, f32[1536]{0:T(1024)S(1)} %copy-done.23, f32[512]{0:T(512)S(1)} %add_rsqrt_fusion.1), kind=kOutput, calls=%fused_computation.44 | convolution fusion | flops 3023044608 | bytes 11411456 | tf_op jit(solution)/shard_map/td,df->tf/dot_general | solution.py:29
  190.3 7.4 %mixer_forward.1 = (f32[512,768]{1,0:T(8,128)S(1)}, f32[512,768]{1,0:T(8,128)S(1)}, f32[512,1]{1,0:T(8,128)S(1)}, f32[6,1,128,128]{3,2,1,0:T(8,128)S(1)}) custom-call(f32[512,1920]{1,0:T(8,128)} %fusion.20.first_ref, f32[4,768]{1,0:T(4,128)S(1)} %copy-done.6, f32[1,768]{1,0:T(1,128)S(1)} %reshape.185.cxb_ref, f32[4,256]{1,0:T(4,128)S(1)} %copy-done.7, ...), custom_call_target="tpu_custom_call" | custom-call | flops 805306368 | bytes 9437184 | tf_op jit(solution)/shard_map/mixer_forward/pallas_call | solution.py:1114
  199.7 6.0 psum.14
  206.3 4.3 convolution_convert_fusion.4
  210.6 1.8 constant_dynamic-slice_fusion.1.x_ref.refs_4_
  212.4 77.6 %middle.1 = (bf16[4096,1536]{1,0:T(8,128)(2,1)}, f32[128,1536]{1,0:T(8,128)}) custom-call(bf16[4,128,1536]{2,1,0:T(8,128)(2,1)} %bitcast.63, bf16[128,1536]{1,0:T(8,128)(2,1)} %constant_dynamic-slice_fusion.1.x_ref.refs_4_, f32[1,1536]{1,0:T(1,128)} %reshape.192.gain_ref), custom_call_target="tpu_custom_call" | custom-call | tf_op jit(solution)/shard_map/middle/pallas_call | solution.py:246
  291.0 58.7 %experts.1 = (bf16[4096,1536]{1,0:T(8,128)(2,1)}, bf16[4096,1536]{1,0:T(8,128)(2,1)}, f32[24576,128]{1,0:T(8,128)}, f32[8,128,1536]{2,1,0:T(8,128)}) custom-call(s32[8,8,512]{2,1,0:T(8,128)} %fusion.12.pos_ref, f32[8,8,512]{2,1,0:T(8,128)} %bitcast.76, bf16[4096,1536]{1,0:T(8,128)(2,1)} %get-tuple-element.55.x_ref, ...), custom_call_target="tpu_custom_call" | custom-call | flops 40265318400 | bytes 88080384 | tf_op jit(solution)/shard_map/experts/pallas_call | solution.py:794
  349.7 3.1 fusion.8
  354.1 2.4 convolution_convert_fusion.2
  356.5 1.6 pad_maximum_fusion
  358.1 3.6 fusion.6.p_ref
  361.7 4.5 copy.86
  369.7 113.5 %turn.1 = (f32[128,1536]{1,0:T(8,128)}, f32[1,1536]{1,0:T(1,128)}, bf16[4,128,1536]{2,1,0:T(8,128)(2,1)}) custom-call(bf16[4096,1536]{1,0:T(8,128)(2,1)} %fusion.6.p_ref, f32[128,1536]{1,0:T(8,128)} %get-tuple-element.58.hidden_ref.refs_1_, bf16[128,1536]{1,0:T(8,128)(2,1)} %constant_dynamic-slice_fusion.g2_ref, f32[1,1536]{1,0:T(1,128)} %reshape.192.gain_ref), custom_call_target="tpu_custom_call" | custom-call | tf_op jit(solution)/shard_map/turn/pallas_call | solution.py:501
  483.2 4.8 multiply_reduce_fusion
  488.0 5.1 psum.15
  493.9 17.0 %mixer_backward.1 = (bf16[512,1920]{1,0:T(8,128)(2,1)}, f32[16,768]{1,0:T(8,128)}) custom-call(f32[512,1920]{1,0:T(8,128)} %fusion.20.first_ref, f32[512,768]{1,0:T(8,128)} %copy-done.2, f32[512,768]{1,0:T(8,128)} %copy-done, f32[512,768]{1,0:T(8,128)} %get-tuple-element.196.dyn_ref, f32[512,1]{1,0:T(8,128)} %copy.81.scale_ref, f32[512,1]{1,0:T(8,128)} %copy.82.product_ref, ...), custom_call_target="tpu_custom_call" | custom-call | flops 2415919104 | bytes 15728640 | tf_op jit(solution)/shard_map/mixer_backward/pallas_call | solution.py:1135
  515.7 3.8 fusion.4.refs_0_
  519.6 2.9 convolution_convert_fusion.1
  522.5 5.5 convolution_convert_fusion
  528.1 4.6 convolution_convert_fusion.3
  533.8 168.8 %tail.1 = (bf16[4,128,1536]{2,1,0:T(8,128)(2,1)}, bf16[4,128,1536]{2,1,0:T(8,128)(2,1)}, f32[16,1536]{1,0:T(8,128)}, f32[2,96,1920]{2,1,0:T(8,128)}, f32[2,96,768]{2,1,0:T(8,128)}) custom-call(bf16[4096,1536]{1,0:T(8,128)(2,1)} %fusion.4.refs_0_, f32[128,1536]{1,0:T(8,128)} %get-tuple-element.58.hidden_ref.refs_1_, bf16[4,128,1536]{2,1,0:T(8,128)(2,1)} %bitcast.64, ...), custom_call_target="tpu_custom_call" | custom-call | tf_op jit(solution)/shard_map/tail/pallas_call | solution.py:688
  703.9 1.6 slice.133
  708.4 3.5 bitcast_convert_fusion
  711.9 1.8 reshape.206
  717.9 2.7 copy.96
  (154 shorter events, 33.1 us)
Async XLA Ops:
  7.2 4.7 copy-start.18
  7.2 5.4 copy-start.21
  7.2 342.5 %all-gather.2.cloned.1.call-start = ((), (), s32[]{:S(2)}) async-start(), calls=%async_computation.1 | async-start | bytes 2654208 | tf_op jit(solution)/shard_map/all_gather | solution.py:1229
  8.1 5.2 copy-start.15
  9.0 7.5 %copy-start.17 = (f32[192,2,256]{2,1,0:T(2,128)S(1)}, f32[192,2,256]{2,1,0:T(2,128)}, u32[]{:S(2)}) copy-start(f32[192,2,256]{2,1,0:T(2,128)} %param.41) | copy-start | bytes 1179652
  10.7 6.6 copy-start.13
  175.1 357.6 %reduce-scatter.4.cloned.1.call-start = ((), (), s32[]{:S(2)}) async-start(), calls=%async_computation.2 | async-start | bytes 2654208
  179.0 2.9 copy-start.31
  179.0 2.9 copy-start.32
  179.1 2.9 copy-start.23
  181.3 108.7 %copy-start.20 = (f32[4096,8]{0,1:T(8,128)}, f32[4096,8]{0,1:T(8,128)S(1)}, u32[]{:S(2)}) copy-start(f32[4096,8]{0,1:T(8,128)S(1)} %copy.80) | copy-start | bytes 393220
  181.7 8.5 %copy-start.28 = (f32[512]{0:T(512)}, f32[512]{0:T(512)S(1)}, u32[]{:S(2)}) copy-start(f32[512]{0:T(512)S(1)} %add_rsqrt_fusion.1) | copy-start | bytes 6148
  181.8 8.4 %copy-start.4 = (f32[1,768]{1,0:T(1,128)}, f32[1,768]{1,0:T(1,128)S(1)}, u32[]{:S(2)}) copy-start(f32[1,768]{1,0:T(1,128)S(1)} %reshape.185.cxb_ref) | copy-start | bytes 9220
  181.9 8.3 %copy-start.5 = (f32[1,768]{1,0:T(1,128)}, f32[1,768]{1,0:T(1,128)S(1)}, u32[]{:S(2)}) copy-start(f32[1,768]{1,0:T(1,128)S(1)} %reshape_reshape.3.skip_ref) | copy-start | bytes 9220
  182.0 8.2 %copy-start.8 = (f32[1,128]{1,0:T(1,128)}, f32[1,128]{1,0:T(1,128)S(1)}, u32[]{:S(2)}) copy-start(f32[1,128]{1,0:T(1,128)S(1)} %get-tuple-element.197.alog_ref) | copy-start | bytes 1540
  182.0 8.2 %copy-start.9 = (f32[1,128]{1,0:T(1,128)}, f32[1,128]{1,0:T(1,128)S(1)}, u32[]{:S(2)}) copy-start(f32[1,128]{1,0:T(1,128)S(1)} %get-tuple-element.198.dtb_ref) | copy-start | bytes 1540
  182.0 8.2 %copy-start.6 = (f32[4,768]{1,0:T(4,128)S(1)}, f32[4,768]{1,0:T(4,128)}, u32[]{:S(2)}) copy-start(f32[4,768]{1,0:T(4,128)} %cx_ref.3) | copy-start | bytes 36868
  182.0 8.2 %copy-start.7 = (f32[4,256]{1,0:T(4,128)S(1)}, f32[4,256]{1,0:T(4,128)}, u32[]{:S(2)}) copy-start(f32[4,256]{1,0:T(4,128)} %cbc_ref.3) | copy-start | bytes 12292
  182.0 8.2 %copy-start.10 = (f32[256]{0:T(256)S(1)}, f32[256]{0:T(256)}, u32[]{:S(2)}) copy-start(f32[256]{0:T(256)} %param.34) | copy-start | bytes 3076
  190.3 15.5 %copy-start.22 = (f32[1536]{0:T(1024)S(1)}, f32[1536]{0:T(1024)}, u32[]{:S(2)}) copy-start(f32[1536]{0:T(1024)} %param.40) | copy-start | bytes 18436
  199.6 283.6 %copy-start = (f32[512,768]{1,0:T(8,128)}, f32[512,768]{1,0:T(8,128)S(1)}, u32[]{:S(2)}) copy-start(f32[512,768]{1,0:T(8,128)S(1)} %get-tuple-element.52.gated_ref) | copy-start | bytes 4718596
  349.7 3.1 copy-start.33
  493.9 21.1 %copy-start.25 = (f32[1,1536]{1,0:T(1,128)S(1)}, f32[1,1536]{1,0:T(1,128)}, u32[]{:S(2)}) copy-start(f32[1,1536]{1,0:T(1,128)} %get-tuple-element.66) | copy-start | bytes 18436
  515.7 3.8 copy-start.1
  515.7 3.8 copy-start.35
  519.6 2.9 copy-start.12
  519.6 2.9 copy-start.29
  519.6 2.9 copy-start.34
  519.6 8.5 %slice-start = ((s8[5898240]{0:T(1024)(128)(4,1)}), s8[4194304]{0:T(1024)(128)(4,1)S(1)}, s32[]{:S(2)}) async-start(s8[5898240]{0:T(1024)(128)(4,1)} %bitcast.83), calls=%async_computation.3 | async-start | bytes 8388608
  522.5 5.6 slice-start.1
  702.5 3.9 copy-start.19
  717.1 3.4 copy-start.16
  (8 other events, 12.8 us)
Sparse Core Ops, SparseCore 0:
  175.2 49.5 all-gather.1
  366.3 88.5 reduce-scatter.3
